TPU v7x, 32 devices: a whole 2x2x4 slice. The times are simulated.
32 devices in a mesh: grp: 4 (over x, core), seq: 8 (over z, y).
Axes of the slice: x: 2, y: 2, z: 4, core: 2. Of those that a mesh axis runs over, the one named last changes fastest.
Arguments:
- signal: float32 [64, 2048, 768], P('grp', 'seq'), may hold values from -36 to 36
- entry_gain: float32 [768], replicated
- entry_shift: float32 [768], replicated, may hold values from -3 to 3
- dilated_kernel: float32 [3, 768, 384], replicated
- middle_gain: float32 [384], replicated
- middle_shift: float32 [384], replicated, may hold values from -3 to 3
- pointwise_kernel: float32 [384, 768], replicated
- pointwise_bias: float32 [768], replicated, may hold values from -3 to 3
- lengths: int32 [64], replicated, may hold values from 128 to 1024, as said below
- assignment: int32 [4, 16], P('grp'), may hold values from 0 to 15, as said below
- cotangent: float32 [65536, 768], P(('grp', 'seq')), may hold values from -6 to 6
Outputs:
- activations: float32 [65536, 768], P(('grp', 'seq'))
- signal_gradient: float32 [64, 2048, 768], P('grp', 'seq')
- entry_gain_gradient: float32 [768], replicated
- entry_shift_gradient: float32 [768], replicated
- dilated_kernel_gradient: float32 [3, 768, 384], replicated
- middle_gain_gradient: float32 [384], replicated
- middle_shift_gradient: float32 [384], replicated
- pointwise_kernel_gradient: float32 [384, 768], replicated
- pointwise_bias_gradient: float32 [768], replicated
Inputs may be any that keep to these rules, and one draw needn't show every extreme that they name: `lengths`: valid rows of a window come first; some window is full with 1024 rows and some has exactly 128. `assignment`: each row lists the 16 windows of one group once.
All inputs are finite; a program needn't handle non-finite values.
Results may differ from a plain program's by a relative error of at most 0.0066.
Values may be sent and summed in bfloat16 or wider, within the bound.
No kernel may reach another device: no remote copies, remote signals or barrier semaphores. Data moves between devices by JAX's collectives and lax.ppermute only.
A program may use at most 128 MiB of HBM per device.

v0:
```python
import jax
import jax.numpy as jnp
from jax import lax
from jax.sharding import PartitionSpec as P

DILATION_STEP = 38
WINDOW_SPAN = 1024
HALF_WINDOW_ROWS = 512


EPSILON = 0.001


def from_partner(block, axis, bit):
    count = lax.axis_size(axis)
    route = []
    for low in range(count):
        high = low | 1 << bit
        if high != low and high < count:
            route += [(low, high), (high, low)]
    return lax.ppermute(block, axis, route)


def smooth(values):
    return jax.nn.gelu(values, approximate=True)


def moments(values, valid_mask, row_count):
    centre = lax.psum(jnp.sum(values * valid_mask, axis=(0, 1)), ("grp", "seq")) / row_count
    deviation = (values - centre) * valid_mask
    spread = lax.psum(jnp.sum(deviation * deviation, axis=(0, 1)), ("grp", "seq")) / row_count
    return (centre, lax.rsqrt(spread + EPSILON))


def extended(resident_rows, neighbour_border):
    position_count = resident_rows.shape[0]
    channel_width = resident_rows.shape[2]
    empty_row_block = jnp.zeros((position_count, DILATION_STEP, channel_width), resident_rows.dtype)
    bottom_portion = jnp.concatenate(
        [empty_row_block, resident_rows[:, :HALF_WINDOW_ROWS], neighbour_border[:, DILATION_STEP:]],
        axis=1,
    )
    top_portion = jnp.concatenate(
        [neighbour_border[:, :DILATION_STEP], resident_rows[:, HALF_WINDOW_ROWS:], empty_row_block],
        axis=1,
    )
    return jnp.stack([bottom_portion, top_portion], axis=1).reshape(
        2 * position_count, HALF_WINDOW_ROWS + 2 * DILATION_STEP, channel_width
    )


def per_device(
    signal,
    entry_gain,
    entry_shift,
    dilated_kernel,
    middle_gain,
    middle_shift,
    pointwise_kernel,
    pointwise_bias,
    lengths,
    assignment,
    cotangent,
):
    seq_count = lax.axis_size("seq")
    seq_place = lax.axis_index("seq")
    grp_place = lax.axis_index("grp")
    group_windows, segment, channel_width = signal.shape
    source_rows = segment // 2
    position_count = group_windows // seq_count
    bin_pairs = signal.reshape(group_windows, source_rows, 2, channel_width)
    first_bin = bin_pairs[:, :, 0]
    second_bin = bin_pairs[:, :, 1]
    take_first = first_bin >= second_bin
    group_lengths = lax.dynamic_slice_in_dim(lengths, grp_place * group_windows, group_windows)
    source_position = seq_place * source_rows + jnp.arange(source_rows, dtype=jnp.int32)
    source_valid = (source_position[None, :] < group_lengths[:, None]).astype(jnp.float32)[
        :, :, None
    ]
    pooled_low = (jnp.where(take_first, first_bin, second_bin) * source_valid).astype(jnp.bfloat16)
    window_order = assignment[0]
    upper_source = (seq_place >= seq_count // 2).astype(jnp.int32)
    targets = jnp.arange(seq_count, dtype=jnp.int32)
    slot_range = jnp.arange(position_count, dtype=jnp.int32)
    picked = window_order[
        (
            jnp.bitwise_xor(targets, upper_source)[:, None] * position_count + slot_range[None, :]
        ).reshape(-1)
    ]
    outgoing = jnp.take(pooled_low, picked, axis=0)
    arrived = lax.all_to_all(outgoing, "seq", split_axis=0, concat_axis=1, tiled=True)
    partner_place = jnp.bitwise_xor(seq_place, 1)
    own_windows = lax.dynamic_slice_in_dim(window_order, seq_place * position_count, position_count)
    partner_windows = lax.dynamic_slice_in_dim(
        window_order, partner_place * position_count, position_count
    )
    row_position = jnp.arange(WINDOW_SPAN, dtype=jnp.int32)
    limit_rows = jnp.where(
        row_position[None, :] < HALF_WINDOW_ROWS,
        jnp.take(group_lengths, own_windows)[:, None],
        jnp.take(group_lengths, partner_windows)[:, None],
    )
    valid_mask = (row_position[None, :] < limit_rows).astype(jnp.float32)[:, :, None]
    row_count = jnp.sum(lengths.astype(jnp.float32))
    pooled = arrived.astype(jnp.float32)
    entry_centre, entry_scale = moments(pooled, valid_mask, row_count)
    entry_norm = (pooled - entry_centre) * entry_scale
    entry_smooth, entry_back = jax.vjp(smooth, entry_norm * entry_gain + entry_shift)
    entry_activation = (entry_smooth * valid_mask).astype(jnp.bfloat16)
    kernel_low = dilated_kernel.astype(jnp.bfloat16)
    entry_border = from_partner(
        entry_activation[:, HALF_WINDOW_ROWS - DILATION_STEP : HALF_WINDOW_ROWS + DILATION_STEP],
        "seq",
        0,
    )
    entry_widened = extended(entry_activation, entry_border)
    dilated_out = jnp.zeros(
        (2 * position_count, HALF_WINDOW_ROWS, kernel_low.shape[2]), jnp.float32
    )
    for kernel_tap_index in range(3):
        displaced_rows = entry_widened[
            :,
            kernel_tap_index * DILATION_STEP : kernel_tap_index * DILATION_STEP + HALF_WINDOW_ROWS,
        ]
        dilated_out = dilated_out + jnp.einsum(
            "hrc,cf->hrf",
            displaced_rows,
            kernel_low[kernel_tap_index],
            preferred_element_type=jnp.float32,
        )
    dilated_out = dilated_out.reshape(position_count, WINDOW_SPAN, -1)
    middle_centre, middle_scale = moments(dilated_out, valid_mask, row_count)
    middle_norm = (dilated_out - middle_centre) * middle_scale
    middle_smooth, middle_back = jax.vjp(smooth, middle_norm * middle_gain + middle_shift)
    middle_act = (middle_smooth * valid_mask).astype(jnp.bfloat16)
    pointwise_low = pointwise_kernel.astype(jnp.bfloat16)
    mixed_out = jnp.einsum(
        "krf,fd->krd", middle_act, pointwise_low, preferred_element_type=jnp.float32
    )
    activations = (valid_mask * (pooled + mixed_out + pointwise_bias)).reshape(-1, channel_width)
    grad_block = cotangent.reshape(position_count, WINDOW_SPAN, channel_width) * valid_mask
    grad_mixed = grad_block.astype(jnp.bfloat16)
    bias_part = jnp.sum(grad_block, axis=(0, 1))
    pointwise_part = jnp.einsum(
        "krf,krd->fd", middle_act, grad_mixed, preferred_element_type=jnp.float32
    )
    grad_middle = jnp.einsum(
        "krd,fd->krf", grad_mixed, pointwise_low, preferred_element_type=jnp.float32
    )
    grad_middle_pre = middle_back(grad_middle * valid_mask)[0]
    middle_gain_part = jnp.sum(grad_middle_pre * middle_norm, axis=(0, 1))
    middle_shift_part = jnp.sum(grad_middle_pre, axis=(0, 1))
    (
        middle_gain_gradient,
        middle_shift_gradient,
        pointwise_kernel_gradient,
        pointwise_bias_gradient,
    ) = lax.psum((middle_gain_part, middle_shift_part, pointwise_part, bias_part), ("grp", "seq"))
    dilated_gradient = (
        middle_gain
        * middle_scale
        * (
            grad_middle_pre
            - (middle_shift_gradient + middle_norm * middle_gain_gradient) / row_count
        )
        * valid_mask
    )
    dilated_gradient = dilated_gradient.astype(jnp.bfloat16)
    border_gradient = from_partner(
        dilated_gradient[:, HALF_WINDOW_ROWS - DILATION_STEP : HALF_WINDOW_ROWS + DILATION_STEP],
        "seq",
        0,
    )
    grad_wide = extended(dilated_gradient, border_gradient)
    grad_halves = dilated_gradient.reshape(2 * position_count, HALF_WINDOW_ROWS, -1)
    kernel_pieces = []
    grad_entry = jnp.zeros((2 * position_count, HALF_WINDOW_ROWS, channel_width), jnp.float32)
    for kernel_tap_index in range(3):
        displaced_rows = entry_widened[
            :,
            kernel_tap_index * DILATION_STEP : kernel_tap_index * DILATION_STEP + HALF_WINDOW_ROWS,
        ]
        kernel_pieces.append(
            jnp.einsum(
                "hrc,hrf->cf", displaced_rows, grad_halves, preferred_element_type=jnp.float32
            )
        )
        backward_offset = (2 - kernel_tap_index) * DILATION_STEP
        grad_shifted = grad_wide[:, backward_offset : backward_offset + HALF_WINDOW_ROWS]
        grad_entry = grad_entry + jnp.einsum(
            "hrf,cf->hrc",
            grad_shifted,
            kernel_low[kernel_tap_index],
            preferred_element_type=jnp.float32,
        )
    kernel_part = jnp.stack(kernel_pieces)
    grad_entry = grad_entry.reshape(position_count, WINDOW_SPAN, channel_width)
    grad_entry_pre = entry_back(grad_entry * valid_mask)[0]
    entry_gain_part = jnp.sum(grad_entry_pre * entry_norm, axis=(0, 1))
    entry_shift_part = jnp.sum(grad_entry_pre, axis=(0, 1))
    entry_gain_gradient, entry_shift_gradient, dilated_kernel_gradient = lax.psum(
        (entry_gain_part, entry_shift_part, kernel_part), ("grp", "seq")
    )
    grad_pooled = (
        entry_gain
        * entry_scale
        * (grad_entry_pre - (entry_shift_gradient + entry_norm * entry_gain_gradient) / row_count)
        * valid_mask
        + grad_block
    )
    returned = lax.all_to_all(
        grad_pooled.astype(jnp.bfloat16), "seq", split_axis=1, concat_axis=0, tiled=True
    )
    inverse = (
        jnp.zeros((group_windows,), jnp.int32)
        .at[picked]
        .set(jnp.arange(group_windows, dtype=jnp.int32))
    )
    grad_source = jnp.take(returned, inverse, axis=0).astype(jnp.float32) * source_valid
    zero_part = jnp.zeros_like(grad_source)
    signal_gradient = jnp.stack(
        [
            jnp.where(take_first, grad_source, zero_part),
            jnp.where(take_first, zero_part, grad_source),
        ],
        axis=2,
    ).reshape(group_windows, segment, channel_width)
    return (
        activations,
        signal_gradient,
        entry_gain_gradient,
        entry_shift_gradient,
        dilated_kernel_gradient,
        middle_gain_gradient,
        middle_shift_gradient,
        pointwise_kernel_gradient,
        pointwise_bias_gradient,
    )


def solution(mesh):
    return jax.shard_map(
        per_device,
        mesh=mesh,
        in_specs=(
            P("grp", "seq", None),
            P(),
            P(),
            P(),
            P(),
            P(),
            P(),
            P(),
            P(),
            P("grp", None),
            P(("grp", "seq"), None),
        ),
        out_specs=(
            P(("grp", "seq"), None),
            P("grp", "seq", None),
            P(),
            P(),
            P(),
            P(),
            P(),
            P(),
            P(),
        ),
        check_vma=False,
    )
```

profile of v0, /device:TPU:17, one launch (start us, length us, event | category | flops | bytes accessed | tf_op | source)
XLA Modules:
  0.0 654.7 jit_solution(9878125855591612174)
XLA Ops:
  8.7 16.6 %copy.79 = f32[16,256,768]{2,0,1:T(8,128)} copy(f32[16,256,768]{2,1,0:T(8,128)} %param.15) | data formatting | bytes 25165824 | tf_op args[0]
  25.4 10.5 %fusion.86 = (f32[16,128,1,768]{3,0,2,1:T(8,128)}, f32[16,128,1,768]{3,0,2,1:T(8,128)}) fusion(f32[16,128,2,768]{3,0,2,1:T(8,128)} %bitcast.168), kind=kLoop, calls=%fused_computation.166 | loop fusion | bytes 25165824 | tf_op jit(solution)/shard_map/slice | solution.py:73
  36.1 11.4 %multiply_convert_fusion.1 = (bf16[16,128,768]{2,1,0:T(8,128)(2,1)}, pred[16,128,768]{2,1,0:T(8,128)(4,1)}) fusion(f32[16,128,1,768]{3,0,2,1:T(8,128)} %get-tuple-element.66, f32[16,128,1,768]{3,0,2,1:T(8,128)} %get-tuple-element.65, f32[16,128]{1,0:T(8,128)S(1)} %compare_convert_fusion.2), kind=kLoop, calls=%fused_computation.48 | loop fusion | flops 6291456 | bytes 17309696 | tf_op jit(solution)/shard_map/convert_element_type | solution.py:80
  47.5 2.6 gather_fusion.3
  52.1 5.7 all-to-all-start
  59.7 3.7 convert_element_type.105
  64.3 5.2 multiply_convert_fusion.2
  69.5 3.5 fusion.38
  73.1 51.6 %all-to-all-done = bf16[16,128,768]{2,1,0:T(8,128)(2,1)S(1)} async-done(((bf16[16,128,768]{2,1,0:T(8,128)(2,1)}), bf16[16,128,768]{2,1,0:T(8,128)(2,1)S(1)}, u32[]{:S(2)}, u32[]{:S(2)}) %all-to-all-start) | async-done | bytes 3145760 | tf_op jit(solution)/shard_map/all_to_all | solution.py:91
  125.4 41.5 %psum.77 = f32[768]{0:T(1024)S(1)} all-reduce(f32[768]{0:T(1024)S(1)} %multiply_reduce_fusion.2), channel_id=1, replica_groups=mesh['grp'=4,'seq'=8] {'grp','seq'}, use_global_device_ids=true, to_apply=%region_1.4 | all-reduce | flops 768 | bytes 6144 | tf_op jit(solution)/shard_map/psum | solution.py:29
  168.6 39.7 %psum.78 = f32[768]{0:T(1024)S(1)} all-reduce(f32[768]{0:T(1024)S(1)} %multiply_reduce_fusion.1), channel_id=1, replica_groups=mesh['grp'=4,'seq'=8] {'grp','seq'}, use_global_device_ids=true, to_apply=%region_4.7 | all-reduce | flops 768 | bytes 6144 | tf_op jit(solution)/shard_map/psum | solution.py:31
  210.4 3.4 multiply_convert_fusion
  215.3 4.3 collective-permute-done
  229.1 41.8 %psum.79 = f32[384]{0:T(512)S(1)} all-reduce(f32[384]{0:T(512)S(1)} %get-tuple-element.86), channel_id=1, replica_groups=mesh['grp'=4,'seq'=8] {'grp','seq'}, use_global_device_ids=true, to_apply=%region_6.9 | all-reduce | flops 384 | bytes 3072 | tf_op jit(solution)/shard_map/psum | solution.py:29
  272.0 38.9 %psum.80 = f32[384]{0:T(512)S(1)} all-reduce(f32[384]{0:T(512)S(1)} %multiply_reduce_fusion.5), channel_id=1, replica_groups=mesh['grp'=4,'seq'=8] {'grp','seq'}, use_global_device_ids=true, to_apply=%region_8.11 | all-reduce | flops 384 | bytes 3072 | tf_op jit(solution)/shard_map/psum | solution.py:31
  311.6 6.1 fusion.81
  317.6 41.3 %all-reduce.1 = (f32[384]{0:T(512)S(1)}, f32[384]{0:T(512)S(1)}) all-reduce(f32[384]{0:T(512)S(1)} %get-tuple-element.50, f32[384]{0:T(512)S(1)} %get-tuple-element.49), channel_id=1, replica_groups=mesh['grp'=4,'seq'=8] {'grp','seq'}, use_global_device_ids=true, to_apply=%region_12.15 | all-reduce | flops 768 | bytes 6144 | tf_op jit(solution)/shard_map/psum | solution.py:158
  358.9 3.0 multiply_convert_fusion.5
  371.5 8.2 %fusion.80 = (f32[768]{0:T(1024)S(1)}, f32[768]{0:T(1024)S(1)}, f32[4,512,768]{2,1,0:T(8,128)}) fusion(f32[768]{0:T(1024)S(1)} %get-tuple-element.59, f32[4,512,768]{2,1,0:T(8,128)S(1)} %bitcast.163, f32[768]{0:T(1024)S(1)} %broadcast_divide_fusion, f32[768]{0:T(1024)S(1)} %copy-done.15, f32[768]{0:T(1024)S(1)} %copy-done.13, f32[4,512]{1,0:T(4,128)S(1)} %fusion.74, ...), kind=kOutput, calls=%fused_computation.162 | convolution fusion | flops 1253571072 | bytes 27359232 | tf_op jit(solution)/shard_map/hrf,cf->hrc/dot_general | solution.py:190
  379.7 40.8 %all-reduce = (f32[768]{0:T(1024)S(1)}, f32[768]{0:T(1024)S(1)}, f32[768]{0:T(1024)}) all-reduce(f32[768]{0:T(1024)S(1)} %get-tuple-element.48, f32[768]{0:T(1024)S(1)} %get-tuple-element.47, f32[768]{0:T(1024)S(1)} %get-tuple-element.68), channel_id=1, replica_groups=mesh['grp'=4,'seq'=8] {'grp','seq'}, use_global_device_ids=true, to_apply=%region_16.19 | all-reduce | flops 2304 | bytes 18432 | tf_op jit(solution)/shard_map/psum | solution.py:201
  420.5 11.1 %fusion.10 = bf16[2,1024,768]{2,1,0:T(8,128)(2,1)S(1)} fusion(f32[2,1024,768]{2,1,0:T(8,128)} %bitcast.164, f32[2,8,128,768]{3,2,1,0:T(8,128)} %copy-done.1, f32[]{:T(128)} %convert_reduce_fusion, f32[768]{0:T(1024)S(1)} %get-tuple-element.95, f32[768]{0:T(1024)S(1)} %get-tuple-element.96, f32[768]{0:T(1024)S(1)} %get-tuple-element.58, ...), kind=kLoop, calls=%fused_computation.21 | loop fusion | flops 51904512 | bytes 22049796 | tf_op jit(solution)/shard_map/convert_element_type | solution.py:212
  431.6 5.0 copy.86
  436.6 6.9 %all-to-all-start.1 = ((bf16[2,1024,768]{2,0,1:T(2,128)(2,1)}), bf16[2,1024,768]{2,0,1:T(2,128)(2,1)}, u32[]{:S(2)}, u32[]{:S(2)}) async-start(bf16[2,1024,768]{2,0,1:T(2,128)(2,1)} %copy.86), calls=%async_computation.1 | async-start | bytes 6291456 | tf_op jit(solution)/shard_map/all_to_all | solution.py:211
  443.5 4.3 fusion.60
  459.5 7.3 %fusion.19 = f32[2,1024,768]{2,1,0:T(8,128)} fusion(f32[2,8,128,768]{3,2,1,0:T(8,128)} %copy-done.1, f32[768]{0:T(1024)S(1)} %copy-done.17, f32[2,1024]{1,0:T(2,128)S(1)} %compare_convert_fusion.1, bf16[2,1024,384]{2,1,0:T(8,128)(2,1)S(1)} %copy-done.5, f32[384,768]{1,0:T(8,128)S(1)} %copy-done.7), kind=kOutput, calls=%fused_computation.36 | convolution fusion | flops 1212973056 | bytes 15346688 | tf_op jit(solution)/shard_map/krf,fd->krd/dot_general | solution.py:137
  466.9 60.3 %all-to-all-done.1 = bf16[2,1024,768]{2,0,1:T(2,128)(2,1)} async-done(((bf16[2,1024,768]{2,0,1:T(2,128)(2,1)}), bf16[2,1024,768]{2,0,1:T(2,128)(2,1)}, u32[]{:S(2)}, u32[]{:S(2)}) %all-to-all-start.1) | async-done | bytes 3145760 | tf_op jit(solution)/shard_map/all_to_all | solution.py:211
  532.2 5.3 select_bitcast_fusion.1
  537.5 9.1 %pad_maximum_fusion = f32[16,128,2,768]{3,1,0,2:T(8,128)} fusion(f32[16,128,1,768]{3,1,0,2:T(8,128)} %get-tuple-element.70, f32[16,128,1,768]{3,1,0,2:T(8,128)S(1)} %get-tuple-element.69), kind=kLoop, calls=%fused_computation.6 | loop fusion | flops 3145728 | bytes 25165824 | tf_op jit(solution)/shard_map/stack | solution.py:221
  546.6 16.6 %copy.89 = f32[16,128,2,768]{3,0,2,1:T(8,128)} copy(f32[16,128,2,768]{3,1,0,2:T(8,128)} %pad_maximum_fusion) | data formatting | bytes 25165824 | tf_op jit(solution)/shard_map/stack | solution.py:221
  563.2 16.9 %copy.94 = f32[16,256,768]{2,1,0:T(8,128)} copy(f32[16,256,768]{2,0,1:T(8,128)} %bitcast.169) | data formatting | bytes 25165824
  580.1 62.4 %all-reduce.5.cloned.1.call-done = (f32[3,768,384]{2,1,0:T(8,128)}, f32[384,768]{1,0:T(8,128)}) async-done(((f32[3,768,384]{2,1,0:T(8,128)}, f32[384,768]{1,0:T(8,128)}), (f32[3,768,384]{2,1,0:T(8,128)}, f32[384,768]{1,0:T(8,128)})) %all-reduce.5.cloned.1.call-update) | async-done | bytes 4718608 | tf_op jit(solution)/shard_map/psum | solution.py:201
  642.5 4.1 copy.127
  (144 shorter events, 50.6 us)
Async XLA Ops:
  25.4 10.5 %copy-start.22 = (s32[64]{0:T(128)S(1)}, s32[64]{0:T(128)}, u32[]{:S(2)}) copy-start(s32[64]{0:T(128)} %param.23) | copy-start | bytes 772
  52.1 5.8 copy-start
  52.1 72.6 %all-to-all-start = ((bf16[16,128,768]{2,1,0:T(8,128)(2,1)}), bf16[16,128,768]{2,1,0:T(8,128)(2,1)S(1)}, u32[]{:S(2)}, u32[]{:S(2)}) async-start(bf16[16,128,768]{2,1,0:T(8,128)(2,1)} %broadcast_select_fusion.1), calls=%async_computation | async-start | bytes 6291456 | tf_op jit(solution)/shard_map/all_to_all | solution.py:91
  59.7 9.9 %slice-start.2 = ((s8[6291456]{0:T(1024)(128)(4,1)}), s8[4194304]{0:T(1024)(128)(4,1)S(1)}, s32[]{:S(2)}) async-start(s8[6291456]{0:T(1024)(128)(4,1)} %bitcast.165), calls=%async_computation.5 | async-start | bytes 8388608
  64.3 5.2 slice-start.3
  64.3 5.2 copy-start.6
  209.0 0.7 copy-start.13
  209.0 1.3 copy-start.15
  209.7 4.1 copy-start.1
  213.9 5.8 collective-permute-start
  221.2 2.1 copy-start.10
  221.5 5.5 copy-start.8
  229.0 81.9 %copy-start.14 = (f32[384]{0:T(512)S(1)}, f32[384]{0:T(512)}, u32[]{:S(2)}) copy-start(f32[384]{0:T(512)} %param.19) | copy-start | bytes 4612
  229.1 82.5 %copy-start.16 = (f32[384]{0:T(512)S(1)}, f32[384]{0:T(512)}, u32[]{:S(2)}) copy-start(f32[384]{0:T(512)} %param.20) | copy-start | bytes 4612
  358.9 3.1 copy-start.20
  358.9 3.1 copy-start.21
  362.0 1.5 copy-start.3
  362.0 3.8 collective-permute-start.1
  366.3 1.5 copy-start.11
  366.5 4.9 slice-start
  367.8 3.7 slice-start.1
  420.5 11.1 %copy-start.18 = (f32[768]{0:T(1024)}, f32[768]{0:T(1024)S(1)}, u32[]{:S(2)}) copy-start(f32[768]{0:T(1024)S(1)} %get-tuple-element.95) | copy-start | bytes 9220
  420.5 11.1 %copy-start.19 = (f32[768]{0:T(1024)}, f32[768]{0:T(1024)S(1)}, u32[]{:S(2)}) copy-start(f32[768]{0:T(1024)S(1)} %get-tuple-element.96) | copy-start | bytes 9220
  436.6 90.6 %all-to-all-start.1 = ((bf16[2,1024,768]{2,0,1:T(2,128)(2,1)}), bf16[2,1024,768]{2,0,1:T(2,128)(2,1)}, u32[]{:S(2)}, u32[]{:S(2)}) async-start(bf16[2,1024,768]{2,0,1:T(2,128)(2,1)} %copy.86), calls=%async_computation.1 | async-start | bytes 6291456 | tf_op jit(solution)/shard_map/all_to_all | solution.py:211
  443.4 199.0 %all-reduce.5.cloned.1.call-start = ((), (), s32[]{:S(2)}) async-start(), calls=%async_computation.2 | async-start | bytes 9437184 | tf_op jit(solution)/shard_map/psum | solution.py:201
  443.4 4.3 copy-start.4
  443.5 4.3 copy-start.9
  453.5 1.9 copy-start.2
  457.8 1.4 copy-start.5
  457.8 1.7 copy-start.7
  457.8 1.7 copy-start.17
  642.5 4.1 copy-start.12
Sparse Core Ops, SparseCore 0:
  457.9 184.4 all-reduce.4
where the time goes:
time: 668 us; the launch traced here: 655 us
  blocking collectives  244 us (37%)
  waiting for transfers between devices  181 us (27%)
  local copies, waits for them, and re-layouts  88.4 us (13%)
  other arithmetic  72.6 us (11%)
  matrix products  38.7 us (6%)
  starting transfers between devices  15.3 us (2%)
  between operations  14.9 us (2%)
    psum x2, blocking collectives, moments(): lax.psum(jnp.sum(values * valid_mask, axis=(0, 1)), ('grp', 'seq'))  83.3 us
    psum x2, blocking collectives, moments(): lax.psum(jnp.sum(deviation * deviation, axis=(0, 1)), ('grp', 'seq'))  78.6 us
    psum x1, waiting for transfers between devices, per_device(): lax.psum((entry_gain_part, entry_shift_part, kernel_part), ('grp', 'seq'))  62.4 us
    all_to_all x1, waiting for transfers between devices, per_device(): lax.all_to_all(grad_pooled.astype(jnp.bfloat16), 'seq', split_axis=1, con...  60.3 us
    all_to_all x1, waiting for transfers between devices, per_device(): lax.all_to_all(outgoing, 'seq', split_axis=0, concat_axis=1, tiled=True)  51.6 us
    unnamed x61, local copies, waits for them, and re-layouts  43.3 us
    psum x1, blocking collectives, per_device(): lax.psum((middle_gain_part, middle_shift_part, pointwise_part, bias_part)...  41.3 us
    psum x1, blocking collectives, per_device(): lax.psum((entry_gain_part, entry_shift_part, kernel_part), ('grp', 'seq'))  40.8 us
  transfers between devices with their start and end apart: 5, of which 5 were waited for; matrix products, arithmetic and copies ran while one was open for 14% of the time, Pallas kernels for 0%

commit v1 on v0

--- a/solution.py
+++ b/solution.py
@@ -1,6 +1,8 @@
 import jax
 import jax.numpy as jnp
 from jax import lax
+from jax.experimental import pallas as pl
+from jax.experimental.pallas import tpu as pltpu
 from jax.sharding import PartitionSpec as P
 
 DILATION_STEP = 38
@@ -11,25 +13,183 @@
 EPSILON = 0.001
 
 
-def from_partner(block, axis, bit):
+def from_partner(block, axis, mask):
     count = lax.axis_size(axis)
-    route = []
-    for low in range(count):
-        high = low | 1 << bit
-        if high != low and high < count:
-            route += [(low, high), (high, low)]
-    return lax.ppermute(block, axis, route)
+    return lax.ppermute(block, axis, [(place, place ^ mask) for place in range(count)])
+
+
+def exchange_steps():
+    steps = []
+    for axis in ("grp", "seq"):
+        mask = 1
+        while mask < lax.axis_size(axis):
+            steps.append((axis, mask))
+            mask *= 2
+    return steps
+
+
+def total(values):
+    for axis, mask in exchange_steps():
+        values = values + from_partner(values, axis, mask)
+    return values
+
+
+def merge_moments(left, right):
+    left_count, right_count = left[2:3], right[2:3]
+    gap = left[0:1] / jnp.maximum(left_count, 1.0) - right[0:1] / jnp.maximum(right_count, 1.0)
+    weight = left_count * right_count / jnp.maximum(left_count + right_count, 1.0)
+    spread = left[1:2] + right[1:2] + gap * gap * weight
+    return jnp.concatenate([left[0:1] + right[0:1], spread, left_count + right_count], axis=0)
+
+
+def global_moments(local_sum, local_spread, local_count, row_count):
+    packed = jnp.stack(
+        [local_sum, local_spread, jnp.broadcast_to(local_count, local_sum.shape)], axis=0
+    )
+    for axis, mask in exchange_steps():
+        packed = merge_moments(packed, from_partner(packed, axis, mask))
+    return packed[0] / row_count, lax.rsqrt(packed[1] / row_count + EPSILON)
+
+
+def total_of_large(buffer):
+    steps = exchange_steps()
+    marks = []
+    for axis, mask in steps:
+        half = buffer.shape[0] // 2
+        upper = (lax.axis_index(axis) // mask) % 2
+        kept = lax.dynamic_slice_in_dim(buffer, upper * half, half)
+        sent = lax.dynamic_slice_in_dim(buffer, (1 - upper) * half, half)
+        buffer = kept + from_partner(sent, axis, mask)
+        marks.append(upper)
+    for (axis, mask), upper in zip(reversed(steps), reversed(marks)):
+        other = from_partner(buffer, axis, mask)
+        buffer = jnp.where(
+            upper == 0,
+            jnp.concatenate([buffer, other], axis=0),
+            jnp.concatenate([other, buffer], axis=0),
+        )
+    return buffer
+
+
+LANES = 128
+
+
+def pool_kernel(order_ref, count_ref, before_ref, *refs):
+    pooled_ref, first_ref, moments_ref = refs[-3:]
+    place = pl.program_id(0)
+    rows = pooled_ref.shape[1]
+    count = count_ref[place]
+    count_f = count.astype(jnp.float32)
+    before_f = before_ref[place].astype(jnp.float32)
+    weight = before_f * count_f / jnp.maximum(before_f + count_f, 1.0)
+    inside = lax.broadcasted_iota(jnp.int32, (rows, LANES), 0) < count
+
+    @pl.when(place == 0)
+    def _():
+        moments_ref[...] = jnp.zeros_like(moments_ref)
+
+    for column, signal_ref in enumerate(refs[:-3]):
+        lanes = slice(column * LANES, (column + 1) * LANES)
+        first_bin = signal_ref[0, pl.ds(0, rows, stride=2), :]
+        second_bin = signal_ref[0, pl.ds(1, rows, stride=2), :]
+        take_first = first_bin >= second_bin
+        raw = jnp.where(take_first, first_bin, second_bin)
+        first_ref[0, :, lanes] = jnp.where(take_first, 1.0, 0.0).astype(jnp.bfloat16)
+        low = jnp.where(inside, raw, 0.0).astype(jnp.bfloat16)
+        pooled_ref[0, :, lanes] = low
+        values = low.astype(jnp.float32)
+        block_sum = jnp.sum(values, axis=0, keepdims=True)
+        block_mean = block_sum / jnp.maximum(count_f, 1.0)
+        deviation = jnp.where(inside, values - block_mean, 0.0)
+        block_spread = jnp.sum(deviation * deviation, axis=0, keepdims=True)
+        held_sum = moments_ref[0:1, lanes]
+        gap = held_sum / jnp.maximum(before_f, 1.0) - block_mean
+        moments_ref[0:1, lanes] = held_sum + block_sum
+        moments_ref[1:2, lanes] = moments_ref[1:2, lanes] + block_spread + gap * gap * weight
+
+
+def pool(signal, picked, counts, before):
+    windows, segment, width = signal.shape
+    rows = segment // 2
+    columns = width // LANES
+    return pl.pallas_call(
+        pool_kernel,
+        grid_spec=pltpu.PrefetchScalarGridSpec(
+            num_scalar_prefetch=3,
+            grid=(windows,),
+            in_specs=[
+                pl.BlockSpec((1, segment, LANES), lambda p, o, c, b, column=column: (o[p], 0, column))
+                for column in range(columns)
+            ],
+            out_specs=[
+                pl.BlockSpec((1, rows, width), lambda p, o, c, b: (p, 0, 0)),
+                pl.BlockSpec((1, rows, width), lambda p, o, c, b: (p, 0, 0)),
+                pl.BlockSpec((2, width), lambda p, o, c, b: (0, 0)),
+            ],
+        ),
+        out_shape=[
+            jax.ShapeDtypeStruct((windows, rows, width), jnp.bfloat16),
+            jax.ShapeDtypeStruct((windows, rows, width), jnp.bfloat16),
+            jax.ShapeDtypeStruct((2, width), jnp.float32),
+        ],
+        compiler_params=pltpu.CompilerParams(vmem_limit_bytes=16 << 20),
+        cost_estimate=pl.CostEstimate(
+            flops=10 * windows * rows * width,
+            bytes_accessed=windows * rows * width * 12,
+            transcendentals=0,
+        ),
+        name="pool",
+    )(picked, counts, before, *([signal] * columns))
+
+
+def unpool_kernel(
+    order_ref, count_ref, returned_ref, pooled_ref, first_ref, terms_ref, out_ref
+):
+    place = pl.program_id(0)
+    rows, width = pooled_ref.shape[1:]
+    inside = lax.broadcasted_iota(jnp.int32, (rows, width), 0) < count_ref[place]
+    centred = pooled_ref[0].astype(jnp.float32) - terms_ref[0:1]
+    gradient = returned_ref[0].astype(jnp.float32) - (terms_ref[1:2] + centred * terms_ref[2:3])
+    gradient = jnp.where(inside, gradient, 0.0)
+    chosen = first_ref[0].astype(jnp.float32) > 0.5
+    pair = jnp.concatenate(
+        [
+            jnp.where(chosen, gradient, 0.0).astype(jnp.bfloat16),
+            jnp.where(chosen, 0.0, gradient).astype(jnp.bfloat16),
+        ],
+        axis=0,
+    )
+    bin_index = lax.broadcasted_iota(jnp.int32, (2 * rows, 2 * rows), 0)
+    pair_index = lax.broadcasted_iota(jnp.int32, (2 * rows, 2 * rows), 1)
+    source = bin_index // 2 + (bin_index % 2) * rows
+    spread = jnp.where(pair_index == source, 1.0, 0.0).astype(jnp.bfloat16)
+    out_ref[0] = jnp.dot(spread, pair, preferred_element_type=jnp.float32)
+
+
+def unpool(returned, pooled, first, terms, picked, counts):
+    windows, rows, width = returned.shape
+    block = pl.BlockSpec((1, rows, width), lambda p, o, c: (p, 0, 0))
+    return pl.pallas_call(
+        unpool_kernel,
+        grid_spec=pltpu.PrefetchScalarGridSpec(
+            num_scalar_prefetch=2,
+            grid=(windows,),
+            in_specs=[block, block, block, pl.BlockSpec((3, width), lambda p, o, c: (0, 0))],
+            out_specs=pl.BlockSpec((1, 2 * rows, width), lambda p, o, c: (o[p], 0, 0)),
+        ),
+        out_shape=jax.ShapeDtypeStruct((windows, 2 * rows, width), jnp.float32),
+        compiler_params=pltpu.CompilerParams(vmem_limit_bytes=16 << 20),
+        cost_estimate=pl.CostEstimate(
+            flops=10 * windows * rows * width,
+            bytes_accessed=windows * rows * width * 14,
+            transcendentals=0,
+        ),
+        name="unpool",
+    )(picked, counts, returned, pooled, first, terms)
 
 
 def smooth(values):
     return jax.nn.gelu(values, approximate=True)
-
-
-def moments(values, valid_mask, row_count):
-    centre = lax.psum(jnp.sum(values * valid_mask, axis=(0, 1)), ("grp", "seq")) / row_count
-    deviation = (values - centre) * valid_mask
-    spread = lax.psum(jnp.sum(deviation * deviation, axis=(0, 1)), ("grp", "seq")) / row_count
-    return (centre, lax.rsqrt(spread + EPSILON))
 
 
 def extended(resident_rows, neighbour_border):
@@ -68,16 +228,7 @@
     group_windows, segment, channel_width = signal.shape
     source_rows = segment // 2
     position_count = group_windows // seq_count
-    bin_pairs = signal.reshape(group_windows, source_rows, 2, channel_width)
-    first_bin = bin_pairs[:, :, 0]
-    second_bin = bin_pairs[:, :, 1]
-    take_first = first_bin >= second_bin
     group_lengths = lax.dynamic_slice_in_dim(lengths, grp_place * group_windows, group_windows)
-    source_position = seq_place * source_rows + jnp.arange(source_rows, dtype=jnp.int32)
-    source_valid = (source_position[None, :] < group_lengths[:, None]).astype(jnp.float32)[
-        :, :, None
-    ]
-    pooled_low = (jnp.where(take_first, first_bin, second_bin) * source_valid).astype(jnp.bfloat16)
     window_order = assignment[0]
     upper_source = (seq_place >= seq_count // 2).astype(jnp.int32)
     targets = jnp.arange(seq_count, dtype=jnp.int32)
@@ -87,8 +238,16 @@
             jnp.bitwise_xor(targets, upper_source)[:, None] * position_count + slot_range[None, :]
         ).reshape(-1)
     ]
-    outgoing = jnp.take(pooled_low, picked, axis=0)
+    counts = jnp.clip(group_lengths[picked] - seq_place * source_rows, 0, source_rows)
+    before = jnp.cumsum(counts) - counts
+    row_count = jnp.sum(lengths.astype(jnp.float32))
+
+    outgoing, first_chosen, entry_local = pool(signal, picked, counts, before)
     arrived = lax.all_to_all(outgoing, "seq", split_axis=0, concat_axis=1, tiled=True)
+    entry_centre, entry_scale = global_moments(
+        entry_local[0], entry_local[1], jnp.sum(counts).astype(jnp.float32), row_count
+    )
+
     partner_place = jnp.bitwise_xor(seq_place, 1)
     own_windows = lax.dynamic_slice_in_dim(window_order, seq_place * position_count, position_count)
     partner_windows = lax.dynamic_slice_in_dim(
@@ -101,9 +260,8 @@
         jnp.take(group_lengths, partner_windows)[:, None],
     )
     valid_mask = (row_position[None, :] < limit_rows).astype(jnp.float32)[:, :, None]
-    row_count = jnp.sum(lengths.astype(jnp.float32))
+    resident_count = jnp.sum(valid_mask)
     pooled = arrived.astype(jnp.float32)
-    entry_centre, entry_scale = moments(pooled, valid_mask, row_count)
     entry_norm = (pooled - entry_centre) * entry_scale
     entry_smooth, entry_back = jax.vjp(smooth, entry_norm * entry_gain + entry_shift)
     entry_activation = (entry_smooth * valid_mask).astype(jnp.bfloat16)
@@ -111,7 +269,7 @@
     entry_border = from_partner(
         entry_activation[:, HALF_WINDOW_ROWS - DILATION_STEP : HALF_WINDOW_ROWS + DILATION_STEP],
         "seq",
-        0,
+        1,
     )
     entry_widened = extended(entry_activation, entry_border)
     dilated_out = jnp.zeros(
@@ -129,7 +287,14 @@
             preferred_element_type=jnp.float32,
         )
     dilated_out = dilated_out.reshape(position_count, WINDOW_SPAN, -1)
-    middle_centre, middle_scale = moments(dilated_out, valid_mask, row_count)
+    middle_sum = jnp.sum(dilated_out * valid_mask, axis=(0, 1))
+    middle_deviation = (dilated_out - middle_sum / jnp.maximum(resident_count, 1.0)) * valid_mask
+    middle_centre, middle_scale = global_moments(
+        middle_sum,
+        jnp.sum(middle_deviation * middle_deviation, axis=(0, 1)),
+        resident_count,
+        row_count,
+    )
     middle_norm = (dilated_out - middle_centre) * middle_scale
     middle_smooth, middle_back = jax.vjp(smooth, middle_norm * middle_gain + middle_shift)
     middle_act = (middle_smooth * valid_mask).astype(jnp.bfloat16)
@@ -142,20 +307,21 @@
     grad_mixed = grad_block.astype(jnp.bfloat16)
     bias_part = jnp.sum(grad_block, axis=(0, 1))
     pointwise_part = jnp.einsum(
-        "krf,krd->fd", middle_act, grad_mixed, preferred_element_type=jnp.float32
+        "krd,krf->df", grad_mixed, middle_act, preferred_element_type=jnp.float32
     )
     grad_middle = jnp.einsum(
         "krd,fd->krf", grad_mixed, pointwise_low, preferred_element_type=jnp.float32
     )
     grad_middle_pre = middle_back(grad_middle * valid_mask)[0]
-    middle_gain_part = jnp.sum(grad_middle_pre * middle_norm, axis=(0, 1))
-    middle_shift_part = jnp.sum(grad_middle_pre, axis=(0, 1))
-    (
-        middle_gain_gradient,
-        middle_shift_gradient,
-        pointwise_kernel_gradient,
-        pointwise_bias_gradient,
-    ) = lax.psum((middle_gain_part, middle_shift_part, pointwise_part, bias_part), ("grp", "seq"))
+    middle_sums = total(
+        jnp.stack(
+            [
+                jnp.sum(grad_middle_pre * middle_norm, axis=(0, 1)),
+                jnp.sum(grad_middle_pre, axis=(0, 1)),
+            ]
+        )
+    )
+    middle_gain_gradient, middle_shift_gradient = middle_sums[0], middle_sums[1]
     dilated_gradient = (
         middle_gain
         * middle_scale
@@ -169,7 +335,7 @@
     border_gradient = from_partner(
         dilated_gradient[:, HALF_WINDOW_ROWS - DILATION_STEP : HALF_WINDOW_ROWS + DILATION_STEP],
         "seq",
-        0,
+        1,
     )
     grad_wide = extended(dilated_gradient, border_gradient)
     grad_halves = dilated_gradient.reshape(2 * position_count, HALF_WINDOW_ROWS, -1)
@@ -193,38 +359,32 @@
             kernel_low[kernel_tap_index],
             preferred_element_type=jnp.float32,
         )
-    kernel_part = jnp.stack(kernel_pieces)
     grad_entry = grad_entry.reshape(position_count, WINDOW_SPAN, channel_width)
     grad_entry_pre = entry_back(grad_entry * valid_mask)[0]
-    entry_gain_part = jnp.sum(grad_entry_pre * entry_norm, axis=(0, 1))
-    entry_shift_part = jnp.sum(grad_entry_pre, axis=(0, 1))
-    entry_gain_gradient, entry_shift_gradient, dilated_kernel_gradient = lax.psum(
-        (entry_gain_part, entry_shift_part, kernel_part), ("grp", "seq")
-    )
-    grad_pooled = (
-        entry_gain
-        * entry_scale
-        * (grad_entry_pre - (entry_shift_gradient + entry_norm * entry_gain_gradient) / row_count)
-        * valid_mask
-        + grad_block
-    )
-    returned = lax.all_to_all(
-        grad_pooled.astype(jnp.bfloat16), "seq", split_axis=1, concat_axis=0, tiled=True
-    )
-    inverse = (
-        jnp.zeros((group_windows,), jnp.int32)
-        .at[picked]
-        .set(jnp.arange(group_windows, dtype=jnp.int32))
-    )
-    grad_source = jnp.take(returned, inverse, axis=0).astype(jnp.float32) * source_valid
-    zero_part = jnp.zeros_like(grad_source)
-    signal_gradient = jnp.stack(
-        [
-            jnp.where(take_first, grad_source, zero_part),
-            jnp.where(take_first, zero_part, grad_source),
-        ],
-        axis=2,
-    ).reshape(group_windows, segment, channel_width)
+    entry_sums = total(
+        jnp.stack(
+            [
+                jnp.sum(grad_entry_pre * entry_norm, axis=(0, 1)),
+                jnp.sum(grad_entry_pre, axis=(0, 1)),
+                bias_part,
+            ]
+        )
+    )
+    entry_gain_gradient, entry_shift_gradient = entry_sums[0], entry_sums[1]
+    pointwise_bias_gradient = entry_sums[2]
+    sent_back = (entry_gain * entry_scale * grad_entry_pre + grad_block).astype(jnp.bfloat16)
+    sent_back = sent_back.reshape(position_count, seq_count, source_rows, channel_width)
+    sent_back = jnp.swapaxes(sent_back, 0, 1).reshape(group_windows, source_rows, channel_width)
+    returned = lax.all_to_all(sent_back, "seq", split_axis=0, concat_axis=0, tiled=True)
+    factor = entry_gain * entry_scale / row_count
+    terms = jnp.stack(
+        [entry_centre, factor * entry_shift_gradient, factor * entry_scale * entry_gain_gradient]
+    )
+    signal_gradient = unpool(returned, outgoing, first_chosen, terms, picked, counts)
+    tap_rows = 3 * channel_width
+    weight_sums = total_of_large(jnp.concatenate(kernel_pieces + [pointwise_part], axis=0))
+    dilated_kernel_gradient = weight_sums[:tap_rows].reshape(dilated_kernel.shape)
+    pointwise_kernel_gradient = weight_sums[tap_rows:].T
     return (
         activations,
         signal_gradient,

time: 668 us -> 443 us (0.66); the launches traced: 655 us -> 437 us
  blocking collectives: 244 us -> 0 us
  local copies, waits for them, and re-layouts: 88.4 us -> 30.5 us
  starting transfers between devices: 15.3 us -> 66.2 us
  waiting for transfers between devices: 181 us -> 207 us
  Pallas kernels: 0 us -> 23.6 us
  between operations: 14.9 us -> 3.4 us
  other arithmetic: 72.6 us -> 65.8 us
    psum x6 -> x0, blocking collectives: 244 us -> none  [the longest x2 83.3 us: moments(): lax.psum(jnp.sum(values * valid_mask, axis=(0, 1)), ('grp', 'seq'))]
    ppermute x2 -> x32, waiting for transfers between devices: 6.55 us -> 207 us  [from_partner(): lax.ppermute(block, axis, [(place, place ^ mask) for place in range(count)])]
    psum x1 -> x0, waiting for transfers between devices: 62.4 us -> none  [per_device(): lax.psum((entry_gain_part, entry_shift_part, kernel_part), ('grp', 'seq'))]
    all_to_all x1, waiting for transfers between devices: 60.3 us -> 0.01 us  [per_device(): lax.all_to_all(sent_back, 'seq', split_axis=0, concat_axis=0, tiled=True)]
    ppermute x2 -> x32, starting transfers between devices: 2.65 us -> 55.9 us  [from_partner(): lax.ppermute(block, axis, [(place, place ^ mask) for place in range(count)])]
    all_to_all x1, waiting for transfers between devices: 51.6 us -> 0.01 us  [per_device(): lax.all_to_all(outgoing, 'seq', split_axis=0, concat_axis=1, tiled=True)]
    unnamed x61 -> x112, local copies, waits for them, and re-layouts: 43.3 us -> 17.2 us
    pallas_call x0 -> x2, Pallas kernels: none -> 23.6 us  [the longest x1 15 us: unpool(): pl.pallas_call(unpool_kernel, grid_spec=pltpu.PrefetchScalarGridSpec(num_...]
  transfers between devices with their start and end apart: 5 -> 34, of which waited for: 5 -> 23; matrix products, arithmetic and copies ran while one was open for 14% -> 17% of each run, Pallas kernels for 0% -> 3%
where the time goes in v1:
time: 443 us; the launch traced here: 437 us
  waiting for transfers between devices  207 us (47%)
  starting transfers between devices  66.2 us (15%)
  other arithmetic  65.8 us (15%)
  matrix products  39.9 us (9%)
  local copies, waits for them, and re-layouts  30.5 us (7%)
  Pallas kernels  23.6 us (5%)
    ppermute x32, waiting for transfers between devices, from_partner(): lax.ppermute(block, axis, [(place, place ^ mask) for place in range(count)])  207 us
    ppermute x32, starting transfers between devices, from_partner(): lax.ppermute(block, axis, [(place, place ^ mask) for place in range(count)])  55.9 us
    unnamed x112, local copies, waits for them, and re-layouts  17.2 us
    dot_general x3, matrix products, per_device(): jnp.einsum('hrf,cf->hrc', grad_shifted, kernel_low[kernel_tap_index], pre...  16.7 us
    pallas_call x1, Pallas kernels, unpool(): pl.pallas_call(unpool_kernel, grid_spec=pltpu.PrefetchScalarGridSpec(num_...  15 us
    select_n x5, other arithmetic, total_of_large(): jnp.where(upper == 0, jnp.concatenate([buffer, other], axis=0), jnp.conca...  14.5 us
    convert_element_type x1, other arithmetic, per_device(): (entry_gain * entry_scale * grad_entry_pre + grad_block).astype(jnp.bfloa...  10.2 us
  transfers between devices with their start and end apart: 34, of which 23 were waited for; matrix products, arithmetic and copies ran while one was open for 17% of the time, Pallas kernels for 3%

profile of v1, /device:TPU:17, one launch (start us, length us, event | category | flops | bytes accessed | tf_op | source)
XLA Modules:
  0.0 436.7 jit_solution(15207786031052048836)
XLA Ops:
  4.5 4.6 %copy-done = f32[16,256,768]{2,1,0:T(8,128)S(1)} copy-done((f32[16,256,768]{2,1,0:T(8,128)S(1)}, f32[16,256,768]{2,1,0:T(8,128)}, u32[]{:S(2)}) %copy-start) | copy-done | bytes 12582936
  9.0 8.6 %pool.1 = (bf16[16,128,768]{2,1,0:T(8,128)(2,1)}, bf16[16,128,768]{2,1,0:T(8,128)(2,1)S(1)}, f32[2,768]{1,0:T(2,128)S(1)}) custom-call(s32[16]{0:T(128)S(1)} %gather_fusion, s32[16]{0:T(128)S(1)} %get-tuple-element.76.count_ref, s32[16]{0:T(128)S(1)} %sub.132.before_ref, f32[16,256,768]{2,1,0:T(8,128)S(1)} %copy-done, f32[16,256,768]{2,1,0:T(8,128)S(1)} %copy-done, ...), custom_call_target="tpu_custom_call" | custom-call | flops 15728640 | bytes 18874368 | tf_op jit(solution)/shard_map/pool/pallas_call | solution.py:115
  19.4 5.7 %all-to-all-start = ((bf16[16,128,768]{2,1,0:T(8,128)(2,1)}), bf16[16,128,768]{2,1,0:T(8,128)(2,1)S(1)}, u32[]{:S(2)}, u32[]{:S(2)}) async-start(bf16[16,128,768]{2,1,0:T(8,128)(2,1)} %get-tuple-element.13.pooled_ref), calls=%async_computation | async-start | bytes 6291456 | tf_op jit(solution)/shard_map/all_to_all | solution.py:246
  33.2 17.1 %collective-permute-done.2 = f32[3,768]{1,0:T(4,128)S(1)} collective-permute-done((f32[3,768]{1,0:T(4,128)S(1)}, f32[3,768]{1,0:T(4,128)S(1)}, u32[]{:S(2)}, u32[]{:S(2)}) %collective-permute-start.2) | collective-permute-done | bytes 9248 | tf_op jit(solution)/shard_map/ppermute | solution.py:18
  53.0 24.3 %collective-permute-done.3 = f32[3,768]{1,0:T(4,128)S(1)} collective-permute-done((f32[3,768]{1,0:T(4,128)S(1)}, f32[3,768]{1,0:T(4,128)S(1)}, u32[]{:S(2)}, u32[]{:S(2)}) %collective-permute-start.3) | collective-permute-done | bytes 9248 | tf_op jit(solution)/shard_map/ppermute | solution.py:18
  78.1 3.4 convert_element_type.98
  82.2 10.2 %collective-permute-done.4 = f32[3,768]{1,0:T(4,128)S(1)} collective-permute-done((f32[3,768]{1,0:T(4,128)S(1)}, f32[3,768]{1,0:T(4,128)S(1)}, u32[]{:S(2)}, u32[]{:S(2)}) %collective-permute-start.4) | collective-permute-done | bytes 9248 | tf_op jit(solution)/shard_map/ppermute | solution.py:18
  96.1 3.4 fusion.30
  101.4 4.0 collective-permute-done.5
  126.6 3.4 collective-permute-start.9
  135.3 4.7 %multiply_reduce_fusion.2 = (f32[384]{0:T(512)S(1)}, f32[384]{0:T(512)S(1)}, f32[2,1024,384]{2,1,0:T(8,128)}, bf16[2,1024,384]{2,1,0:T(8,128)(2,1)}) fusion(f32[384]{0:T(512)S(1)} %get-tuple-element.51, f32[384]{0:T(512)S(1)} %get-tuple-element.50, f32[384]{0:T(512)S(1)} %copy-done.43, f32[384]{0:T(512)S(1)} %copy-done.34, f32[2,1024,384]{2,1,0:T(8,128)S(1)} %fusion.51, ...), kind=kLoop, calls=%fused_computation.82 | loop fusion | flops 23592192 | bytes 11027456 | tf_op jit(solution)/shard_map/reduce_sum | solution.py:319
  140.0 4.7 %collective-permute-start.11 = (f32[2,384]{1,0:T(2,128)S(1)}, f32[2,384]{1,0:T(2,128)S(1)}, u32[]{:S(2)}, u32[]{:S(2)}) collective-permute-start(f32[2,384]{1,0:T(2,128)S(1)} %pad_maximum_fusion.14), channel_id=1, source_target_pairs={{0,8},{8,0},{16,24},{24,16},{1,9},{9,1},{17,25},{25,17},{2,10},{10... | collective-permute-start | bytes 9224 | tf_op jit(solution)/shard_map/ppermute | solution.py:18
  148.5 5.1 %multiply_convert_fusion.1 = (bf16[2048,768]{1,0:T(8,128)(2,1)}, f32[768]{0:T(1024)S(1)}) fusion(f32[2048,768]{1,0:T(8,128)} %param.23, f32[2048]{0:T(1024)S(1)} %fusion.89), kind=kLoop, calls=%fused_computation.55 | loop fusion | flops 4717824 | bytes 9448448 | tf_op jit(solution)/shard_map/convert_element_type | solution.py:307
  172.3 3.2 collective-permute-start.22
  177.5 3.7 collective-permute-done.16
  183.2 4.5 %fusion.69 = f32[4,512,768]{2,1,0:T(8,128)} fusion(bf16[4,588,384]{2,1,0:T(8,128)(2,1)S(1)} %bitcast.193, bf16[3,768,384]{2,1,0:T(8,128)(2,1)S(1)} %copy-done.17), kind=kOutput, calls=%fused_computation.107 | convolution fusion | flops 1207959552 | bytes 8454144 | tf_op jit(solution)/shard_map/hrf,cf->hrc/dot_general | solution.py:356
  193.3 10.4 %multiply_reduce_fusion = (f32[768]{0:T(1024)S(1)}, f32[768]{0:T(1024)S(1)}, f32[4,512,768]{2,1,0:T(8,128)}) fusion(f32[4,512,768]{2,1,0:T(8,128)S(1)} %bitcast.181, f32[768]{0:T(1024)S(1)} %copy-done.19, f32[768]{0:T(1024)S(1)} %copy-done.32, f32[768]{0:T(1024)S(1)} %copy-done.38, f32[768]{0:T(1024)S(1)} %copy-done.29, f32[4,512]{1,0:T(4,128)S(1)} %copy-done.22, ...), kind=kOutput, calls=%fused_computation.51 | convolution fusion | flops 1253571072 | bytes 27359232 | tf_op jit(solution)/shard_map/hrf,cf->hrc/dot_general | solution.py:356
  207.6 11.2 %collective-permute-done.23 = f32[768,384]{1,0:T(8,128)} collective-permute-done((f32[768,384]{1,0:T(8,128)S(1)}, f32[768,384]{1,0:T(8,128)}, u32[]{:S(2)}, u32[]{:S(2)}) %collective-permute-start.23) | collective-permute-done | bytes 1179680 | tf_op jit(solution)/shard_map/ppermute | solution.py:18
  224.5 11.3 %collective-permute-done.19 = f32[3,768]{1,0:T(4,128)S(1)} collective-permute-done((f32[3,768]{1,0:T(4,128)S(1)}, f32[3,768]{1,0:T(4,128)S(1)}, u32[]{:S(2)}, u32[]{:S(2)}) %collective-permute-start.19) | collective-permute-done | bytes 9248 | tf_op jit(solution)/shard_map/ppermute | solution.py:18
  251.1 10.2 %fusion.15 = bf16[2,8,128,768]{3,2,0,1:T(8,128)(2,1)} fusion(bf16[8,2,128,768]{3,2,1,0:T(8,128)(2,1)S(1)} %bitcast.185, f32[2,8,128,768]{3,2,1,0:T(8,128)} %bitcast.175, f32[2,8,128,768]{3,2,1,0:T(8,128)} %bitcast.196, f32[768]{0:T(1024)S(1)} %copy-done.39, f32[768]{0:T(1024)S(1)} %copy-done.30, f32[768]{0:T(1024)S(1)} %copy-done.20, f32[768]{0:T(1024)S(1)} %copy-done.33, ...), kind=kLoop, calls=%fused_computation.26 | loop fusion | flops 45613056 | bytes 18897920 | tf_op jit(solution)/shard_map/convert_element_type | solution.py:375
  261.3 4.5 %all-to-all-start.1 = ((bf16[16,128,768]{2,1,0:T(8,128)(2,1)}), bf16[16,128,768]{2,1,0:T(8,128)(2,1)S(1)}, u32[]{:S(2)}, u32[]{:S(2)}) async-start(bf16[16,128,768]{2,1,0:T(8,128)(2,1)} %bitcast.189), calls=%async_computation.1 | async-start | bytes 6291456 | tf_op jit(solution)/shard_map/all_to_all | solution.py:378
  267.4 68.0 %collective-permute-done.27 = f32[96,384]{1,0:T(8,128)} collective-permute-done((f32[96,384]{1,0:T(8,128)}, f32[96,384]{1,0:T(8,128)}, u32[]{:S(2)}, u32[]{:S(2)}) %collective-permute-start.27) | collective-permute-done | bytes 147488 | tf_op jit(solution)/shard_map/ppermute | solution.py:18
  336.6 4.8 %collective-permute-start.28 = (f32[192,384]{1,0:T(8,128)S(1)}, f32[192,384]{1,0:T(8,128)}, u32[]{:S(2)}, u32[]{:S(2)}) collective-permute-start(f32[192,384]{1,0:T(8,128)S(1)} %maximum_select_fusion.4), channel_id=1, source_target_pairs={{0,2},{1,3},{2,0},{3,1},{4,6},{5,7},{6,4},{7,5},{8,10},{9,11},{10,... | collective-permute-start | bytes 884744 | tf_op jit(solution)/shard_map/ppermute | solution.py:18
  341.4 4.2 collective-permute-done.28
  347.6 6.4 %collective-permute-start.29 = (f32[384,384]{1,0:T(8,128)}, f32[384,384]{1,0:T(8,128)}, u32[]{:S(2)}, u32[]{:S(2)}) collective-permute-start(f32[384,384]{1,0:T(8,128)} %maximum_select_fusion.3), channel_id=1, source_target_pairs={{0,1},{1,0},{2,3},{3,2},{4,5},{5,4},{6,7},{7,6},{8,9},{9,8},{10,11... | collective-permute-start | bytes 1769480 | tf_op jit(solution)/shard_map/ppermute | solution.py:18
  354.0 13.0 %collective-permute-done.29 = f32[384,384]{1,0:T(8,128)} collective-permute-done((f32[384,384]{1,0:T(8,128)}, f32[384,384]{1,0:T(8,128)}, u32[]{:S(2)}, u32[]{:S(2)}) %collective-permute-start.29) | collective-permute-done | bytes 589856 | tf_op jit(solution)/shard_map/ppermute | solution.py:18
  367.0 2.8 maximum_select_fusion.2
  370.9 24.9 %collective-permute-done.30 = f32[768,384]{1,0:T(8,128)} collective-permute-done((f32[768,384]{1,0:T(8,128)}, f32[768,384]{1,0:T(8,128)}, u32[]{:S(2)}, u32[]{:S(2)}) %collective-permute-start.30) | collective-permute-done | bytes 1179680 | tf_op jit(solution)/shard_map/ppermute | solution.py:18
  395.9 4.2 maximum_select_fusion.1
  402.6 8.2 %fusion.35 = f32[2,1024,768]{2,1,0:T(8,128)} fusion(f32[2,8,128,768]{3,2,1,0:T(8,128)} %copy-done.4, f32[768]{0:T(1024)S(1)} %copy-done.46, f32[2,1024]{1,0:T(2,128)S(1)} %compare_convert_fusion.2, bf16[2,1024,384]{2,1,0:T(8,128)(2,1)} %get-tuple-element.79, f32[384,768]{1,0:T(8,128)} %param.19), kind=kOutput, calls=%fused_computation.48 | convolution fusion | flops 1212973056 | bytes 15346688 | tf_op jit(solution)/shard_map/krf,fd->krd/dot_general | solution.py:302
  413.5 15.0 %unpool.1 = f32[16,256,768]{2,1,0:T(8,128)} custom-call(s32[16]{0:T(128)S(1)} %gather_fusion, s32[16]{0:T(128)S(1)} %get-tuple-element.76.count_ref, bf16[16,128,768]{2,1,0:T(8,128)(2,1)S(1)} %all-to-all-done.1.returned_ref, bf16[16,128,768]{2,1,0:T(8,128)(2,1)} %get-tuple-element.13.pooled_ref, bf16[16,128,768]{2,1,0:T(8,128)(2,1)S(1)} %copy-done.2, ...), custom_call_target="tpu_custom_call" | custom-call | flops 15728640 | bytes 22020096 | tf_op jit(solution)/shard_map/unpool/pallas_call | solution.py:172
  428.5 4.3 maximum_select_fusion
  (296 shorter events, 119.2 us)
Async XLA Ops:
  19.4 74.3 %all-to-all-start = ((bf16[16,128,768]{2,1,0:T(8,128)(2,1)}), bf16[16,128,768]{2,1,0:T(8,128)(2,1)S(1)}, u32[]{:S(2)}, u32[]{:S(2)}) async-start(bf16[16,128,768]{2,1,0:T(8,128)(2,1)} %get-tuple-element.13.pooled_ref), calls=%async_computation | async-start | bytes 6291456 | tf_op jit(solution)/shard_map/all_to_all | solution.py:246
  25.8 3.1 collective-permute-start
  28.9 2.9 collective-permute-start.1
  31.9 18.5 %collective-permute-start.2 = (f32[3,768]{1,0:T(4,128)S(1)}, f32[3,768]{1,0:T(4,128)S(1)}, u32[]{:S(2)}, u32[]{:S(2)}) collective-permute-start(f32[3,768]{1,0:T(4,128)S(1)} %pad_maximum_fusion.4), channel_id=1, source_target_pairs={{0,1},{1,0},{2,3},{3,2},{4,5},{5,4},{6,7},{7,6},{8,9},{9,8},{10,11... | collective-permute-start | bytes 27656 | tf_op jit(solution)/shard_map/ppermute | solution.py:18
  50.4 26.9 %collective-permute-start.3 = (f32[3,768]{1,0:T(4,128)S(1)}, f32[3,768]{1,0:T(4,128)S(1)}, u32[]{:S(2)}, u32[]{:S(2)}) collective-permute-start(f32[3,768]{1,0:T(4,128)S(1)} %pad_maximum_fusion.5), channel_id=1, source_target_pairs={{0,2},{1,3},{2,0},{3,1},{4,6},{5,7},{6,4},{7,5},{8,10},{9,11},{10,... | collective-permute-start | bytes 27656 | tf_op jit(solution)/shard_map/ppermute | solution.py:18
  77.3 15.0 %collective-permute-start.4 = (f32[3,768]{1,0:T(4,128)S(1)}, f32[3,768]{1,0:T(4,128)S(1)}, u32[]{:S(2)}, u32[]{:S(2)}) collective-permute-start(f32[3,768]{1,0:T(4,128)S(1)} %pad_maximum_fusion.6), channel_id=1, source_target_pairs={{0,4},{1,5},{2,6},{3,7},{4,0},{5,1},{6,2},{7,3},{8,12},{9,13},{10,... | collective-permute-start | bytes 27656 | tf_op jit(solution)/shard_map/ppermute | solution.py:18
  99.6 5.9 %collective-permute-start.5 = (bf16[2,76,768]{2,1,0:T(8,128)(2,1)S(1)}, bf16[2,76,768]{2,1,0:T(8,128)(2,1)S(1)}, u32[]{:S(2)}, u32[]{:S(2)}) collective-permute-start(bf16[2,76,768]{2,1,0:T(8,128)(2,1)S(1)} %slice.273), channel_id=1, source_target_pairs={{0,1},{1,0},{2,3},{3,2},{4,5},{5,4},{6,7},{7,6},{8,9},{9,8},{10,11... | collective-permute-start | bytes 700424 | tf_op jit(solution)/shard_map/ppermute | solution.py:18
  116.3 3.5 collective-permute-start.6
  120.6 2.5 collective-permute-start.7
  123.1 3.4 collective-permute-start.8
  126.6 4.4 %collective-permute-start.9 = (f32[3,384]{1,0:T(4,128)S(1)}, f32[3,384]{1,0:T(4,128)S(1)}, u32[]{:S(2)}, u32[]{:S(2)}) collective-permute-start(f32[3,384]{1,0:T(4,128)S(1)} %pad_maximum_fusion.12), channel_id=1, source_target_pairs={{0,2},{1,3},{2,0},{3,1},{4,6},{5,7},{6,4},{7,5},{8,10},{9,11},{10,... | collective-permute-start | bytes 13832 | tf_op jit(solution)/shard_map/ppermute | solution.py:18
  131.1 3.4 collective-permute-start.10
  140.0 5.5 %collective-permute-start.11 = (f32[2,384]{1,0:T(2,128)S(1)}, f32[2,384]{1,0:T(2,128)S(1)}, u32[]{:S(2)}, u32[]{:S(2)}) collective-permute-start(f32[2,384]{1,0:T(2,128)S(1)} %pad_maximum_fusion.14), channel_id=1, source_target_pairs={{0,8},{8,0},{16,24},{24,16},{1,9},{9,1},{17,25},{25,17},{2,10},{10... | collective-permute-start | bytes 9224 | tf_op jit(solution)/shard_map/ppermute | solution.py:18
  148.1 5.5 %collective-permute-start.13 = (f32[2,384]{1,0:T(2,128)S(1)}, f32[2,384]{1,0:T(2,128)S(1)}, u32[]{:S(2)}, u32[]{:S(2)}) collective-permute-start(f32[2,384]{1,0:T(2,128)S(1)} %fusion.125), channel_id=1, source_target_pairs={{0,1},{1,0},{2,3},{3,2},{4,5},{5,4},{6,7},{7,6},{8,9},{9,8},{10,11... | collective-permute-start | bytes 9224 | tf_op jit(solution)/shard_map/ppermute | solution.py:18
  153.6 3.6 collective-permute-start.14
  157.2 3.4 collective-permute-start.15
  172.3 17.2 %collective-permute-start.22 = (f32[1536,384]{1,0:T(8,128)}, f32[1536,384]{1,0:T(8,128)}, u32[]{:S(2)}, u32[]{:S(2)}) collective-permute-start(f32[1536,384]{1,0:T(8,128)} %constant_dynamic-slice_fusion.4), channel_id=1, source_target_pairs={{0,8},{8,0},{16,24},{24,16},{1,9},{9,1},{17,25},{25,17},{2,10},{10... | collective-permute-start | bytes 7077896 | tf_op jit(solution)/shard_map/ppermute | solution.py:18
  176.2 5.0 %collective-permute-start.16 = (bf16[2,76,384]{2,1,0:T(8,128)(2,1)S(1)}, bf16[2,76,384]{2,1,0:T(8,128)(2,1)S(1)}, u32[]{:S(2)}, u32[]{:S(2)}) collective-permute-start(bf16[2,76,384]{2,1,0:T(8,128)(2,1)S(1)} %slice.301), channel_id=1, source_target_pairs={{0,1},{1,0},{2,3},{3,2},{4,5},{5,4},{6,7},{7,6},{8,9},{9,8},{10,11... | collective-permute-start | bytes 350216 | tf_op jit(solution)/shard_map/ppermute | solution.py:18
  191.9 26.9 %collective-permute-start.23 = (f32[768,384]{1,0:T(8,128)S(1)}, f32[768,384]{1,0:T(8,128)}, u32[]{:S(2)}, u32[]{:S(2)}) collective-permute-start(f32[768,384]{1,0:T(8,128)S(1)} %constant_dynamic-slice_fusion.3), channel_id=1, source_target_pairs={{0,16},{8,24},{16,0},{24,8},{1,17},{9,25},{17,1},{25,9},{2,18},{10... | collective-permute-start | bytes 3538952 | tf_op jit(solution)/shard_map/ppermute | solution.py:18
  207.3 16.0 %collective-permute-start.18 = (f32[3,768]{1,0:T(4,128)S(1)}, f32[3,768]{1,0:T(4,128)S(1)}, u32[]{:S(2)}, u32[]{:S(2)}) collective-permute-start(f32[3,768]{1,0:T(4,128)S(1)} %fusion.110), channel_id=1, source_target_pairs={{0,16},{8,24},{16,0},{24,8},{1,17},{9,25},{17,1},{25,9},{2,18},{10... | collective-permute-start | bytes 27656 | tf_op jit(solution)/shard_map/ppermute | solution.py:18
  222.2 19.6 %collective-permute-start.24 = (f32[384,384]{1,0:T(8,128)}, f32[384,384]{1,0:T(8,128)}, u32[]{:S(2)}, u32[]{:S(2)}) collective-permute-start(f32[384,384]{1,0:T(8,128)} %constant_dynamic-slice_fusion.2), channel_id=1, source_target_pairs={{0,1},{1,0},{2,3},{3,2},{4,5},{5,4},{6,7},{7,6},{8,9},{9,8},{10,11... | collective-permute-start | bytes 1769480 | tf_op jit(solution)/shard_map/ppermute | solution.py:18
  224.1 11.8 %collective-permute-start.19 = (f32[3,768]{1,0:T(4,128)S(1)}, f32[3,768]{1,0:T(4,128)S(1)}, u32[]{:S(2)}, u32[]{:S(2)}) collective-permute-start(f32[3,768]{1,0:T(4,128)S(1)} %fusion.124), channel_id=1, source_target_pairs={{0,1},{1,0},{2,3},{3,2},{4,5},{5,4},{6,7},{7,6},{8,9},{9,8},{10,11... | collective-permute-start | bytes 27656 | tf_op jit(solution)/shard_map/ppermute | solution.py:18
  235.8 2.5 collective-permute-start.20
  238.4 3.4 collective-permute-start.21
  243.2 5.6 %collective-permute-start.25 = (f32[192,384]{1,0:T(8,128)S(1)}, f32[192,384]{1,0:T(8,128)S(1)}, u32[]{:S(2)}, u32[]{:S(2)}) collective-permute-start(f32[192,384]{1,0:T(8,128)S(1)} %constant_dynamic-slice_fusion.1), channel_id=1, source_target_pairs={{0,2},{1,3},{2,0},{3,1},{4,6},{5,7},{6,4},{7,5},{8,10},{9,11},{10,... | collective-permute-start | bytes 884744 | tf_op jit(solution)/shard_map/ppermute | solution.py:18
  249.5 16.2 %collective-permute-start.26 = (f32[96,384]{1,0:T(8,128)}, f32[96,384]{1,0:T(8,128)}, u32[]{:S(2)}, u32[]{:S(2)}) collective-permute-start(f32[96,384]{1,0:T(8,128)} %constant_dynamic-slice_fusion), channel_id=1, source_target_pairs={{0,4},{1,5},{2,6},{3,7},{4,0},{5,1},{6,2},{7,3},{8,12},{9,13},{10,... | collective-permute-start | bytes 442376 | tf_op jit(solution)/shard_map/ppermute | solution.py:18
  261.3 150.3 %all-to-all-start.1 = ((bf16[16,128,768]{2,1,0:T(8,128)(2,1)}), bf16[16,128,768]{2,1,0:T(8,128)(2,1)S(1)}, u32[]{:S(2)}, u32[]{:S(2)}) async-start(bf16[16,128,768]{2,1,0:T(8,128)(2,1)} %bitcast.189), calls=%async_computation.1 | async-start | bytes 6291456 | tf_op jit(solution)/shard_map/all_to_all | solution.py:378
  267.4 68.0 %collective-permute-start.27 = (f32[96,384]{1,0:T(8,128)}, f32[96,384]{1,0:T(8,128)}, u32[]{:S(2)}, u32[]{:S(2)}) collective-permute-start(f32[96,384]{1,0:T(8,128)} %dynamic-slice_add_fusion.4), channel_id=1, source_target_pairs={{0,4},{1,5},{2,6},{3,7},{4,0},{5,1},{6,2},{7,3},{8,12},{9,13},{10,... | collective-permute-start | bytes 442376 | tf_op jit(solution)/shard_map/ppermute | solution.py:18
  336.6 9.1 %collective-permute-start.28 = (f32[192,384]{1,0:T(8,128)S(1)}, f32[192,384]{1,0:T(8,128)}, u32[]{:S(2)}, u32[]{:S(2)}) collective-permute-start(f32[192,384]{1,0:T(8,128)S(1)} %maximum_select_fusion.4), channel_id=1, source_target_pairs={{0,2},{1,3},{2,0},{3,1},{4,6},{5,7},{6,4},{7,5},{8,10},{9,11},{10,... | collective-permute-start | bytes 884744 | tf_op jit(solution)/shard_map/ppermute | solution.py:18
  347.6 19.3 %collective-permute-start.29 = (f32[384,384]{1,0:T(8,128)}, f32[384,384]{1,0:T(8,128)}, u32[]{:S(2)}, u32[]{:S(2)}) collective-permute-start(f32[384,384]{1,0:T(8,128)} %maximum_select_fusion.3), channel_id=1, source_target_pairs={{0,1},{1,0},{2,3},{3,2},{4,5},{5,4},{6,7},{7,6},{8,9},{9,8},{10,11... | collective-permute-start | bytes 1769480 | tf_op jit(solution)/shard_map/ppermute | solution.py:18
  369.7 26.2 %collective-permute-start.30 = (f32[768,384]{1,0:T(8,128)}, f32[768,384]{1,0:T(8,128)}, u32[]{:S(2)}, u32[]{:S(2)}) collective-permute-start(f32[768,384]{1,0:T(8,128)} %maximum_select_fusion.2), channel_id=1, source_target_pairs={{0,16},{8,24},{16,0},{24,8},{1,17},{9,25},{17,1},{25,9},{2,18},{10... | collective-permute-start | bytes 3538952 | tf_op jit(solution)/shard_map/ppermute | solution.py:18
  400.1 28.4 %collective-permute-start.31 = (f32[1536,384]{1,0:T(8,128)}, f32[1536,384]{1,0:T(8,128)}, u32[]{:S(2)}, u32[]{:S(2)}) collective-permute-start(f32[1536,384]{1,0:T(8,128)} %maximum_select_fusion.1), channel_id=1, source_target_pairs={{0,8},{8,0},{16,24},{24,16},{1,9},{9,1},{17,25},{25,17},{2,10},{10... | collective-permute-start | bytes 7077896 | tf_op jit(solution)/shard_map/ppermute | solution.py:18
  (56 other events, 989.1 us)

commit v2 on v0

v2 whole, which is shorter than its diff:
```python
import functools
import math

import jax
import jax.numpy as jnp
from jax import lax
from jax.experimental import pallas as pl
from jax.experimental.pallas import tpu as pltpu
from jax.sharding import PartitionSpec as P

DILATION_STEP = 38
WINDOW_SPAN = 1024
HALF_WINDOW_ROWS = 512


EPSILON = 0.001

LANES = 128
BORDER = 48
STRIP = 64
PAD = 40
PADDED_ROWS = HALF_WINDOW_ROWS + 2 * PAD
GELU_SLOPE = math.sqrt(2.0 / math.pi)
GELU_CUBE = 0.044715

VMEM = pl.BlockSpec(memory_space=pltpu.VMEM)
SMEM = pl.BlockSpec(memory_space=pltpu.SMEM)
HBM = pl.BlockSpec(memory_space=pltpu.HBM)


def from_partner(block, axis, mask):
    count = lax.axis_size(axis)
    return lax.ppermute(block, axis, [(place, place ^ mask) for place in range(count)])


def exchange_steps():
    steps = []
    for axis in ("grp", "seq"):
        mask = 1
        while mask < lax.axis_size(axis):
            steps.append((axis, mask))
            mask *= 2
    return steps


def total(values):
    for axis, mask in exchange_steps():
        values = values + from_partner(values, axis, mask)
    return values


def merged(left, right):
    left_sum, left_spread, left_count = left
    right_sum, right_spread, right_count = right
    gap = left_sum / jnp.maximum(left_count, 1.0) - right_sum / jnp.maximum(right_count, 1.0)
    weight = left_count * right_count / jnp.maximum(left_count + right_count, 1.0)
    return (
        left_sum + right_sum,
        left_spread + right_spread + gap * gap * weight,
        left_count + right_count,
    )


def total_moments(packed):
    for axis, mask in exchange_steps():
        other = from_partner(packed, axis, mask)
        packed = jnp.concatenate(
            merged(
                (packed[0:1], packed[1:2], packed[2:3]), (other[0:1], other[1:2], other[2:3])
            ),
            axis=0,
        )
    return packed


class Facts:
    def __init__(self, ref, windows, slots):
        self.ref, self.windows, self.slots = ref, windows, slots

    def slot_window(self, slot):
        upper = (2 * self.ref[1]) // self.ref[2]
        target = jnp.bitwise_xor(slot // self.slots, upper)
        return self.ref[3 + target * self.slots + slot % self.slots]

    def length(self, window):
        return self.ref[3 + self.windows + self.ref[0] * self.windows + window]

    def slot_count(self, slot, rows):
        return jnp.clip(self.length(self.slot_window(slot)) - self.ref[1] * rows, 0, rows)

    def half_limit(self, slot, half):
        place = jnp.bitwise_xor(self.ref[1], half)
        window = self.ref[3 + place * self.slots + slot]
        return jnp.clip(self.length(window) - half * HALF_WINDOW_ROWS, 0, HALF_WINDOW_ROWS)

    def row_count(self):
        start = 3 + self.windows
        count = self.ref.shape[0] - start
        added = lax.fori_loop(0, count, lambda i, held: held + self.ref[start + i], jnp.int32(0))
        return added.astype(jnp.float32)


def kernel_call(body, name, inputs, specs, outputs, out_specs, scratch=(), flops=0, bytes_moved=0, grant=8 << 20):
    return pl.pallas_call(
        body,
        in_specs=specs,
        out_specs=out_specs,
        out_shape=outputs,
        scratch_shapes=list(scratch),
        compiler_params=pltpu.CompilerParams(vmem_limit_bytes=grant),
        cost_estimate=pl.CostEstimate(
            flops=flops, bytes_accessed=bytes_moved, transcendentals=0
        ),
        name=name,
    )(*inputs)


def shape(dims, dtype):
    return jax.ShapeDtypeStruct(dims, dtype)


def in_hbm(array):
    return pltpu.with_memory_space_constraint(array, pltpu.HBM)


def column_slices(width):
    return [slice(start, start + LANES) for start in range(0, width, LANES)]


def pool_body(
    slots, facts_ref, signal_ref, pooled_ref, first_ref, moments_ref,
    held, low, mark, arrivals, departures,
):
    windows, columns = held.shape[:2]
    rows = low.shape[1]
    facts = Facts(facts_ref, windows, slots)

    def arrival(place, column):
        return pltpu.make_async_copy(
            signal_ref.at[facts.slot_window(place), :, pl.ds(column * LANES, LANES)],
            held.at[place, column],
            arrivals.at[place, column],
        )

    def departure(place):
        return [
            pltpu.make_async_copy(low.at[place], pooled_ref.at[place], departures.at[place, 0]),
            pltpu.make_async_copy(mark.at[place], first_ref.at[place], departures.at[place, 1]),
        ]

    def begin(place, carry):
        for column in range(columns):
            arrival(place, column).start()
        return carry

    lax.fori_loop(0, windows, begin, 0)
    moments_ref[...] = jnp.zeros_like(moments_ref)

    def work(place, before):
        count = facts.slot_count(place, rows)
        count_f = count.astype(jnp.float32)
        before_f = before.astype(jnp.float32)
        weight = before_f * count_f / jnp.maximum(before_f + count_f, 1.0)
        inside = lax.broadcasted_iota(jnp.int32, (rows, LANES), 0) < count
        for column, lanes in enumerate(column_slices(columns * LANES)):
            arrival(place, column).wait()
            first_bin = held[place, column, pl.ds(0, rows, stride=2), :]
            second_bin = held[place, column, pl.ds(1, rows, stride=2), :]
            take_first = first_bin >= second_bin
            raw = jnp.maximum(first_bin, second_bin)
            mark[place, :, lanes] = jnp.where(take_first, 1.0, 0.0).astype(jnp.bfloat16)
            pooled = jnp.where(inside, raw, 0.0).astype(jnp.bfloat16)
            low[place, :, lanes] = pooled
            values = pooled.astype(jnp.float32)
            block_sum = jnp.sum(values, axis=0, keepdims=True)
            block_mean = block_sum / jnp.maximum(count_f, 1.0)
            deviation = jnp.where(inside, values - block_mean, 0.0)
            block_spread = jnp.sum(deviation * deviation, axis=0, keepdims=True)
            held_sum = moments_ref[0:1, lanes]
            gap = held_sum / jnp.maximum(before_f, 1.0) - block_mean
            moments_ref[0:1, lanes] = held_sum + block_sum
            moments_ref[1:2, lanes] = (
                moments_ref[1:2, lanes] + block_spread + gap * gap * weight
            )
            moments_ref[2:3, lanes] = moments_ref[2:3, lanes] + count_f
        for copy in departure(place):
            copy.start()
        return before + count

    lax.fori_loop(0, windows, work, jnp.int32(0))

    def finish(place, carry):
        for copy in departure(place):
            copy.wait()
        return carry

    lax.fori_loop(0, windows, finish, 0)


def pool(facts, signal, slots):
    windows, segment, width = signal.shape
    rows, columns = segment // 2, width // LANES
    block = (windows, rows, width)
    return kernel_call(
        functools.partial(pool_body, slots),
        "pool",
        (facts, in_hbm(signal)),
        [SMEM, HBM],
        [
            pltpu.HBM(block, jnp.bfloat16),
            pltpu.HBM(block, jnp.bfloat16),
            shape((3, width), jnp.float32),
        ],
        [HBM, HBM, VMEM],
        [
            pltpu.VMEM((windows, columns, segment, LANES), jnp.float32),
            pltpu.VMEM(block, jnp.bfloat16),
            pltpu.VMEM(block, jnp.bfloat16),
            pltpu.SemaphoreType.DMA((windows, columns)),
            pltpu.SemaphoreType.DMA((windows, 2)),
        ],
        flops=10 * windows * rows * width,
        bytes_moved=windows * rows * width * 12,
        grant=24 << 20,
    )


def unpool_body(
    slots, slot, windows, facts_ref, returned_ref, pooled_ref, first_ref, moments_ref, sums_ref,
    params_ref, *refs,
):
    out_ref, back, low, mark, held, arrivals, departures = refs[-7:]
    targets, rows, width = back.shape
    columns = held.shape[1]
    facts = Facts(facts_ref, windows, slots)

    def arrival(target):
        place = target * slots + slot
        return [
            pltpu.make_async_copy(returned_ref.at[target], back.at[target], arrivals.at[target, 0]),
            pltpu.make_async_copy(pooled_ref.at[place], low.at[target], arrivals.at[target, 1]),
            pltpu.make_async_copy(first_ref.at[place], mark.at[target], arrivals.at[target, 2]),
        ]

    def departure(target, column):
        window = facts.slot_window(target * slots + slot)
        return pltpu.make_async_copy(
            held.at[target, column],
            out_ref.at[window, :, pl.ds(column * LANES, LANES)],
            departures.at[target, column],
        )

    def begin(target, carry):
        for copy in arrival(target):
            copy.start()
        return carry

    lax.fori_loop(0, targets, begin, 0)
    rows_total = facts.row_count()
    centre = moments_ref[0:1] / rows_total
    scale = lax.rsqrt(moments_ref[1:2] / rows_total + EPSILON)
    factor = params_ref[0:1] * scale / rows_total
    level = factor * sums_ref[1:2]
    tilt = factor * scale * sums_ref[0:1]

    def work(target, carry):
        for copy in arrival(target):
            copy.wait()
        inside = lax.broadcasted_iota(jnp.int32, (rows, LANES), 0) < facts.slot_count(
            target * slots + slot, rows
        )
        for column, lanes in enumerate(column_slices(width)):
            centred = low[target, :, lanes].astype(jnp.float32) - centre[:, lanes]
            gradient = back[target, :, lanes].astype(jnp.float32) - (
                level[:, lanes] + centred * tilt[:, lanes]
            )
            gradient = jnp.where(inside, gradient, 0.0).astype(jnp.bfloat16).astype(jnp.float32)
            first = gradient * mark[target, :, lanes].astype(jnp.float32)
            held[target, column, pl.ds(0, rows, stride=2), :] = first
            held[target, column, pl.ds(1, rows, stride=2), :] = gradient - first
            departure(target, column).start()
        return carry

    lax.fori_loop(0, targets, work, 0)

    def finish(target, carry):
        for column in range(columns):
            departure(target, column).wait()
        return carry

    lax.fori_loop(0, targets, finish, 0)


def unpool(facts, returned, pooled, first, moments, sums, params, slots, slot, held_output):
    targets, rows, width = returned.shape
    windows, columns = targets * slots, width // LANES
    inputs = [facts, in_hbm(returned), in_hbm(pooled), in_hbm(first), moments, sums, params]
    specs = [SMEM, HBM, HBM, HBM, VMEM, VMEM, VMEM]
    aliases = {}
    if held_output is not None:
        aliases = {len(inputs): 0}
        inputs.append(in_hbm(held_output))
        specs.append(HBM)
    block = (targets, rows, width)
    return pl.pallas_call(
        functools.partial(unpool_body, slots, slot, windows),
        in_specs=specs,
        out_specs=HBM,
        out_shape=pltpu.HBM((windows, 2 * rows, width), jnp.float32),
        input_output_aliases=aliases,
        scratch_shapes=[
            pltpu.VMEM(block, jnp.bfloat16),
            pltpu.VMEM(block, jnp.bfloat16),
            pltpu.VMEM(block, jnp.bfloat16),
            pltpu.VMEM((targets, columns, 2 * rows, LANES), jnp.float32),
            pltpu.SemaphoreType.DMA((targets, 3)),
            pltpu.SemaphoreType.DMA((targets, columns)),
        ],
        compiler_params=pltpu.CompilerParams(vmem_limit_bytes=16 << 20),
        cost_estimate=pl.CostEstimate(
            flops=10 * targets * rows * width,
            bytes_accessed=targets * rows * width * 14,
            transcendentals=0,
        ),
        name="unpool",
    )(*inputs)


def prepare_body(slots, windows, facts_ref, cot_ref, weight_ref, low_ref, middle_ref, bias_ref):
    step = pl.program_id(0)
    rows = cot_ref.shape[0]
    facts = Facts(facts_ref, windows, slots)
    first_row = step * rows
    piece = first_row // HALF_WINDOW_ROWS
    limit = facts.half_limit(piece // 2, piece % 2) - first_row % HALF_WINDOW_ROWS

    @pl.when(step == 0)
    def _():
        bias_ref[...] = jnp.zeros_like(bias_ref)

    inside = lax.broadcasted_iota(jnp.int32, (rows, 1), 0) < limit
    block = jnp.where(inside, cot_ref[...], 0.0)
    bias_ref[...] = bias_ref[...] + jnp.sum(block, axis=0, keepdims=True)
    low = block.astype(jnp.bfloat16)
    low_ref[...] = low
    middle_ref[...] = lax.dot_general(
        low, weight_ref[...], (((1,), (1,)), ((), ())), preferred_element_type=jnp.float32
    )


def prepare(facts, cotangent, weight, slots, windows):
    total_rows, width = cotangent.shape
    inner = weight.shape[0]
    rows = 256
    return pl.pallas_call(
        functools.partial(prepare_body, slots, windows),
        grid=(total_rows // rows,),
        in_specs=[
            SMEM,
            pl.BlockSpec((rows, width), lambda i: (i, 0)),
            pl.BlockSpec((inner, width), lambda i: (0, 0)),
        ],
        out_specs=[
            pl.BlockSpec((rows, width), lambda i: (i, 0)),
            pl.BlockSpec((rows, inner), lambda i: (i, 0)),
            pl.BlockSpec((1, width), lambda i: (0, 0)),
        ],
        out_shape=[
            shape((total_rows, width), jnp.bfloat16),
            shape((total_rows, inner), jnp.float32),
            shape((1, width), jnp.float32),
        ],
        compiler_params=pltpu.CompilerParams(vmem_limit_bytes=16 << 20),
        cost_estimate=pl.CostEstimate(
            flops=2 * total_rows * width * inner,
            bytes_accessed=total_rows * (width * 6 + inner * 4),
            transcendentals=0,
        ),
        name="prepare_cotangent",
    )(facts, cotangent, weight)


def norm_terms(moments_ref, params_ref, rows_total):
    centre = moments_ref[0:1] / rows_total
    scale = lax.rsqrt(moments_ref[1:2] / rows_total + EPSILON)
    return centre, scale, params_ref[0:1] * scale, params_ref[1:2]


def half_terms(moments_ref, params_ref, rows_total):
    centre, _, slope, offset = norm_terms(moments_ref, params_ref, rows_total)
    return 0.5 * slope, 0.5 * (offset - centre * slope)


def bent(half):
    square = half * half
    return jnp.tanh(half * (2.0 * GELU_SLOPE + (8.0 * GELU_SLOPE * GELU_CUBE) * square)), square


def gelu_slope(half, bend, square):
    inner = GELU_SLOPE + (12.0 * GELU_SLOPE * GELU_CUBE) * square
    return (0.5 + 0.5 * bend) + (half - half * bend * bend) * inner


def activate_body(
    slots, windows, facts_ref, arrived_ref, moments_ref, params_ref, act_ref, border_ref
):
    blocks, rows, width = arrived_ref.shape
    facts = Facts(facts_ref, windows, slots)
    per_half = HALF_WINDOW_ROWS // rows
    slope, offset = half_terms(moments_ref, params_ref, facts.row_count())

    def work(block, carry):
        source, slot = block // slots, block % slots
        half, start = source // per_half, (source % per_half) * rows
        inside = lax.broadcasted_iota(jnp.int32, (rows, 1), 0) < (
            facts.half_limit(slot, half) - start
        )
        for lanes in column_slices(width):
            values = arrived_ref[block, :, lanes].astype(jnp.float32)
            half_pre = values * slope[:, lanes] + offset[:, lanes]
            bend, _ = bent(half_pre)
            act = jnp.where(inside, half_pre + half_pre * bend, 0.0)
            act_ref[slot * 2 + half, pl.ds(pl.multiple_of(start, rows), rows), lanes] = act.astype(
                jnp.bfloat16
            )
        return carry

    lax.fori_loop(0, blocks, work, 0)
    for piece in range(act_ref.shape[0]):
        start = 0 if piece % 2 else HALF_WINDOW_ROWS - BORDER
        border_ref[piece] = act_ref[piece, start : start + BORDER]


def activate(facts, arrived, moments, params, slots, windows):
    width = arrived.shape[2]
    return kernel_call(
        functools.partial(activate_body, slots, windows),
        "activate",
        (facts, arrived, moments, params),
        [SMEM, VMEM, VMEM, VMEM],
        [
            shape((2 * slots, HALF_WINDOW_ROWS, width), jnp.bfloat16),
            shape((2 * slots, BORDER, width), jnp.bfloat16),
        ],
        [VMEM, VMEM],
        flops=20 * arrived.size,
        bytes_moved=4 * arrived.size,
    )


def slope_body(slots, windows, piece, facts_ref, arrived_ref, moments_ref, params_ref, slope_ref):
    blocks, rows, width = arrived_ref.shape
    facts = Facts(facts_ref, windows, slots)
    per_half = HALF_WINDOW_ROWS // rows
    slope, offset = half_terms(moments_ref, params_ref, facts.row_count())
    slot, half = piece // 2, piece % 2
    limit = facts.half_limit(slot, half)

    def work(part, carry):
        start = part * rows
        inside = lax.broadcasted_iota(jnp.int32, (rows, 1), 0) < limit - start
        for lanes in column_slices(width):
            values = arrived_ref[(half * per_half + part) * slots + slot, :, lanes]
            half_pre = values.astype(jnp.float32) * slope[:, lanes] + offset[:, lanes]
            found = jnp.where(inside, gelu_slope(half_pre, *bent(half_pre)), 0.0)
            slope_ref[pl.ds(pl.multiple_of(start, rows), rows), lanes] = found
        return carry

    lax.fori_loop(0, per_half, work, 0)


def entry_slope(facts, arrived, moments, params, slots, windows, piece):
    width = arrived.shape[2]
    return kernel_call(
        functools.partial(slope_body, slots, windows, piece),
        "entry_slope",
        (facts, arrived, moments, params),
        [SMEM, VMEM, VMEM, VMEM],
        shape((HALF_WINDOW_ROWS, width), jnp.float32),
        VMEM,
        flops=25 * HALF_WINDOW_ROWS * width,
        bytes_moved=6 * HALF_WINDOW_ROWS * width,
    )


def block_moments(values, inside, count):
    block_sum = jnp.sum(jnp.where(inside, values, 0.0), axis=0, keepdims=True)
    deviation = jnp.where(inside, values - block_sum / jnp.maximum(count, 1.0), 0.0)
    return block_sum, jnp.sum(deviation * deviation, axis=0, keepdims=True), count


def convolve_body(slots, windows, facts_ref, act_ref, weight_ref, out_ref, moments_ref, wide):
    facts = Facts(facts_ref, windows, slots)
    pieces, rows, inner = out_ref.shape
    tiles = inner // LANES
    for tile in range(3 * tiles):
        wide[tile, 0:PAD] = jnp.zeros((PAD, LANES), jnp.float32)
        wide[tile, PAD + rows : PADDED_ROWS] = jnp.zeros((PAD, LANES), jnp.float32)
    moments_ref[...] = jnp.zeros_like(moments_ref)
    below, above = PAD - DILATION_STEP, PAD + DILATION_STEP

    def work(piece, carry):
        product = jnp.dot(act_ref[piece], weight_ref[...], preferred_element_type=jnp.float32)
        for tile, lanes in enumerate(column_slices(3 * inner)):
            wide[tile, PAD : PAD + rows] = product[:, lanes]
        half = piece % 2
        limit = facts.half_limit(piece // 2, half)
        start = half * STRIP
        row = lax.broadcasted_iota(jnp.int32, (rows, 1), 0)
        end = jnp.minimum(limit, rows - STRIP + start)
        inside = jnp.logical_and(row >= start, row < end)
        count = jnp.maximum(end - start, 0).astype(jnp.float32)
        for tile, lanes in enumerate(column_slices(inner)):
            out = (
                wide[tiles + tile, PAD : PAD + rows]
                + wide[tile, below : below + rows]
                + wide[2 * tiles + tile, above : above + rows]
            )
            out_ref[piece, :, lanes] = out
            held = (moments_ref[0:1, lanes], moments_ref[1:2, lanes], moments_ref[2:3, lanes])
            moments_ref[0:1, lanes], moments_ref[1:2, lanes], moments_ref[2:3, lanes] = merged(
                held, block_moments(out, inside, count)
            )
        return carry

    lax.fori_loop(0, pieces, work, 0)


def convolve(facts, act, weight, slots, windows):
    pieces, rows, width = act.shape
    inner = weight.shape[1] // 3
    return kernel_call(
        functools.partial(convolve_body, slots, windows),
        "convolve",
        (facts, act, weight),
        [SMEM, VMEM, VMEM],
        [shape((pieces, rows, inner), jnp.float32), shape((3, inner), jnp.float32)],
        [VMEM, VMEM],
        [pltpu.VMEM((3 * inner // LANES, PADDED_ROWS, LANES), jnp.float32)],
        flops=6 * pieces * rows * width * inner,
        bytes_moved=pieces * rows * (width * 2 + inner * 4),
    )


def join_body(
    slots, windows, facts_ref, out_ref, border_ref, weight_ref, held_ref, strip_ref, moments_ref,
    moved,
):
    facts = Facts(facts_ref, windows, slots)
    pieces, rows, inner = out_ref.shape
    found = (held_ref[0:1], held_ref[1:2], held_ref[2:3])
    gap = STRIP - DILATION_STEP
    skip = BORDER - DILATION_STEP
    for piece in range(pieces):
        half = piece % 2
        other = piece + 1 - 2 * half
        moved[...] = jnp.zeros_like(moved)
        if half == 0:
            moved[gap : gap + BORDER] = jnp.dot(
                border_ref[other], weight_ref[:, 2 * inner :], preferred_element_type=jnp.float32
            )
            strip = out_ref[piece, rows - STRIP : rows] + moved[0:STRIP]
        else:
            moved[0:BORDER] = jnp.dot(
                border_ref[other], weight_ref[:, :inner], preferred_element_type=jnp.float32
            )
            strip = out_ref[piece, 0:STRIP] + moved[skip : skip + STRIP]
        strip_ref[piece] = strip
        limit = facts.half_limit(piece // 2, half) - (1 - half) * (rows - STRIP)
        count = jnp.clip(limit, 0, STRIP)
        inside = lax.broadcasted_iota(jnp.int32, (STRIP, 1), 0) < count
        found = merged(found, block_moments(strip, inside, count.astype(jnp.float32)))
    for number, value in enumerate(found):
        moments_ref[number : number + 1] = jnp.broadcast_to(value, (1, inner))


def join(facts, out, border, weight, held, slots, windows):
    pieces, rows, inner = out.shape
    return kernel_call(
        functools.partial(join_body, slots, windows),
        "join_halves",
        (facts, out, border, weight, held),
        [SMEM, VMEM, VMEM, VMEM, VMEM],
        [shape((pieces, STRIP, inner), jnp.float32), shape((3, inner), jnp.float32)],
        [VMEM, VMEM],
        [pltpu.VMEM((2 * STRIP, inner), jnp.float32)],
        flops=2 * pieces * BORDER * border.shape[2] * inner,
        bytes_moved=pieces * STRIP * inner * 8,
    )


def middle_body(
    slots, windows, facts_ref, out_ref, strip_ref, moments_ref, params_ref, grad_ref,
    act_ref, slope_ref, norm_ref, sums_ref,
):
    facts = Facts(facts_ref, windows, slots)
    pieces, rows, inner = out_ref.shape
    centre, scale, _, _ = norm_terms(moments_ref, params_ref, facts.row_count())
    gain, offset = 0.5 * params_ref[0:1], 0.5 * params_ref[1:2]
    sums_ref[...] = jnp.zeros_like(sums_ref)

    def chunk(piece, start, values):
        size = values.shape[0]
        limit = facts.half_limit(piece // 2, piece % 2)
        inside = lax.broadcasted_iota(jnp.int32, (size, 1), 0) < limit - start
        here = pl.ds(start, size)
        for lanes in column_slices(inner):
            norm = (values[:, lanes] - centre[:, lanes]) * scale[:, lanes]
            half_pre = norm * gain[:, lanes] + offset[:, lanes]
            bend, square = bent(half_pre)
            act = jnp.where(inside, half_pre + half_pre * bend, 0.0)
            act_ref[piece, here, lanes] = act.astype(jnp.bfloat16)
            grad = grad_ref[piece, here, lanes] * gelu_slope(half_pre, bend, square)
            grad = jnp.where(inside, grad, 0.0)
            slope_ref[piece, here, lanes] = grad
            norm_ref[piece, here, lanes] = norm
            sums_ref[0:1, lanes] = sums_ref[0:1, lanes] + jnp.sum(
                grad * norm, axis=0, keepdims=True
            )
            sums_ref[1:2, lanes] = sums_ref[1:2, lanes] + jnp.sum(grad, axis=0, keepdims=True)

    size = 2 * STRIP
    steps = rows // size - 1

    def main(step, carry):
        piece = step // steps
        start = pl.multiple_of((step % steps + piece % 2) * size, size)
        chunk(piece, start, out_ref[piece, pl.ds(start, size), :])
        return carry

    lax.fori_loop(0, pieces * steps, main, 0)

    def edge(slot, carry):
        low, high = 2 * slot, 2 * slot + 1
        start = rows - size
        values = jnp.concatenate([out_ref[low, start : start + STRIP], strip_ref[low]], axis=0)
        chunk(low, start, values)
        chunk(high, 0, jnp.concatenate([strip_ref[high], out_ref[high, STRIP:size]], axis=0))
        return carry

    lax.fori_loop(0, slots, edge, 0)


def middle(facts, out, strip, moments, params, grad, slots, windows):
    dims = out.shape
    return kernel_call(
        functools.partial(middle_body, slots, windows),
        "middle_norm",
        (facts, out, strip, moments, params, grad),
        [SMEM] + [VMEM] * 5,
        [
            shape(dims, jnp.bfloat16),
            shape(dims, jnp.float32),
            shape(dims, jnp.float32),
            shape((2, dims[2]), jnp.float32),
        ],
        [VMEM] * 4,
        flops=40 * out.size,
        bytes_moved=18 * out.size,
    )


def middle_grad_body(
    slots, windows, facts_ref, grad_ref, norm_ref, moments_ref, params_ref, sums_ref,
    padded_ref, border_ref,
):
    facts = Facts(facts_ref, windows, slots)
    pieces, rows, inner = grad_ref.shape
    rows_total = facts.row_count()
    _, _, slope, _ = norm_terms(moments_ref, params_ref, rows_total)
    level, tilt = sums_ref[1:2] / rows_total, sums_ref[0:1] / rows_total
    tiles = inner // LANES
    for piece in range(pieces):
        for tile in range(tiles):
            padded_ref[piece, tile, 0:PAD] = jnp.zeros((PAD, LANES), jnp.float32)
            padded_ref[piece, tile, PAD + rows : PADDED_ROWS] = jnp.zeros(
                (PAD, LANES), jnp.float32
            )
    size = 2 * STRIP

    def work(step, carry):
        piece, part = step // (rows // size), step % (rows // size)
        start = pl.multiple_of(part * size, size)
        limit = facts.half_limit(piece // 2, piece % 2)
        inside = lax.broadcasted_iota(jnp.int32, (size, 1), 0) < limit - start
        for tile, lanes in enumerate(column_slices(inner)):
            norm = norm_ref[piece, pl.ds(start, size), lanes]
            grad = slope[:, lanes] * (
                grad_ref[piece, pl.ds(start, size), lanes]
                - (level[:, lanes] + norm * tilt[:, lanes])
            )
            low = jnp.where(inside, grad, 0.0).astype(jnp.bfloat16)
            padded_ref[piece, tile, pl.ds(pl.multiple_of(start + PAD, 8), size), :] = low.astype(
                jnp.float32
            )
        return carry

    lax.fori_loop(0, pieces * (rows // size), work, 0)
    for piece in range(pieces):
        start = PAD + (0 if piece % 2 else rows - BORDER)
        for tile, lanes in enumerate(column_slices(inner)):
            border_ref[piece, :, lanes] = padded_ref[piece, tile, start : start + BORDER].astype(
                jnp.bfloat16
            )


def middle_grad(facts, grad, norm, moments, params, sums, slots, windows):
    pieces, _, inner = grad.shape
    return kernel_call(
        functools.partial(middle_grad_body, slots, windows),
        "middle_grad",
        (facts, grad, norm, moments, params, sums),
        [SMEM] + [VMEM] * 5,
        [
            shape((pieces, inner // LANES, PADDED_ROWS, LANES), jnp.float32),
            shape((pieces, BORDER, inner), jnp.bfloat16),
        ],
        [VMEM, VMEM],
        flops=8 * grad.size,
        bytes_moved=12 * grad.size,
    )


def output_body(
    slots, windows, facts_ref, act_ref, weight_ref, arrived_ref, params_ref, out_ref
):
    source, slot = pl.program_id(0), pl.program_id(1)
    rows = out_ref.shape[0]
    facts = Facts(facts_ref, windows, slots)
    per_half = HALF_WINDOW_ROWS // rows
    half, start = source // per_half, (source % per_half) * rows
    inside = lax.broadcasted_iota(jnp.int32, (rows, 1), 0) < facts.half_limit(slot, half) - start
    mixed = jnp.dot(act_ref[...], weight_ref[...], preferred_element_type=jnp.float32)
    block = arrived_ref[0].astype(jnp.float32) + mixed + params_ref[2:3]
    out_ref[...] = jnp.where(inside, block, 0.0)


def output_rows(facts, act, weight, arrived, params, slots, windows):
    blocks, rows, width = arrived.shape
    inner = act.shape[1]
    sources = blocks // slots
    place = lambda s, j: (j * sources + s, 0)
    return pl.pallas_call(
        functools.partial(output_body, slots, windows),
        grid=(sources, slots),
        in_specs=[
            SMEM,
            pl.BlockSpec((rows, inner), place),
            pl.BlockSpec((inner, width), lambda s, j: (0, 0)),
            pl.BlockSpec((1, rows, width), lambda s, j: (s * slots + j, 0, 0)),
            pl.BlockSpec((3, width), lambda s, j: (0, 0)),
        ],
        out_specs=pl.BlockSpec((rows, width), place),
        out_shape=shape((blocks * rows, width), jnp.float32),
        compiler_params=pltpu.CompilerParams(vmem_limit_bytes=16 << 20),
        cost_estimate=pl.CostEstimate(
            flops=2 * act.size * width, bytes_accessed=8 * arrived.size, transcendentals=0
        ),
        name="output_rows",
    )(facts, act, weight, arrived, params)


def entry_grad_body(
    slots, windows, slot, facts_ref, padded_ref, border_ref, weight_ref, *refs
):
    slope_refs, (arrived_ref, block_ref, moments_ref, params_ref) = refs[:2], refs[2:6]
    sent_ref, taps_ref, sums_ref, wide, packed, departures = refs[6:]
    facts = Facts(facts_ref, windows, slots)
    sources, rows, width = packed.shape
    tiles = padded_ref.shape[1]
    per_half = HALF_WINDOW_ROWS // rows
    centre, scale, slope, _ = norm_terms(moments_ref, params_ref, facts.row_count())
    skip = BORDER - DILATION_STEP
    sums_ref[...] = jnp.zeros_like(sums_ref)

    def departure(source):
        return pltpu.make_async_copy(
            packed.at[source], sent_ref.at[source], departures.at[source]
        )

    for half in range(2):
        piece = slot * 2 + half
        other = slot * 2 + 1 - half
        for tile, lanes in enumerate(column_slices(tiles * LANES)):
            border = border_ref[other, :, lanes].astype(jnp.float32)
            wide[tile] = padded_ref[piece, tile]
            if half == 0:
                end = PAD + HALF_WINDOW_ROWS
                wide[tile, end : end + DILATION_STEP] = border[0:DILATION_STEP]
            else:
                wide[tile, PAD - DILATION_STEP : PAD] = border[skip:BORDER]
            for tap in range(3):
                start = PAD - (tap - 1) * DILATION_STEP
                first = (tap * tiles + tile) * LANES
                taps_ref[half, :, first : first + LANES] = wide[
                    tile, start : start + HALF_WINDOW_ROWS
                ].astype(jnp.bfloat16)
        for column in range(0, width, 2 * LANES):
            grad = jnp.dot(
                taps_ref[half],
                weight_ref[:, column : column + 2 * LANES],
                preferred_element_type=jnp.float32,
            )
            for part in range(per_half):
                source = half * per_half + part
                here = slice(part * rows, (part + 1) * rows)
                for start in (column, column + LANES):
                    lanes = slice(start, start + LANES)
                    pre = grad[here, start - column : start - column + LANES]
                    pre = pre * slope_refs[half][here, lanes]
                    values = arrived_ref[source * slots + slot, :, lanes].astype(jnp.float32)
                    sums_ref[0:1, lanes] = sums_ref[0:1, lanes] + jnp.sum(
                        pre * values, axis=0, keepdims=True
                    )
                    sums_ref[1:2, lanes] = sums_ref[1:2, lanes] + jnp.sum(
                        pre, axis=0, keepdims=True
                    )
                    block = block_ref[piece, here, lanes].astype(jnp.float32)
                    packed[source, :, lanes] = (pre * slope[:, lanes] + block).astype(
                        jnp.bfloat16
                    )
        for part in range(per_half):
            departure(half * per_half + part).start()
    sums_ref[0:1] = (sums_ref[0:1] - centre * sums_ref[1:2]) * scale
    for source in range(sources):
        departure(source).wait()


def entry_grad(
    facts, padded, border, weight, slopes, arrived, block, moments, params, slots, windows, slot
):
    blocks, rows, width = arrived.shape
    inner = border.shape[2]
    sources = blocks // slots
    return kernel_call(
        functools.partial(entry_grad_body, slots, windows, slot),
        "entry_grad",
        (facts, padded, border, weight, *slopes, arrived, block, moments, params),
        [SMEM] + [VMEM] * 9,
        [
            pltpu.HBM((sources, rows, width), jnp.bfloat16),
            shape((2, HALF_WINDOW_ROWS, 3 * inner), jnp.bfloat16),
            shape((2, width), jnp.float32),
        ],
        [HBM, VMEM, VMEM],
        [
            pltpu.VMEM((inner // LANES, PADDED_ROWS, LANES), jnp.float32),
            pltpu.VMEM((sources, rows, width), jnp.bfloat16),
            pltpu.SemaphoreType.DMA((sources,)),
        ],
        flops=2 * 2 * HALF_WINDOW_ROWS * 3 * inner * width,
        bytes_moved=2 * HALF_WINDOW_ROWS * (width * 10 + inner * 10),
    )


def flat_mask(bits):
    return sum(mask * (lax.axis_size("seq") if axis == "grp" else 1) for axis, mask in bits)


def from_flat_partner(block, mask):
    count = lax.axis_size("grp") * lax.axis_size("seq")
    return lax.ppermute(
        block, ("grp", "seq"), [(place, place ^ mask) for place in range(count)]
    )


def bit_of(axis, mask):
    return (lax.axis_index(axis) // mask) % 2


def square_phases():
    steps = exchange_steps()[1:]
    outer = [step for step in steps if step[0] == "grp"]
    inner = [step for step in steps if step[0] == "seq"]
    ordered = []
    while outer and inner:
        ordered += [outer.pop(0), inner.pop(0)]
    ordered += outer + inner
    return [ordered[start : start + 2] for start in range(0, len(ordered), 2)]


def phase_place(phase):
    return sum(bit_of(*step) * 2**number for number, step in enumerate(phase))


def phase_parts(phase):
    parts = 2 ** len(phase)
    masks = [
        flat_mask([step for number, step in enumerate(phase) if part >> number & 1])
        for part in range(parts)
    ]
    return parts, masks


def scatter_starts(phase, rows):
    parts, _ = phase_parts(phase)
    mine = phase_place(phase)
    return [jnp.bitwise_xor(mine, part) * (rows // parts) for part in range(parts)]


def scatter_sum(buffer, phase, starts):
    parts, masks = phase_parts(phase)
    rows = buffer.shape[0] // parts
    kept = lax.dynamic_slice_in_dim(buffer, starts[0], rows)
    for part in range(1, parts):
        sent = lax.dynamic_slice_in_dim(buffer, starts[part], rows).astype(jnp.bfloat16)
        kept = kept + from_flat_partner(sent, masks[part]).astype(jnp.float32)
    return kept


def gather_parts(buffer, phase, mine):
    parts, masks = phase_parts(phase)
    found = [buffer] + [from_flat_partner(buffer, masks[part]) for part in range(1, parts)]
    orders = [
        jnp.concatenate([found[place ^ own] for place in range(parts)], axis=0)
        for own in range(parts)
    ]
    result = orders[0]
    for own in range(1, parts):
        result = jnp.where(mine == own, orders[own], result)
    return result


def finish_body(facts_ref, mine_ref, other_ref, dilated_ref, pointwise_ref):
    inner = dilated_ref.shape[2]

    def write(low_ref, high_ref):
        dilated_ref[0] = low_ref[:, :inner].astype(jnp.float32)
        dilated_ref[1] = low_ref[:, inner:].astype(jnp.float32)
        dilated_ref[2] = high_ref[:, :inner].astype(jnp.float32)
        pointwise_ref[...] = high_ref[:, inner:].astype(jnp.float32).T

    upper = facts_ref[0] % 2

    @pl.when(upper == 0)
    def _():
        write(mine_ref, other_ref)

    @pl.when(upper == 1)
    def _():
        write(other_ref, mine_ref)


def finish_weights(facts, mine, other):
    width, both = mine.shape
    inner = both // 2
    return kernel_call(
        finish_body,
        "finish_weights",
        (facts, mine, other),
        [SMEM, VMEM, VMEM],
        [shape((3, width, inner), jnp.float32), shape((inner, width), jnp.float32)],
        [VMEM, VMEM],
        flops=width * both,
        bytes_moved=12 * width * both,
        grant=16 << 20,
    )


def per_device(
    signal,
    entry_gain,
    entry_shift,
    dilated_kernel,
    middle_gain,
    middle_shift,
    pointwise_kernel,
    pointwise_bias,
    lengths,
    assignment,
    cotangent,
):
    seq_count = lax.axis_size("seq")
    windows, segment, width = signal.shape
    inner = pointwise_kernel.shape[0]
    slots = windows // seq_count
    rows = segment // 2
    pieces = 2 * slots
    places = jnp.stack([lax.axis_index("grp"), lax.axis_index("seq"), jnp.int32(seq_count)])
    facts = jnp.concatenate([places.astype(jnp.int32), assignment[0], lengths])
    entry_params = jnp.stack([entry_gain, entry_shift, pointwise_bias])
    middle_params = jnp.stack([middle_gain, middle_shift])

    outgoing, first_chosen, entry_local = pool(facts, signal, slots)
    arrived = lax.all_to_all(outgoing, "seq", split_axis=0, concat_axis=0, tiled=True)
    entry_moments = total_moments(entry_local)

    kernel_low = dilated_kernel.astype(jnp.bfloat16)
    wide_kernel = jnp.concatenate([kernel_low[tap] for tap in range(3)], axis=1)
    pointwise_low = pointwise_kernel.astype(jnp.bfloat16)
    back_kernel = jnp.swapaxes(kernel_low, 1, 2).reshape(3 * inner, width)
    grad_block, grad_middle, bias_part = prepare(
        facts, cotangent, pointwise_low, slots, windows
    )
    phases = square_phases()
    starts, held_rows = [], width
    for phase in phases:
        starts.append(scatter_starts(phase, held_rows))
        held_rows //= 2 ** len(phase)
    spots = [phase_place(phase) for phase in phases]
    first_axis, first_mask = exchange_steps()[0]
    upper = bit_of(first_axis, first_mask)
    (
        arrived,
        grad_block,
        grad_middle,
        wide_kernel,
        back_kernel,
        pointwise_low,
        starts,
        spots,
        upper,
        middle_params,
        facts,
    ) = lax.optimization_barrier(
        (
            arrived,
            grad_block,
            grad_middle,
            wide_kernel,
            back_kernel,
            pointwise_low,
            starts,
            spots,
            upper,
            middle_params,
            facts,
        )
    )
    upper = upper == 1

    act, act_border = activate(facts, arrived, entry_moments, entry_params, slots, windows)
    act_border = from_partner(act_border, "seq", 1)
    dilated, held_moments = convolve(facts, act, wide_kernel, slots, windows)
    strip, middle_moments = join(
        facts, dilated, act_border, wide_kernel, held_moments, slots, windows
    )
    slopes = []
    for number, (axis, mask) in enumerate(exchange_steps()):
        other = from_partner(middle_moments, axis, mask)
        if number and len(slopes) < pieces:
            tied, middle_moments = lax.optimization_barrier((arrived, middle_moments))
            found = entry_slope(
                facts, tied, entry_moments, entry_params, slots, windows, len(slopes)
            )
            other, found = lax.optimization_barrier((other, found))
            slopes.append(found)
        middle_moments = jnp.concatenate(
            merged(
                (middle_moments[0:1], middle_moments[1:2], middle_moments[2:3]),
                (other[0:1], other[1:2], other[2:3]),
            ),
            axis=0,
        )
    while len(slopes) < pieces:
        slopes.append(
            entry_slope(facts, arrived, entry_moments, entry_params, slots, windows, len(slopes))
        )
    middle_act, middle_slope, middle_norm, middle_sums = middle(
        facts,
        dilated,
        strip,
        middle_moments,
        middle_params,
        grad_middle.reshape(pieces, HALF_WINDOW_ROWS, inner),
        slots,
        windows,
    )
    flat_act = middle_act.reshape(-1, inner)
    for number, (axis, mask) in enumerate(exchange_steps()):
        other = from_partner(middle_sums, axis, mask)
        if number == 1:
            tied, middle_sums = lax.optimization_barrier((flat_act, middle_sums))
            pointwise_part = jnp.einsum(
                "rd,rf->df", grad_block, tied, preferred_element_type=jnp.float32
            )
            other, pointwise_part = lax.optimization_barrier((other, pointwise_part))
        middle_sums = middle_sums + other
    padded, grad_border = middle_grad(
        facts, middle_slope, middle_norm, middle_moments, middle_params, middle_sums, slots, windows
    )
    grad_border = from_partner(grad_border, "seq", 1)
    block_pieces = grad_block.reshape(pieces, HALF_WINDOW_ROWS, width)
    sent, taps, entry_part = [], [], jnp.concatenate([jnp.zeros_like(bias_part)] * 2)
    for slot in range(slots):
        slot_sent, slot_taps, part = entry_grad(
            facts, padded, grad_border, back_kernel, slopes[2 * slot : 2 * slot + 2], arrived,
            block_pieces, entry_moments, entry_params, slots, windows, slot,
        )
        sent.append(slot_sent)
        taps.append(slot_taps)
        entry_part = entry_part + part
    entry_sums = jnp.concatenate([entry_part, bias_part])

    def send_back(block):
        return lax.all_to_all(block, "seq", split_axis=0, concat_axis=0, tiled=True)

    returned = [send_back(sent[0])]
    flat_act, act, *taps = lax.optimization_barrier((flat_act, act, *taps, sent[-1]))[:-1]
    activations = output_rows(
        facts, flat_act, pointwise_low, arrived, entry_params, slots, windows
    )
    dilated_part = sum(
        jnp.einsum(
            "hrc,hrf->cf",
            act[2 * slot : 2 * slot + 2],
            slot_taps,
            preferred_element_type=jnp.float32,
        )
        for slot, slot_taps in enumerate(taps)
    )
    low_half = dilated_part[:, : 2 * inner]
    high_half = jnp.concatenate([dilated_part[:, 2 * inner :], pointwise_part], axis=1)
    other = from_partner(
        jnp.where(upper, low_half, high_half).astype(jnp.bfloat16), first_axis, first_mask
    )
    buffer = jnp.where(upper, high_half, low_half) + other.astype(jnp.float32)
    for number, phase in enumerate(phases):
        if number == len(phases) - 1:
            buffer, entry_sums, returned[0], activations = lax.optimization_barrier(
                (buffer, entry_sums, returned[0], activations)
            )
        buffer = scatter_sum(buffer, phase, starts[number])
    entry_sums = total(entry_sums)
    buffer = buffer.astype(jnp.bfloat16)
    for number, phase in reversed(list(enumerate(phases))):
        buffer = gather_parts(buffer, phase, spots[number])
        if number == len(phases) - 1:
            buffer, entry_sums, *later = lax.optimization_barrier(
                (buffer, entry_sums, *sent[1:])
            )
            returned += [send_back(block) for block in later]
    other = from_partner(buffer, first_axis, first_mask)
    dilated_kernel_gradient, pointwise_kernel_gradient = finish_weights(facts, buffer, other)
    signal_gradient = None
    for slot in range(slots):
        signal_gradient = unpool(
            facts, returned[slot], outgoing, first_chosen, entry_moments, entry_sums,
            entry_params, slots, slot, signal_gradient,
        )
    return (
        activations,
        signal_gradient,
        entry_sums[0],
        entry_sums[1],
        dilated_kernel_gradient,
        middle_sums[0],
        middle_sums[1],
        pointwise_kernel_gradient,
        entry_sums[2],
    )


def solution(mesh):
    return jax.shard_map(
        per_device,
        mesh=mesh,
        in_specs=(
            P("grp", "seq", None),
            P(),
            P(),
            P(),
            P(),
            P(),
            P(),
            P(),
            P(),
            P("grp", None),
            P(("grp", "seq"), None),
        ),
        out_specs=(
            P(("grp", "seq"), None),
            P("grp", "seq", None),
            P(),
            P(),
            P(),
            P(),
            P(),
            P(),
            P(),
        ),
        check_vma=False,
    )
```

time: 668 us -> 299 us (0.45); the launches traced: 655 us -> 295 us
  blocking collectives: 244 us -> 0 us
  waiting for transfers between devices: 181 us -> 101 us
  Pallas kernels: 0 us -> 71.9 us
  other arithmetic: 72.6 us -> 12.2 us
  local copies, waits for them, and re-layouts: 88.4 us -> 34 us
  starting transfers between devices: 15.3 us -> 64.2 us
  matrix products: 38.7 us -> 9.65 us
  between operations: 14.9 us -> 1.57 us
    psum x6 -> x0, blocking collectives: 244 us -> none  [the longest x2 83.3 us: moments(): lax.psum(jnp.sum(values * valid_mask, axis=(0, 1)), ('grp', 'seq'))]
    all_to_all x2 -> x3, waiting for transfers between devices: 112 us -> 0.01 us  [the longest x2 0.01 us: send_back(): return lax.all_to_all(block, 'seq', split_axis=0, concat_axis=0, tiled=True)]
    ppermute x2 -> x36, waiting for transfers between devices: 6.55 us -> 101 us  [the longest x24 65.3 us: from_partner(): lax.ppermute(block, axis, [(place, place ^ mask) for place in range(count)])]
    pallas_call x0 -> x17, Pallas kernels: none -> 71.9 us  [the longest x13 48.1 us: kernel_call(): pl.pallas_call(body, in_specs=specs, out_specs=out_specs, out_shape=outpu...]
    psum x1 -> x0, waiting for transfers between devices: 62.4 us -> none  [per_device(): lax.psum((entry_gain_part, entry_shift_part, kernel_part), ('grp', 'seq'))]
    ppermute x2 -> x36, starting transfers between devices: 2.65 us -> 47.6 us  [the longest x24 36 us: from_partner(): lax.ppermute(block, axis, [(place, place ^ mask) for place in range(count)])]
    convert_element_type x12 -> x3, other arithmetic: 36.7 us -> 1.53 us  [the longest x1 1.42 us: per_device(): jnp.where(upper, low_half, high_half).astype(jnp.bfloat16)]
    dot_general x12 -> x3, matrix products: 38.7 us -> 9.65 us  [the longest x2 6.81 us: per_device(): jnp.einsum('hrc,hrf->cf', act[2 * slot:2 * slot + 2], slot_taps, preferre...]
  transfers between devices with their start and end apart: 5 -> 39, of which waited for: 5 -> 22; matrix products, arithmetic and copies ran while one was open for 14% -> 9% of each run, Pallas kernels for 0% -> 12%
where the time goes in v2:
time: 299 us; the launch traced here: 295 us
  waiting for transfers between devices  101 us (34%)
  Pallas kernels  71.9 us (24%)
  starting transfers between devices  64.2 us (21%)
  local copies, waits for them, and re-layouts  34 us (11%)
  other arithmetic  12.2 us (4%)
  matrix products  9.65 us (3%)
    ppermute x24, waiting for transfers between devices, from_partner(): lax.ppermute(block, axis, [(place, place ^ mask) for place in range(count)])  65.3 us
    pallas_call x13, Pallas kernels, kernel_call(): pl.pallas_call(body, in_specs=specs, out_specs=out_specs, out_shape=outpu...  48.1 us
    ppermute x12, waiting for transfers between devices, from_flat_partner(): lax.ppermute(block, ('grp', 'seq'), [(place, place ^ mask) for place in r...  36.1 us
    ppermute x24, starting transfers between devices, from_partner(): lax.ppermute(block, axis, [(place, place ^ mask) for place in range(count)])  36 us
    unnamed x80, local copies, waits for them, and re-layouts  26.8 us
    ppermute x12, starting transfers between devices, from_flat_partner(): lax.ppermute(block, ('grp', 'seq'), [(place, place ^ mask) for place in r...  11.6 us
    all_to_all x2, starting transfers between devices, send_back(): return lax.all_to_all(block, 'seq', split_axis=0, concat_axis=0, tiled=True)  11 us
    pallas_call x2, Pallas kernels, unpool(): pl.pallas_call(functools.partial(unpool_body, slots, slot, windows), in_s...  10.6 us
  transfers between devices with their start and end apart: 39, of which 22 were waited for; matrix products, arithmetic and copies ran while one was open for 9% of the time, Pallas kernels for 12%

profile of v2, /device:TPU:17, one launch (start us, length us, event | category | flops | bytes accessed | tf_op | source)
XLA Modules:
  0.0 294.9 jit_solution(10858680562822287074)
XLA Ops:
  1.4 10.3 %pool.1 = (bf16[16,128,768]{2,1,0:T(8,128)(2,1)}, bf16[16,128,768]{2,1,0:T(8,128)(2,1)}, f32[3,768]{1,0:T(4,128)S(1)}) custom-call(s32[83]{0:T(128)S(1)} %concatenate.66.facts_ref, f32[16,256,768]{2,1,0:T(8,128)} %signal_ref.1), custom_call_target="tpu_custom_call" | custom-call | flops 15728640 | bytes 18874368 | tf_op jit(solution)/shard_map/pool/pallas_call | solution.py:104
  11.7 5.6 %all-to-all-start = ((bf16[16,128,768]{2,1,0:T(8,128)(2,1)}), bf16[16,128,768]{2,1,0:T(8,128)(2,1)S(1)}, u32[]{:S(2)}, u32[]{:S(2)}) async-start(bf16[16,128,768]{2,1,0:T(8,128)(2,1)} %get-tuple-element.85.pooled_ref), calls=%async_computation | async-start | bytes 6291456 | tf_op jit(solution)/shard_map/all_to_all | solution.py:985
  18.6 3.5 %convert_bitcast_fusion = bf16[3,384,768]{1,2,0:T(8,128)(2,1)} fusion(f32[3,768,384]{2,1,0:T(8,128)} %param.14), kind=kLoop, calls=%fused_computation.79 | loop fusion | flops 884736 | bytes 5308416 | tf_op jit(solution)/shard_map/transpose | solution.py:991
  28.0 14.6 %collective-permute-done.2 = f32[3,768]{1,0:T(4,128)S(1)} collective-permute-done((f32[3,768]{1,0:T(4,128)S(1)}, f32[3,768]{1,0:T(4,128)S(1)}, u32[]{:S(2)}, u32[]{:S(2)}) %collective-permute-start.2) | collective-permute-done | bytes 9248 | tf_op jit(solution)/shard_map/ppermute | solution.py:33
  44.6 4.2 %prepare_cotangent.1 = (bf16[2048,768]{1,0:T(8,128)(2,1)S(1)}, f32[2048,384]{1,0:T(8,128)S(1)}, f32[1,768]{1,0:T(1,128)S(1)}) custom-call(s32[83]{0:T(128)S(1)} %concatenate.66.facts_ref, f32[2048,768]{1,0:T(8,128)S(1)} %bitcast.34, bf16[384,768]{1,0:T(8,128)(2,1)S(1)} %convert_element_type.51.weight_ref), custom_call_target="tpu_custom_call" | custom-call | flops 1207959552 | bytes 12582912 | tf_op jit(solution)/shard_map/prepare_cotangent/pallas_call | solution.py:355
  52.1 17.4 %collective-permute-done.3 = f32[3,768]{1,0:T(4,128)S(1)} collective-permute-done((f32[3,768]{1,0:T(4,128)S(1)}, f32[3,768]{1,0:T(4,128)S(1)}, u32[]{:S(2)}, u32[]{:S(2)}) %collective-permute-start.3) | collective-permute-done | bytes 9248 | tf_op jit(solution)/shard_map/ppermute | solution.py:33
  69.8 3.8 %copy.21 = bf16[3,384,768]{2,1,0:T(8,128)(2,1)} copy(bf16[3,384,768]{1,2,0:T(8,128)(2,1)} %convert_bitcast_fusion) | data formatting | bytes 3538944 | tf_op jit(solution)/shard_map/transpose | solution.py:991
  73.7 11.0 %collective-permute-done.4 = f32[3,768]{1,0:T(4,128)S(1)} collective-permute-done((f32[3,768]{1,0:T(4,128)S(1)}, f32[3,768]{1,0:T(4,128)S(1)}, u32[]{:S(2)}, u32[]{:S(2)}) %collective-permute-start.4) | collective-permute-done | bytes 9248 | tf_op jit(solution)/shard_map/ppermute | solution.py:33
  84.7 3.7 %activate.1 = (bf16[4,512,768]{2,1,0:T(8,128)(2,1)S(1)}, bf16[4,48,768]{2,1,0:T(8,128)(2,1)S(1)}) custom-call(s32[83]{0:T(128)S(1)} %concatenate.66.facts_ref, bf16[16,128,768]{2,1,0:T(8,128)(2,1)S(1)} %all-to-all-done.arrived_ref.refs_2_, f32[3,768]{1,0:T(4,128)S(1)} %get-tuple-element.205.moments_ref.refs_4_, ...), custom_call_target="tpu_custom_call" | custom-call | flops 31457280 | bytes 6291456 | tf_op jit(solution)/shard_map/activate/pallas_call | solution.py:104
  90.0 6.6 %convolve.1 = (f32[4,512,384]{2,1,0:T(8,128)S(1)}, f32[3,384]{1,0:T(4,128)S(1)}) custom-call(s32[83]{0:T(128)S(1)} %concatenate.66.facts_ref, bf16[4,512,768]{2,1,0:T(8,128)(2,1)S(1)} %get-tuple-element.131.act_ref, bf16[768,1152]{1,0:T(8,128)(2,1)S(1)} %copy-done.7), custom_call_target="tpu_custom_call" | custom-call | flops 3623878656 | bytes 6291456 | tf_op jit(solution)/shard_map/convolve/pallas_call | solution.py:104
  108.9 3.2 %collective-permute-start.9 = (f32[3,384]{1,0:T(4,128)S(1)}, f32[3,384]{1,0:T(4,128)S(1)}, u32[]{:S(2)}, u32[]{:S(2)}) collective-permute-start(f32[3,384]{1,0:T(4,128)S(1)} %pad_maximum_fusion.11), channel_id=1, source_target_pairs={{0,2},{1,3},{2,0},{3,1},{4,6},{5,7},{6,4},{7,5},{8,10},{9,11},{10,... | collective-permute-start | bytes 13832 | tf_op jit(solution)/shard_map/ppermute | solution.py:33
  118.8 4.2 %middle_norm.1 = (bf16[4,512,384]{2,1,0:T(8,128)(2,1)S(1)}, f32[4,512,384]{2,1,0:T(8,128)S(1)}, f32[4,512,384]{2,1,0:T(8,128)S(1)}, f32[2,384]{1,0:T(2,128)S(1)}) custom-call(s32[83]{0:T(128)S(1)} %concatenate.66.facts_ref, f32[4,512,384]{2,1,0:T(8,128)S(1)} %get-tuple-element.94.out_ref, f32[4,64,384]{2,1,0:T(8,128)S(1)} %get-tuple-element.97.strip_ref, ...), custom_call_target="tpu_custom_call" | custom-call | flops 31457280 | bytes 14155776 | tf_op jit(solution)/shard_map/middle_norm/pallas_call | solution.py:104
  123.0 2.4 collective-permute-start.11
  126.5 2.8 fusion.7
  142.6 2.9 collective-permute-done.16.border_ref
  153.7 4.7 %entry_grad.2 = (bf16[8,128,768]{2,1,0:T(8,128)(2,1)}, bf16[2,512,1152]{2,1,0:T(8,128)(2,1)S(1)}, f32[2,768]{1,0:T(2,128)S(1)}) custom-call(s32[83]{0:T(128)S(1)} %concatenate.66.facts_ref, f32[4,3,592,128]{3,2,1,0:T(8,128)S(1)} %copy-done.6, bf16[4,48,384]{2,1,0:T(8,128)(2,1)S(1)} %collective-permute-done.16.border_ref, bf16[1152,768]{1,0:T(8,128)(2,1)S(1)} %bitcast.29, ...), custom_call_target="tpu_custom_call" | custom-call | flops 1811939328 | bytes 11796480 | tf_op jit(solution)/shard_map/entry_grad/pallas_call | solution.py:104
  159.8 4.9 %entry_grad.3 = (bf16[8,128,768]{2,1,0:T(8,128)(2,1)}, bf16[2,512,1152]{2,1,0:T(8,128)(2,1)S(1)}, f32[2,768]{1,0:T(2,128)S(1)}) custom-call(s32[83]{0:T(128)S(1)} %concatenate.66.facts_ref, f32[4,3,592,128]{3,2,1,0:T(8,128)S(1)} %copy-done.6, bf16[4,48,384]{2,1,0:T(8,128)(2,1)S(1)} %collective-permute-done.16.border_ref, bf16[1152,768]{1,0:T(8,128)(2,1)S(1)} %bitcast.30, ...), custom_call_target="tpu_custom_call" | custom-call | flops 1811939328 | bytes 11796480 | tf_op jit(solution)/shard_map/entry_grad/pallas_call | solution.py:104
  166.1 5.4 %all-to-all-start.1 = ((bf16[8,128,768]{2,1,0:T(8,128)(2,1)}), bf16[8,128,768]{2,1,0:T(8,128)(2,1)}, u32[]{:S(2)}, u32[]{:S(2)}) async-start(bf16[8,128,768]{2,1,0:T(8,128)(2,1)} %get-tuple-element.142), calls=%async_computation.1 | async-start | bytes 3145728 | tf_op jit(solution)/shard_map/all_to_all | solution.py:1096
  171.6 4.5 %convolution_bitcast_fusion.1 = f32[768,1152]{1,0:T(8,128)S(1)} fusion(bf16[4,512,768]{2,1,0:T(8,128)(2,1)} %copy-done.23, bf16[2,512,1152]{2,1,0:T(8,128)(2,1)} %copy-done.22), kind=kOutput, calls=%fused_computation.2 | convolution fusion | flops 1811939328 | bytes 9043968 | tf_op jit(solution)/shard_map/hrc,hrf->cf/dot_general | solution.py:1104
  182.0 5.6 %collective-permute-start.17 = (bf16[768,768]{1,0:T(8,128)(2,1)}, bf16[768,768]{1,0:T(8,128)(2,1)}, u32[]{:S(2)}, u32[]{:S(2)}) collective-permute-start(bf16[768,768]{1,0:T(8,128)(2,1)} %select_convert_fusion), channel_id=1, source_target_pairs={{0,8},{8,0},{16,24},{24,16},{1,9},{9,1},{17,25},{25,17},{2,10},{10... | collective-permute-start | bytes 3538952 | tf_op jit(solution)/shard_map/ppermute | solution.py:33
  187.6 2.8 collective-permute-done.17
  190.4 3.0 %convert_add_fusion = f32[768,768]{1,0:T(8,128)S(1)} fusion(bf16[768,768]{1,0:T(8,128)(2,1)} %collective-permute-done.17, f32[768,1152]{1,0:T(8,128)} %copy-done.30, f32[768,384]{1,0:T(8,128)} %fusion.7, f32[768,384]{1,0:T(8,128)} %copy-done.28, pred[]{:T(512)S(6)} %eq.31), kind=kLoop, calls=%fused_computation.4 | loop fusion | flops 2359296 | bytes 8257537 | tf_op jit(solution)/shard_map/add | solution.py:1117
  201.0 9.0 %output_rows.1 = f32[2048,768]{1,0:T(8,128)} custom-call(s32[83]{0:T(128)S(1)} %concatenate.66.facts_ref, bf16[2048,384]{1,0:T(8,128)(2,1)S(1)} %bitcast.32, bf16[384,768]{1,0:T(8,128)(2,1)S(1)} %copy-done.19, bf16[16,128,768]{2,1,0:T(8,128)(2,1)S(1)} %all-to-all-done.arrived_ref.refs_2_, f32[3,768]{1,0:T(4,128)S(1)} %get-tuple-element.206.params_ref.refs_5_), custom_call_target="tpu_custom_call" | custom-call | flops 1207959552 | bytes 12582912 | tf_op jit(solution)/shard_map/output_rows/pallas_call | solution.py:743
  210.0 5.4 %collective-permute-done.19 = bf16[192,768]{1,0:T(8,128)(2,1)} collective-permute-done((bf16[192,768]{1,0:T(8,128)(2,1)}, bf16[192,768]{1,0:T(8,128)(2,1)}, u32[]{:S(2)}, u32[]{:S(2)}) %collective-permute-start.19) | collective-permute-done | bytes 294944 | tf_op jit(solution)/shard_map/ppermute | solution.py:862
  221.2 2.5 collective-permute-done.22
  235.8 2.4 collective-permute-start.30
  242.9 5.5 %all-to-all-start.2 = ((bf16[8,128,768]{2,1,0:T(8,128)(2,1)}), bf16[8,128,768]{2,1,0:T(8,128)(2,1)}, u32[]{:S(2)}, u32[]{:S(2)}) async-start(bf16[8,128,768]{2,1,0:T(8,128)(2,1)} %get-tuple-element.153), calls=%async_computation.2 | async-start | bytes 3145728 | tf_op jit(solution)/shard_map/all_to_all | solution.py:1096
  251.1 2.9 collective-permute-done.34
  254.0 23.6 %collective-permute-done.33 = bf16[192,768]{1,0:T(8,128)(2,1)S(1)} collective-permute-done((bf16[192,768]{1,0:T(8,128)(2,1)S(1)}, bf16[192,768]{1,0:T(8,128)(2,1)S(1)}, u32[]{:S(2)}, u32[]{:S(2)}) %collective-permute-start.33) | collective-permute-done | bytes 294944 | tf_op jit(solution)/shard_map/ppermute | solution.py:862
  280.3 5.3 %unpool.2.refs_0_ = f32[16,256,768]{2,1,0:T(8,128)} custom-call(s32[83]{0:T(128)S(1)} %concatenate.66.facts_ref, bf16[8,128,768]{2,1,0:T(8,128)(2,1)} %all-to-all-done.1.returned_ref, bf16[16,128,768]{2,1,0:T(8,128)(2,1)} %get-tuple-element.85.pooled_ref, bf16[16,128,768]{2,1,0:T(8,128)(2,1)} %get-tuple-element.154.first_ref, ...), custom_call_target="tpu_custom_call" | custom-call | flops 7864320 | bytes 11010048 | tf_op jit(solution)/shard_map/unpool/pallas_call | solution.py:305
  286.3 3.1 %finish_weights.1 = (f32[3,768,384]{2,1,0:T(8,128)}, f32[384,768]{1,0:T(8,128)}) custom-call(s32[83]{0:T(128)S(1)} %concatenate.66.facts_ref, bf16[768,768]{1,0:T(8,128)(2,1)S(1)} %maximum_select_fusion.mine_ref, bf16[768,768]{1,0:T(8,128)(2,1)S(1)} %collective-permute-done.35.other_ref), custom_call_target="tpu_custom_call" | custom-call | flops 589824 | bytes 7077888 | tf_op jit(solution)/shard_map/finish_weights/pallas_call | solution.py:104
  289.4 5.3 %unpool.3 = f32[16,256,768]{2,1,0:T(8,128)} custom-call(s32[83]{0:T(128)S(1)} %concatenate.66.facts_ref, bf16[8,128,768]{2,1,0:T(8,128)(2,1)} %all-to-all-done.2.returned_ref, bf16[16,128,768]{2,1,0:T(8,128)(2,1)} %get-tuple-element.85.pooled_ref, bf16[16,128,768]{2,1,0:T(8,128)(2,1)} %get-tuple-element.154.first_ref, ...), custom_call_target="tpu_custom_call", output_to_operand_aliasing={{}: (7, {})} | custom-call | flops 7864320 | bytes 11010048 | tf_op jit(solution)/shard_map/unpool/pallas_call | solution.py:305
  (203 shorter events, 100.9 us)
Async XLA Ops:
  11.7 73.0 %all-to-all-start = ((bf16[16,128,768]{2,1,0:T(8,128)(2,1)}), bf16[16,128,768]{2,1,0:T(8,128)(2,1)S(1)}, u32[]{:S(2)}, u32[]{:S(2)}) async-start(bf16[16,128,768]{2,1,0:T(8,128)(2,1)} %get-tuple-element.85.pooled_ref), calls=%async_computation | async-start | bytes 6291456 | tf_op jit(solution)/shard_map/all_to_all | solution.py:985
  17.3 4.9 %collective-permute-start = (f32[3,768]{1,0:T(4,128)S(1)}, f32[3,768]{1,0:T(4,128)S(1)}, u32[]{:S(2)}, u32[]{:S(2)}) collective-permute-start(f32[3,768]{1,0:T(4,128)S(1)} %get-tuple-element.91), channel_id=1, source_target_pairs={{0,8},{8,0},{16,24},{24,16},{1,9},{9,1},{17,25},{25,17},{2,10},{10... | collective-permute-start | bytes 27656 | tf_op jit(solution)/shard_map/ppermute | solution.py:33
  25.3 17.3 %collective-permute-start.2 = (f32[3,768]{1,0:T(4,128)S(1)}, f32[3,768]{1,0:T(4,128)S(1)}, u32[]{:S(2)}, u32[]{:S(2)}) collective-permute-start(f32[3,768]{1,0:T(4,128)S(1)} %pad_maximum_fusion.3), channel_id=1, source_target_pairs={{0,1},{1,0},{2,3},{3,2},{4,5},{5,4},{6,7},{7,6},{8,9},{9,8},{10,11... | collective-permute-start | bytes 27656 | tf_op jit(solution)/shard_map/ppermute | solution.py:33
  42.7 26.9 %collective-permute-start.3 = (f32[3,768]{1,0:T(4,128)S(1)}, f32[3,768]{1,0:T(4,128)S(1)}, u32[]{:S(2)}, u32[]{:S(2)}) collective-permute-start(f32[3,768]{1,0:T(4,128)S(1)} %pad_maximum_fusion.4), channel_id=1, source_target_pairs={{0,2},{1,3},{2,0},{3,1},{4,6},{5,7},{6,4},{7,5},{8,10},{9,11},{10,... | collective-permute-start | bytes 27656 | tf_op jit(solution)/shard_map/ppermute | solution.py:33
  69.6 15.0 %collective-permute-start.4 = (f32[3,768]{1,0:T(4,128)S(1)}, f32[3,768]{1,0:T(4,128)S(1)}, u32[]{:S(2)}, u32[]{:S(2)}) collective-permute-start(f32[3,768]{1,0:T(4,128)S(1)} %pad_maximum_fusion.5), channel_id=1, source_target_pairs={{0,4},{1,5},{2,6},{3,7},{4,0},{5,1},{6,2},{7,3},{8,12},{9,13},{10,... | collective-permute-start | bytes 27656 | tf_op jit(solution)/shard_map/ppermute | solution.py:33
  88.4 8.3 %collective-permute-start.5 = (bf16[4,48,768]{2,1,0:T(8,128)(2,1)S(1)}, bf16[4,48,768]{2,1,0:T(8,128)(2,1)S(1)}, u32[]{:S(2)}, u32[]{:S(2)}) collective-permute-start(bf16[4,48,768]{2,1,0:T(8,128)(2,1)S(1)} %get-tuple-element.95), channel_id=1, source_target_pairs={{0,1},{1,0},{2,3},{3,2},{4,5},{5,4},{6,7},{7,6},{8,9},{9,8},{10,11... | collective-permute-start | bytes 884744 | tf_op jit(solution)/shard_map/ppermute | solution.py:33
  100.4 4.3 %collective-permute-start.7 = (f32[3,384]{1,0:T(4,128)S(1)}, f32[3,384]{1,0:T(4,128)S(1)}, u32[]{:S(2)}, u32[]{:S(2)}) collective-permute-start(f32[3,384]{1,0:T(4,128)S(1)} %pad_maximum_fusion.9), channel_id=1, source_target_pairs={{0,16},{8,24},{16,0},{24,8},{1,17},{9,25},{17,1},{25,9},{2,18},{10... | collective-permute-start | bytes 13832 | tf_op jit(solution)/shard_map/ppermute | solution.py:33
  104.7 4.2 %collective-permute-start.8 = (f32[3,384]{1,0:T(4,128)S(1)}, f32[3,384]{1,0:T(4,128)S(1)}, u32[]{:S(2)}, u32[]{:S(2)}) collective-permute-start(f32[3,384]{1,0:T(4,128)S(1)} %pad_maximum_fusion.10), channel_id=1, source_target_pairs={{0,1},{1,0},{2,3},{3,2},{4,5},{5,4},{6,7},{7,6},{8,9},{9,8},{10,11... | collective-permute-start | bytes 13832 | tf_op jit(solution)/shard_map/ppermute | solution.py:33
  108.9 6.3 %collective-permute-start.9 = (f32[3,384]{1,0:T(4,128)S(1)}, f32[3,384]{1,0:T(4,128)S(1)}, u32[]{:S(2)}, u32[]{:S(2)}) collective-permute-start(f32[3,384]{1,0:T(4,128)S(1)} %pad_maximum_fusion.11), channel_id=1, source_target_pairs={{0,2},{1,3},{2,0},{3,1},{4,6},{5,7},{6,4},{7,5},{8,10},{9,11},{10,... | collective-permute-start | bytes 13832 | tf_op jit(solution)/shard_map/ppermute | solution.py:33
  115.3 3.4 %collective-permute-start.10 = (f32[3,384]{1,0:T(4,128)S(1)}, f32[3,384]{1,0:T(4,128)S(1)}, u32[]{:S(2)}, u32[]{:S(2)}) collective-permute-start(f32[3,384]{1,0:T(4,128)S(1)} %pad_maximum_fusion.12), channel_id=1, source_target_pairs={{0,4},{1,5},{2,6},{3,7},{4,0},{5,1},{6,2},{7,3},{8,12},{9,13},{10,... | collective-permute-start | bytes 13832 | tf_op jit(solution)/shard_map/ppermute | solution.py:33
  123.0 3.2 %collective-permute-start.11 = (f32[2,384]{1,0:T(2,128)S(1)}, f32[2,384]{1,0:T(2,128)S(1)}, u32[]{:S(2)}, u32[]{:S(2)}) collective-permute-start(f32[2,384]{1,0:T(2,128)S(1)} %get-tuple-element.116), channel_id=1, source_target_pairs={{0,8},{8,0},{16,24},{24,16},{1,9},{9,1},{17,25},{25,17},{2,10},{10... | collective-permute-start | bytes 9224 | tf_op jit(solution)/shard_map/ppermute | solution.py:33
  126.2 3.1 %collective-permute-start.12 = (f32[2,384]{1,0:T(2,128)S(1)}, f32[2,384]{1,0:T(2,128)S(1)}, u32[]{:S(2)}, u32[]{:S(2)}) collective-permute-start(f32[2,384]{1,0:T(2,128)S(1)} %add.291), channel_id=1, source_target_pairs={{0,16},{8,24},{16,0},{24,8},{1,17},{9,25},{17,1},{25,9},{2,18},{10... | collective-permute-start | bytes 9224 | tf_op jit(solution)/shard_map/ppermute | solution.py:33
  134.3 3.3 %collective-permute-start.15 = (f32[2,384]{1,0:T(2,128)S(1)}, f32[2,384]{1,0:T(2,128)S(1)}, u32[]{:S(2)}, u32[]{:S(2)}) collective-permute-start(f32[2,384]{1,0:T(2,128)S(1)} %add.294), channel_id=1, source_target_pairs={{0,4},{1,5},{2,6},{3,7},{4,0},{5,1},{6,2},{7,3},{8,12},{9,13},{10,... | collective-permute-start | bytes 9224 | tf_op jit(solution)/shard_map/ppermute | solution.py:33
  141.5 4.0 %collective-permute-start.16 = (bf16[4,48,384]{2,1,0:T(8,128)(2,1)S(1)}, bf16[4,48,384]{2,1,0:T(8,128)(2,1)S(1)}, u32[]{:S(2)}, u32[]{:S(2)}) collective-permute-start(bf16[4,48,384]{2,1,0:T(8,128)(2,1)S(1)} %get-tuple-element.122), channel_id=1, source_target_pairs={{0,1},{1,0},{2,3},{3,2},{4,5},{5,4},{6,7},{7,6},{8,9},{9,8},{10,11... | collective-permute-start | bytes 442376 | tf_op jit(solution)/shard_map/ppermute | solution.py:33
  166.1 50.7 %all-to-all-start.1 = ((bf16[8,128,768]{2,1,0:T(8,128)(2,1)}), bf16[8,128,768]{2,1,0:T(8,128)(2,1)}, u32[]{:S(2)}, u32[]{:S(2)}) async-start(bf16[8,128,768]{2,1,0:T(8,128)(2,1)} %get-tuple-element.142), calls=%async_computation.1 | async-start | bytes 3145728 | tf_op jit(solution)/shard_map/all_to_all | solution.py:1096
  182.0 8.4 %collective-permute-start.17 = (bf16[768,768]{1,0:T(8,128)(2,1)}, bf16[768,768]{1,0:T(8,128)(2,1)}, u32[]{:S(2)}, u32[]{:S(2)}) collective-permute-start(bf16[768,768]{1,0:T(8,128)(2,1)} %select_convert_fusion), channel_id=1, source_target_pairs={{0,8},{8,0},{16,24},{24,16},{1,9},{9,1},{17,25},{25,17},{2,10},{10... | collective-permute-start | bytes 3538952 | tf_op jit(solution)/shard_map/ppermute | solution.py:33
  195.9 14.1 %collective-permute-start.20 = (bf16[192,768]{1,0:T(8,128)(2,1)}, bf16[192,768]{1,0:T(8,128)(2,1)S(1)}, u32[]{:S(2)}, u32[]{:S(2)}) collective-permute-start(bf16[192,768]{1,0:T(8,128)(2,1)} %get-tuple-element.185), channel_id=1, source_target_pairs={{0,17},{1,16},{2,19},{3,18},{4,21},{5,20},{6,23},{7,22},{8,25},{9,... | collective-permute-start | bytes 884744 | tf_op jit(solution)/shard_map/ppermute | solution.py:862
  197.9 17.6 %collective-permute-start.19 = (bf16[192,768]{1,0:T(8,128)(2,1)}, bf16[192,768]{1,0:T(8,128)(2,1)}, u32[]{:S(2)}, u32[]{:S(2)}) collective-permute-start(bf16[192,768]{1,0:T(8,128)(2,1)} %get-tuple-element.186), channel_id=1, source_target_pairs={{0,1},{1,0},{2,3},{3,2},{4,5},{5,4},{6,7},{7,6},{8,9},{9,8},{10,11... | collective-permute-start | bytes 884744 | tf_op jit(solution)/shard_map/ppermute | solution.py:862
  198.1 17.3 %collective-permute-start.18 = (bf16[192,768]{1,0:T(8,128)(2,1)}, bf16[192,768]{1,0:T(8,128)(2,1)}, u32[]{:S(2)}, u32[]{:S(2)}) collective-permute-start(bf16[192,768]{1,0:T(8,128)(2,1)} %get-tuple-element.184), channel_id=1, source_target_pairs={{0,16},{1,17},{2,18},{3,19},{4,20},{5,21},{6,22},{7,23},{8,24},{9,... | collective-permute-start | bytes 884744 | tf_op jit(solution)/shard_map/ppermute | solution.py:862
  216.9 4.3 %collective-permute-start.23 = (bf16[48,768]{1,0:T(8,128)(2,1)S(1)}, bf16[48,768]{1,0:T(8,128)(2,1)S(1)}, u32[]{:S(2)}, u32[]{:S(2)}) collective-permute-start(bf16[48,768]{1,0:T(8,128)(2,1)S(1)} %get-tuple-element.191), channel_id=1, source_target_pairs={{0,6},{1,7},{2,4},{3,5},{4,2},{5,3},{6,0},{7,1},{8,14},{9,15},{10,... | collective-permute-start | bytes 221192 | tf_op jit(solution)/shard_map/ppermute | solution.py:862
  217.0 6.7 %collective-permute-start.22 = (bf16[48,768]{1,0:T(8,128)(2,1)S(1)}, bf16[48,768]{1,0:T(8,128)(2,1)S(1)}, u32[]{:S(2)}, u32[]{:S(2)}) collective-permute-start(bf16[48,768]{1,0:T(8,128)(2,1)S(1)} %get-tuple-element.192), channel_id=1, source_target_pairs={{0,4},{1,5},{2,6},{3,7},{4,0},{5,1},{6,2},{7,3},{8,12},{9,13},{10,... | collective-permute-start | bytes 221192 | tf_op jit(solution)/shard_map/ppermute | solution.py:862
  219.4 4.3 %collective-permute-start.21 = (bf16[48,768]{1,0:T(8,128)(2,1)S(1)}, bf16[48,768]{1,0:T(8,128)(2,1)S(1)}, u32[]{:S(2)}, u32[]{:S(2)}) collective-permute-start(bf16[48,768]{1,0:T(8,128)(2,1)S(1)} %get-tuple-element.190), channel_id=1, source_target_pairs={{0,2},{1,3},{2,0},{3,1},{4,6},{5,7},{6,4},{7,5},{8,10},{9,11},{10,... | collective-permute-start | bytes 221192 | tf_op jit(solution)/shard_map/ppermute | solution.py:862
  223.8 19.0 %collective-permute-start.26 = (bf16[48,768]{1,0:T(8,128)(2,1)S(1)}, bf16[48,768]{1,0:T(8,128)(2,1)S(1)}, u32[]{:S(2)}, u32[]{:S(2)}) collective-permute-start(bf16[48,768]{1,0:T(8,128)(2,1)S(1)} %add_convert_fusion), channel_id=1, source_target_pairs={{0,2},{1,3},{2,0},{3,1},{4,6},{5,7},{6,4},{7,5},{8,10},{9,11},{10,... | collective-permute-start | bytes 221192 | tf_op jit(solution)/shard_map/ppermute | solution.py:862
  226.1 16.6 %collective-permute-start.25 = (bf16[48,768]{1,0:T(8,128)(2,1)S(1)}, bf16[48,768]{1,0:T(8,128)(2,1)S(1)}, u32[]{:S(2)}, u32[]{:S(2)}) collective-permute-start(bf16[48,768]{1,0:T(8,128)(2,1)S(1)} %add_convert_fusion), channel_id=1, source_target_pairs={{0,4},{1,5},{2,6},{3,7},{4,0},{5,1},{6,2},{7,3},{8,12},{9,13},{10,... | collective-permute-start | bytes 221192 | tf_op jit(solution)/shard_map/ppermute | solution.py:862
  227.0 15.7 %collective-permute-start.24 = (bf16[48,768]{1,0:T(8,128)(2,1)S(1)}, bf16[48,768]{1,0:T(8,128)(2,1)S(1)}, u32[]{:S(2)}, u32[]{:S(2)}) collective-permute-start(bf16[48,768]{1,0:T(8,128)(2,1)S(1)} %add_convert_fusion), channel_id=1, source_target_pairs={{0,6},{1,7},{2,4},{3,5},{4,2},{5,3},{6,0},{7,1},{8,14},{9,15},{10,... | collective-permute-start | bytes 221192 | tf_op jit(solution)/shard_map/ppermute | solution.py:862
  235.8 3.5 %collective-permute-start.30 = (f32[3,768]{1,0:T(4,128)S(1)}, f32[3,768]{1,0:T(4,128)S(1)}, u32[]{:S(2)}, u32[]{:S(2)}) collective-permute-start(f32[3,768]{1,0:T(4,128)S(1)} %add.315), channel_id=1, source_target_pairs={{0,2},{1,3},{2,0},{3,1},{4,6},{5,7},{6,4},{7,5},{8,10},{9,11},{10,... | collective-permute-start | bytes 27656 | tf_op jit(solution)/shard_map/ppermute | solution.py:33
  239.3 3.4 %collective-permute-start.31 = (f32[3,768]{1,0:T(4,128)S(1)}, f32[3,768]{1,0:T(4,128)S(1)}, u32[]{:S(2)}, u32[]{:S(2)}) collective-permute-start(f32[3,768]{1,0:T(4,128)S(1)} %add.316), channel_id=1, source_target_pairs={{0,4},{1,5},{2,6},{3,7},{4,0},{5,1},{6,2},{7,3},{8,12},{9,13},{10,... | collective-permute-start | bytes 27656 | tf_op jit(solution)/shard_map/ppermute | solution.py:33
  242.9 46.6 %all-to-all-start.2 = ((bf16[8,128,768]{2,1,0:T(8,128)(2,1)}), bf16[8,128,768]{2,1,0:T(8,128)(2,1)}, u32[]{:S(2)}, u32[]{:S(2)}) async-start(bf16[8,128,768]{2,1,0:T(8,128)(2,1)} %get-tuple-element.153), calls=%async_computation.2 | async-start | bytes 3145728 | tf_op jit(solution)/shard_map/all_to_all | solution.py:1096
  248.4 5.6 %collective-permute-start.34 = (bf16[192,768]{1,0:T(8,128)(2,1)S(1)}, bf16[192,768]{1,0:T(8,128)(2,1)S(1)}, u32[]{:S(2)}, u32[]{:S(2)}) collective-permute-start(bf16[192,768]{1,0:T(8,128)(2,1)S(1)} %maximum_select_fusion.3), channel_id=1, source_target_pairs={{0,16},{1,17},{2,18},{3,19},{4,20},{5,21},{6,22},{7,23},{8,24},{9,... | collective-permute-start | bytes 884744 | tf_op jit(solution)/shard_map/ppermute | solution.py:862
  249.5 28.1 %collective-permute-start.33 = (bf16[192,768]{1,0:T(8,128)(2,1)S(1)}, bf16[192,768]{1,0:T(8,128)(2,1)S(1)}, u32[]{:S(2)}, u32[]{:S(2)}) collective-permute-start(bf16[192,768]{1,0:T(8,128)(2,1)S(1)} %maximum_select_fusion.3), channel_id=1, source_target_pairs={{0,1},{1,0},{2,3},{3,2},{4,5},{5,4},{6,7},{7,6},{8,9},{9,8},{10,11... | collective-permute-start | bytes 884744 | tf_op jit(solution)/shard_map/ppermute | solution.py:862
  250.7 26.9 %collective-permute-start.32 = (bf16[192,768]{1,0:T(8,128)(2,1)S(1)}, bf16[192,768]{1,0:T(8,128)(2,1)S(1)}, u32[]{:S(2)}, u32[]{:S(2)}) collective-permute-start(bf16[192,768]{1,0:T(8,128)(2,1)S(1)} %maximum_select_fusion.3), channel_id=1, source_target_pairs={{0,17},{1,16},{2,19},{3,18},{4,21},{5,20},{6,23},{7,22},{8,25},{9,... | collective-permute-start | bytes 884744 | tf_op jit(solution)/shard_map/ppermute | solution.py:862
  278.3 8.0 %collective-permute-start.35 = (bf16[768,768]{1,0:T(8,128)(2,1)S(1)}, bf16[768,768]{1,0:T(8,128)(2,1)S(1)}, u32[]{:S(2)}, u32[]{:S(2)}) collective-permute-start(bf16[768,768]{1,0:T(8,128)(2,1)S(1)} %maximum_select_fusion.mine_ref), channel_id=1, source_target_pairs={{0,8},{8,0},{16,24},{24,16},{1,9},{9,1},{17,25},{25,17},{2,10},{10... | collective-permute-start | bytes 3538952 | tf_op jit(solution)/shard_map/ppermute | solution.py:33
  (47 other events, 267.2 us)

commit v3 on v2

--- a/solution.py
+++ b/solution.py
@@ -20,6 +20,7 @@
 STRIP = 64
 PAD = 40
 PADDED_ROWS = HALF_WINDOW_ROWS + 2 * PAD
+EXTRA = 8
 GELU_SLOPE = math.sqrt(2.0 / math.pi)
 GELU_CUBE = 0.044715
 
@@ -129,7 +130,7 @@
 
 def pool_body(
     slots, facts_ref, signal_ref, pooled_ref, first_ref, moments_ref,
-    held, low, mark, arrivals, departures,
+    held, low, mark, blocks, arrivals, departures,
 ):
     windows, columns = held.shape[:2]
     rows = low.shape[1]
@@ -156,38 +157,40 @@
     lax.fori_loop(0, windows, begin, 0)
     moments_ref[...] = jnp.zeros_like(moments_ref)
 
-    def work(place, before):
+    def work(place, carry):
         count = facts.slot_count(place, rows)
-        count_f = count.astype(jnp.float32)
-        before_f = before.astype(jnp.float32)
-        weight = before_f * count_f / jnp.maximum(before_f + count_f, 1.0)
         inside = lax.broadcasted_iota(jnp.int32, (rows, LANES), 0) < count
+        for column in range(columns):
+            arrival(place, column).wait()
         for column, lanes in enumerate(column_slices(columns * LANES)):
-            arrival(place, column).wait()
             first_bin = held[place, column, pl.ds(0, rows, stride=2), :]
             second_bin = held[place, column, pl.ds(1, rows, stride=2), :]
-            take_first = first_bin >= second_bin
-            raw = jnp.maximum(first_bin, second_bin)
-            mark[place, :, lanes] = jnp.where(take_first, 1.0, 0.0).astype(jnp.bfloat16)
-            pooled = jnp.where(inside, raw, 0.0).astype(jnp.bfloat16)
+            mark[place, :, lanes] = jnp.where(first_bin >= second_bin, 1.0, 0.0).astype(
+                jnp.bfloat16
+            )
+            pooled = jnp.where(inside, jnp.maximum(first_bin, second_bin), 0.0)
+            pooled = pooled.astype(jnp.bfloat16)
             low[place, :, lanes] = pooled
-            values = pooled.astype(jnp.float32)
-            block_sum = jnp.sum(values, axis=0, keepdims=True)
-            block_mean = block_sum / jnp.maximum(count_f, 1.0)
-            deviation = jnp.where(inside, values - block_mean, 0.0)
-            block_spread = jnp.sum(deviation * deviation, axis=0, keepdims=True)
-            held_sum = moments_ref[0:1, lanes]
-            gap = held_sum / jnp.maximum(before_f, 1.0) - block_mean
-            moments_ref[0:1, lanes] = held_sum + block_sum
-            moments_ref[1:2, lanes] = (
-                moments_ref[1:2, lanes] + block_spread + gap * gap * weight
-            )
-            moments_ref[2:3, lanes] = moments_ref[2:3, lanes] + count_f
+            found = block_moments(pooled.astype(jnp.float32), inside, count.astype(jnp.float32))
+            blocks[place, 0:1, lanes] = found[0]
+            blocks[place, 1:2, lanes] = found[1]
         for copy in departure(place):
             copy.start()
-        return before + count
-
-    lax.fori_loop(0, windows, work, jnp.int32(0))
+        return carry
+
+    lax.fori_loop(0, windows, work, 0)
+
+    def join_blocks(place, carry):
+        count = jnp.broadcast_to(
+            facts.slot_count(place, rows).astype(jnp.float32), (1, columns * LANES)
+        )
+        held_moments = (moments_ref[0:1], moments_ref[1:2], moments_ref[2:3])
+        moments_ref[0:1], moments_ref[1:2], moments_ref[2:3] = merged(
+            held_moments, (blocks[place, 0:1], blocks[place, 1:2], count)
+        )
+        return carry
+
+    lax.fori_loop(0, windows, join_blocks, 0)
 
     def finish(place, carry):
         for copy in departure(place):
@@ -216,6 +219,7 @@
             pltpu.VMEM((windows, columns, segment, LANES), jnp.float32),
             pltpu.VMEM(block, jnp.bfloat16),
             pltpu.VMEM(block, jnp.bfloat16),
+            pltpu.VMEM((windows, 2, width), jnp.float32),
             pltpu.SemaphoreType.DMA((windows, columns)),
             pltpu.SemaphoreType.DMA((windows, 2)),
         ],
@@ -278,6 +282,7 @@
             first = gradient * mark[target, :, lanes].astype(jnp.float32)
             held[target, column, pl.ds(0, rows, stride=2), :] = first
             held[target, column, pl.ds(1, rows, stride=2), :] = gradient - first
+        for column in range(columns):
             departure(target, column).start()
         return carry
 
@@ -764,7 +769,7 @@
     slots, windows, slot, facts_ref, padded_ref, border_ref, weight_ref, *refs
 ):
     slope_refs, (arrived_ref, block_ref, moments_ref, params_ref) = refs[:2], refs[2:6]
-    sent_ref, taps_ref, sums_ref, wide, packed, departures = refs[6:]
+    sent_ref, kept_ref, sums_ref, wide, packed, taps_ref, departures, kept = refs[-8:]
     facts = Facts(facts_ref, windows, slots)
     sources, rows, width = packed.shape
     tiles = padded_ref.shape[1]
@@ -776,6 +781,11 @@
     def departure(source):
         return pltpu.make_async_copy(
             packed.at[source], sent_ref.at[source], departures.at[source]
+        )
+
+    def keeping(half):
+        return pltpu.make_async_copy(
+            taps_ref.at[half], kept_ref.at[slot * 2 + half], kept.at[half]
         )
 
     for half in range(2):
@@ -795,6 +805,7 @@
                 taps_ref[half, :, first : first + LANES] = wide[
                     tile, start : start + HALF_WINDOW_ROWS
                 ].astype(jnp.bfloat16)
+        keeping(half).start()
         for column in range(0, width, 2 * LANES):
             grad = jnp.dot(
                 taps_ref[half],
@@ -822,35 +833,51 @@
         for part in range(per_half):
             departure(half * per_half + part).start()
     sums_ref[0:1] = (sums_ref[0:1] - centre * sums_ref[1:2]) * scale
+    for half in range(2):
+        keeping(half).wait()
     for source in range(sources):
         departure(source).wait()
 
 
 def entry_grad(
-    facts, padded, border, weight, slopes, arrived, block, moments, params, slots, windows, slot
+    facts, padded, border, weight, slopes, arrived, block, moments, params, taps, slots, windows,
+    slot,
 ):
     blocks, rows, width = arrived.shape
-    inner = border.shape[2]
-    sources = blocks // slots
-    return kernel_call(
+    inner, sources = border.shape[2], blocks // slots
+    inputs = [facts, padded, border, weight, *slopes, arrived, block, moments, params]
+    specs = [SMEM] + [VMEM] * 9
+    aliases = {}
+    if taps is not None:
+        aliases = {len(inputs): 1}
+        inputs.append(in_hbm(taps))
+        specs.append(HBM)
+    taps_shape = (HALF_WINDOW_ROWS, 3 * inner)
+    return pl.pallas_call(
         functools.partial(entry_grad_body, slots, windows, slot),
-        "entry_grad",
-        (facts, padded, border, weight, *slopes, arrived, block, moments, params),
-        [SMEM] + [VMEM] * 9,
-        [
+        in_specs=specs,
+        out_specs=[HBM, HBM, VMEM],
+        out_shape=[
             pltpu.HBM((sources, rows, width), jnp.bfloat16),
-            shape((2, HALF_WINDOW_ROWS, 3 * inner), jnp.bfloat16),
+            pltpu.HBM((2 * slots, *taps_shape), jnp.bfloat16),
             shape((2, width), jnp.float32),
         ],
-        [HBM, VMEM, VMEM],
-        [
+        input_output_aliases=aliases,
+        scratch_shapes=[
             pltpu.VMEM((inner // LANES, PADDED_ROWS, LANES), jnp.float32),
             pltpu.VMEM((sources, rows, width), jnp.bfloat16),
+            pltpu.VMEM((2, *taps_shape), jnp.bfloat16),
             pltpu.SemaphoreType.DMA((sources,)),
+            pltpu.SemaphoreType.DMA((2,)),
         ],
-        flops=2 * 2 * HALF_WINDOW_ROWS * 3 * inner * width,
-        bytes_moved=2 * HALF_WINDOW_ROWS * (width * 10 + inner * 10),
-    )
+        compiler_params=pltpu.CompilerParams(vmem_limit_bytes=10 << 20),
+        cost_estimate=pl.CostEstimate(
+            flops=2 * 2 * HALF_WINDOW_ROWS * 3 * inner * width,
+            bytes_accessed=2 * HALF_WINDOW_ROWS * (width * 10 + inner * 10),
+            transcendentals=0,
+        ),
+        name="entry_grad",
+    )(*inputs)
 
 
 def flat_mask(bits):
@@ -892,32 +919,218 @@
     return parts, masks
 
 
-def scatter_starts(phase, rows):
-    parts, _ = phase_parts(phase)
-    mine = phase_place(phase)
-    return [jnp.bitwise_xor(mine, part) * (rows // parts) for part in range(parts)]
-
-
-def scatter_sum(buffer, phase, starts):
-    parts, masks = phase_parts(phase)
-    rows = buffer.shape[0] // parts
-    kept = lax.dynamic_slice_in_dim(buffer, starts[0], rows)
-    for part in range(1, parts):
-        sent = lax.dynamic_slice_in_dim(buffer, starts[part], rows).astype(jnp.bfloat16)
-        kept = kept + from_flat_partner(sent, masks[part]).astype(jnp.float32)
-    return kept
-
-
-def gather_parts(buffer, phase, mine):
-    parts, masks = phase_parts(phase)
-    found = [buffer] + [from_flat_partner(buffer, masks[part]) for part in range(1, parts)]
+def exchange_parts(parts, phase):
+    _, masks = phase_parts(phase)
+    return [from_flat_partner(part, mask) for part, mask in zip(parts, masks[1:])]
+
+
+def place_in(facts_ref, phase):
+    bits = [
+        (facts_ref[0 if axis == "grp" else 1] // mask) % 2 * 2**number
+        for number, (axis, mask) in enumerate(phase)
+    ]
+    return sum(bits)
+
+
+def encoded(sums, rows_ref):
+    count = sums.shape[0]
+    high = sums.astype(jnp.bfloat16).astype(jnp.float32)
+    low = (sums - high).astype(jnp.bfloat16).astype(jnp.float32)
+    rows_ref[...] = jnp.zeros_like(rows_ref)
+    rows_ref[0:count] = high
+    rows_ref[count : 2 * count] = low
+    return rows_ref[...].astype(jnp.bfloat16), high + low
+
+
+def decoded(found_ref, count, rows_ref):
+    rows_ref[...] = found_ref[found_ref.shape[0] - EXTRA :, :].astype(jnp.float32)
+    return rows_ref[0:count] + rows_ref[count : 2 * count]
+
+
+def pair_sum(values):
+    while len(values) > 1:
+        values = [values[i] + values[i + 1] for i in range(0, len(values), 2)]
+    return values[0]
+
+
+def other_half_body(
+    facts_ref, dilated_ref, pointwise_ref, sums_ref, sent_ref, held_ref, rows_ref
+):
+    width, inner = pointwise_ref.shape
+    sent_ref[width:, :], held_ref[...] = encoded(sums_ref[...], rows_ref)
+
+    @pl.when(facts_ref[0] % 2 == 0)
+    def _():
+        sent_ref[:width, :inner] = dilated_ref[:, 2 * inner :].astype(jnp.bfloat16)
+        sent_ref[:width, inner:] = pointwise_ref[...].astype(jnp.bfloat16)
+
+    @pl.when(facts_ref[0] % 2 == 1)
+    def _():
+        sent_ref[:width, :] = dilated_ref[:, : 2 * inner].astype(jnp.bfloat16)
+
+
+def other_half(facts, dilated, pointwise, sums):
+    width, inner = pointwise.shape
+    return kernel_call(
+        other_half_body,
+        "other_half",
+        (facts, dilated, pointwise, sums),
+        [SMEM, VMEM, VMEM, VMEM],
+        [shape((width + EXTRA, 2 * inner), jnp.bfloat16), shape(sums.shape, jnp.float32)],
+        [VMEM, VMEM],
+        [pltpu.VMEM((EXTRA, 2 * inner), jnp.float32)],
+        flops=2 * width * inner,
+        bytes_moved=12 * width * inner,
+        grant=10 << 20,
+    )
+
+
+def part_rows(mine, part, rows):
+    return pl.ds(pl.multiple_of(jnp.bitwise_xor(mine, part) * rows, rows), rows)
+
+
+def own_half_body(
+    phase, facts_ref, dilated_ref, pointwise_ref, sums_ref, other_ref, total_ref, *refs
+):
+    part_refs, rows_ref = refs[:-1], refs[-1]
+    inner = pointwise_ref.shape[1]
+    rows = part_refs[0].shape[0]
+    mine = place_in(facts_ref, phase)
+    sums = sums_ref[...] + decoded(other_ref, sums_ref.shape[0], rows_ref)
+    extra, total_ref[...] = encoded(sums, rows_ref)
+    for part_ref in part_refs[1:]:
+        part_ref[rows:, :] = extra
+
+    def write(low, high):
+        for part, part_ref in enumerate(part_refs):
+            here = part_rows(mine, part, rows)
+            for piece, lanes in ((low, slice(0, inner)), (high, slice(inner, 2 * inner))):
+                value = piece(here) + other_ref[here, lanes].astype(jnp.float32)
+                part_ref[:rows, lanes] = value.astype(part_ref.dtype)
+
+    @pl.when(facts_ref[0] % 2 == 0)
+    def _():
+        write(
+            lambda here: dilated_ref[here, :inner],
+            lambda here: dilated_ref[here, inner : 2 * inner],
+        )
+
+    @pl.when(facts_ref[0] % 2 == 1)
+    def _():
+        write(lambda here: dilated_ref[here, 2 * inner :], lambda here: pointwise_ref[here, :])
+
+
+def part_shapes(sums, rows, columns, phase):
+    parts = 2 ** len(phase)
+    rows //= parts
+    return [
+        shape(sums.shape, jnp.float32),
+        shape((rows, columns), jnp.float32),
+        *[shape((rows + EXTRA, columns), jnp.bfloat16)] * (parts - 1),
+    ]
+
+
+def own_half(facts, dilated, pointwise, sums, other, phase):
+    width, inner = pointwise.shape
+    outputs = part_shapes(sums, width, 2 * inner, phase)
+    return kernel_call(
+        functools.partial(own_half_body, phase),
+        "own_half",
+        (facts, dilated, pointwise, sums, other),
+        [SMEM] + [VMEM] * 4,
+        outputs,
+        [VMEM] * len(outputs),
+        [pltpu.VMEM((EXTRA, 2 * inner), jnp.float32)],
+        flops=2 * width * inner,
+        bytes_moved=20 * width * inner,
+        grant=12 << 20,
+    )
+
+
+def next_parts_body(count, phase, facts_ref, kept_ref, sums_ref, *refs):
+    found_refs, total_ref, part_refs, rows_ref = (
+        refs[:count],
+        refs[count],
+        refs[count + 1 : -1],
+        refs[-1],
+    )
+    sums = pair_sum(
+        [sums_ref[...]] + [decoded(ref, sums_ref.shape[0], rows_ref) for ref in found_refs]
+    )
+    total_ref[...] = sums
+    rows = part_refs[0].shape[0]
+    if phase:
+        mine = place_in(facts_ref, phase)
+        extra, total_ref[...] = encoded(sums, rows_ref)
+        for part_ref in part_refs[1:]:
+            part_ref[rows:, :] = extra
+    for part, part_ref in enumerate(part_refs):
+        here = part_rows(mine, part, rows) if phase else slice(0, rows)
+        value = kept_ref[here, :]
+        for found_ref in found_refs:
+            value = value + found_ref[here, :].astype(jnp.float32)
+        part_ref[:rows, :] = value.astype(part_ref.dtype)
+
+
+def plain_parts(kept, sums, found, phase):
+    rows, count = kept.shape[0], sums.shape[0]
+    totals = [sums]
+    for block in found:
+        kept = kept + block[:rows].astype(jnp.float32)
+        tail = block[rows:].astype(jnp.float32)
+        totals.append(tail[:count] + tail[count : 2 * count])
+    sums = pair_sum(totals)
+    if not phase:
+        return [sums, kept.astype(jnp.bfloat16)]
+    high = lax.reduce_precision(sums, 8, 7)
+    low = lax.reduce_precision(sums - high, 8, 7)
+    rest = jnp.zeros((EXTRA - 2 * count, sums.shape[1]), jnp.float32)
+    extra, sums = jnp.concatenate([high, low, rest]).astype(jnp.bfloat16), high + low
+    parts = 2 ** len(phase)
+    mine, rows = phase_place(phase), rows // parts
+    slices = [
+        lax.dynamic_slice_in_dim(kept, jnp.bitwise_xor(mine, part) * rows, rows)
+        for part in range(parts)
+    ]
+    return [sums, slices[0]] + [
+        jnp.concatenate([block.astype(jnp.bfloat16), extra]) for block in slices[1:]
+    ]
+
+
+def next_parts(facts, kept, sums, found, phase):
+    rows, columns = kept.shape
+    if rows // 2 ** len(phase) % 16:
+        return plain_parts(kept, sums, found, phase)
+    outputs = part_shapes(sums, rows, columns, phase)
+    if not phase:
+        outputs = [outputs[0], shape((rows, columns), jnp.bfloat16)]
+    return kernel_call(
+        functools.partial(next_parts_body, len(found), phase),
+        "next_parts",
+        (facts, kept, sums, *found),
+        [SMEM] + [VMEM] * (2 + len(found)),
+        outputs,
+        [VMEM] * len(outputs),
+        [pltpu.VMEM((EXTRA, columns), jnp.float32)],
+        flops=4 * rows * columns,
+        bytes_moved=16 * rows * columns,
+    )
+
+
+def gather_parts(buffer, phase):
+    _, masks = phase_parts(phase)
+    return [buffer] + [from_flat_partner(buffer, mask) for mask in masks[1:]]
+
+
+def in_order(found, owners):
+    parts = len(found)
     orders = [
         jnp.concatenate([found[place ^ own] for place in range(parts)], axis=0)
         for own in range(parts)
     ]
     result = orders[0]
     for own in range(1, parts):
-        result = jnp.where(mine == own, orders[own], result)
+        result = jnp.where(owners[own], orders[own], result)
     return result
 
 
@@ -993,13 +1206,11 @@
         facts, cotangent, pointwise_low, slots, windows
     )
     phases = square_phases()
-    starts, held_rows = [], width
-    for phase in phases:
-        starts.append(scatter_starts(phase, held_rows))
-        held_rows //= 2 ** len(phase)
-    spots = [phase_place(phase) for phase in phases]
+    owners = [
+        [phase_place(phase) == own for own in range(2 ** len(phase))] for phase in phases
+    ]
     first_axis, first_mask = exchange_steps()[0]
-    upper = bit_of(first_axis, first_mask)
+    upper = bit_of(first_axis, first_mask) == 1
     (
         arrived,
         grad_block,
@@ -1007,8 +1218,7 @@
         wide_kernel,
         back_kernel,
         pointwise_low,
-        starts,
-        spots,
+        owners,
         upper,
         middle_params,
         facts,
@@ -1020,14 +1230,12 @@
             wide_kernel,
             back_kernel,
             pointwise_low,
-            starts,
-            spots,
+            owners,
             upper,
             middle_params,
             facts,
         )
     )
-    upper = upper == 1
 
     act, act_border = activate(facts, arrived, entry_moments, entry_params, slots, windows)
     act_border = from_partner(act_border, "seq", 1)
@@ -1081,59 +1289,54 @@
     )
     grad_border = from_partner(grad_border, "seq", 1)
     block_pieces = grad_block.reshape(pieces, HALF_WINDOW_ROWS, width)
-    sent, taps, entry_part = [], [], jnp.concatenate([jnp.zeros_like(bias_part)] * 2)
+    sent, taps, entry_part = [], None, jnp.concatenate([jnp.zeros_like(bias_part)] * 2)
+    returned = []
+
+    def send_back(block):
+        return lax.all_to_all(block, "seq", split_axis=0, concat_axis=0, tiled=True)
+
     for slot in range(slots):
-        slot_sent, slot_taps, part = entry_grad(
-            facts, padded, grad_border, back_kernel, slopes[2 * slot : 2 * slot + 2], arrived,
-            block_pieces, entry_moments, entry_params, slots, windows, slot,
-        )
-        sent.append(slot_sent)
-        taps.append(slot_taps)
+        block, taps, part = entry_grad(
+            facts, padded, grad_border, back_kernel, slopes[2 * slot : 2 * slot + 2],
+            arrived, block_pieces, entry_moments, entry_params, taps, slots, windows, slot,
+        )
+        sent.append(block)
         entry_part = entry_part + part
     entry_sums = jnp.concatenate([entry_part, bias_part])
-
-    def send_back(block):
-        return lax.all_to_all(block, "seq", split_axis=0, concat_axis=0, tiled=True)
-
+    tied = lax.optimization_barrier((*sent, entry_sums))
+    sent, entry_sums = list(tied[:-1]), tied[-1]
     returned = [send_back(sent[0])]
-    flat_act, act, *taps = lax.optimization_barrier((flat_act, act, *taps, sent[-1]))[:-1]
-    activations = output_rows(
-        facts, flat_act, pointwise_low, arrived, entry_params, slots, windows
-    )
-    dilated_part = sum(
-        jnp.einsum(
-            "hrc,hrf->cf",
-            act[2 * slot : 2 * slot + 2],
-            slot_taps,
-            preferred_element_type=jnp.float32,
-        )
-        for slot, slot_taps in enumerate(taps)
-    )
-    low_half = dilated_part[:, : 2 * inner]
-    high_half = jnp.concatenate([dilated_part[:, 2 * inner :], pointwise_part], axis=1)
-    other = from_partner(
-        jnp.where(upper, low_half, high_half).astype(jnp.bfloat16), first_axis, first_mask
-    )
-    buffer = jnp.where(upper, high_half, low_half) + other.astype(jnp.float32)
-    for number, phase in enumerate(phases):
+    dilated_part = jnp.einsum("hrc,hrf->cf", act, taps, preferred_element_type=jnp.float32)
+    other, entry_sums = other_half(facts, dilated_part, pointwise_part, entry_sums)
+    other = from_partner(other, first_axis, first_mask)
+    entry_sums, *parts = own_half(
+        facts, dilated_part, pointwise_part, entry_sums, other, phases[0]
+    )
+    for held, phase in zip(phases, phases[1:] + [[]]):
+        found = exchange_parts(parts[1:], held)
+        entry_sums, *parts = next_parts(facts, parts[0], entry_sums, found, phase)
+    buffer, signal_gradient, activations = parts[0], None, None
+    for number, phase in reversed(list(enumerate(phases))):
+        found = gather_parts(buffer, phase)
+        if number == 0:
+            signal_gradient = unpool(
+                facts, returned[0], outgoing, first_chosen, entry_moments, entry_sums,
+                entry_params, slots, 0, None,
+            )
+            activations = output_rows(
+                facts, flat_act, pointwise_low, arrived, entry_params, slots, windows
+            )
+            tied = lax.optimization_barrier((signal_gradient, activations, *found))
+            signal_gradient, activations, found = tied[0], tied[1], tied[2:]
+        buffer = in_order(found, owners[number])
         if number == len(phases) - 1:
-            buffer, entry_sums, returned[0], activations = lax.optimization_barrier(
-                (buffer, entry_sums, returned[0], activations)
-            )
-        buffer = scatter_sum(buffer, phase, starts[number])
-    entry_sums = total(entry_sums)
-    buffer = buffer.astype(jnp.bfloat16)
-    for number, phase in reversed(list(enumerate(phases))):
-        buffer = gather_parts(buffer, phase, spots[number])
-        if number == len(phases) - 1:
-            buffer, entry_sums, *later = lax.optimization_barrier(
-                (buffer, entry_sums, *sent[1:])
+            buffer, flat_act, entry_sums, *later = lax.optimization_barrier(
+                (buffer, flat_act, entry_sums, *sent[1:])
             )
             returned += [send_back(block) for block in later]
     other = from_partner(buffer, first_axis, first_mask)
     dilated_kernel_gradient, pointwise_kernel_gradient = finish_weights(facts, buffer, other)
-    signal_gradient = None
-    for slot in range(slots):
+    for slot in range(1, slots):
         signal_gradient = unpool(
             facts, returned[slot], outgoing, first_chosen, entry_moments, entry_sums,
             entry_params, slots, slot, signal_gradient,

time: 299 us -> 266 us (0.89)
  local copies, waits for them, and re-layouts: 34 us -> 11.9 us
  starting transfers between devices: 64.2 us -> 55.4 us
  other arithmetic: 12.2 us -> 6.31 us
    unnamed x80 -> x42, local copies, waits for them, and re-layouts: 26.8 us -> 5.88 us
    pallas_call x0 -> x2, Pallas kernels: none -> 9.77 us  [entry_grad(): pl.pallas_call(functools.partial(entry_grad_body, slots, windows, slot),...]
    pallas_call x13 -> x15, Pallas kernels: 48.1 us -> 40.3 us  [kernel_call(): pl.pallas_call(body, in_specs=specs, out_specs=out_specs, out_shape=outpu...]
    ppermute x12, waiting for transfers between devices: 36.1 us -> 43 us  [from_flat_partner(): lax.ppermute(block, ('grp', 'seq'), [(place, place ^ mask) for place in r...]
    ppermute x24 -> x19, starting transfers between devices: 36 us -> 29.6 us  [from_partner(): lax.ppermute(block, axis, [(place, place ^ mask) for place in range(count)])]
    ppermute x24 -> x19, waiting for transfers between devices: 65.3 us -> 60.3 us  [from_partner(): lax.ppermute(block, axis, [(place, place ^ mask) for place in range(count)])]
    add x7 -> x0, other arithmetic: 4.5 us -> none  [the longest x1 3.03 us: per_device(): buffer = jnp.where(upper, high_half, low_half) + other.astype(jnp.float32)]
    dot_general x2 -> x1, matrix products: 6.81 us -> 7.79 us  [per_device(): jnp.einsum('hrc,hrf->cf', act, taps, preferred_element_type=jnp.float32)]
  transfers between devices with their start and end apart: 39 -> 34, of which waited for: 22 -> 22; matrix products, arithmetic and copies ran while one was open for 9% -> 8% of each run, Pallas kernels for 12% -> 15%
where the time goes in v3:
time: 266 us; the launch traced here: 263 us
  waiting for transfers between devices  103 us (39%)
  Pallas kernels  73.6 us (28%)
  starting transfers between devices  55.4 us (21%)
  local copies, waits for them, and re-layouts  11.9 us (4%)
  matrix products  10.6 us (4%)
  other arithmetic  6.31 us (2%)
    ppermute x19, waiting for transfers between devices, from_partner(): lax.ppermute(block, axis, [(place, place ^ mask) for place in range(count)])  60.3 us
    ppermute x12, waiting for transfers between devices, from_flat_partner(): lax.ppermute(block, ('grp', 'seq'), [(place, place ^ mask) for place in r...  43 us
    pallas_call x15, Pallas kernels, kernel_call(): pl.pallas_call(body, in_specs=specs, out_specs=out_specs, out_shape=outpu...  40.3 us
    ppermute x19, starting transfers between devices, from_partner(): lax.ppermute(block, axis, [(place, place ^ mask) for place in range(count)])  29.6 us
    ppermute x12, starting transfers between devices, from_flat_partner(): lax.ppermute(block, ('grp', 'seq'), [(place, place ^ mask) for place in r...  10.9 us
    pallas_call x2, Pallas kernels, unpool(): pl.pallas_call(functools.partial(unpool_body, slots, slot, windows), in_s...  10.4 us
    pallas_call x2, Pallas kernels, entry_grad(): pl.pallas_call(functools.partial(entry_grad_body, slots, windows, slot),...  9.77 us
    all_to_all x2, starting transfers between devices, send_back(): return lax.all_to_all(block, 'seq', split_axis=0, concat_axis=0, tiled=True)  9.24 us
  transfers between devices with their start and end apart: 34, of which 22 were waited for; matrix products, arithmetic and copies ran while one was open for 8% of the time, Pallas kernels for 15%

profile of v3, /device:TPU:17, one launch (start us, length us, event | category | flops | bytes accessed | tf_op | source)
XLA Modules:
  0.0 262.6 jit_solution(12625833702297727431)
XLA Ops:
  1.4 9.2 %pool.1 = (bf16[16,128,768]{2,1,0:T(8,128)(2,1)}, bf16[16,128,768]{2,1,0:T(8,128)(2,1)}, f32[3,768]{1,0:T(4,128)S(1)}) custom-call(s32[83]{0:T(128)S(1)} %concatenate.63.facts_ref, f32[16,256,768]{2,1,0:T(8,128)} %signal_ref.1), custom_call_target="tpu_custom_call" | custom-call | flops 15728640 | bytes 18874368 | tf_op jit(solution)/shard_map/pool/pallas_call | solution.py:105
  10.6 5.6 %all-to-all-start = ((bf16[16,128,768]{2,1,0:T(8,128)(2,1)}), bf16[16,128,768]{2,1,0:T(8,128)(2,1)S(1)}, u32[]{:S(2)}, u32[]{:S(2)}) async-start(bf16[16,128,768]{2,1,0:T(8,128)(2,1)} %get-tuple-element.96.pooled_ref), calls=%async_computation | async-start | bytes 6291456 | tf_op jit(solution)/shard_map/all_to_all | solution.py:1198
  17.5 3.4 %convert_bitcast_fusion = bf16[3,384,768]{1,2,0:T(8,128)(2,1)} fusion(f32[3,768,384]{2,1,0:T(8,128)} %param.14), kind=kLoop, calls=%fused_computation.66 | loop fusion | flops 884736 | bytes 5308416 | tf_op jit(solution)/shard_map/transpose | solution.py:1204
  26.9 14.6 %collective-permute-done.2 = f32[3,768]{1,0:T(4,128)S(1)} collective-permute-done((f32[3,768]{1,0:T(4,128)S(1)}, f32[3,768]{1,0:T(4,128)S(1)}, u32[]{:S(2)}, u32[]{:S(2)}) %collective-permute-start.2) | collective-permute-done | bytes 9248 | tf_op jit(solution)/shard_map/ppermute | solution.py:34
  43.5 4.2 %prepare_cotangent.1 = (bf16[2048,768]{1,0:T(8,128)(2,1)S(1)}, f32[2048,384]{1,0:T(8,128)S(1)}, f32[1,768]{1,0:T(1,128)S(1)}) custom-call(s32[83]{0:T(128)S(1)} %concatenate.63.facts_ref, f32[2048,768]{1,0:T(8,128)S(1)} %bitcast.28, bf16[384,768]{1,0:T(8,128)(2,1)S(1)} %convert_element_type.6.weight_ref), custom_call_target="tpu_custom_call" | custom-call | flops 1207959552 | bytes 12582912 | tf_op jit(solution)/shard_map/prepare_cotangent/pallas_call | solution.py:360
  51.0 17.4 %collective-permute-done.3 = f32[3,768]{1,0:T(4,128)S(1)} collective-permute-done((f32[3,768]{1,0:T(4,128)S(1)}, f32[3,768]{1,0:T(4,128)S(1)}, u32[]{:S(2)}, u32[]{:S(2)}) %collective-permute-start.3) | collective-permute-done | bytes 9248 | tf_op jit(solution)/shard_map/ppermute | solution.py:34
  68.7 3.9 %copy.22 = bf16[3,384,768]{2,1,0:T(8,128)(2,1)} copy(bf16[3,384,768]{1,2,0:T(8,128)(2,1)} %convert_bitcast_fusion) | data formatting | bytes 3538944 | tf_op jit(solution)/shard_map/transpose | solution.py:1204
  72.6 10.9 %collective-permute-done.4 = f32[3,768]{1,0:T(4,128)S(1)} collective-permute-done((f32[3,768]{1,0:T(4,128)S(1)}, f32[3,768]{1,0:T(4,128)S(1)}, u32[]{:S(2)}, u32[]{:S(2)}) %collective-permute-start.4) | collective-permute-done | bytes 9248 | tf_op jit(solution)/shard_map/ppermute | solution.py:34
  83.6 3.7 %activate.1 = (bf16[4,512,768]{2,1,0:T(8,128)(2,1)S(1)}, bf16[4,48,768]{2,1,0:T(8,128)(2,1)S(1)}) custom-call(s32[83]{0:T(128)S(1)} %concatenate.63.facts_ref, bf16[16,128,768]{2,1,0:T(8,128)(2,1)S(1)} %all-to-all-done.arrived_ref.refs_2_, f32[3,768]{1,0:T(4,128)S(1)} %get-tuple-element.221.moments_ref.refs_4_, ...), custom_call_target="tpu_custom_call" | custom-call | flops 31457280 | bytes 6291456 | tf_op jit(solution)/shard_map/activate/pallas_call | solution.py:105
  88.9 6.7 %convolve.1 = (f32[4,512,384]{2,1,0:T(8,128)S(1)}, f32[3,384]{1,0:T(4,128)S(1)}) custom-call(s32[83]{0:T(128)S(1)} %concatenate.63.facts_ref, bf16[4,512,768]{2,1,0:T(8,128)(2,1)S(1)} %get-tuple-element.102.act_ref, bf16[768,1152]{1,0:T(8,128)(2,1)S(1)} %copy-done.4), custom_call_target="tpu_custom_call" | custom-call | flops 3623878656 | bytes 6291456 | tf_op jit(solution)/shard_map/convolve/pallas_call | solution.py:105
  105.5 3.4 %collective-permute-start.9 = (f32[3,384]{1,0:T(4,128)S(1)}, f32[3,384]{1,0:T(4,128)S(1)}, u32[]{:S(2)}, u32[]{:S(2)}) collective-permute-start(f32[3,384]{1,0:T(4,128)S(1)} %pad_maximum_fusion.10), channel_id=1, source_target_pairs={{0,2},{1,3},{2,0},{3,1},{4,6},{5,7},{6,4},{7,5},{8,10},{9,11},{10,... | collective-permute-start | bytes 13832 | tf_op jit(solution)/shard_map/ppermute | solution.py:34
  114.4 4.2 %middle_norm.1 = (bf16[4,512,384]{2,1,0:T(8,128)(2,1)S(1)}, f32[4,512,384]{2,1,0:T(8,128)S(1)}, f32[4,512,384]{2,1,0:T(8,128)S(1)}, f32[2,384]{1,0:T(2,128)S(1)}) custom-call(s32[83]{0:T(128)S(1)} %concatenate.63.facts_ref, f32[4,512,384]{2,1,0:T(8,128)S(1)} %get-tuple-element.104.out_ref, f32[4,64,384]{2,1,0:T(8,128)S(1)} %get-tuple-element.107.strip_ref, ...), custom_call_target="tpu_custom_call" | custom-call | flops 31457280 | bytes 14155776 | tf_op jit(solution)/shard_map/middle_norm/pallas_call | solution.py:105
  118.7 3.5 %collective-permute-start.11 = (f32[2,384]{1,0:T(2,128)S(1)}, f32[2,384]{1,0:T(2,128)S(1)}, u32[]{:S(2)}, u32[]{:S(2)}) collective-permute-start(f32[2,384]{1,0:T(2,128)S(1)} %get-tuple-element.126), channel_id=1, source_target_pairs={{0,8},{8,0},{16,24},{24,16},{1,9},{9,1},{17,25},{25,17},{2,10},{10... | collective-permute-start | bytes 9224 | tf_op jit(solution)/shard_map/ppermute | solution.py:34
  124.2 2.8 %fusion.6.pointwise_ref = f32[768,384]{1,0:T(8,128)} fusion(bf16[2048,768]{1,0:T(8,128)(2,1)S(1)} %copy-done.1, bf16[2048,384]{1,0:T(8,128)(2,1)S(1)} %bitcast.25), kind=kOutput, calls=%fused_computation.65 | convolution fusion | flops 1207959552 | bytes 5898240 | tf_op jit(solution)/shard_map/rd,rf->df/dot_general | solution.py:1282
  132.8 2.6 collective-permute-done.15
  137.8 3.6 %collective-permute-done.16.border_ref = bf16[4,48,384]{2,1,0:T(8,128)(2,1)S(1)} collective-permute-done((bf16[4,48,384]{2,1,0:T(8,128)(2,1)S(1)}, bf16[4,48,384]{2,1,0:T(8,128)(2,1)S(1)}, u32[]{:S(2)}, u32[]{:S(2)}) %collective-permute-start.16) | collective-permute-done | bytes 147488 | tf_op jit(solution)/shard_map/ppermute | solution.py:34
  141.4 4.8 %entry_grad.2 = (bf16[8,128,768]{2,1,0:T(8,128)(2,1)}, bf16[4,512,1152]{2,1,0:T(8,128)(2,1)}, f32[2,768]{1,0:T(2,128)S(1)}) custom-call(s32[83]{0:T(128)S(1)} %concatenate.63.facts_ref, f32[4,3,592,128]{3,2,1,0:T(8,128)S(1)} %get-tuple-element.131.padded_ref, bf16[4,48,384]{2,1,0:T(8,128)(2,1)S(1)} %collective-permute-done.16.border_ref, ...), custom_call_target="tpu_custom_call" | custom-call | flops 1811939328 | bytes 11796480 | tf_op jit(solution)/shard_map/entry_grad/pallas_call | solution.py:856
  146.2 5.0 %entry_grad.3 = (bf16[8,128,768]{2,1,0:T(8,128)(2,1)}, bf16[4,512,1152]{2,1,0:T(8,128)(2,1)}, f32[2,768]{1,0:T(2,128)S(1)}) custom-call(s32[83]{0:T(128)S(1)} %concatenate.63.facts_ref, f32[4,3,592,128]{3,2,1,0:T(8,128)S(1)} %get-tuple-element.131.padded_ref, ...), custom_call_target="tpu_custom_call", output_to_operand_aliasing={{1}: (10, {})} | custom-call | flops 1811939328 | bytes 11796480 | tf_op jit(solution)/shard_map/entry_grad/pallas_call | solution.py:856
  151.2 4.9 %all-to-all-start.1 = ((bf16[8,128,768]{2,1,0:T(8,128)(2,1)}), bf16[8,128,768]{2,1,0:T(8,128)(2,1)}, u32[]{:S(2)}, u32[]{:S(2)}) async-start(bf16[8,128,768]{2,1,0:T(8,128)(2,1)} %get-tuple-element.144), calls=%async_computation.1 | async-start | bytes 3145728 | tf_op jit(solution)/shard_map/all_to_all | solution.py:1296
  156.2 7.8 %convolution_bitcast_fusion.dilated_ref = f32[768,1152]{1,0:T(8,128)S(1)} fusion(bf16[4,512,768]{2,1,0:T(8,128)(2,1)} %copy-done.11, bf16[4,512,1152]{2,1,0:T(8,128)(2,1)} %get-tuple-element.147), kind=kOutput, calls=%fused_computation | convolution fusion | flops 3623878656 | bytes 11403264 | tf_op jit(solution)/shard_map/hrc,hrf->cf/dot_general | solution.py:1309
  164.7 5.8 %collective-permute-start.17 = (bf16[776,768]{1,0:T(8,128)(2,1)S(1)}, bf16[776,768]{1,0:T(8,128)(2,1)S(1)}, u32[]{:S(2)}, u32[]{:S(2)}) collective-permute-start(bf16[776,768]{1,0:T(8,128)(2,1)S(1)} %get-tuple-element.151), channel_id=1, source_target_pairs={{0,8},{8,0},{16,24},{24,16},{1,9},{9,1},{17,25},{25,17},{2,10},{10... | collective-permute-start | bytes 3575816 | tf_op jit(solution)/shard_map/ppermute | solution.py:34
  170.5 2.5 collective-permute-done.17.other_ref
  176.5 6.0 %collective-permute-done.18.refs_0_ = bf16[200,768]{1,0:T(8,128)(2,1)S(1)} collective-permute-done((bf16[200,768]{1,0:T(8,128)(2,1)S(1)}, bf16[200,768]{1,0:T(8,128)(2,1)S(1)}, u32[]{:S(2)}, u32[]{:S(2)}) %collective-permute-start.18) | collective-permute-done | bytes 307232 | tf_op jit(solution)/shard_map/ppermute | solution.py:889
  182.5 12.9 %collective-permute-done.19.refs_1_ = bf16[200,768]{1,0:T(8,128)(2,1)S(1)} collective-permute-done((bf16[200,768]{1,0:T(8,128)(2,1)S(1)}, bf16[200,768]{1,0:T(8,128)(2,1)S(1)}, u32[]{:S(2)}, u32[]{:S(2)}) %collective-permute-start.19) | collective-permute-done | bytes 307232 | tf_op jit(solution)/shard_map/ppermute | solution.py:889
  201.4 5.0 %collective-permute-done.23.refs_2_ = bf16[56,768]{1,0:T(8,128)(2,1)S(1)} collective-permute-done((bf16[56,768]{1,0:T(8,128)(2,1)S(1)}, bf16[56,768]{1,0:T(8,128)(2,1)S(1)}, u32[]{:S(2)}, u32[]{:S(2)}) %collective-permute-start.23) | collective-permute-done | bytes 86048 | tf_op jit(solution)/shard_map/ppermute | solution.py:889
  211.6 4.4 %collective-permute-done.24 = bf16[48,768]{1,0:T(8,128)(2,1)S(1)} collective-permute-done((bf16[48,768]{1,0:T(8,128)(2,1)S(1)}, bf16[48,768]{1,0:T(8,128)(2,1)S(1)}, u32[]{:S(2)}, u32[]{:S(2)}) %collective-permute-start.24) | collective-permute-done | bytes 73760 | tf_op jit(solution)/shard_map/ppermute | solution.py:889
  216.1 4.3 %all-to-all-start.2 = ((bf16[8,128,768]{2,1,0:T(8,128)(2,1)}), bf16[8,128,768]{2,1,0:T(8,128)(2,1)}, u32[]{:S(2)}, u32[]{:S(2)}) async-start(bf16[8,128,768]{2,1,0:T(8,128)(2,1)} %get-tuple-element.172), calls=%async_computation.2 | async-start | bytes 3145728 | tf_op jit(solution)/shard_map/all_to_all | solution.py:1296
  225.7 9.0 %output_rows.1 = f32[2048,768]{1,0:T(8,128)} custom-call(s32[83]{0:T(128)S(1)} %concatenate.63.facts_ref, bf16[2048,384]{1,0:T(8,128)(2,1)S(1)} %bitcast.26, bf16[384,768]{1,0:T(8,128)(2,1)S(1)} %copy-done.8, bf16[16,128,768]{2,1,0:T(8,128)(2,1)S(1)} %all-to-all-done.arrived_ref.refs_2_, f32[3,768]{1,0:T(4,128)S(1)} %get-tuple-element.222.params_ref.refs_5_), custom_call_target="tpu_custom_call" | custom-call | flops 1207959552 | bytes 12582912 | tf_op jit(solution)/shard_map/output_rows/pallas_call | solution.py:748
  234.6 5.2 %unpool.2.refs_0_ = f32[16,256,768]{2,1,0:T(8,128)} custom-call(s32[83]{0:T(128)S(1)} %concatenate.63.facts_ref, bf16[8,128,768]{2,1,0:T(8,128)(2,1)} %all-to-all-done.1.returned_ref, bf16[16,128,768]{2,1,0:T(8,128)(2,1)} %get-tuple-element.96.pooled_ref, bf16[16,128,768]{2,1,0:T(8,128)(2,1)} %get-tuple-element.145.first_ref, ...), custom_call_target="tpu_custom_call" | custom-call | flops 7864320 | bytes 11010048 | tf_op jit(solution)/shard_map/unpool/pallas_call | solution.py:310
  239.8 10.3 %collective-permute-done.28 = bf16[192,768]{1,0:T(8,128)(2,1)S(1)} collective-permute-done((bf16[192,768]{1,0:T(8,128)(2,1)S(1)}, bf16[192,768]{1,0:T(8,128)(2,1)S(1)}, u32[]{:S(2)}, u32[]{:S(2)}) %collective-permute-start.28) | collective-permute-done | bytes 294944 | tf_op jit(solution)/shard_map/ppermute | solution.py:889
  254.1 3.1 %finish_weights.1 = (f32[3,768,384]{2,1,0:T(8,128)}, f32[384,768]{1,0:T(8,128)}) custom-call(s32[83]{0:T(128)S(1)} %concatenate.63.facts_ref, bf16[768,768]{1,0:T(8,128)(2,1)S(1)} %maximum_select_fusion.mine_ref, bf16[768,768]{1,0:T(8,128)(2,1)S(1)} %collective-permute-done.30.other_ref), custom_call_target="tpu_custom_call" | custom-call | flops 589824 | bytes 7077888 | tf_op jit(solution)/shard_map/finish_weights/pallas_call | solution.py:105
  257.3 5.2 %unpool.3 = f32[16,256,768]{2,1,0:T(8,128)} custom-call(s32[83]{0:T(128)S(1)} %concatenate.63.facts_ref, bf16[8,128,768]{2,1,0:T(8,128)(2,1)} %all-to-all-done.2.returned_ref, bf16[16,128,768]{2,1,0:T(8,128)(2,1)} %get-tuple-element.96.pooled_ref, bf16[16,128,768]{2,1,0:T(8,128)(2,1)} %get-tuple-element.145.first_ref, ...), custom_call_target="tpu_custom_call", output_to_operand_aliasing={{}: (7, {})} | custom-call | flops 7864320 | bytes 11010048 | tf_op jit(solution)/shard_map/unpool/pallas_call | solution.py:310
  (146 shorter events, 65.3 us)
Async XLA Ops:
  10.6 73.0 %all-to-all-start = ((bf16[16,128,768]{2,1,0:T(8,128)(2,1)}), bf16[16,128,768]{2,1,0:T(8,128)(2,1)S(1)}, u32[]{:S(2)}, u32[]{:S(2)}) async-start(bf16[16,128,768]{2,1,0:T(8,128)(2,1)} %get-tuple-element.96.pooled_ref), calls=%async_computation | async-start | bytes 6291456 | tf_op jit(solution)/shard_map/all_to_all | solution.py:1198
  16.3 4.8 %collective-permute-start = (f32[3,768]{1,0:T(4,128)S(1)}, f32[3,768]{1,0:T(4,128)S(1)}, u32[]{:S(2)}, u32[]{:S(2)}) collective-permute-start(f32[3,768]{1,0:T(4,128)S(1)} %get-tuple-element.101), channel_id=1, source_target_pairs={{0,8},{8,0},{16,24},{24,16},{1,9},{9,1},{17,25},{25,17},{2,10},{10... | collective-permute-start | bytes 27656 | tf_op jit(solution)/shard_map/ppermute | solution.py:34
  21.2 2.9 %collective-permute-start.1 = (f32[3,768]{1,0:T(4,128)S(1)}, f32[3,768]{1,0:T(4,128)S(1)}, u32[]{:S(2)}, u32[]{:S(2)}) collective-permute-start(f32[3,768]{1,0:T(4,128)S(1)} %pad_maximum_fusion.1), channel_id=1, source_target_pairs={{0,16},{8,24},{16,0},{24,8},{1,17},{9,25},{17,1},{25,9},{2,18},{10... | collective-permute-start | bytes 27656 | tf_op jit(solution)/shard_map/ppermute | solution.py:34
  24.1 17.4 %collective-permute-start.2 = (f32[3,768]{1,0:T(4,128)S(1)}, f32[3,768]{1,0:T(4,128)S(1)}, u32[]{:S(2)}, u32[]{:S(2)}) collective-permute-start(f32[3,768]{1,0:T(4,128)S(1)} %pad_maximum_fusion.2), channel_id=1, source_target_pairs={{0,1},{1,0},{2,3},{3,2},{4,5},{5,4},{6,7},{7,6},{8,9},{9,8},{10,11... | collective-permute-start | bytes 27656 | tf_op jit(solution)/shard_map/ppermute | solution.py:34
  41.6 26.9 %collective-permute-start.3 = (f32[3,768]{1,0:T(4,128)S(1)}, f32[3,768]{1,0:T(4,128)S(1)}, u32[]{:S(2)}, u32[]{:S(2)}) collective-permute-start(f32[3,768]{1,0:T(4,128)S(1)} %pad_maximum_fusion.3), channel_id=1, source_target_pairs={{0,2},{1,3},{2,0},{3,1},{4,6},{5,7},{6,4},{7,5},{8,10},{9,11},{10,... | collective-permute-start | bytes 27656 | tf_op jit(solution)/shard_map/ppermute | solution.py:34
  68.5 15.0 %collective-permute-start.4 = (f32[3,768]{1,0:T(4,128)S(1)}, f32[3,768]{1,0:T(4,128)S(1)}, u32[]{:S(2)}, u32[]{:S(2)}) collective-permute-start(f32[3,768]{1,0:T(4,128)S(1)} %pad_maximum_fusion.4), channel_id=1, source_target_pairs={{0,4},{1,5},{2,6},{3,7},{4,0},{5,1},{6,2},{7,3},{8,12},{9,13},{10,... | collective-permute-start | bytes 27656 | tf_op jit(solution)/shard_map/ppermute | solution.py:34
  87.3 8.3 %collective-permute-start.5 = (bf16[4,48,768]{2,1,0:T(8,128)(2,1)S(1)}, bf16[4,48,768]{2,1,0:T(8,128)(2,1)S(1)}, u32[]{:S(2)}, u32[]{:S(2)}) collective-permute-start(bf16[4,48,768]{2,1,0:T(8,128)(2,1)S(1)} %get-tuple-element.105), channel_id=1, source_target_pairs={{0,1},{1,0},{2,3},{3,2},{4,5},{5,4},{6,7},{7,6},{8,9},{9,8},{10,11... | collective-permute-start | bytes 884744 | tf_op jit(solution)/shard_map/ppermute | solution.py:34
  96.6 2.6 collective-permute-start.6
  99.3 3.2 %collective-permute-start.7 = (f32[3,384]{1,0:T(4,128)S(1)}, f32[3,384]{1,0:T(4,128)S(1)}, u32[]{:S(2)}, u32[]{:S(2)}) collective-permute-start(f32[3,384]{1,0:T(4,128)S(1)} %pad_maximum_fusion.8), channel_id=1, source_target_pairs={{0,16},{8,24},{16,0},{24,8},{1,17},{9,25},{17,1},{25,9},{2,18},{10... | collective-permute-start | bytes 13832 | tf_op jit(solution)/shard_map/ppermute | solution.py:34
  102.5 3.0 %collective-permute-start.8 = (f32[3,384]{1,0:T(4,128)S(1)}, f32[3,384]{1,0:T(4,128)S(1)}, u32[]{:S(2)}, u32[]{:S(2)}) collective-permute-start(f32[3,384]{1,0:T(4,128)S(1)} %pad_maximum_fusion.9), channel_id=1, source_target_pairs={{0,1},{1,0},{2,3},{3,2},{4,5},{5,4},{6,7},{7,6},{8,9},{9,8},{10,11... | collective-permute-start | bytes 13832 | tf_op jit(solution)/shard_map/ppermute | solution.py:34
  105.5 5.3 %collective-permute-start.9 = (f32[3,384]{1,0:T(4,128)S(1)}, f32[3,384]{1,0:T(4,128)S(1)}, u32[]{:S(2)}, u32[]{:S(2)}) collective-permute-start(f32[3,384]{1,0:T(4,128)S(1)} %pad_maximum_fusion.10), channel_id=1, source_target_pairs={{0,2},{1,3},{2,0},{3,1},{4,6},{5,7},{6,4},{7,5},{8,10},{9,11},{10,... | collective-permute-start | bytes 13832 | tf_op jit(solution)/shard_map/ppermute | solution.py:34
  110.9 3.4 %collective-permute-start.10 = (f32[3,384]{1,0:T(4,128)S(1)}, f32[3,384]{1,0:T(4,128)S(1)}, u32[]{:S(2)}, u32[]{:S(2)}) collective-permute-start(f32[3,384]{1,0:T(4,128)S(1)} %pad_maximum_fusion.11), channel_id=1, source_target_pairs={{0,4},{1,5},{2,6},{3,7},{4,0},{5,1},{6,2},{7,3},{8,12},{9,13},{10,... | collective-permute-start | bytes 13832 | tf_op jit(solution)/shard_map/ppermute | solution.py:34
  118.7 4.3 %collective-permute-start.11 = (f32[2,384]{1,0:T(2,128)S(1)}, f32[2,384]{1,0:T(2,128)S(1)}, u32[]{:S(2)}, u32[]{:S(2)}) collective-permute-start(f32[2,384]{1,0:T(2,128)S(1)} %get-tuple-element.126), channel_id=1, source_target_pairs={{0,8},{8,0},{16,24},{24,16},{1,9},{9,1},{17,25},{25,17},{2,10},{10... | collective-permute-start | bytes 9224 | tf_op jit(solution)/shard_map/ppermute | solution.py:34
  123.0 4.1 %collective-permute-start.12 = (f32[2,384]{1,0:T(2,128)S(1)}, f32[2,384]{1,0:T(2,128)S(1)}, u32[]{:S(2)}, u32[]{:S(2)}) collective-permute-start(f32[2,384]{1,0:T(2,128)S(1)} %add.237), channel_id=1, source_target_pairs={{0,16},{8,24},{16,0},{24,8},{1,17},{9,25},{17,1},{25,9},{2,18},{10... | collective-permute-start | bytes 9224 | tf_op jit(solution)/shard_map/ppermute | solution.py:34
  132.0 3.3 %collective-permute-start.15 = (f32[2,384]{1,0:T(2,128)S(1)}, f32[2,384]{1,0:T(2,128)S(1)}, u32[]{:S(2)}, u32[]{:S(2)}) collective-permute-start(f32[2,384]{1,0:T(2,128)S(1)} %add.240), channel_id=1, source_target_pairs={{0,4},{1,5},{2,6},{3,7},{4,0},{5,1},{6,2},{7,3},{8,12},{9,13},{10,... | collective-permute-start | bytes 9224 | tf_op jit(solution)/shard_map/ppermute | solution.py:34
  137.3 4.1 %collective-permute-start.16 = (bf16[4,48,384]{2,1,0:T(8,128)(2,1)S(1)}, bf16[4,48,384]{2,1,0:T(8,128)(2,1)S(1)}, u32[]{:S(2)}, u32[]{:S(2)}) collective-permute-start(bf16[4,48,384]{2,1,0:T(8,128)(2,1)S(1)} %get-tuple-element.132), channel_id=1, source_target_pairs={{0,1},{1,0},{2,3},{3,2},{4,5},{5,4},{6,7},{7,6},{8,9},{9,8},{10,11... | collective-permute-start | bytes 442376 | tf_op jit(solution)/shard_map/ppermute | solution.py:34
  151.2 64.8 %all-to-all-start.1 = ((bf16[8,128,768]{2,1,0:T(8,128)(2,1)}), bf16[8,128,768]{2,1,0:T(8,128)(2,1)}, u32[]{:S(2)}, u32[]{:S(2)}) async-start(bf16[8,128,768]{2,1,0:T(8,128)(2,1)} %get-tuple-element.144), calls=%async_computation.1 | async-start | bytes 3145728 | tf_op jit(solution)/shard_map/all_to_all | solution.py:1296
  164.7 8.3 %collective-permute-start.17 = (bf16[776,768]{1,0:T(8,128)(2,1)S(1)}, bf16[776,768]{1,0:T(8,128)(2,1)S(1)}, u32[]{:S(2)}, u32[]{:S(2)}) collective-permute-start(bf16[776,768]{1,0:T(8,128)(2,1)S(1)} %get-tuple-element.151), channel_id=1, source_target_pairs={{0,8},{8,0},{16,24},{24,16},{1,9},{9,1},{17,25},{25,17},{2,10},{10... | collective-permute-start | bytes 3575816 | tf_op jit(solution)/shard_map/ppermute | solution.py:34
  173.8 8.7 %collective-permute-start.18 = (bf16[200,768]{1,0:T(8,128)(2,1)S(1)}, bf16[200,768]{1,0:T(8,128)(2,1)S(1)}, u32[]{:S(2)}, u32[]{:S(2)}) collective-permute-start(bf16[200,768]{1,0:T(8,128)(2,1)S(1)} %get-tuple-element.154), channel_id=1, source_target_pairs={{0,16},{1,17},{2,18},{3,19},{4,20},{5,21},{6,22},{7,23},{8,24},{9,... | collective-permute-start | bytes 921608 | tf_op jit(solution)/shard_map/ppermute | solution.py:889
  174.3 21.1 %collective-permute-start.19 = (bf16[200,768]{1,0:T(8,128)(2,1)S(1)}, bf16[200,768]{1,0:T(8,128)(2,1)S(1)}, u32[]{:S(2)}, u32[]{:S(2)}) collective-permute-start(bf16[200,768]{1,0:T(8,128)(2,1)S(1)} %get-tuple-element.155), channel_id=1, source_target_pairs={{0,1},{1,0},{2,3},{3,2},{4,5},{5,4},{6,7},{7,6},{8,9},{9,8},{10,11... | collective-permute-start | bytes 921608 | tf_op jit(solution)/shard_map/ppermute | solution.py:889
  175.5 19.9 %collective-permute-start.20 = (bf16[200,768]{1,0:T(8,128)(2,1)S(1)}, bf16[200,768]{1,0:T(8,128)(2,1)S(1)}, u32[]{:S(2)}, u32[]{:S(2)}) collective-permute-start(bf16[200,768]{1,0:T(8,128)(2,1)S(1)} %get-tuple-element.156), channel_id=1, source_target_pairs={{0,17},{1,16},{2,19},{3,18},{4,21},{5,20},{6,23},{7,22},{8,25},{9,... | collective-permute-start | bytes 921608 | tf_op jit(solution)/shard_map/ppermute | solution.py:889
  196.1 3.4 %collective-permute-start.21 = (bf16[56,768]{1,0:T(8,128)(2,1)S(1)}, bf16[56,768]{1,0:T(8,128)(2,1)S(1)}, u32[]{:S(2)}, u32[]{:S(2)}) collective-permute-start(bf16[56,768]{1,0:T(8,128)(2,1)S(1)} %get-tuple-element.159), channel_id=1, source_target_pairs={{0,2},{1,3},{2,0},{3,1},{4,6},{5,7},{6,4},{7,5},{8,10},{9,11},{10,... | collective-permute-start | bytes 258056 | tf_op jit(solution)/shard_map/ppermute | solution.py:889
  196.2 5.2 %collective-permute-start.22 = (bf16[56,768]{1,0:T(8,128)(2,1)S(1)}, bf16[56,768]{1,0:T(8,128)(2,1)S(1)}, u32[]{:S(2)}, u32[]{:S(2)}) collective-permute-start(bf16[56,768]{1,0:T(8,128)(2,1)S(1)} %get-tuple-element.160), channel_id=1, source_target_pairs={{0,4},{1,5},{2,6},{3,7},{4,0},{5,1},{6,2},{7,3},{8,12},{9,13},{10,... | collective-permute-start | bytes 258056 | tf_op jit(solution)/shard_map/ppermute | solution.py:889
  196.6 9.9 %collective-permute-start.23 = (bf16[56,768]{1,0:T(8,128)(2,1)S(1)}, bf16[56,768]{1,0:T(8,128)(2,1)S(1)}, u32[]{:S(2)}, u32[]{:S(2)}) collective-permute-start(bf16[56,768]{1,0:T(8,128)(2,1)S(1)} %get-tuple-element.161), channel_id=1, source_target_pairs={{0,6},{1,7},{2,4},{3,5},{4,2},{5,3},{6,0},{7,1},{8,14},{9,15},{10,... | collective-permute-start | bytes 258056 | tf_op jit(solution)/shard_map/ppermute | solution.py:889
  207.1 3.3 %collective-permute-start.26 = (bf16[48,768]{1,0:T(8,128)(2,1)S(1)}, bf16[48,768]{1,0:T(8,128)(2,1)S(1)}, u32[]{:S(2)}, u32[]{:S(2)}) collective-permute-start(bf16[48,768]{1,0:T(8,128)(2,1)S(1)} %get-tuple-element.162), channel_id=1, source_target_pairs={{0,2},{1,3},{2,0},{3,1},{4,6},{5,7},{6,4},{7,5},{8,10},{9,11},{10,... | collective-permute-start | bytes 221192 | tf_op jit(solution)/shard_map/ppermute | solution.py:889
  207.1 4.4 %collective-permute-start.25 = (bf16[48,768]{1,0:T(8,128)(2,1)S(1)}, bf16[48,768]{1,0:T(8,128)(2,1)S(1)}, u32[]{:S(2)}, u32[]{:S(2)}) collective-permute-start(bf16[48,768]{1,0:T(8,128)(2,1)S(1)} %get-tuple-element.162), channel_id=1, source_target_pairs={{0,4},{1,5},{2,6},{3,7},{4,0},{5,1},{6,2},{7,3},{8,12},{9,13},{10,... | collective-permute-start | bytes 221192 | tf_op jit(solution)/shard_map/ppermute | solution.py:889
  208.1 7.9 %collective-permute-start.24 = (bf16[48,768]{1,0:T(8,128)(2,1)S(1)}, bf16[48,768]{1,0:T(8,128)(2,1)S(1)}, u32[]{:S(2)}, u32[]{:S(2)}) collective-permute-start(bf16[48,768]{1,0:T(8,128)(2,1)S(1)} %get-tuple-element.162), channel_id=1, source_target_pairs={{0,6},{1,7},{2,4},{3,5},{4,2},{5,3},{6,0},{7,1},{8,14},{9,15},{10,... | collective-permute-start | bytes 221192 | tf_op jit(solution)/shard_map/ppermute | solution.py:889
  216.1 41.2 %all-to-all-start.2 = ((bf16[8,128,768]{2,1,0:T(8,128)(2,1)}), bf16[8,128,768]{2,1,0:T(8,128)(2,1)}, u32[]{:S(2)}, u32[]{:S(2)}) async-start(bf16[8,128,768]{2,1,0:T(8,128)(2,1)} %get-tuple-element.172), calls=%async_computation.2 | async-start | bytes 3145728 | tf_op jit(solution)/shard_map/all_to_all | solution.py:1296
  220.4 19.5 %collective-permute-start.27 = (bf16[192,768]{1,0:T(8,128)(2,1)S(1)}, bf16[192,768]{1,0:T(8,128)(2,1)S(1)}, u32[]{:S(2)}, u32[]{:S(2)}) collective-permute-start(bf16[192,768]{1,0:T(8,128)(2,1)S(1)} %maximum_select_fusion.3), channel_id=1, source_target_pairs={{0,16},{1,17},{2,18},{3,19},{4,20},{5,21},{6,22},{7,23},{8,24},{9,... | collective-permute-start | bytes 884744 | tf_op jit(solution)/shard_map/ppermute | solution.py:889
  221.9 28.2 %collective-permute-start.28 = (bf16[192,768]{1,0:T(8,128)(2,1)S(1)}, bf16[192,768]{1,0:T(8,128)(2,1)S(1)}, u32[]{:S(2)}, u32[]{:S(2)}) collective-permute-start(bf16[192,768]{1,0:T(8,128)(2,1)S(1)} %maximum_select_fusion.3), channel_id=1, source_target_pairs={{0,1},{1,0},{2,3},{3,2},{4,5},{5,4},{6,7},{7,6},{8,9},{9,8},{10,11... | collective-permute-start | bytes 884744 | tf_op jit(solution)/shard_map/ppermute | solution.py:889
  222.4 27.8 %collective-permute-start.29 = (bf16[192,768]{1,0:T(8,128)(2,1)S(1)}, bf16[192,768]{1,0:T(8,128)(2,1)S(1)}, u32[]{:S(2)}, u32[]{:S(2)}) collective-permute-start(bf16[192,768]{1,0:T(8,128)(2,1)S(1)} %maximum_select_fusion.3), channel_id=1, source_target_pairs={{0,17},{1,16},{2,19},{3,18},{4,21},{5,20},{6,23},{7,22},{8,25},{9,... | collective-permute-start | bytes 884744 | tf_op jit(solution)/shard_map/ppermute | solution.py:889
  250.9 3.3 %collective-permute-start.30 = (bf16[768,768]{1,0:T(8,128)(2,1)S(1)}, bf16[768,768]{1,0:T(8,128)(2,1)S(1)}, u32[]{:S(2)}, u32[]{:S(2)}) collective-permute-start(bf16[768,768]{1,0:T(8,128)(2,1)S(1)} %maximum_select_fusion.mine_ref), channel_id=1, source_target_pairs={{0,8},{8,0},{16,24},{24,16},{1,9},{9,1},{17,25},{25,17},{2,10},{10... | collective-permute-start | bytes 3538952 | tf_op jit(solution)/shard_map/ppermute | solution.py:34
  (23 other events, 217.9 us)

commit v4 on v3

--- a/solution.py
+++ b/solution.py
@@ -62,8 +62,11 @@
     )
 
 
-def total_moments(packed):
-    for axis, mask in exchange_steps():
+def total_moments(packed, others):
+    steps = exchange_steps()
+    for number, (axis, mask) in enumerate(steps):
+        if number == len(steps) - 1:
+            packed, *others = lax.optimization_barrier((packed, *others))
         other = from_partner(packed, axis, mask)
         packed = jnp.concatenate(
             merged(
@@ -71,7 +74,7 @@
             ),
             axis=0,
         )
-    return packed
+    return packed, others
 
 
 class Facts:
@@ -128,54 +131,73 @@
     return [slice(start, start + LANES) for start in range(0, width, LANES)]
 
 
+def bin_copy(facts, signal_ref, held, arrivals, place, column):
+    return pltpu.make_async_copy(
+        signal_ref.at[facts.slot_window(place), :, pl.ds(column * LANES, LANES)],
+        held.at[place, column],
+        arrivals.at[place, column],
+    )
+
+
+def begin_bins(facts, signal_ref, held, arrivals):
+    windows, columns = held.shape[:2]
+
+    def begin(place, carry):
+        for column in range(columns):
+            bin_copy(facts, signal_ref, held, arrivals, place, column).start()
+        return carry
+
+    lax.fori_loop(0, windows, begin, 0)
+
+
+def bins_of(facts, signal_ref, held, arrivals, place, rows):
+    columns = held.shape[1]
+    for column in range(columns):
+        bin_copy(facts, signal_ref, held, arrivals, place, column).wait()
+    return [
+        (
+            lanes,
+            held[place, column, pl.ds(0, rows, stride=2), :],
+            held[place, column, pl.ds(1, rows, stride=2), :],
+        )
+        for column, lanes in enumerate(column_slices(columns * LANES))
+    ]
+
+
+def finish_copies(copy_of, count):
+    def finish(place, carry):
+        copy_of(place).wait()
+        return carry
+
+    lax.fori_loop(0, count, finish, 0)
+
+
 def pool_body(
-    slots, facts_ref, signal_ref, pooled_ref, first_ref, moments_ref,
-    held, low, mark, blocks, arrivals, departures,
+    slots, facts_ref, signal_ref, pooled_ref, moments_ref, held, low, blocks, arrivals, departures
 ):
     windows, columns = held.shape[:2]
     rows = low.shape[1]
     facts = Facts(facts_ref, windows, slots)
 
-    def arrival(place, column):
-        return pltpu.make_async_copy(
-            signal_ref.at[facts.slot_window(place), :, pl.ds(column * LANES, LANES)],
-            held.at[place, column],
-            arrivals.at[place, column],
-        )
-
     def departure(place):
-        return [
-            pltpu.make_async_copy(low.at[place], pooled_ref.at[place], departures.at[place, 0]),
-            pltpu.make_async_copy(mark.at[place], first_ref.at[place], departures.at[place, 1]),
-        ]
-
-    def begin(place, carry):
-        for column in range(columns):
-            arrival(place, column).start()
-        return carry
-
-    lax.fori_loop(0, windows, begin, 0)
+        return pltpu.make_async_copy(low.at[place], pooled_ref.at[place], departures.at[place])
+
+    begin_bins(facts, signal_ref, held, arrivals)
     moments_ref[...] = jnp.zeros_like(moments_ref)
 
     def work(place, carry):
         count = facts.slot_count(place, rows)
         inside = lax.broadcasted_iota(jnp.int32, (rows, LANES), 0) < count
-        for column in range(columns):
-            arrival(place, column).wait()
-        for column, lanes in enumerate(column_slices(columns * LANES)):
-            first_bin = held[place, column, pl.ds(0, rows, stride=2), :]
-            second_bin = held[place, column, pl.ds(1, rows, stride=2), :]
-            mark[place, :, lanes] = jnp.where(first_bin >= second_bin, 1.0, 0.0).astype(
-                jnp.bfloat16
-            )
+        for lanes, first_bin, second_bin in bins_of(
+            facts, signal_ref, held, arrivals, place, rows
+        ):
             pooled = jnp.where(inside, jnp.maximum(first_bin, second_bin), 0.0)
             pooled = pooled.astype(jnp.bfloat16)
             low[place, :, lanes] = pooled
             found = block_moments(pooled.astype(jnp.float32), inside, count.astype(jnp.float32))
             blocks[place, 0:1, lanes] = found[0]
             blocks[place, 1:2, lanes] = found[1]
-        for copy in departure(place):
-            copy.start()
+        departure(place).start()
         return carry
 
     lax.fori_loop(0, windows, work, 0)
@@ -191,13 +213,7 @@
         return carry
 
     lax.fori_loop(0, windows, join_blocks, 0)
-
-    def finish(place, carry):
-        for copy in departure(place):
-            copy.wait()
-        return carry
-
-    lax.fori_loop(0, windows, finish, 0)
+    finish_copies(departure, windows)
 
 
 def pool(facts, signal, slots):
@@ -209,22 +225,64 @@
         "pool",
         (facts, in_hbm(signal)),
         [SMEM, HBM],
-        [
-            pltpu.HBM(block, jnp.bfloat16),
-            pltpu.HBM(block, jnp.bfloat16),
-            shape((3, width), jnp.float32),
-        ],
-        [HBM, HBM, VMEM],
+        [pltpu.HBM(block, jnp.bfloat16), shape((3, width), jnp.float32)],
+        [HBM, VMEM],
         [
             pltpu.VMEM((windows, columns, segment, LANES), jnp.float32),
             pltpu.VMEM(block, jnp.bfloat16),
-            pltpu.VMEM(block, jnp.bfloat16),
             pltpu.VMEM((windows, 2, width), jnp.float32),
             pltpu.SemaphoreType.DMA((windows, columns)),
-            pltpu.SemaphoreType.DMA((windows, 2)),
+            pltpu.SemaphoreType.DMA((windows,)),
         ],
         flops=10 * windows * rows * width,
-        bytes_moved=windows * rows * width * 12,
+        bytes_moved=windows * rows * width * 10,
+        grant=24 << 20,
+    )
+
+
+def marks_body(slots, facts_ref, signal_ref, first_ref, held, mark, arrivals, departures):
+    windows = held.shape[0]
+    rows = mark.shape[1]
+    facts = Facts(facts_ref, windows, slots)
+
+    def departure(place):
+        return pltpu.make_async_copy(mark.at[place], first_ref.at[place], departures.at[place])
+
+    begin_bins(facts, signal_ref, held, arrivals)
+
+    def work(place, carry):
+        for lanes, first_bin, second_bin in bins_of(
+            facts, signal_ref, held, arrivals, place, rows
+        ):
+            mark[place, :, lanes] = jnp.where(first_bin >= second_bin, 1.0, 0.0).astype(
+                jnp.bfloat16
+            )
+        departure(place).start()
+        return carry
+
+    lax.fori_loop(0, windows, work, 0)
+    finish_copies(departure, windows)
+
+
+def first_marks(facts, signal, slots):
+    windows, segment, width = signal.shape
+    rows, columns = segment // 2, width // LANES
+    block = (windows, rows, width)
+    return kernel_call(
+        functools.partial(marks_body, slots),
+        "first_marks",
+        (facts, in_hbm(signal)),
+        [SMEM, HBM],
+        pltpu.HBM(block, jnp.bfloat16),
+        HBM,
+        [
+            pltpu.VMEM((windows, columns, segment, LANES), jnp.float32),
+            pltpu.VMEM(block, jnp.bfloat16),
+            pltpu.SemaphoreType.DMA((windows, columns)),
+            pltpu.SemaphoreType.DMA((windows,)),
+        ],
+        flops=3 * windows * rows * width,
+        bytes_moved=windows * rows * width * 10,
         grant=24 << 20,
     )
 
@@ -385,6 +443,34 @@
     )(facts, cotangent, weight)
 
 
+def weights_body(dilated_ref, pointwise_ref, wide_ref, back_ref, low_ref):
+    inner = dilated_ref.shape[2]
+    for number, tap in enumerate((0, 2, 1)):
+        values = dilated_ref[tap]
+        wide_ref[:, tap * inner : (tap + 1) * inner] = values.astype(jnp.bfloat16)
+        back_ref[number * inner : (number + 1) * inner, :] = values.T.astype(jnp.bfloat16)
+    low_ref[...] = pointwise_ref[...].astype(jnp.bfloat16)
+
+
+def prepare_weights(dilated_kernel, pointwise_kernel):
+    taps, width, inner = dilated_kernel.shape
+    return kernel_call(
+        weights_body,
+        "prepare_weights",
+        (dilated_kernel, pointwise_kernel),
+        [VMEM, VMEM],
+        [
+            shape((width, taps * inner), jnp.bfloat16),
+            shape((taps * inner, width), jnp.bfloat16),
+            shape(pointwise_kernel.shape, jnp.bfloat16),
+        ],
+        [VMEM, VMEM, VMEM],
+        flops=4 * width * inner,
+        bytes_moved=30 * width * inner,
+        grant=16 << 20,
+    )
+
+
 def norm_terms(moments_ref, params_ref, rows_total):
     centre = moments_ref[0:1] / rows_total
     scale = lax.rsqrt(moments_ref[1:2] / rows_total + EPSILON)
@@ -667,7 +753,7 @@
 
 def middle_grad_body(
     slots, windows, facts_ref, grad_ref, norm_ref, moments_ref, params_ref, sums_ref,
-    padded_ref, border_ref,
+    padded_ref, border_ref, centre_ref,
 ):
     facts = Facts(facts_ref, windows, slots)
     pieces, rows, inner = grad_ref.shape
@@ -695,6 +781,7 @@
                 - (level[:, lanes] + norm * tilt[:, lanes])
             )
             low = jnp.where(inside, grad, 0.0).astype(jnp.bfloat16)
+            centre_ref[piece, pl.ds(start, size), lanes] = low
             padded_ref[piece, tile, pl.ds(pl.multiple_of(start + PAD, 8), size), :] = low.astype(
                 jnp.float32
             )
@@ -719,8 +806,9 @@
         [
             shape((pieces, inner // LANES, PADDED_ROWS, LANES), jnp.float32),
             shape((pieces, BORDER, inner), jnp.bfloat16),
+            shape(grad.shape, jnp.bfloat16),
         ],
-        [VMEM, VMEM],
+        [VMEM, VMEM, VMEM],
         flops=8 * grad.size,
         bytes_moved=12 * grad.size,
     )
@@ -759,7 +847,7 @@
         out_shape=shape((blocks * rows, width), jnp.float32),
         compiler_params=pltpu.CompilerParams(vmem_limit_bytes=16 << 20),
         cost_estimate=pl.CostEstimate(
-            flops=2 * act.size * width, bytes_accessed=8 * arrived.size, transcendentals=0
+            flops=2 * act.size * width * 8, bytes_accessed=8 * arrived.size * 8, transcendentals=0
         ),
         name="output_rows",
     )(facts, act, weight, arrived, params)
@@ -785,7 +873,9 @@
 
     def keeping(half):
         return pltpu.make_async_copy(
-            taps_ref.at[half], kept_ref.at[slot * 2 + half], kept.at[half]
+            taps_ref.at[half, :, pl.ds(0, kept_ref.shape[2])],
+            kept_ref.at[slot * 2 + half],
+            kept.at[half],
         )
 
     for half in range(2):
@@ -799,9 +889,9 @@
                 wide[tile, end : end + DILATION_STEP] = border[0:DILATION_STEP]
             else:
                 wide[tile, PAD - DILATION_STEP : PAD] = border[skip:BORDER]
-            for tap in range(3):
+            for number, tap in enumerate((0, 2, 1)):
                 start = PAD - (tap - 1) * DILATION_STEP
-                first = (tap * tiles + tile) * LANES
+                first = (number * tiles + tile) * LANES
                 taps_ref[half, :, first : first + LANES] = wide[
                     tile, start : start + HALF_WINDOW_ROWS
                 ].astype(jnp.bfloat16)
@@ -859,7 +949,7 @@
         out_specs=[HBM, HBM, VMEM],
         out_shape=[
             pltpu.HBM((sources, rows, width), jnp.bfloat16),
-            pltpu.HBM((2 * slots, *taps_shape), jnp.bfloat16),
+            pltpu.HBM((2 * slots, HALF_WINDOW_ROWS, 2 * inner), jnp.bfloat16),
             shape((2, width), jnp.float32),
         ],
         input_output_aliases=aliases,
@@ -954,28 +1044,29 @@
 
 
 def other_half_body(
-    facts_ref, dilated_ref, pointwise_ref, sums_ref, sent_ref, held_ref, rows_ref
+    facts_ref, sides_ref, centre_ref, pointwise_ref, sums_ref, sent_ref, held_ref, rows_ref
 ):
     width, inner = pointwise_ref.shape
     sent_ref[width:, :], held_ref[...] = encoded(sums_ref[...], rows_ref)
 
     @pl.when(facts_ref[0] % 2 == 0)
     def _():
-        sent_ref[:width, :inner] = dilated_ref[:, 2 * inner :].astype(jnp.bfloat16)
+        sent_ref[:width, :inner] = sides_ref[:, inner:].astype(jnp.bfloat16)
         sent_ref[:width, inner:] = pointwise_ref[...].astype(jnp.bfloat16)
 
     @pl.when(facts_ref[0] % 2 == 1)
     def _():
-        sent_ref[:width, :] = dilated_ref[:, : 2 * inner].astype(jnp.bfloat16)
-
-
-def other_half(facts, dilated, pointwise, sums):
+        sent_ref[:width, :inner] = sides_ref[:, :inner].astype(jnp.bfloat16)
+        sent_ref[:width, inner:] = centre_ref[...].astype(jnp.bfloat16)
+
+
+def other_half(facts, sides, centre, pointwise, sums):
     width, inner = pointwise.shape
     return kernel_call(
         other_half_body,
         "other_half",
-        (facts, dilated, pointwise, sums),
-        [SMEM, VMEM, VMEM, VMEM],
+        (facts, sides, centre, pointwise, sums),
+        [SMEM] + [VMEM] * 4,
         [shape((width + EXTRA, 2 * inner), jnp.bfloat16), shape(sums.shape, jnp.float32)],
         [VMEM, VMEM],
         [pltpu.VMEM((EXTRA, 2 * inner), jnp.float32)],
@@ -990,7 +1081,7 @@
 
 
 def own_half_body(
-    phase, facts_ref, dilated_ref, pointwise_ref, sums_ref, other_ref, total_ref, *refs
+    phase, facts_ref, sides_ref, centre_ref, pointwise_ref, sums_ref, other_ref, total_ref, *refs
 ):
     part_refs, rows_ref = refs[:-1], refs[-1]
     inner = pointwise_ref.shape[1]
@@ -1011,13 +1102,13 @@
     @pl.when(facts_ref[0] % 2 == 0)
     def _():
         write(
-            lambda here: dilated_ref[here, :inner],
-            lambda here: dilated_ref[here, inner : 2 * inner],
+            lambda here: sides_ref[here, :inner],
+            lambda here: centre_ref[here, :],
         )
 
     @pl.when(facts_ref[0] % 2 == 1)
     def _():
-        write(lambda here: dilated_ref[here, 2 * inner :], lambda here: pointwise_ref[here, :])
+        write(lambda here: sides_ref[here, inner:], lambda here: pointwise_ref[here, :])
 
 
 def part_shapes(sums, rows, columns, phase):
@@ -1030,14 +1121,14 @@
     ]
 
 
-def own_half(facts, dilated, pointwise, sums, other, phase):
+def own_half(facts, sides, centre, pointwise, sums, other, phase):
     width, inner = pointwise.shape
     outputs = part_shapes(sums, width, 2 * inner, phase)
     return kernel_call(
         functools.partial(own_half_body, phase),
         "own_half",
-        (facts, dilated, pointwise, sums, other),
-        [SMEM] + [VMEM] * 4,
+        (facts, sides, centre, pointwise, sums, other),
+        [SMEM] + [VMEM] * 5,
         outputs,
         [VMEM] * len(outputs),
         [pltpu.VMEM((EXTRA, 2 * inner), jnp.float32)],
@@ -1194,17 +1285,20 @@
     entry_params = jnp.stack([entry_gain, entry_shift, pointwise_bias])
     middle_params = jnp.stack([middle_gain, middle_shift])
 
-    outgoing, first_chosen, entry_local = pool(facts, signal, slots)
+    outgoing, entry_local = pool(facts, signal, slots)
     arrived = lax.all_to_all(outgoing, "seq", split_axis=0, concat_axis=0, tiled=True)
-    entry_moments = total_moments(entry_local)
-
-    kernel_low = dilated_kernel.astype(jnp.bfloat16)
-    wide_kernel = jnp.concatenate([kernel_low[tap] for tap in range(3)], axis=1)
-    pointwise_low = pointwise_kernel.astype(jnp.bfloat16)
-    back_kernel = jnp.swapaxes(kernel_low, 1, 2).reshape(3 * inner, width)
+
+    late_facts, _ = lax.optimization_barrier((facts, entry_local))
+    first_chosen = first_marks(late_facts, signal, slots)
+    wide_kernel, back_kernel, pointwise_low = prepare_weights(dilated_kernel, pointwise_kernel)
     grad_block, grad_middle, bias_part = prepare(
         facts, cotangent, pointwise_low, slots, windows
     )
+    entry_moments, prepared = total_moments(
+        entry_local,
+        [first_chosen, grad_block, grad_middle, wide_kernel, back_kernel, pointwise_low],
+    )
+    first_chosen, grad_block, grad_middle, wide_kernel, back_kernel, pointwise_low = prepared
     phases = square_phases()
     owners = [
         [phase_place(phase) == own for own in range(2 ** len(phase))] for phase in phases
@@ -1213,6 +1307,7 @@
     upper = bit_of(first_axis, first_mask) == 1
     (
         arrived,
+        first_chosen,
         grad_block,
         grad_middle,
         wide_kernel,
@@ -1225,6 +1320,7 @@
     ) = lax.optimization_barrier(
         (
             arrived,
+            first_chosen,
             grad_block,
             grad_middle,
             wide_kernel,
@@ -1284,10 +1380,12 @@
             )
             other, pointwise_part = lax.optimization_barrier((other, pointwise_part))
         middle_sums = middle_sums + other
-    padded, grad_border = middle_grad(
+    padded, grad_border, grad_centre = middle_grad(
         facts, middle_slope, middle_norm, middle_moments, middle_params, middle_sums, slots, windows
     )
+    centre_part = jnp.einsum("hrc,hrf->cf", act, grad_centre, preferred_element_type=jnp.float32)
     grad_border = from_partner(grad_border, "seq", 1)
+    grad_border, centre_part = lax.optimization_barrier((grad_border, centre_part))
     block_pieces = grad_block.reshape(pieces, HALF_WINDOW_ROWS, width)
     sent, taps, entry_part = [], None, jnp.concatenate([jnp.zeros_like(bias_part)] * 2)
     returned = []
@@ -1306,11 +1404,11 @@
     tied = lax.optimization_barrier((*sent, entry_sums))
     sent, entry_sums = list(tied[:-1]), tied[-1]
     returned = [send_back(sent[0])]
-    dilated_part = jnp.einsum("hrc,hrf->cf", act, taps, preferred_element_type=jnp.float32)
-    other, entry_sums = other_half(facts, dilated_part, pointwise_part, entry_sums)
+    side_parts = jnp.einsum("hrc,hrf->cf", act, taps, preferred_element_type=jnp.float32)
+    other, entry_sums = other_half(facts, side_parts, centre_part, pointwise_part, entry_sums)
     other = from_partner(other, first_axis, first_mask)
     entry_sums, *parts = own_half(
-        facts, dilated_part, pointwise_part, entry_sums, other, phases[0]
+        facts, side_parts, centre_part, pointwise_part, entry_sums, other, phases[0]
     )
     for held, phase in zip(phases, phases[1:] + [[]]):
         found = exchange_parts(parts[1:], held)
@@ -1318,6 +1416,11 @@
     buffer, signal_gradient, activations = parts[0], None, None
     for number, phase in reversed(list(enumerate(phases))):
         found = gather_parts(buffer, phase)
+        if number == len(phases) - 1:
+            found[1], flat_act, entry_sums, *later = lax.optimization_barrier(
+                (found[1], flat_act, entry_sums, *sent[1:])
+            )
+            returned += [send_back(block) for block in later]
         if number == 0:
             signal_gradient = unpool(
                 facts, returned[0], outgoing, first_chosen, entry_moments, entry_sums,
@@ -1326,14 +1429,10 @@
             activations = output_rows(
                 facts, flat_act, pointwise_low, arrived, entry_params, slots, windows
             )
-            tied = lax.optimization_barrier((signal_gradient, activations, *found))
-            signal_gradient, activations, found = tied[0], tied[1], tied[2:]
+            vectors = [entry_sums[0], entry_sums[1], middle_sums[0], middle_sums[1], entry_sums[2]]
+            tied = lax.optimization_barrier((signal_gradient, activations, *vectors, *found))
+            signal_gradient, activations, vectors, found = tied[0], tied[1], tied[2:7], tied[7:]
         buffer = in_order(found, owners[number])
-        if number == len(phases) - 1:
-            buffer, flat_act, entry_sums, *later = lax.optimization_barrier(
-                (buffer, flat_act, entry_sums, *sent[1:])
-            )
-            returned += [send_back(block) for block in later]
     other = from_partner(buffer, first_axis, first_mask)
     dilated_kernel_gradient, pointwise_kernel_gradient = finish_weights(facts, buffer, other)
     for slot in range(1, slots):
@@ -1344,13 +1443,13 @@
     return (
         activations,
         signal_gradient,
-        entry_sums[0],
-        entry_sums[1],
+        vectors[0],
+        vectors[1],
         dilated_kernel_gradient,
-        middle_sums[0],
-        middle_sums[1],
+        vectors[2],
+        vectors[3],
         pointwise_kernel_gradient,
-        entry_sums[2],
+        vectors[4],
     )
 
 

time: 266 us -> 258 us (0.970)
  waiting for transfers between devices: 103 us -> 87.1 us
  Pallas kernels: 73.6 us -> 81.6 us
  other arithmetic: 6.31 us -> 1.16 us
  local copies, waits for them, and re-layouts: 11.9 us -> 14.8 us
    ppermute x19, waiting for transfers between devices: 60.3 us -> 51.9 us  [from_partner(): lax.ppermute(block, axis, [(place, place ^ mask) for place in range(count)])]
    pallas_call x15 -> x17, Pallas kernels: 40.3 us -> 48.4 us  [kernel_call(): pl.pallas_call(body, in_specs=specs, out_specs=out_specs, out_shape=outpu...]
    ppermute x12, waiting for transfers between devices: 43 us -> 35.2 us  [from_flat_partner(): lax.ppermute(block, ('grp', 'seq'), [(place, place ^ mask) for place in r...]
    unnamed x42 -> x46, local copies, waits for them, and re-layouts: 5.88 us -> 12.8 us
    transpose x1 -> x0, local copies, waits for them, and re-layouts: 3.86 us -> none  [per_device(): back_kernel = jnp.swapaxes(kernel_low, 1, 2).reshape(3 * inner, width)]
    transpose x1 -> x0, other arithmetic: 3.4 us -> none  [per_device(): back_kernel = jnp.swapaxes(kernel_low, 1, 2).reshape(3 * inner, width)]
    dot_general x0 -> x1, matrix products: none -> 2.85 us  [per_device(): jnp.einsum('hrc,hrf->cf', act, grad_centre, preferred_element_type=jnp.fl...]
  transfers between devices with their start and end apart: 34 -> 34, of which waited for: 22 -> 21; matrix products, arithmetic and copies ran while one was open for 8% -> 5% of each run, Pallas kernels for 15% -> 19%
where the time goes in v4:
time: 258 us; the launch traced here: 254 us
  waiting for transfers between devices  87.1 us (34%)
  Pallas kernels  81.6 us (32%)
  starting transfers between devices  56.8 us (22%)
  local copies, waits for them, and re-layouts  14.8 us (6%)
  matrix products  11.4 us (4%)
    ppermute x19, waiting for transfers between devices, from_partner(): lax.ppermute(block, axis, [(place, place ^ mask) for place in range(count)])  51.9 us
    pallas_call x17, Pallas kernels, kernel_call(): pl.pallas_call(body, in_specs=specs, out_specs=out_specs, out_shape=outpu...  48.4 us
    ppermute x12, waiting for transfers between devices, from_flat_partner(): lax.ppermute(block, ('grp', 'seq'), [(place, place ^ mask) for place in r...  35.2 us
    ppermute x19, starting transfers between devices, from_partner(): lax.ppermute(block, axis, [(place, place ^ mask) for place in range(count)])  30.4 us
    unnamed x46, local copies, waits for them, and re-layouts  12.8 us
    ppermute x12, starting transfers between devices, from_flat_partner(): lax.ppermute(block, ('grp', 'seq'), [(place, place ^ mask) for place in r...  10.8 us
    pallas_call x2, Pallas kernels, unpool(): pl.pallas_call(functools.partial(unpool_body, slots, slot, windows), in_s...  10.4 us
    all_to_all x2, starting transfers between devices, send_back(): return lax.all_to_all(block, 'seq', split_axis=0, concat_axis=0, tiled=True)  9.98 us
  transfers between devices with their start and end apart: 34, of which 21 were waited for; matrix products, arithmetic and copies ran while one was open for 5% of the time, Pallas kernels for 19%

profile of v4, /device:TPU:17, one launch (start us, length us, event | category | flops | bytes accessed | tf_op | source)
XLA Modules:
  0.0 254.3 jit_solution(16208508993340315986)
XLA Ops:
  1.4 8.2 %pool.1 = (bf16[16,128,768]{2,1,0:T(8,128)(2,1)}, f32[3,768]{1,0:T(4,128)S(1)}) custom-call(s32[83]{0:T(128)S(1)} %concatenate.60.facts_ref, f32[16,256,768]{2,1,0:T(8,128)} %signal_ref.3), custom_call_target="tpu_custom_call" | custom-call | flops 15728640 | bytes 15728640 | tf_op jit(solution)/shard_map/pool/pallas_call | solution.py:108
  9.6 5.6 %all-to-all-start = ((bf16[16,128,768]{2,1,0:T(8,128)(2,1)}), bf16[16,128,768]{2,1,0:T(8,128)(2,1)S(1)}, u32[]{:S(2)}, u32[]{:S(2)}) async-start(bf16[16,128,768]{2,1,0:T(8,128)(2,1)} %get-tuple-element.115.pooled_ref), calls=%async_computation | async-start | bytes 6291456 | tf_op jit(solution)/shard_map/all_to_all | solution.py:1289
  27.9 12.5 %collective-permute-done.2 = f32[3,768]{1,0:T(4,128)S(1)} collective-permute-done((f32[3,768]{1,0:T(4,128)S(1)}, f32[3,768]{1,0:T(4,128)S(1)}, u32[]{:S(2)}, u32[]{:S(2)}) %collective-permute-start.2) | collective-permute-done | bytes 9248 | tf_op jit(solution)/shard_map/ppermute | solution.py:34
  42.4 2.8 %copy-done.6 = f32[2048,768]{1,0:T(8,128)S(1)} copy-done((f32[2048,768]{1,0:T(8,128)S(1)}, f32[2048,768]{1,0:T(8,128)}, u32[]{:S(2)}) %copy-start.6) | copy-done | bytes 6291480
  45.1 4.1 %prepare_cotangent.1 = (bf16[2048,768]{1,0:T(8,128)(2,1)S(1)}, f32[2048,384]{1,0:T(8,128)S(1)}, f32[1,768]{1,0:T(1,128)S(1)}) custom-call(s32[83]{0:T(128)S(1)} %concatenate.60.facts_ref, f32[2048,768]{1,0:T(8,128)S(1)} %copy-done.6, bf16[384,768]{1,0:T(8,128)(2,1)S(1)} %get-tuple-element.199.weight_ref), custom_call_target="tpu_custom_call" | custom-call | flops 1207959552 | bytes 12582912 | tf_op jit(solution)/shard_map/prepare_cotangent/pallas_call | solution.py:418
  51.0 8.5 %first_marks.1.first_ref = bf16[16,128,768]{2,1,0:T(8,128)(2,1)} custom-call(s32[83]{0:T(128)S(1)} %concatenate.60.facts_ref, f32[16,256,768]{2,1,0:T(8,128)} %signal_ref.3), custom_call_target="tpu_custom_call" | custom-call | flops 4718592 | bytes 15728640 | tf_op jit(solution)/shard_map/first_marks/pallas_call | solution.py:108
  59.5 7.8 %collective-permute-done.3 = f32[3,768]{1,0:T(4,128)S(1)} collective-permute-done((f32[3,768]{1,0:T(4,128)S(1)}, f32[3,768]{1,0:T(4,128)S(1)}, u32[]{:S(2)}, u32[]{:S(2)}) %collective-permute-start.3) | collective-permute-done | bytes 9248 | tf_op jit(solution)/shard_map/ppermute | solution.py:34
  67.7 14.8 %collective-permute-done.4 = f32[3,768]{1,0:T(4,128)S(1)} collective-permute-done((f32[3,768]{1,0:T(4,128)S(1)}, f32[3,768]{1,0:T(4,128)S(1)}, u32[]{:S(2)}, u32[]{:S(2)}) %collective-permute-start.4) | collective-permute-done | bytes 9248 | tf_op jit(solution)/shard_map/ppermute | solution.py:34
  82.5 3.7 %activate.1 = (bf16[4,512,768]{2,1,0:T(8,128)(2,1)S(1)}, bf16[4,48,768]{2,1,0:T(8,128)(2,1)S(1)}) custom-call(s32[83]{0:T(128)S(1)} %concatenate.60.facts_ref, bf16[16,128,768]{2,1,0:T(8,128)(2,1)S(1)} %all-to-all-done.arrived_ref.refs_2_, f32[3,768]{1,0:T(4,128)S(1)} %get-tuple-element.256.moments_ref.refs_4_, ...), custom_call_target="tpu_custom_call" | custom-call | flops 31457280 | bytes 6291456 | tf_op jit(solution)/shard_map/activate/pallas_call | solution.py:108
  87.8 6.6 %convolve.1 = (f32[4,512,384]{2,1,0:T(8,128)S(1)}, f32[3,384]{1,0:T(4,128)S(1)}) custom-call(s32[83]{0:T(128)S(1)} %concatenate.60.facts_ref, bf16[4,512,768]{2,1,0:T(8,128)(2,1)S(1)} %get-tuple-element.132.act_ref, bf16[768,1152]{1,0:T(8,128)(2,1)S(1)} %copy-done.12), custom_call_target="tpu_custom_call" | custom-call | flops 3623878656 | bytes 6291456 | tf_op jit(solution)/shard_map/convolve/pallas_call | solution.py:108
  104.5 3.4 %collective-permute-start.9 = (f32[3,384]{1,0:T(4,128)S(1)}, f32[3,384]{1,0:T(4,128)S(1)}, u32[]{:S(2)}, u32[]{:S(2)}) collective-permute-start(f32[3,384]{1,0:T(4,128)S(1)} %pad_maximum_fusion.9), channel_id=1, source_target_pairs={{0,2},{1,3},{2,0},{3,1},{4,6},{5,7},{6,4},{7,5},{8,10},{9,11},{10,... | collective-permute-start | bytes 13832 | tf_op jit(solution)/shard_map/ppermute | solution.py:34
  113.4 4.2 %middle_norm.1 = (bf16[4,512,384]{2,1,0:T(8,128)(2,1)S(1)}, f32[4,512,384]{2,1,0:T(8,128)S(1)}, f32[4,512,384]{2,1,0:T(8,128)S(1)}, f32[2,384]{1,0:T(2,128)S(1)}) custom-call(s32[83]{0:T(128)S(1)} %concatenate.60.facts_ref, f32[4,512,384]{2,1,0:T(8,128)S(1)} %get-tuple-element.134.out_ref, f32[4,64,384]{2,1,0:T(8,128)S(1)} %get-tuple-element.137.strip_ref, ...), custom_call_target="tpu_custom_call" | custom-call | flops 31457280 | bytes 14155776 | tf_op jit(solution)/shard_map/middle_norm/pallas_call | solution.py:108
  117.6 3.5 %collective-permute-start.11 = (f32[2,384]{1,0:T(2,128)S(1)}, f32[2,384]{1,0:T(2,128)S(1)}, u32[]{:S(2)}, u32[]{:S(2)}) collective-permute-start(f32[2,384]{1,0:T(2,128)S(1)} %get-tuple-element.156), channel_id=1, source_target_pairs={{0,8},{8,0},{16,24},{24,16},{1,9},{9,1},{17,25},{25,17},{2,10},{10... | collective-permute-start | bytes 9224 | tf_op jit(solution)/shard_map/ppermute | solution.py:34
  123.1 2.8 %fusion.6.pointwise_ref = f32[768,384]{1,0:T(8,128)} fusion(bf16[2048,768]{1,0:T(8,128)(2,1)S(1)} %copy-done.1, bf16[2048,384]{1,0:T(8,128)(2,1)S(1)} %bitcast.19), kind=kOutput, calls=%fused_computation.62 | convolution fusion | flops 1207959552 | bytes 5898240 | tf_op jit(solution)/shard_map/rd,rf->df/dot_general | solution.py:1378
  131.6 2.7 %collective-permute-done.15 = f32[2,384]{1,0:T(2,128)S(1)} collective-permute-done((f32[2,384]{1,0:T(2,128)S(1)}, f32[2,384]{1,0:T(2,128)S(1)}, u32[]{:S(2)}, u32[]{:S(2)}) %collective-permute-start.15) | collective-permute-done | bytes 3104 | tf_op jit(solution)/shard_map/ppermute | solution.py:34
  136.8 2.8 %convolution_bitcast_fusion.1.centre_ref = f32[768,384]{1,0:T(8,128)} fusion(bf16[4,512,768]{2,1,0:T(8,128)(2,1)S(1)} %get-tuple-element.132.act_ref, bf16[4,512,384]{2,1,0:T(8,128)(2,1)S(1)} %get-tuple-element.163), kind=kOutput, calls=%fused_computation.1 | convolution fusion | flops 1207959552 | bytes 5898240 | tf_op jit(solution)/shard_map/hrc,hrf->cf/dot_general | solution.py:1386
  140.4 4.8 %entry_grad.2 = (bf16[8,128,768]{2,1,0:T(8,128)(2,1)}, bf16[4,512,768]{2,1,0:T(8,128)(2,1)}, f32[2,768]{1,0:T(2,128)S(1)}) custom-call(s32[83]{0:T(128)S(1)} %concatenate.60.facts_ref, f32[4,3,592,128]{3,2,1,0:T(8,128)S(1)} %get-tuple-element.161.padded_ref, bf16[4,48,384]{2,1,0:T(8,128)(2,1)S(1)} %collective-permute-done.16.border_ref, ...), custom_call_target="tpu_custom_call" | custom-call | flops 1811939328 | bytes 11796480 | tf_op jit(solution)/shard_map/entry_grad/pallas_call | solution.py:946
  145.2 5.0 %entry_grad.3 = (bf16[8,128,768]{2,1,0:T(8,128)(2,1)}, bf16[4,512,768]{2,1,0:T(8,128)(2,1)}, f32[2,768]{1,0:T(2,128)S(1)}) custom-call(s32[83]{0:T(128)S(1)} %concatenate.60.facts_ref, f32[4,3,592,128]{3,2,1,0:T(8,128)S(1)} %get-tuple-element.161.padded_ref, ...), custom_call_target="tpu_custom_call", output_to_operand_aliasing={{1}: (10, {})} | custom-call | flops 1811939328 | bytes 11796480 | tf_op jit(solution)/shard_map/entry_grad/pallas_call | solution.py:946
  150.2 4.9 %all-to-all-start.1 = ((bf16[8,128,768]{2,1,0:T(8,128)(2,1)}), bf16[8,128,768]{2,1,0:T(8,128)(2,1)}, u32[]{:S(2)}, u32[]{:S(2)}) async-start(bf16[8,128,768]{2,1,0:T(8,128)(2,1)} %get-tuple-element.176), calls=%async_computation.1 | async-start | bytes 3145728 | tf_op jit(solution)/shard_map/all_to_all | solution.py:1394
  155.1 5.7 %convolution_bitcast_fusion.sides_ref = f32[768,768]{1,0:T(8,128)S(1)} fusion(bf16[4,512,768]{2,1,0:T(8,128)(2,1)} %copy-done.10, bf16[4,512,768]{2,1,0:T(8,128)(2,1)} %get-tuple-element.178), kind=kOutput, calls=%fused_computation | convolution fusion | flops 2415919104 | bytes 8650752 | tf_op jit(solution)/shard_map/hrc,hrf->cf/dot_general | solution.py:1407
  161.5 5.8 %collective-permute-start.17 = (bf16[776,768]{1,0:T(8,128)(2,1)S(1)}, bf16[776,768]{1,0:T(8,128)(2,1)S(1)}, u32[]{:S(2)}, u32[]{:S(2)}) collective-permute-start(bf16[776,768]{1,0:T(8,128)(2,1)S(1)} %get-tuple-element.183), channel_id=1, source_target_pairs={{0,8},{8,0},{16,24},{24,16},{1,9},{9,1},{17,25},{25,17},{2,10},{10... | collective-permute-start | bytes 3575816 | tf_op jit(solution)/shard_map/ppermute | solution.py:34
  167.3 2.5 collective-permute-done.17.other_ref
  173.4 5.9 %collective-permute-done.18.refs_0_ = bf16[200,768]{1,0:T(8,128)(2,1)S(1)} collective-permute-done((bf16[200,768]{1,0:T(8,128)(2,1)S(1)}, bf16[200,768]{1,0:T(8,128)(2,1)S(1)}, u32[]{:S(2)}, u32[]{:S(2)}) %collective-permute-start.18) | collective-permute-done | bytes 307232 | tf_op jit(solution)/shard_map/ppermute | solution.py:979
  179.3 12.9 %collective-permute-done.19.refs_1_ = bf16[200,768]{1,0:T(8,128)(2,1)S(1)} collective-permute-done((bf16[200,768]{1,0:T(8,128)(2,1)S(1)}, bf16[200,768]{1,0:T(8,128)(2,1)S(1)}, u32[]{:S(2)}, u32[]{:S(2)}) %collective-permute-start.19) | collective-permute-done | bytes 307232 | tf_op jit(solution)/shard_map/ppermute | solution.py:979
  198.4 4.6 %collective-permute-done.23.refs_2_ = bf16[56,768]{1,0:T(8,128)(2,1)S(1)} collective-permute-done((bf16[56,768]{1,0:T(8,128)(2,1)S(1)}, bf16[56,768]{1,0:T(8,128)(2,1)S(1)}, u32[]{:S(2)}, u32[]{:S(2)}) %collective-permute-start.23) | collective-permute-done | bytes 86048 | tf_op jit(solution)/shard_map/ppermute | solution.py:979
  206.9 5.1 %all-to-all-start.2 = ((bf16[8,128,768]{2,1,0:T(8,128)(2,1)}), bf16[8,128,768]{2,1,0:T(8,128)(2,1)}, u32[]{:S(2)}, u32[]{:S(2)}) async-start(bf16[8,128,768]{2,1,0:T(8,128)(2,1)} %get-tuple-element.205), calls=%async_computation.2 | async-start | bytes 3145728 | tf_op jit(solution)/shard_map/all_to_all | solution.py:1394
  217.7 9.0 %output_rows.1 = f32[2048,768]{1,0:T(8,128)} custom-call(s32[83]{0:T(128)S(1)} %concatenate.60.facts_ref, bf16[2048,384]{1,0:T(8,128)(2,1)S(1)} %bitcast.20, bf16[384,768]{1,0:T(8,128)(2,1)S(1)} %copy-done.17, bf16[16,128,768]{2,1,0:T(8,128)(2,1)S(1)} %all-to-all-done.arrived_ref.refs_2_, f32[3,768]{1,0:T(4,128)S(1)} %get-tuple-element.257.params_ref.refs_5_), custom_call_target="tpu_custom_call" | custom-call | flops 9663676416 | bytes 100663296 | tf_op jit(solution)/shard_map/output_rows/pallas_call | solution.py:836
  227.3 5.2 %unpool.2.refs_0_ = f32[16,256,768]{2,1,0:T(8,128)} custom-call(s32[83]{0:T(128)S(1)} %concatenate.60.facts_ref, bf16[8,128,768]{2,1,0:T(8,128)(2,1)} %all-to-all-done.1.returned_ref, bf16[16,128,768]{2,1,0:T(8,128)(2,1)} %get-tuple-element.115.pooled_ref, bf16[16,128,768]{2,1,0:T(8,128)(2,1)} %first_marks.1.first_ref, ...), custom_call_target="tpu_custom_call" | custom-call | flops 7864320 | bytes 11010048 | tf_op jit(solution)/shard_map/unpool/pallas_call | solution.py:368
  232.5 8.7 %collective-permute-done.28 = bf16[192,768]{1,0:T(8,128)(2,1)S(1)} collective-permute-done((bf16[192,768]{1,0:T(8,128)(2,1)S(1)}, bf16[192,768]{1,0:T(8,128)(2,1)S(1)}, u32[]{:S(2)}, u32[]{:S(2)}) %collective-permute-start.28) | collective-permute-done | bytes 294944 | tf_op jit(solution)/shard_map/ppermute | solution.py:979
  243.3 2.5 collective-permute-done.30.other_ref
  245.8 3.1 %finish_weights.1 = (f32[3,768,384]{2,1,0:T(8,128)}, f32[384,768]{1,0:T(8,128)}) custom-call(s32[83]{0:T(128)S(1)} %concatenate.60.facts_ref, bf16[768,768]{1,0:T(8,128)(2,1)S(1)} %maximum_select_fusion.mine_ref, bf16[768,768]{1,0:T(8,128)(2,1)S(1)} %collective-permute-done.30.other_ref), custom_call_target="tpu_custom_call" | custom-call | flops 589824 | bytes 7077888 | tf_op jit(solution)/shard_map/finish_weights/pallas_call | solution.py:108
  249.0 5.2 %unpool.3 = f32[16,256,768]{2,1,0:T(8,128)} custom-call(s32[83]{0:T(128)S(1)} %concatenate.60.facts_ref, bf16[8,128,768]{2,1,0:T(8,128)(2,1)} %all-to-all-done.2.returned_ref, bf16[16,128,768]{2,1,0:T(8,128)(2,1)} %get-tuple-element.115.pooled_ref, bf16[16,128,768]{2,1,0:T(8,128)(2,1)} %first_marks.1.first_ref, ...), custom_call_target="tpu_custom_call", output_to_operand_aliasing={{}: (7, {})} | custom-call | flops 7864320 | bytes 11010048 | tf_op jit(solution)/shard_map/unpool/pallas_call | solution.py:368
  (146 shorter events, 68.1 us)
Async XLA Ops:
  9.6 73.0 %all-to-all-start = ((bf16[16,128,768]{2,1,0:T(8,128)(2,1)}), bf16[16,128,768]{2,1,0:T(8,128)(2,1)S(1)}, u32[]{:S(2)}, u32[]{:S(2)}) async-start(bf16[16,128,768]{2,1,0:T(8,128)(2,1)} %get-tuple-element.115.pooled_ref), calls=%async_computation | async-start | bytes 6291456 | tf_op jit(solution)/shard_map/all_to_all | solution.py:1289
  17.3 2.9 %collective-permute-start.1 = (f32[3,768]{1,0:T(4,128)S(1)}, f32[3,768]{1,0:T(4,128)S(1)}, u32[]{:S(2)}, u32[]{:S(2)}) collective-permute-start(f32[3,768]{1,0:T(4,128)S(1)} %pad_maximum_fusion), channel_id=1, source_target_pairs={{0,16},{8,24},{16,0},{24,8},{1,17},{9,25},{17,1},{25,9},{2,18},{10... | collective-permute-start | bytes 27656 | tf_op jit(solution)/shard_map/ppermute | solution.py:34
  20.3 20.2 %collective-permute-start.2 = (f32[3,768]{1,0:T(4,128)S(1)}, f32[3,768]{1,0:T(4,128)S(1)}, u32[]{:S(2)}, u32[]{:S(2)}) collective-permute-start(f32[3,768]{1,0:T(4,128)S(1)} %pad_maximum_fusion.1), channel_id=1, source_target_pairs={{0,1},{1,0},{2,3},{3,2},{4,5},{5,4},{6,7},{7,6},{8,9},{9,8},{10,11... | collective-permute-start | bytes 27656 | tf_op jit(solution)/shard_map/ppermute | solution.py:34
  40.5 26.9 %collective-permute-start.3 = (f32[3,768]{1,0:T(4,128)S(1)}, f32[3,768]{1,0:T(4,128)S(1)}, u32[]{:S(2)}, u32[]{:S(2)}) collective-permute-start(f32[3,768]{1,0:T(4,128)S(1)} %pad_maximum_fusion.2), channel_id=1, source_target_pairs={{0,2},{1,3},{2,0},{3,1},{4,6},{5,7},{6,4},{7,5},{8,10},{9,11},{10,... | collective-permute-start | bytes 27656 | tf_op jit(solution)/shard_map/ppermute | solution.py:34
  67.4 15.0 %collective-permute-start.4 = (f32[3,768]{1,0:T(4,128)S(1)}, f32[3,768]{1,0:T(4,128)S(1)}, u32[]{:S(2)}, u32[]{:S(2)}) collective-permute-start(f32[3,768]{1,0:T(4,128)S(1)} %pad_maximum_fusion.3), channel_id=1, source_target_pairs={{0,4},{1,5},{2,6},{3,7},{4,0},{5,1},{6,2},{7,3},{8,12},{9,13},{10,... | collective-permute-start | bytes 27656 | tf_op jit(solution)/shard_map/ppermute | solution.py:34
  86.2 8.2 %collective-permute-start.5 = (bf16[4,48,768]{2,1,0:T(8,128)(2,1)S(1)}, bf16[4,48,768]{2,1,0:T(8,128)(2,1)S(1)}, u32[]{:S(2)}, u32[]{:S(2)}) collective-permute-start(bf16[4,48,768]{2,1,0:T(8,128)(2,1)S(1)} %get-tuple-element.135), channel_id=1, source_target_pairs={{0,1},{1,0},{2,3},{3,2},{4,5},{5,4},{6,7},{7,6},{8,9},{9,8},{10,11... | collective-permute-start | bytes 884744 | tf_op jit(solution)/shard_map/ppermute | solution.py:34
  95.5 2.6 %collective-permute-start.6 = (f32[3,384]{1,0:T(4,128)S(1)}, f32[3,384]{1,0:T(4,128)S(1)}, u32[]{:S(2)}, u32[]{:S(2)}) collective-permute-start(f32[3,384]{1,0:T(4,128)S(1)} %get-tuple-element.138), channel_id=1, source_target_pairs={{0,8},{8,0},{16,24},{24,16},{1,9},{9,1},{17,25},{25,17},{2,10},{10... | collective-permute-start | bytes 13832 | tf_op jit(solution)/shard_map/ppermute | solution.py:34
  98.1 3.2 %collective-permute-start.7 = (f32[3,384]{1,0:T(4,128)S(1)}, f32[3,384]{1,0:T(4,128)S(1)}, u32[]{:S(2)}, u32[]{:S(2)}) collective-permute-start(f32[3,384]{1,0:T(4,128)S(1)} %pad_maximum_fusion.7), channel_id=1, source_target_pairs={{0,16},{8,24},{16,0},{24,8},{1,17},{9,25},{17,1},{25,9},{2,18},{10... | collective-permute-start | bytes 13832 | tf_op jit(solution)/shard_map/ppermute | solution.py:34
  101.4 3.1 %collective-permute-start.8 = (f32[3,384]{1,0:T(4,128)S(1)}, f32[3,384]{1,0:T(4,128)S(1)}, u32[]{:S(2)}, u32[]{:S(2)}) collective-permute-start(f32[3,384]{1,0:T(4,128)S(1)} %pad_maximum_fusion.8), channel_id=1, source_target_pairs={{0,1},{1,0},{2,3},{3,2},{4,5},{5,4},{6,7},{7,6},{8,9},{9,8},{10,11... | collective-permute-start | bytes 13832 | tf_op jit(solution)/shard_map/ppermute | solution.py:34
  104.5 5.3 %collective-permute-start.9 = (f32[3,384]{1,0:T(4,128)S(1)}, f32[3,384]{1,0:T(4,128)S(1)}, u32[]{:S(2)}, u32[]{:S(2)}) collective-permute-start(f32[3,384]{1,0:T(4,128)S(1)} %pad_maximum_fusion.9), channel_id=1, source_target_pairs={{0,2},{1,3},{2,0},{3,1},{4,6},{5,7},{6,4},{7,5},{8,10},{9,11},{10,... | collective-permute-start | bytes 13832 | tf_op jit(solution)/shard_map/ppermute | solution.py:34
  109.9 3.4 %collective-permute-start.10 = (f32[3,384]{1,0:T(4,128)S(1)}, f32[3,384]{1,0:T(4,128)S(1)}, u32[]{:S(2)}, u32[]{:S(2)}) collective-permute-start(f32[3,384]{1,0:T(4,128)S(1)} %pad_maximum_fusion.10), channel_id=1, source_target_pairs={{0,4},{1,5},{2,6},{3,7},{4,0},{5,1},{6,2},{7,3},{8,12},{9,13},{10,... | collective-permute-start | bytes 13832 | tf_op jit(solution)/shard_map/ppermute | solution.py:34
  117.6 4.3 %collective-permute-start.11 = (f32[2,384]{1,0:T(2,128)S(1)}, f32[2,384]{1,0:T(2,128)S(1)}, u32[]{:S(2)}, u32[]{:S(2)}) collective-permute-start(f32[2,384]{1,0:T(2,128)S(1)} %get-tuple-element.156), channel_id=1, source_target_pairs={{0,8},{8,0},{16,24},{24,16},{1,9},{9,1},{17,25},{25,17},{2,10},{10... | collective-permute-start | bytes 9224 | tf_op jit(solution)/shard_map/ppermute | solution.py:34
  121.9 4.1 %collective-permute-start.12 = (f32[2,384]{1,0:T(2,128)S(1)}, f32[2,384]{1,0:T(2,128)S(1)}, u32[]{:S(2)}, u32[]{:S(2)}) collective-permute-start(f32[2,384]{1,0:T(2,128)S(1)} %add.237), channel_id=1, source_target_pairs={{0,16},{8,24},{16,0},{24,8},{1,17},{9,25},{17,1},{25,9},{2,18},{10... | collective-permute-start | bytes 9224 | tf_op jit(solution)/shard_map/ppermute | solution.py:34
  126.0 2.5 collective-permute-start.13
  130.9 3.3 %collective-permute-start.15 = (f32[2,384]{1,0:T(2,128)S(1)}, f32[2,384]{1,0:T(2,128)S(1)}, u32[]{:S(2)}, u32[]{:S(2)}) collective-permute-start(f32[2,384]{1,0:T(2,128)S(1)} %add.240), channel_id=1, source_target_pairs={{0,4},{1,5},{2,6},{3,7},{4,0},{5,1},{6,2},{7,3},{8,12},{9,13},{10,... | collective-permute-start | bytes 9224 | tf_op jit(solution)/shard_map/ppermute | solution.py:34
  136.4 4.1 %collective-permute-start.16 = (bf16[4,48,384]{2,1,0:T(8,128)(2,1)S(1)}, bf16[4,48,384]{2,1,0:T(8,128)(2,1)S(1)}, u32[]{:S(2)}, u32[]{:S(2)}) collective-permute-start(bf16[4,48,384]{2,1,0:T(8,128)(2,1)S(1)} %get-tuple-element.162), channel_id=1, source_target_pairs={{0,1},{1,0},{2,3},{3,2},{4,5},{5,4},{6,7},{7,6},{8,9},{9,8},{10,11... | collective-permute-start | bytes 442376 | tf_op jit(solution)/shard_map/ppermute | solution.py:34
  150.2 56.7 %all-to-all-start.1 = ((bf16[8,128,768]{2,1,0:T(8,128)(2,1)}), bf16[8,128,768]{2,1,0:T(8,128)(2,1)}, u32[]{:S(2)}, u32[]{:S(2)}) async-start(bf16[8,128,768]{2,1,0:T(8,128)(2,1)} %get-tuple-element.176), calls=%async_computation.1 | async-start | bytes 3145728 | tf_op jit(solution)/shard_map/all_to_all | solution.py:1394
  161.5 8.3 %collective-permute-start.17 = (bf16[776,768]{1,0:T(8,128)(2,1)S(1)}, bf16[776,768]{1,0:T(8,128)(2,1)S(1)}, u32[]{:S(2)}, u32[]{:S(2)}) collective-permute-start(bf16[776,768]{1,0:T(8,128)(2,1)S(1)} %get-tuple-element.183), channel_id=1, source_target_pairs={{0,8},{8,0},{16,24},{24,16},{1,9},{9,1},{17,25},{25,17},{2,10},{10... | collective-permute-start | bytes 3575816 | tf_op jit(solution)/shard_map/ppermute | solution.py:34
  170.7 8.6 %collective-permute-start.18 = (bf16[200,768]{1,0:T(8,128)(2,1)S(1)}, bf16[200,768]{1,0:T(8,128)(2,1)S(1)}, u32[]{:S(2)}, u32[]{:S(2)}) collective-permute-start(bf16[200,768]{1,0:T(8,128)(2,1)S(1)} %get-tuple-element.186), channel_id=1, source_target_pairs={{0,16},{1,17},{2,18},{3,19},{4,20},{5,21},{6,22},{7,23},{8,24},{9,... | collective-permute-start | bytes 921608 | tf_op jit(solution)/shard_map/ppermute | solution.py:979
  171.1 21.0 %collective-permute-start.19 = (bf16[200,768]{1,0:T(8,128)(2,1)S(1)}, bf16[200,768]{1,0:T(8,128)(2,1)S(1)}, u32[]{:S(2)}, u32[]{:S(2)}) collective-permute-start(bf16[200,768]{1,0:T(8,128)(2,1)S(1)} %get-tuple-element.187), channel_id=1, source_target_pairs={{0,1},{1,0},{2,3},{3,2},{4,5},{5,4},{6,7},{7,6},{8,9},{9,8},{10,11... | collective-permute-start | bytes 921608 | tf_op jit(solution)/shard_map/ppermute | solution.py:979
  172.3 19.9 %collective-permute-start.20 = (bf16[200,768]{1,0:T(8,128)(2,1)S(1)}, bf16[200,768]{1,0:T(8,128)(2,1)S(1)}, u32[]{:S(2)}, u32[]{:S(2)}) collective-permute-start(bf16[200,768]{1,0:T(8,128)(2,1)S(1)} %get-tuple-element.188), channel_id=1, source_target_pairs={{0,17},{1,16},{2,19},{3,18},{4,21},{5,20},{6,23},{7,22},{8,25},{9,... | collective-permute-start | bytes 921608 | tf_op jit(solution)/shard_map/ppermute | solution.py:979
  192.9 3.4 %collective-permute-start.21 = (bf16[56,768]{1,0:T(8,128)(2,1)S(1)}, bf16[56,768]{1,0:T(8,128)(2,1)S(1)}, u32[]{:S(2)}, u32[]{:S(2)}) collective-permute-start(bf16[56,768]{1,0:T(8,128)(2,1)S(1)} %get-tuple-element.191), channel_id=1, source_target_pairs={{0,2},{1,3},{2,0},{3,1},{4,6},{5,7},{6,4},{7,5},{8,10},{9,11},{10,... | collective-permute-start | bytes 258056 | tf_op jit(solution)/shard_map/ppermute | solution.py:979
  193.4 4.9 %collective-permute-start.22 = (bf16[56,768]{1,0:T(8,128)(2,1)S(1)}, bf16[56,768]{1,0:T(8,128)(2,1)S(1)}, u32[]{:S(2)}, u32[]{:S(2)}) collective-permute-start(bf16[56,768]{1,0:T(8,128)(2,1)S(1)} %get-tuple-element.192), channel_id=1, source_target_pairs={{0,4},{1,5},{2,6},{3,7},{4,0},{5,1},{6,2},{7,3},{8,12},{9,13},{10,... | collective-permute-start | bytes 258056 | tf_op jit(solution)/shard_map/ppermute | solution.py:979
  193.5 9.5 %collective-permute-start.23 = (bf16[56,768]{1,0:T(8,128)(2,1)S(1)}, bf16[56,768]{1,0:T(8,128)(2,1)S(1)}, u32[]{:S(2)}, u32[]{:S(2)}) collective-permute-start(bf16[56,768]{1,0:T(8,128)(2,1)S(1)} %get-tuple-element.193), channel_id=1, source_target_pairs={{0,6},{1,7},{2,4},{3,5},{4,2},{5,3},{6,0},{7,1},{8,14},{9,15},{10,... | collective-permute-start | bytes 258056 | tf_op jit(solution)/shard_map/ppermute | solution.py:979
  203.6 3.3 %collective-permute-start.24 = (bf16[48,768]{1,0:T(8,128)(2,1)S(1)}, bf16[48,768]{1,0:T(8,128)(2,1)S(1)}, u32[]{:S(2)}, u32[]{:S(2)}) collective-permute-start(bf16[48,768]{1,0:T(8,128)(2,1)S(1)} %get-tuple-element.194), channel_id=1, source_target_pairs={{0,2},{1,3},{2,0},{3,1},{4,6},{5,7},{6,4},{7,5},{8,10},{9,11},{10,... | collective-permute-start | bytes 221192 | tf_op jit(solution)/shard_map/ppermute | solution.py:979
  203.7 8.3 %collective-permute-start.26 = (bf16[48,768]{1,0:T(8,128)(2,1)S(1)}, bf16[48,768]{1,0:T(8,128)(2,1)S(1)}, u32[]{:S(2)}, u32[]{:S(2)}) collective-permute-start(bf16[48,768]{1,0:T(8,128)(2,1)S(1)} %get-tuple-element.194), channel_id=1, source_target_pairs={{0,4},{1,5},{2,6},{3,7},{4,0},{5,1},{6,2},{7,3},{8,12},{9,13},{10,... | collective-permute-start | bytes 221192 | tf_op jit(solution)/shard_map/ppermute | solution.py:979
  204.9 7.6 %collective-permute-start.25 = (bf16[48,768]{1,0:T(8,128)(2,1)S(1)}, bf16[48,768]{1,0:T(8,128)(2,1)S(1)}, u32[]{:S(2)}, u32[]{:S(2)}) collective-permute-start(bf16[48,768]{1,0:T(8,128)(2,1)S(1)} %get-tuple-element.194), channel_id=1, source_target_pairs={{0,6},{1,7},{2,4},{3,5},{4,2},{5,3},{6,0},{7,1},{8,14},{9,15},{10,... | collective-permute-start | bytes 221192 | tf_op jit(solution)/shard_map/ppermute | solution.py:979
  206.9 42.0 %all-to-all-start.2 = ((bf16[8,128,768]{2,1,0:T(8,128)(2,1)}), bf16[8,128,768]{2,1,0:T(8,128)(2,1)}, u32[]{:S(2)}, u32[]{:S(2)}) async-start(bf16[8,128,768]{2,1,0:T(8,128)(2,1)} %get-tuple-element.205), calls=%async_computation.2 | async-start | bytes 3145728 | tf_op jit(solution)/shard_map/all_to_all | solution.py:1394
  212.5 20.0 %collective-permute-start.27 = (bf16[192,768]{1,0:T(8,128)(2,1)S(1)}, bf16[192,768]{1,0:T(8,128)(2,1)S(1)}, u32[]{:S(2)}, u32[]{:S(2)}) collective-permute-start(bf16[192,768]{1,0:T(8,128)(2,1)S(1)} %maximum_select_fusion.3), channel_id=1, source_target_pairs={{0,16},{1,17},{2,18},{3,19},{4,20},{5,21},{6,22},{7,23},{8,24},{9,... | collective-permute-start | bytes 884744 | tf_op jit(solution)/shard_map/ppermute | solution.py:979
  213.5 27.6 %collective-permute-start.28 = (bf16[192,768]{1,0:T(8,128)(2,1)S(1)}, bf16[192,768]{1,0:T(8,128)(2,1)S(1)}, u32[]{:S(2)}, u32[]{:S(2)}) collective-permute-start(bf16[192,768]{1,0:T(8,128)(2,1)S(1)} %maximum_select_fusion.3), channel_id=1, source_target_pairs={{0,1},{1,0},{2,3},{3,2},{4,5},{5,4},{6,7},{7,6},{8,9},{9,8},{10,11... | collective-permute-start | bytes 884744 | tf_op jit(solution)/shard_map/ppermute | solution.py:979
  214.3 26.8 %collective-permute-start.29 = (bf16[192,768]{1,0:T(8,128)(2,1)S(1)}, bf16[192,768]{1,0:T(8,128)(2,1)S(1)}, u32[]{:S(2)}, u32[]{:S(2)}) collective-permute-start(bf16[192,768]{1,0:T(8,128)(2,1)S(1)} %maximum_select_fusion.3), channel_id=1, source_target_pairs={{0,17},{1,16},{2,19},{3,18},{4,21},{5,20},{6,23},{7,22},{8,25},{9,... | collective-permute-start | bytes 884744 | tf_op jit(solution)/shard_map/ppermute | solution.py:979
  241.8 4.0 %collective-permute-start.30 = (bf16[768,768]{1,0:T(8,128)(2,1)S(1)}, bf16[768,768]{1,0:T(8,128)(2,1)S(1)}, u32[]{:S(2)}, u32[]{:S(2)}) collective-permute-start(bf16[768,768]{1,0:T(8,128)(2,1)S(1)} %maximum_select_fusion.mine_ref), channel_id=1, source_target_pairs={{0,8},{8,0},{16,24},{24,16},{1,9},{9,1},{17,25},{25,17},{2,10},{10... | collective-permute-start | bytes 3538952 | tf_op jit(solution)/shard_map/ppermute | solution.py:34
  (25 other events, 201.4 us)

commit v5 on v4

--- a/solution.py
+++ b/solution.py
@@ -173,42 +173,77 @@
 
 
 def pool_body(
-    slots, facts_ref, signal_ref, pooled_ref, moments_ref, held, low, blocks, arrivals, departures
+    slots, order_ref, lengths_ref, signal_ref, pooled_ref, moments_ref,
+    held, low, blocks, order, lengths, places, arrivals, departures, facts_copies,
 ):
     windows, columns = held.shape[:2]
     rows = low.shape[1]
-    facts = Facts(facts_ref, windows, slots)
-
-    def departure(place):
-        return pltpu.make_async_copy(low.at[place], pooled_ref.at[place], departures.at[place])
-
-    begin_bins(facts, signal_ref, held, arrivals)
+    grp, seq = lax.axis_index("grp"), lax.axis_index("seq")
+    upper = (2 * seq) // (windows // slots)
+
+    def arrival(window, column):
+        return pltpu.make_async_copy(
+            signal_ref.at[window, :, pl.ds(column * LANES, LANES)],
+            held.at[window, column],
+            arrivals.at[window, column],
+        )
+
+    def departure(window):
+        return pltpu.make_async_copy(
+            low.at[window], pooled_ref.at[places[window]], departures.at[window]
+        )
+
+    fetches = [
+        pltpu.make_async_copy(order_ref, order, facts_copies.at[0]),
+        pltpu.make_async_copy(lengths_ref, lengths, facts_copies.at[1]),
+    ]
+    for fetch in fetches:
+        fetch.start()
+
+    def begin(window, carry):
+        for column in range(columns):
+            arrival(window, column).start()
+        return carry
+
+    lax.fori_loop(0, windows, begin, 0)
     moments_ref[...] = jnp.zeros_like(moments_ref)
-
-    def work(place, carry):
-        count = facts.slot_count(place, rows)
+    for fetch in fetches:
+        fetch.wait()
+
+    def note(place, carry):
+        target = jnp.bitwise_xor(place // slots, upper)
+        places[order[0, target * slots + place % slots]] = place
+        return carry
+
+    lax.fori_loop(0, windows, note, 0)
+
+    def count_of(window):
+        return jnp.clip(lengths[grp * windows + window] - seq * rows, 0, rows)
+
+    def work(window, carry):
+        count = count_of(window)
         inside = lax.broadcasted_iota(jnp.int32, (rows, LANES), 0) < count
-        for lanes, first_bin, second_bin in bins_of(
-            facts, signal_ref, held, arrivals, place, rows
-        ):
+        for column in range(columns):
+            arrival(window, column).wait()
+        for column, lanes in enumerate(column_slices(columns * LANES)):
+            first_bin = held[window, column, pl.ds(0, rows, stride=2), :]
+            second_bin = held[window, column, pl.ds(1, rows, stride=2), :]
             pooled = jnp.where(inside, jnp.maximum(first_bin, second_bin), 0.0)
             pooled = pooled.astype(jnp.bfloat16)
-            low[place, :, lanes] = pooled
+            low[window, :, lanes] = pooled
             found = block_moments(pooled.astype(jnp.float32), inside, count.astype(jnp.float32))
-            blocks[place, 0:1, lanes] = found[0]
-            blocks[place, 1:2, lanes] = found[1]
-        departure(place).start()
+            blocks[window, 0:1, lanes] = found[0]
+            blocks[window, 1:2, lanes] = found[1]
+        departure(window).start()
         return carry
 
     lax.fori_loop(0, windows, work, 0)
 
-    def join_blocks(place, carry):
-        count = jnp.broadcast_to(
-            facts.slot_count(place, rows).astype(jnp.float32), (1, columns * LANES)
-        )
+    def join_blocks(window, carry):
+        count = jnp.broadcast_to(count_of(window).astype(jnp.float32), (1, columns * LANES))
         held_moments = (moments_ref[0:1], moments_ref[1:2], moments_ref[2:3])
         moments_ref[0:1], moments_ref[1:2], moments_ref[2:3] = merged(
-            held_moments, (blocks[place, 0:1], blocks[place, 1:2], count)
+            held_moments, (blocks[window, 0:1], blocks[window, 1:2], count)
         )
         return carry
 
@@ -216,23 +251,27 @@
     finish_copies(departure, windows)
 
 
-def pool(facts, signal, slots):
+def pool(order, lengths, signal, slots):
     windows, segment, width = signal.shape
     rows, columns = segment // 2, width // LANES
     block = (windows, rows, width)
     return kernel_call(
         functools.partial(pool_body, slots),
         "pool",
-        (facts, in_hbm(signal)),
-        [SMEM, HBM],
+        (in_hbm(order), in_hbm(lengths), in_hbm(signal)),
+        [HBM, HBM, HBM],
         [pltpu.HBM(block, jnp.bfloat16), shape((3, width), jnp.float32)],
         [HBM, VMEM],
         [
             pltpu.VMEM((windows, columns, segment, LANES), jnp.float32),
             pltpu.VMEM(block, jnp.bfloat16),
             pltpu.VMEM((windows, 2, width), jnp.float32),
+            pltpu.SMEM(order.shape, jnp.int32),
+            pltpu.SMEM(lengths.shape, jnp.int32),
+            pltpu.SMEM((windows,), jnp.int32),
             pltpu.SemaphoreType.DMA((windows, columns)),
             pltpu.SemaphoreType.DMA((windows,)),
+            pltpu.SemaphoreType.DMA((2,)),
         ],
         flops=10 * windows * rows * width,
         bytes_moved=windows * rows * width * 10,
@@ -847,58 +886,63 @@
         out_shape=shape((blocks * rows, width), jnp.float32),
         compiler_params=pltpu.CompilerParams(vmem_limit_bytes=16 << 20),
         cost_estimate=pl.CostEstimate(
-            flops=2 * act.size * width * 8, bytes_accessed=8 * arrived.size * 8, transcendentals=0
+            flops=2 * act.size * width * 7, bytes_accessed=8 * arrived.size * 7, transcendentals=0
         ),
         name="output_rows",
     )(facts, act, weight, arrived, params)
 
 
-def entry_grad_body(
-    slots, windows, slot, facts_ref, padded_ref, border_ref, weight_ref, *refs
-):
-    slope_refs, (arrived_ref, block_ref, moments_ref, params_ref) = refs[:2], refs[2:6]
-    sent_ref, kept_ref, sums_ref, wide, packed, taps_ref, departures, kept = refs[-8:]
+def entry_grad_body(slots, windows, facts_ref, padded_ref, border_ref, weight_ref, *refs):
+    pieces = 2 * slots
+    slope_refs, refs = refs[:pieces], refs[pieces:]
+    (arrived_ref, block_ref, moments_ref, params_ref, bias_ref), refs = refs[:5], refs[5:]
+    sent_refs, (kept_ref, sums_ref, wide, packed, taps_ref, departures, kept) = (
+        refs[:slots],
+        refs[slots:],
+    )
     facts = Facts(facts_ref, windows, slots)
-    sources, rows, width = packed.shape
+    _, sources, rows, width = packed.shape
     tiles = padded_ref.shape[1]
     per_half = HALF_WINDOW_ROWS // rows
     centre, scale, slope, _ = norm_terms(moments_ref, params_ref, facts.row_count())
     skip = BORDER - DILATION_STEP
     sums_ref[...] = jnp.zeros_like(sums_ref)
 
-    def departure(source):
+    def departure(slot, source):
         return pltpu.make_async_copy(
-            packed.at[source], sent_ref.at[source], departures.at[source]
+            packed.at[slot, source], sent_refs[slot].at[source], departures.at[slot, source]
         )
 
-    def keeping(half):
+    def keeping(piece):
         return pltpu.make_async_copy(
-            taps_ref.at[half, :, pl.ds(0, kept_ref.shape[2])],
-            kept_ref.at[slot * 2 + half],
-            kept.at[half],
+            taps_ref.at[piece, :, pl.ds(0, kept_ref.shape[2])], kept_ref.at[piece], kept.at[piece]
         )
 
-    for half in range(2):
-        piece = slot * 2 + half
-        other = slot * 2 + 1 - half
+    def lay_taps(piece):
+        half, turn = piece % 2, piece % 2
         for tile, lanes in enumerate(column_slices(tiles * LANES)):
-            border = border_ref[other, :, lanes].astype(jnp.float32)
-            wide[tile] = padded_ref[piece, tile]
+            border = border_ref[piece + 1 - 2 * half, :, lanes].astype(jnp.float32)
+            wide[turn, tile] = padded_ref[piece, tile]
             if half == 0:
                 end = PAD + HALF_WINDOW_ROWS
-                wide[tile, end : end + DILATION_STEP] = border[0:DILATION_STEP]
+                wide[turn, tile, end : end + DILATION_STEP] = border[0:DILATION_STEP]
             else:
-                wide[tile, PAD - DILATION_STEP : PAD] = border[skip:BORDER]
+                wide[turn, tile, PAD - DILATION_STEP : PAD] = border[skip:BORDER]
             for number, tap in enumerate((0, 2, 1)):
                 start = PAD - (tap - 1) * DILATION_STEP
                 first = (number * tiles + tile) * LANES
-                taps_ref[half, :, first : first + LANES] = wide[
-                    tile, start : start + HALF_WINDOW_ROWS
+                taps_ref[piece, :, first : first + LANES] = wide[
+                    turn, tile, start : start + HALF_WINDOW_ROWS
                 ].astype(jnp.bfloat16)
-        keeping(half).start()
+
+    lay_taps(0)
+    for piece in range(pieces):
+        slot, half = piece // 2, piece % 2
+        if piece + 1 < pieces:
+            lay_taps(piece + 1)
         for column in range(0, width, 2 * LANES):
             grad = jnp.dot(
-                taps_ref[half],
+                taps_ref[piece],
                 weight_ref[:, column : column + 2 * LANES],
                 preferred_element_type=jnp.float32,
             )
@@ -908,7 +952,7 @@
                 for start in (column, column + LANES):
                     lanes = slice(start, start + LANES)
                     pre = grad[here, start - column : start - column + LANES]
-                    pre = pre * slope_refs[half][here, lanes]
+                    pre = pre * slope_refs[piece][here, lanes]
                     values = arrived_ref[source * slots + slot, :, lanes].astype(jnp.float32)
                     sums_ref[0:1, lanes] = sums_ref[0:1, lanes] + jnp.sum(
                         pre * values, axis=0, keepdims=True
@@ -917,57 +961,51 @@
                         pre, axis=0, keepdims=True
                     )
                     block = block_ref[piece, here, lanes].astype(jnp.float32)
-                    packed[source, :, lanes] = (pre * slope[:, lanes] + block).astype(
+                    packed[slot, source, :, lanes] = (pre * slope[:, lanes] + block).astype(
                         jnp.bfloat16
                     )
         for part in range(per_half):
-            departure(half * per_half + part).start()
+            departure(slot, half * per_half + part).start()
+        keeping(piece).start()
     sums_ref[0:1] = (sums_ref[0:1] - centre * sums_ref[1:2]) * scale
-    for half in range(2):
-        keeping(half).wait()
-    for source in range(sources):
-        departure(source).wait()
+    sums_ref[2:3] = bias_ref[...]
+    for piece in range(pieces):
+        keeping(piece).wait()
+    for slot in range(slots):
+        for source in range(sources):
+            departure(slot, source).wait()
 
 
 def entry_grad(
-    facts, padded, border, weight, slopes, arrived, block, moments, params, taps, slots, windows,
-    slot,
+    facts, padded, border, weight, slopes, arrived, block, moments, params, bias, slots, windows
 ):
     blocks, rows, width = arrived.shape
     inner, sources = border.shape[2], blocks // slots
-    inputs = [facts, padded, border, weight, *slopes, arrived, block, moments, params]
-    specs = [SMEM] + [VMEM] * 9
-    aliases = {}
-    if taps is not None:
-        aliases = {len(inputs): 1}
-        inputs.append(in_hbm(taps))
-        specs.append(HBM)
+    pieces = 2 * slots
+    inputs = [facts, padded, border, weight, *slopes, arrived, block, moments, params, bias]
     taps_shape = (HALF_WINDOW_ROWS, 3 * inner)
-    return pl.pallas_call(
-        functools.partial(entry_grad_body, slots, windows, slot),
-        in_specs=specs,
-        out_specs=[HBM, HBM, VMEM],
-        out_shape=[
-            pltpu.HBM((sources, rows, width), jnp.bfloat16),
-            pltpu.HBM((2 * slots, HALF_WINDOW_ROWS, 2 * inner), jnp.bfloat16),
-            shape((2, width), jnp.float32),
+    return kernel_call(
+        functools.partial(entry_grad_body, slots, windows),
+        "entry_grad",
+        inputs,
+        [SMEM] + [VMEM] * (len(inputs) - 1),
+        [
+            *[pltpu.HBM((sources, rows, width), jnp.bfloat16)] * slots,
+            pltpu.HBM((pieces, HALF_WINDOW_ROWS, 2 * inner), jnp.bfloat16),
+            shape((3, width), jnp.float32),
         ],
-        input_output_aliases=aliases,
-        scratch_shapes=[
-            pltpu.VMEM((inner // LANES, PADDED_ROWS, LANES), jnp.float32),
-            pltpu.VMEM((sources, rows, width), jnp.bfloat16),
-            pltpu.VMEM((2, *taps_shape), jnp.bfloat16),
-            pltpu.SemaphoreType.DMA((sources,)),
-            pltpu.SemaphoreType.DMA((2,)),
+        [HBM] * (slots + 1) + [VMEM],
+        [
+            pltpu.VMEM((2, inner // LANES, PADDED_ROWS, LANES), jnp.float32),
+            pltpu.VMEM((slots, sources, rows, width), jnp.bfloat16),
+            pltpu.VMEM((pieces, *taps_shape), jnp.bfloat16),
+            pltpu.SemaphoreType.DMA((slots, sources)),
+            pltpu.SemaphoreType.DMA((pieces,)),
         ],
-        compiler_params=pltpu.CompilerParams(vmem_limit_bytes=10 << 20),
-        cost_estimate=pl.CostEstimate(
-            flops=2 * 2 * HALF_WINDOW_ROWS * 3 * inner * width,
-            bytes_accessed=2 * HALF_WINDOW_ROWS * (width * 10 + inner * 10),
-            transcendentals=0,
-        ),
-        name="entry_grad",
-    )(*inputs)
+        flops=2 * pieces * HALF_WINDOW_ROWS * 3 * inner * width,
+        bytes_moved=pieces * HALF_WINDOW_ROWS * (width * 10 + inner * 10),
+        grant=16 << 20,
+    )
 
 
 def flat_mask(bits):
@@ -1225,40 +1263,64 @@
     return result
 
 
-def finish_body(facts_ref, mine_ref, other_ref, dilated_ref, pointwise_ref):
+def finish_body(own, facts_ref, half_ref, *refs):
+    dilated_ref, pointwise_ref, held, turned, copies = refs[-5:]
     inner = dilated_ref.shape[2]
 
-    def write(low_ref, high_ref):
-        dilated_ref[0] = low_ref[:, :inner].astype(jnp.float32)
-        dilated_ref[1] = low_ref[:, inner:].astype(jnp.float32)
-        dilated_ref[2] = high_ref[:, :inner].astype(jnp.float32)
-        pointwise_ref[...] = high_ref[:, inner:].astype(jnp.float32).T
+    def write(places):
+        for number, place in enumerate(places):
+            held[number] = half_ref[:, number * inner : (number + 1) * inner].astype(jnp.float32)
+            pltpu.make_async_copy(
+                held.at[number], dilated_ref.at[place], copies.at[number]
+            ).start()
+        if len(places) == 1:
+            turned[...] = half_ref[:, inner:].astype(jnp.float32).T
+            pltpu.make_async_copy(turned, pointwise_ref, copies.at[1]).start()
+            pltpu.make_async_copy(turned, pointwise_ref, copies.at[1]).wait()
+        for number, place in enumerate(places):
+            pltpu.make_async_copy(
+                held.at[number], dilated_ref.at[place], copies.at[number]
+            ).wait()
 
     upper = facts_ref[0] % 2
 
-    @pl.when(upper == 0)
+    @pl.when(upper == 1 - own)
     def _():
-        write(mine_ref, other_ref)
-
-    @pl.when(upper == 1)
+        write((0, 1))
+
+    @pl.when(upper == own)
     def _():
-        write(other_ref, mine_ref)
-
-
-def finish_weights(facts, mine, other):
-    width, both = mine.shape
+        write((2,))
+
+
+def finish_weights(facts, half, own, begun):
+    width, both = half.shape
     inner = both // 2
-    return kernel_call(
-        finish_body,
-        "finish_weights",
-        (facts, mine, other),
-        [SMEM, VMEM, VMEM],
-        [shape((3, width, inner), jnp.float32), shape((inner, width), jnp.float32)],
-        [VMEM, VMEM],
-        flops=width * both,
-        bytes_moved=12 * width * both,
-        grant=16 << 20,
-    )
+    inputs, specs, aliases = [facts, half], [SMEM, VMEM], {}
+    if begun is not None:
+        aliases = {2: 0, 3: 1}
+        inputs += [in_hbm(array) for array in begun]
+        specs += [HBM, HBM]
+    return pl.pallas_call(
+        functools.partial(finish_body, own),
+        in_specs=specs,
+        out_specs=[HBM, HBM],
+        out_shape=[
+            pltpu.HBM((3, width, inner), jnp.float32),
+            pltpu.HBM((inner, width), jnp.float32),
+        ],
+        input_output_aliases=aliases,
+        scratch_shapes=[
+            pltpu.VMEM((2, width, inner), jnp.float32),
+            pltpu.VMEM((inner, width), jnp.float32),
+            pltpu.SemaphoreType.DMA((2,)),
+        ],
+        compiler_params=pltpu.CompilerParams(vmem_limit_bytes=12 << 20),
+        cost_estimate=pl.CostEstimate(
+            flops=width * both, bytes_accessed=6 * width * both, transcendentals=0
+        ),
+        name="finish_weights",
+    )(*inputs)
 
 
 def per_device(
@@ -1285,7 +1347,7 @@
     entry_params = jnp.stack([entry_gain, entry_shift, pointwise_bias])
     middle_params = jnp.stack([middle_gain, middle_shift])
 
-    outgoing, entry_local = pool(facts, signal, slots)
+    outgoing, entry_local = pool(assignment, lengths, signal, slots)
     arrived = lax.all_to_all(outgoing, "seq", split_axis=0, concat_axis=0, tiled=True)
 
     late_facts, _ = lax.optimization_barrier((facts, entry_local))
@@ -1387,20 +1449,13 @@
     grad_border = from_partner(grad_border, "seq", 1)
     grad_border, centre_part = lax.optimization_barrier((grad_border, centre_part))
     block_pieces = grad_block.reshape(pieces, HALF_WINDOW_ROWS, width)
-    sent, taps, entry_part = [], None, jnp.concatenate([jnp.zeros_like(bias_part)] * 2)
-    returned = []
-
     def send_back(block):
         return lax.all_to_all(block, "seq", split_axis=0, concat_axis=0, tiled=True)
 
-    for slot in range(slots):
-        block, taps, part = entry_grad(
-            facts, padded, grad_border, back_kernel, slopes[2 * slot : 2 * slot + 2],
-            arrived, block_pieces, entry_moments, entry_params, taps, slots, windows, slot,
-        )
-        sent.append(block)
-        entry_part = entry_part + part
-    entry_sums = jnp.concatenate([entry_part, bias_part])
+    *sent, taps, entry_sums = entry_grad(
+        facts, padded, grad_border, back_kernel, slopes, arrived, block_pieces, entry_moments,
+        entry_params, bias_part, slots, windows,
+    )
     tied = lax.optimization_barrier((*sent, entry_sums))
     sent, entry_sums = list(tied[:-1]), tied[-1]
     returned = [send_back(sent[0])]
@@ -1429,12 +1484,15 @@
             activations = output_rows(
                 facts, flat_act, pointwise_low, arrived, entry_params, slots, windows
             )
+            signal_gradient, middle_sums = lax.optimization_barrier((signal_gradient, middle_sums))
             vectors = [entry_sums[0], entry_sums[1], middle_sums[0], middle_sums[1], entry_sums[2]]
             tied = lax.optimization_barrier((signal_gradient, activations, *vectors, *found))
             signal_gradient, activations, vectors, found = tied[0], tied[1], tied[2:7], tied[7:]
         buffer = in_order(found, owners[number])
     other = from_partner(buffer, first_axis, first_mask)
-    dilated_kernel_gradient, pointwise_kernel_gradient = finish_weights(facts, buffer, other)
+    begun = finish_weights(facts, buffer, 1, None)
+    other, *begun = lax.optimization_barrier((other, *begun))
+    dilated_kernel_gradient, pointwise_kernel_gradient = finish_weights(facts, other, 0, begun)
     for slot in range(1, slots):
         signal_gradient = unpool(
             facts, returned[slot], outgoing, first_chosen, entry_moments, entry_sums,

time: 258 us -> 253 us (0.981)
    pallas_call x2, Pallas kernels: 9.71 us -> 4.28 us  [finish_weights(): pl.pallas_call(functools.partial(finish_body, own), in_specs=specs, out_s...]
    pallas_call x17, Pallas kernels: 48.4 us -> 52.4 us  [kernel_call(): pl.pallas_call(body, in_specs=specs, out_specs=out_specs, out_shape=outpu...]
    unnamed x46 -> x50, local copies, waits for them, and re-layouts: 12.8 us -> 12.8 us
  transfers between devices with their start and end apart: 34 -> 34, of which waited for: 21 -> 22; matrix products, arithmetic and copies ran while one was open for 5% -> 6% of each run, Pallas kernels for 19% -> 20%
where the time goes in v5:
time: 253 us; the launch traced here: 249 us
  waiting for transfers between devices  84.7 us (33%)
  Pallas kernels  80.2 us (32%)
  starting transfers between devices  56.3 us (22%)
  local copies, waits for them, and re-layouts  14.1 us (6%)
  matrix products  11.4 us (5%)
    pallas_call x17, Pallas kernels, kernel_call(): pl.pallas_call(body, in_specs=specs, out_specs=out_specs, out_shape=outpu...  52.4 us
    ppermute x19, waiting for transfers between devices, from_partner(): lax.ppermute(block, axis, [(place, place ^ mask) for place in range(count)])  49.5 us
    ppermute x12, waiting for transfers between devices, from_flat_partner(): lax.ppermute(block, ('grp', 'seq'), [(place, place ^ mask) for place in r...  35.1 us
    ppermute x19, starting transfers between devices, from_partner(): lax.ppermute(block, axis, [(place, place ^ mask) for place in range(count)])  30.4 us
    unnamed x50, local copies, waits for them, and re-layouts  12.8 us
    ppermute x12, starting transfers between devices, from_flat_partner(): lax.ppermute(block, ('grp', 'seq'), [(place, place ^ mask) for place in r...  10.8 us
    pallas_call x2, Pallas kernels, unpool(): pl.pallas_call(functools.partial(unpool_body, slots, slot, windows), in_s...  10.4 us
    all_to_all x2, starting transfers between devices, send_back(): return lax.all_to_all(block, 'seq', split_axis=0, concat_axis=0, tiled=True)  9.44 us
  transfers between devices with their start and end apart: 34, of which 22 were waited for; matrix products, arithmetic and copies ran while one was open for 6% of the time, Pallas kernels for 20%

profile of v5, /device:TPU:17, one launch (start us, length us, event | category | flops | bytes accessed | tf_op | source)
XLA Modules:
  0.0 249.3 jit_solution(4702637675181857153)
XLA Ops:
  0.6 7.5 %pool.1 = (bf16[16,128,768]{2,1,0:T(8,128)(2,1)}, f32[3,768]{1,0:T(4,128)S(1)}) custom-call(s32[1,16]{1,0:T(1,128)} %order_ref.1, s32[64]{0:T(128)} %lengths_ref.1, f32[16,256,768]{2,1,0:T(8,128)} %signal_ref.3), custom_call_target="tpu_custom_call" | custom-call | flops 15728640 | bytes 15728640 | tf_op jit(solution)/shard_map/pool/pallas_call | solution.py:108
  8.2 5.6 %all-to-all-start = ((bf16[16,128,768]{2,1,0:T(8,128)(2,1)}), bf16[16,128,768]{2,1,0:T(8,128)(2,1)S(1)}, u32[]{:S(2)}, u32[]{:S(2)}) async-start(bf16[16,128,768]{2,1,0:T(8,128)(2,1)} %get-tuple-element.120.pooled_ref), calls=%async_computation | async-start | bytes 6291456 | tf_op jit(solution)/shard_map/all_to_all | solution.py:1351
  26.6 12.4 %collective-permute-done.2 = f32[3,768]{1,0:T(4,128)S(1)} collective-permute-done((f32[3,768]{1,0:T(4,128)S(1)}, f32[3,768]{1,0:T(4,128)S(1)}, u32[]{:S(2)}, u32[]{:S(2)}) %collective-permute-start.2) | collective-permute-done | bytes 9248 | tf_op jit(solution)/shard_map/ppermute | solution.py:34
  41.0 2.8 %copy-done.4 = f32[2048,768]{1,0:T(8,128)S(1)} copy-done((f32[2048,768]{1,0:T(8,128)S(1)}, f32[2048,768]{1,0:T(8,128)}, u32[]{:S(2)}) %copy-start.4) | copy-done | bytes 6291480
  43.8 4.1 %prepare_cotangent.1 = (bf16[2048,768]{1,0:T(8,128)(2,1)S(1)}, f32[2048,384]{1,0:T(8,128)S(1)}, f32[1,768]{1,0:T(1,128)S(1)}) custom-call(s32[83]{0:T(128)S(1)} %concatenate.61.facts_ref, f32[2048,768]{1,0:T(8,128)S(1)} %copy-done.4, bf16[384,768]{1,0:T(8,128)(2,1)S(1)} %get-tuple-element.203.weight_ref), custom_call_target="tpu_custom_call" | custom-call | flops 1207959552 | bytes 12582912 | tf_op jit(solution)/shard_map/prepare_cotangent/pallas_call | solution.py:457
  49.6 8.5 %first_marks.1.first_ref = bf16[16,128,768]{2,1,0:T(8,128)(2,1)} custom-call(s32[83]{0:T(128)S(1)} %concatenate.61.facts_ref, f32[16,256,768]{2,1,0:T(8,128)} %signal_ref.3), custom_call_target="tpu_custom_call" | custom-call | flops 4718592 | bytes 15728640 | tf_op jit(solution)/shard_map/first_marks/pallas_call | solution.py:108
  58.2 7.8 %collective-permute-done.3 = f32[3,768]{1,0:T(4,128)S(1)} collective-permute-done((f32[3,768]{1,0:T(4,128)S(1)}, f32[3,768]{1,0:T(4,128)S(1)}, u32[]{:S(2)}, u32[]{:S(2)}) %collective-permute-start.3) | collective-permute-done | bytes 9248 | tf_op jit(solution)/shard_map/ppermute | solution.py:34
  66.3 14.8 %collective-permute-done.4 = f32[3,768]{1,0:T(4,128)S(1)} collective-permute-done((f32[3,768]{1,0:T(4,128)S(1)}, f32[3,768]{1,0:T(4,128)S(1)}, u32[]{:S(2)}, u32[]{:S(2)}) %collective-permute-start.4) | collective-permute-done | bytes 9248 | tf_op jit(solution)/shard_map/ppermute | solution.py:34
  81.1 3.7 %activate.1 = (bf16[4,512,768]{2,1,0:T(8,128)(2,1)S(1)}, bf16[4,48,768]{2,1,0:T(8,128)(2,1)S(1)}) custom-call(s32[83]{0:T(128)S(1)} %concatenate.61.facts_ref, bf16[16,128,768]{2,1,0:T(8,128)(2,1)S(1)} %all-to-all-done.arrived_ref.refs_4_, f32[3,768]{1,0:T(4,128)S(1)} %get-tuple-element.266.moments_ref.refs_6_, ...), custom_call_target="tpu_custom_call" | custom-call | flops 31457280 | bytes 6291456 | tf_op jit(solution)/shard_map/activate/pallas_call | solution.py:108
  86.4 6.6 %convolve.1 = (f32[4,512,384]{2,1,0:T(8,128)S(1)}, f32[3,384]{1,0:T(4,128)S(1)}) custom-call(s32[83]{0:T(128)S(1)} %concatenate.61.facts_ref, bf16[4,512,768]{2,1,0:T(8,128)(2,1)S(1)} %get-tuple-element.137.act_ref, bf16[768,1152]{1,0:T(8,128)(2,1)S(1)} %copy-done.10), custom_call_target="tpu_custom_call" | custom-call | flops 3623878656 | bytes 6291456 | tf_op jit(solution)/shard_map/convolve/pallas_call | solution.py:108
  103.1 3.4 %collective-permute-start.9 = (f32[3,384]{1,0:T(4,128)S(1)}, f32[3,384]{1,0:T(4,128)S(1)}, u32[]{:S(2)}, u32[]{:S(2)}) collective-permute-start(f32[3,384]{1,0:T(4,128)S(1)} %pad_maximum_fusion.8), channel_id=1, source_target_pairs={{0,2},{1,3},{2,0},{3,1},{4,6},{5,7},{6,4},{7,5},{8,10},{9,11},{10,... | collective-permute-start | bytes 13832 | tf_op jit(solution)/shard_map/ppermute | solution.py:34
  112.0 4.2 %middle_norm.1 = (bf16[4,512,384]{2,1,0:T(8,128)(2,1)S(1)}, f32[4,512,384]{2,1,0:T(8,128)S(1)}, f32[4,512,384]{2,1,0:T(8,128)S(1)}, f32[2,384]{1,0:T(2,128)S(1)}) custom-call(s32[83]{0:T(128)S(1)} %concatenate.61.facts_ref, f32[4,512,384]{2,1,0:T(8,128)S(1)} %get-tuple-element.139.out_ref, f32[4,64,384]{2,1,0:T(8,128)S(1)} %get-tuple-element.142.strip_ref, ...), custom_call_target="tpu_custom_call" | custom-call | flops 31457280 | bytes 14155776 | tf_op jit(solution)/shard_map/middle_norm/pallas_call | solution.py:108
  116.2 3.5 %collective-permute-start.11 = (f32[2,384]{1,0:T(2,128)S(1)}, f32[2,384]{1,0:T(2,128)S(1)}, u32[]{:S(2)}, u32[]{:S(2)}) collective-permute-start(f32[2,384]{1,0:T(2,128)S(1)} %get-tuple-element.161), channel_id=1, source_target_pairs={{0,8},{8,0},{16,24},{24,16},{1,9},{9,1},{17,25},{25,17},{2,10},{10... | collective-permute-start | bytes 9224 | tf_op jit(solution)/shard_map/ppermute | solution.py:34
  121.7 2.9 %fusion.6.pointwise_ref = f32[768,384]{1,0:T(8,128)} fusion(bf16[2048,768]{1,0:T(8,128)(2,1)S(1)} %copy-done.1, bf16[2048,384]{1,0:T(8,128)(2,1)S(1)} %bitcast.18), kind=kOutput, calls=%fused_computation.61 | convolution fusion | flops 1207959552 | bytes 5898240 | tf_op jit(solution)/shard_map/rd,rf->df/dot_general | solution.py:1440
  125.1 2.1 collective-permute-done.13
  130.3 2.7 %collective-permute-done.15 = f32[2,384]{1,0:T(2,128)S(1)} collective-permute-done((f32[2,384]{1,0:T(2,128)S(1)}, f32[2,384]{1,0:T(2,128)S(1)}, u32[]{:S(2)}, u32[]{:S(2)}) %collective-permute-start.15) | collective-permute-done | bytes 3104 | tf_op jit(solution)/shard_map/ppermute | solution.py:34
  133.0 2.1 middle_grad.1
  135.5 2.8 %convolution_bitcast_fusion.1.centre_ref = f32[768,384]{1,0:T(8,128)} fusion(bf16[4,512,768]{2,1,0:T(8,128)(2,1)S(1)} %get-tuple-element.137.act_ref, bf16[4,512,384]{2,1,0:T(8,128)(2,1)S(1)} %get-tuple-element.168), kind=kOutput, calls=%fused_computation.1 | convolution fusion | flops 1207959552 | bytes 5898240 | tf_op jit(solution)/shard_map/hrc,hrf->cf/dot_general | solution.py:1448
  139.1 7.8 %entry_grad.1 = (bf16[8,128,768]{2,1,0:T(8,128)(2,1)}, bf16[8,128,768]{2,1,0:T(8,128)(2,1)}, bf16[4,512,768]{2,1,0:T(8,128)(2,1)}, f32[3,768]{1,0:T(4,128)S(1)}) custom-call(s32[83]{0:T(128)S(1)} %concatenate.61.facts_ref, f32[4,3,592,128]{3,2,1,0:T(8,128)S(1)} %get-tuple-element.166.padded_ref, bf16[4,48,384]{2,1,0:T(8,128)(2,1)S(1)} %collective-permute-done.16.border_ref, ...), custom_call_target="tpu_custom_call" | custom-call | flops 3623878656 | bytes 23592960 | tf_op jit(solution)/shard_map/entry_grad/pallas_call | solution.py:108
  146.9 4.9 %all-to-all-start.1 = ((bf16[8,128,768]{2,1,0:T(8,128)(2,1)}), bf16[8,128,768]{2,1,0:T(8,128)(2,1)}, u32[]{:S(2)}, u32[]{:S(2)}) async-start(bf16[8,128,768]{2,1,0:T(8,128)(2,1)} %get-tuple-element.179), calls=%async_computation.1 | async-start | bytes 3145728 | tf_op jit(solution)/shard_map/all_to_all | solution.py:1453
  151.8 5.7 %convolution_bitcast_fusion.sides_ref = f32[768,768]{1,0:T(8,128)S(1)} fusion(bf16[4,512,768]{2,1,0:T(8,128)(2,1)} %copy-done.8, bf16[4,512,768]{2,1,0:T(8,128)(2,1)} %get-tuple-element.181), kind=kOutput, calls=%fused_computation | convolution fusion | flops 2415919104 | bytes 8650752 | tf_op jit(solution)/shard_map/hrc,hrf->cf/dot_general | solution.py:1462
  158.3 5.8 %collective-permute-start.17 = (bf16[776,768]{1,0:T(8,128)(2,1)S(1)}, bf16[776,768]{1,0:T(8,128)(2,1)S(1)}, u32[]{:S(2)}, u32[]{:S(2)}) collective-permute-start(bf16[776,768]{1,0:T(8,128)(2,1)S(1)} %get-tuple-element.186), channel_id=1, source_target_pairs={{0,8},{8,0},{16,24},{24,16},{1,9},{9,1},{17,25},{25,17},{2,10},{10... | collective-permute-start | bytes 3575816 | tf_op jit(solution)/shard_map/ppermute | solution.py:34
  164.1 2.5 collective-permute-done.17.other_ref
  170.1 5.9 %collective-permute-done.18.refs_0_ = bf16[200,768]{1,0:T(8,128)(2,1)S(1)} collective-permute-done((bf16[200,768]{1,0:T(8,128)(2,1)S(1)}, bf16[200,768]{1,0:T(8,128)(2,1)S(1)}, u32[]{:S(2)}, u32[]{:S(2)}) %collective-permute-start.18) | collective-permute-done | bytes 307232 | tf_op jit(solution)/shard_map/ppermute | solution.py:1017
  176.1 12.8 %collective-permute-done.19.refs_1_ = bf16[200,768]{1,0:T(8,128)(2,1)S(1)} collective-permute-done((bf16[200,768]{1,0:T(8,128)(2,1)S(1)}, bf16[200,768]{1,0:T(8,128)(2,1)S(1)}, u32[]{:S(2)}, u32[]{:S(2)}) %collective-permute-start.19) | collective-permute-done | bytes 307232 | tf_op jit(solution)/shard_map/ppermute | solution.py:1017
  195.1 4.6 %collective-permute-done.23.refs_2_ = bf16[56,768]{1,0:T(8,128)(2,1)S(1)} collective-permute-done((bf16[56,768]{1,0:T(8,128)(2,1)S(1)}, bf16[56,768]{1,0:T(8,128)(2,1)S(1)}, u32[]{:S(2)}, u32[]{:S(2)}) %collective-permute-start.23) | collective-permute-done | bytes 86048 | tf_op jit(solution)/shard_map/ppermute | solution.py:1017
  203.6 4.5 %all-to-all-start.2 = ((bf16[8,128,768]{2,1,0:T(8,128)(2,1)}), bf16[8,128,768]{2,1,0:T(8,128)(2,1)}, u32[]{:S(2)}, u32[]{:S(2)}) async-start(bf16[8,128,768]{2,1,0:T(8,128)(2,1)} %get-tuple-element.210), calls=%async_computation.2 | async-start | bytes 3145728 | tf_op jit(solution)/shard_map/all_to_all | solution.py:1453
  214.4 9.0 %output_rows.1 = f32[2048,768]{1,0:T(8,128)} custom-call(s32[83]{0:T(128)S(1)} %concatenate.61.facts_ref, bf16[2048,384]{1,0:T(8,128)(2,1)S(1)} %bitcast.19, bf16[384,768]{1,0:T(8,128)(2,1)S(1)} %copy-done.17, bf16[16,128,768]{2,1,0:T(8,128)(2,1)S(1)} %all-to-all-done.arrived_ref.refs_4_, f32[3,768]{1,0:T(4,128)S(1)} %get-tuple-element.267.params_ref.refs_7_), custom_call_target="tpu_custom_call" | custom-call | flops 8455716864 | bytes 88080384 | tf_op jit(solution)/shard_map/output_rows/pallas_call | solution.py:875
  224.0 5.2 %unpool.2.refs_0_ = f32[16,256,768]{2,1,0:T(8,128)} custom-call(s32[83]{0:T(128)S(1)} %concatenate.61.facts_ref, bf16[8,128,768]{2,1,0:T(8,128)(2,1)} %all-to-all-done.1.returned_ref, bf16[16,128,768]{2,1,0:T(8,128)(2,1)} %get-tuple-element.120.pooled_ref, bf16[16,128,768]{2,1,0:T(8,128)(2,1)} %first_marks.1.first_ref, ...), custom_call_target="tpu_custom_call" | custom-call | flops 7864320 | bytes 11010048 | tf_op jit(solution)/shard_map/unpool/pallas_call | solution.py:407
  229.8 7.5 %collective-permute-done.28 = bf16[192,768]{1,0:T(8,128)(2,1)S(1)} collective-permute-done((bf16[192,768]{1,0:T(8,128)(2,1)S(1)}, bf16[192,768]{1,0:T(8,128)(2,1)S(1)}, u32[]{:S(2)}, u32[]{:S(2)}) %collective-permute-start.28) | collective-permute-done | bytes 294944 | tf_op jit(solution)/shard_map/ppermute | solution.py:1017
  239.4 2.2 finish_weights.2
  244.0 5.2 %unpool.3 = f32[16,256,768]{2,1,0:T(8,128)} custom-call(s32[83]{0:T(128)S(1)} %concatenate.61.facts_ref, bf16[8,128,768]{2,1,0:T(8,128)(2,1)} %all-to-all-done.2.returned_ref, bf16[16,128,768]{2,1,0:T(8,128)(2,1)} %get-tuple-element.120.pooled_ref, bf16[16,128,768]{2,1,0:T(8,128)(2,1)} %first_marks.1.first_ref, ...), custom_call_target="tpu_custom_call", output_to_operand_aliasing={{}: (7, {})} | custom-call | flops 7864320 | bytes 11010048 | tf_op jit(solution)/shard_map/unpool/pallas_call | solution.py:407
  (148 shorter events, 66.7 us)
Async XLA Ops:
  8.2 73.0 %all-to-all-start = ((bf16[16,128,768]{2,1,0:T(8,128)(2,1)}), bf16[16,128,768]{2,1,0:T(8,128)(2,1)S(1)}, u32[]{:S(2)}, u32[]{:S(2)}) async-start(bf16[16,128,768]{2,1,0:T(8,128)(2,1)} %get-tuple-element.120.pooled_ref), calls=%async_computation | async-start | bytes 6291456 | tf_op jit(solution)/shard_map/all_to_all | solution.py:1351
  15.9 2.9 %collective-permute-start.1 = (f32[3,768]{1,0:T(4,128)S(1)}, f32[3,768]{1,0:T(4,128)S(1)}, u32[]{:S(2)}, u32[]{:S(2)}) collective-permute-start(f32[3,768]{1,0:T(4,128)S(1)} %pad_maximum_fusion), channel_id=1, source_target_pairs={{0,16},{8,24},{16,0},{24,8},{1,17},{9,25},{17,1},{25,9},{2,18},{10... | collective-permute-start | bytes 27656 | tf_op jit(solution)/shard_map/ppermute | solution.py:34
  18.9 20.2 %collective-permute-start.2 = (f32[3,768]{1,0:T(4,128)S(1)}, f32[3,768]{1,0:T(4,128)S(1)}, u32[]{:S(2)}, u32[]{:S(2)}) collective-permute-start(f32[3,768]{1,0:T(4,128)S(1)} %pad_maximum_fusion.1), channel_id=1, source_target_pairs={{0,1},{1,0},{2,3},{3,2},{4,5},{5,4},{6,7},{7,6},{8,9},{9,8},{10,11... | collective-permute-start | bytes 27656 | tf_op jit(solution)/shard_map/ppermute | solution.py:34
  39.1 26.9 %collective-permute-start.3 = (f32[3,768]{1,0:T(4,128)S(1)}, f32[3,768]{1,0:T(4,128)S(1)}, u32[]{:S(2)}, u32[]{:S(2)}) collective-permute-start(f32[3,768]{1,0:T(4,128)S(1)} %pad_maximum_fusion.2), channel_id=1, source_target_pairs={{0,2},{1,3},{2,0},{3,1},{4,6},{5,7},{6,4},{7,5},{8,10},{9,11},{10,... | collective-permute-start | bytes 27656 | tf_op jit(solution)/shard_map/ppermute | solution.py:34
  66.0 15.0 %collective-permute-start.4 = (f32[3,768]{1,0:T(4,128)S(1)}, f32[3,768]{1,0:T(4,128)S(1)}, u32[]{:S(2)}, u32[]{:S(2)}) collective-permute-start(f32[3,768]{1,0:T(4,128)S(1)} %pad_maximum_fusion.3), channel_id=1, source_target_pairs={{0,4},{1,5},{2,6},{3,7},{4,0},{5,1},{6,2},{7,3},{8,12},{9,13},{10,... | collective-permute-start | bytes 27656 | tf_op jit(solution)/shard_map/ppermute | solution.py:34
  84.8 8.2 %collective-permute-start.5 = (bf16[4,48,768]{2,1,0:T(8,128)(2,1)S(1)}, bf16[4,48,768]{2,1,0:T(8,128)(2,1)S(1)}, u32[]{:S(2)}, u32[]{:S(2)}) collective-permute-start(bf16[4,48,768]{2,1,0:T(8,128)(2,1)S(1)} %get-tuple-element.140), channel_id=1, source_target_pairs={{0,1},{1,0},{2,3},{3,2},{4,5},{5,4},{6,7},{7,6},{8,9},{9,8},{10,11... | collective-permute-start | bytes 884744 | tf_op jit(solution)/shard_map/ppermute | solution.py:34
  94.1 2.6 %collective-permute-start.6 = (f32[3,384]{1,0:T(4,128)S(1)}, f32[3,384]{1,0:T(4,128)S(1)}, u32[]{:S(2)}, u32[]{:S(2)}) collective-permute-start(f32[3,384]{1,0:T(4,128)S(1)} %get-tuple-element.143), channel_id=1, source_target_pairs={{0,8},{8,0},{16,24},{24,16},{1,9},{9,1},{17,25},{25,17},{2,10},{10... | collective-permute-start | bytes 13832 | tf_op jit(solution)/shard_map/ppermute | solution.py:34
  96.7 3.2 %collective-permute-start.7 = (f32[3,384]{1,0:T(4,128)S(1)}, f32[3,384]{1,0:T(4,128)S(1)}, u32[]{:S(2)}, u32[]{:S(2)}) collective-permute-start(f32[3,384]{1,0:T(4,128)S(1)} %pad_maximum_fusion.6), channel_id=1, source_target_pairs={{0,16},{8,24},{16,0},{24,8},{1,17},{9,25},{17,1},{25,9},{2,18},{10... | collective-permute-start | bytes 13832 | tf_op jit(solution)/shard_map/ppermute | solution.py:34
  100.0 3.1 %collective-permute-start.8 = (f32[3,384]{1,0:T(4,128)S(1)}, f32[3,384]{1,0:T(4,128)S(1)}, u32[]{:S(2)}, u32[]{:S(2)}) collective-permute-start(f32[3,384]{1,0:T(4,128)S(1)} %pad_maximum_fusion.7), channel_id=1, source_target_pairs={{0,1},{1,0},{2,3},{3,2},{4,5},{5,4},{6,7},{7,6},{8,9},{9,8},{10,11... | collective-permute-start | bytes 13832 | tf_op jit(solution)/shard_map/ppermute | solution.py:34
  103.1 5.3 %collective-permute-start.9 = (f32[3,384]{1,0:T(4,128)S(1)}, f32[3,384]{1,0:T(4,128)S(1)}, u32[]{:S(2)}, u32[]{:S(2)}) collective-permute-start(f32[3,384]{1,0:T(4,128)S(1)} %pad_maximum_fusion.8), channel_id=1, source_target_pairs={{0,2},{1,3},{2,0},{3,1},{4,6},{5,7},{6,4},{7,5},{8,10},{9,11},{10,... | collective-permute-start | bytes 13832 | tf_op jit(solution)/shard_map/ppermute | solution.py:34
  108.5 3.4 %collective-permute-start.10 = (f32[3,384]{1,0:T(4,128)S(1)}, f32[3,384]{1,0:T(4,128)S(1)}, u32[]{:S(2)}, u32[]{:S(2)}) collective-permute-start(f32[3,384]{1,0:T(4,128)S(1)} %pad_maximum_fusion.9), channel_id=1, source_target_pairs={{0,4},{1,5},{2,6},{3,7},{4,0},{5,1},{6,2},{7,3},{8,12},{9,13},{10,... | collective-permute-start | bytes 13832 | tf_op jit(solution)/shard_map/ppermute | solution.py:34
  116.2 4.3 %collective-permute-start.11 = (f32[2,384]{1,0:T(2,128)S(1)}, f32[2,384]{1,0:T(2,128)S(1)}, u32[]{:S(2)}, u32[]{:S(2)}) collective-permute-start(f32[2,384]{1,0:T(2,128)S(1)} %get-tuple-element.161), channel_id=1, source_target_pairs={{0,8},{8,0},{16,24},{24,16},{1,9},{9,1},{17,25},{25,17},{2,10},{10... | collective-permute-start | bytes 9224 | tf_op jit(solution)/shard_map/ppermute | solution.py:34
  120.5 4.1 %collective-permute-start.12 = (f32[2,384]{1,0:T(2,128)S(1)}, f32[2,384]{1,0:T(2,128)S(1)}, u32[]{:S(2)}, u32[]{:S(2)}) collective-permute-start(f32[2,384]{1,0:T(2,128)S(1)} %add.234), channel_id=1, source_target_pairs={{0,16},{8,24},{16,0},{24,8},{1,17},{9,25},{17,1},{25,9},{2,18},{10... | collective-permute-start | bytes 9224 | tf_op jit(solution)/shard_map/ppermute | solution.py:34
  124.6 2.5 %collective-permute-start.13 = (f32[2,384]{1,0:T(2,128)S(1)}, f32[2,384]{1,0:T(2,128)S(1)}, u32[]{:S(2)}, u32[]{:S(2)}) collective-permute-start(f32[2,384]{1,0:T(2,128)S(1)} %add.235), channel_id=1, source_target_pairs={{0,1},{1,0},{2,3},{3,2},{4,5},{5,4},{6,7},{7,6},{8,9},{9,8},{10,11... | collective-permute-start | bytes 9224 | tf_op jit(solution)/shard_map/ppermute | solution.py:34
  129.6 3.3 %collective-permute-start.15 = (f32[2,384]{1,0:T(2,128)S(1)}, f32[2,384]{1,0:T(2,128)S(1)}, u32[]{:S(2)}, u32[]{:S(2)}) collective-permute-start(f32[2,384]{1,0:T(2,128)S(1)} %add.237), channel_id=1, source_target_pairs={{0,4},{1,5},{2,6},{3,7},{4,0},{5,1},{6,2},{7,3},{8,12},{9,13},{10,... | collective-permute-start | bytes 9224 | tf_op jit(solution)/shard_map/ppermute | solution.py:34
  135.0 4.1 %collective-permute-start.16 = (bf16[4,48,384]{2,1,0:T(8,128)(2,1)S(1)}, bf16[4,48,384]{2,1,0:T(8,128)(2,1)S(1)}, u32[]{:S(2)}, u32[]{:S(2)}) collective-permute-start(bf16[4,48,384]{2,1,0:T(8,128)(2,1)S(1)} %get-tuple-element.167), channel_id=1, source_target_pairs={{0,1},{1,0},{2,3},{3,2},{4,5},{5,4},{6,7},{7,6},{8,9},{9,8},{10,11... | collective-permute-start | bytes 442376 | tf_op jit(solution)/shard_map/ppermute | solution.py:34
  146.9 56.6 %all-to-all-start.1 = ((bf16[8,128,768]{2,1,0:T(8,128)(2,1)}), bf16[8,128,768]{2,1,0:T(8,128)(2,1)}, u32[]{:S(2)}, u32[]{:S(2)}) async-start(bf16[8,128,768]{2,1,0:T(8,128)(2,1)} %get-tuple-element.179), calls=%async_computation.1 | async-start | bytes 3145728 | tf_op jit(solution)/shard_map/all_to_all | solution.py:1453
  158.3 8.3 %collective-permute-start.17 = (bf16[776,768]{1,0:T(8,128)(2,1)S(1)}, bf16[776,768]{1,0:T(8,128)(2,1)S(1)}, u32[]{:S(2)}, u32[]{:S(2)}) collective-permute-start(bf16[776,768]{1,0:T(8,128)(2,1)S(1)} %get-tuple-element.186), channel_id=1, source_target_pairs={{0,8},{8,0},{16,24},{24,16},{1,9},{9,1},{17,25},{25,17},{2,10},{10... | collective-permute-start | bytes 3575816 | tf_op jit(solution)/shard_map/ppermute | solution.py:34
  167.4 8.6 %collective-permute-start.18 = (bf16[200,768]{1,0:T(8,128)(2,1)S(1)}, bf16[200,768]{1,0:T(8,128)(2,1)S(1)}, u32[]{:S(2)}, u32[]{:S(2)}) collective-permute-start(bf16[200,768]{1,0:T(8,128)(2,1)S(1)} %get-tuple-element.189), channel_id=1, source_target_pairs={{0,16},{1,17},{2,18},{3,19},{4,20},{5,21},{6,22},{7,23},{8,24},{9,... | collective-permute-start | bytes 921608 | tf_op jit(solution)/shard_map/ppermute | solution.py:1017
  167.8 21.0 %collective-permute-start.19 = (bf16[200,768]{1,0:T(8,128)(2,1)S(1)}, bf16[200,768]{1,0:T(8,128)(2,1)S(1)}, u32[]{:S(2)}, u32[]{:S(2)}) collective-permute-start(bf16[200,768]{1,0:T(8,128)(2,1)S(1)} %get-tuple-element.190), channel_id=1, source_target_pairs={{0,1},{1,0},{2,3},{3,2},{4,5},{5,4},{6,7},{7,6},{8,9},{9,8},{10,11... | collective-permute-start | bytes 921608 | tf_op jit(solution)/shard_map/ppermute | solution.py:1017
  169.0 19.9 %collective-permute-start.20 = (bf16[200,768]{1,0:T(8,128)(2,1)S(1)}, bf16[200,768]{1,0:T(8,128)(2,1)S(1)}, u32[]{:S(2)}, u32[]{:S(2)}) collective-permute-start(bf16[200,768]{1,0:T(8,128)(2,1)S(1)} %get-tuple-element.191), channel_id=1, source_target_pairs={{0,17},{1,16},{2,19},{3,18},{4,21},{5,20},{6,23},{7,22},{8,25},{9,... | collective-permute-start | bytes 921608 | tf_op jit(solution)/shard_map/ppermute | solution.py:1017
  189.6 3.4 %collective-permute-start.21 = (bf16[56,768]{1,0:T(8,128)(2,1)S(1)}, bf16[56,768]{1,0:T(8,128)(2,1)S(1)}, u32[]{:S(2)}, u32[]{:S(2)}) collective-permute-start(bf16[56,768]{1,0:T(8,128)(2,1)S(1)} %get-tuple-element.194), channel_id=1, source_target_pairs={{0,2},{1,3},{2,0},{3,1},{4,6},{5,7},{6,4},{7,5},{8,10},{9,11},{10,... | collective-permute-start | bytes 258056 | tf_op jit(solution)/shard_map/ppermute | solution.py:1017
  190.1 4.9 %collective-permute-start.22 = (bf16[56,768]{1,0:T(8,128)(2,1)S(1)}, bf16[56,768]{1,0:T(8,128)(2,1)S(1)}, u32[]{:S(2)}, u32[]{:S(2)}) collective-permute-start(bf16[56,768]{1,0:T(8,128)(2,1)S(1)} %get-tuple-element.195), channel_id=1, source_target_pairs={{0,4},{1,5},{2,6},{3,7},{4,0},{5,1},{6,2},{7,3},{8,12},{9,13},{10,... | collective-permute-start | bytes 258056 | tf_op jit(solution)/shard_map/ppermute | solution.py:1017
  190.3 9.4 %collective-permute-start.23 = (bf16[56,768]{1,0:T(8,128)(2,1)S(1)}, bf16[56,768]{1,0:T(8,128)(2,1)S(1)}, u32[]{:S(2)}, u32[]{:S(2)}) collective-permute-start(bf16[56,768]{1,0:T(8,128)(2,1)S(1)} %get-tuple-element.196), channel_id=1, source_target_pairs={{0,6},{1,7},{2,4},{3,5},{4,2},{5,3},{6,0},{7,1},{8,14},{9,15},{10,... | collective-permute-start | bytes 258056 | tf_op jit(solution)/shard_map/ppermute | solution.py:1017
  200.3 3.3 %collective-permute-start.24 = (bf16[48,768]{1,0:T(8,128)(2,1)S(1)}, bf16[48,768]{1,0:T(8,128)(2,1)S(1)}, u32[]{:S(2)}, u32[]{:S(2)}) collective-permute-start(bf16[48,768]{1,0:T(8,128)(2,1)S(1)} %get-tuple-element.197), channel_id=1, source_target_pairs={{0,2},{1,3},{2,0},{3,1},{4,6},{5,7},{6,4},{7,5},{8,10},{9,11},{10,... | collective-permute-start | bytes 221192 | tf_op jit(solution)/shard_map/ppermute | solution.py:1017
  200.4 7.7 %collective-permute-start.26 = (bf16[48,768]{1,0:T(8,128)(2,1)S(1)}, bf16[48,768]{1,0:T(8,128)(2,1)S(1)}, u32[]{:S(2)}, u32[]{:S(2)}) collective-permute-start(bf16[48,768]{1,0:T(8,128)(2,1)S(1)} %get-tuple-element.197), channel_id=1, source_target_pairs={{0,4},{1,5},{2,6},{3,7},{4,0},{5,1},{6,2},{7,3},{8,12},{9,13},{10,... | collective-permute-start | bytes 221192 | tf_op jit(solution)/shard_map/ppermute | solution.py:1017
  201.6 7.5 %collective-permute-start.25 = (bf16[48,768]{1,0:T(8,128)(2,1)S(1)}, bf16[48,768]{1,0:T(8,128)(2,1)S(1)}, u32[]{:S(2)}, u32[]{:S(2)}) collective-permute-start(bf16[48,768]{1,0:T(8,128)(2,1)S(1)} %get-tuple-element.197), channel_id=1, source_target_pairs={{0,6},{1,7},{2,4},{3,5},{4,2},{5,3},{6,0},{7,1},{8,14},{9,15},{10,... | collective-permute-start | bytes 221192 | tf_op jit(solution)/shard_map/ppermute | solution.py:1017
  203.6 40.4 %all-to-all-start.2 = ((bf16[8,128,768]{2,1,0:T(8,128)(2,1)}), bf16[8,128,768]{2,1,0:T(8,128)(2,1)}, u32[]{:S(2)}, u32[]{:S(2)}) async-start(bf16[8,128,768]{2,1,0:T(8,128)(2,1)} %get-tuple-element.210), calls=%async_computation.2 | async-start | bytes 3145728 | tf_op jit(solution)/shard_map/all_to_all | solution.py:1453
  209.2 20.6 %collective-permute-start.27 = (bf16[192,768]{1,0:T(8,128)(2,1)S(1)}, bf16[192,768]{1,0:T(8,128)(2,1)S(1)}, u32[]{:S(2)}, u32[]{:S(2)}) collective-permute-start(bf16[192,768]{1,0:T(8,128)(2,1)S(1)} %maximum_select_fusion.3), channel_id=1, source_target_pairs={{0,16},{1,17},{2,18},{3,19},{4,20},{5,21},{6,22},{7,23},{8,24},{9,... | collective-permute-start | bytes 884744 | tf_op jit(solution)/shard_map/ppermute | solution.py:1017
  210.3 27.0 %collective-permute-start.28 = (bf16[192,768]{1,0:T(8,128)(2,1)S(1)}, bf16[192,768]{1,0:T(8,128)(2,1)S(1)}, u32[]{:S(2)}, u32[]{:S(2)}) collective-permute-start(bf16[192,768]{1,0:T(8,128)(2,1)S(1)} %maximum_select_fusion.3), channel_id=1, source_target_pairs={{0,1},{1,0},{2,3},{3,2},{4,5},{5,4},{6,7},{7,6},{8,9},{9,8},{10,11... | collective-permute-start | bytes 884744 | tf_op jit(solution)/shard_map/ppermute | solution.py:1017
  210.5 26.7 %collective-permute-start.29 = (bf16[192,768]{1,0:T(8,128)(2,1)S(1)}, bf16[192,768]{1,0:T(8,128)(2,1)S(1)}, u32[]{:S(2)}, u32[]{:S(2)}) collective-permute-start(bf16[192,768]{1,0:T(8,128)(2,1)S(1)} %maximum_select_fusion.3), channel_id=1, source_target_pairs={{0,17},{1,16},{2,19},{3,18},{4,21},{5,20},{6,23},{7,22},{8,25},{9,... | collective-permute-start | bytes 884744 | tf_op jit(solution)/shard_map/ppermute | solution.py:1017
  237.9 4.0 %collective-permute-start.30 = (bf16[768,768]{1,0:T(8,128)(2,1)S(1)}, bf16[768,768]{1,0:T(8,128)(2,1)S(1)}, u32[]{:S(2)}, u32[]{:S(2)}) collective-permute-start(bf16[768,768]{1,0:T(8,128)(2,1)S(1)} %maximum_select_fusion.half_ref), channel_id=1, source_target_pairs={{0,8},{8,0},{16,24},{24,16},{1,9},{9,1},{17,25},{25,17},{2,10},{10... | collective-permute-start | bytes 3538952 | tf_op jit(solution)/shard_map/ppermute | solution.py:34
  (27 other events, 225.3 us)

commit v6 on v5

--- a/solution.py
+++ b/solution.py
@@ -531,50 +531,48 @@
     return (0.5 + 0.5 * bend) + (half - half * bend * bend) * inner
 
 
-def activate_body(
-    slots, windows, facts_ref, arrived_ref, moments_ref, params_ref, act_ref, border_ref
-):
-    blocks, rows, width = arrived_ref.shape
+def activated(values, inside, slope, offset):
+    half_pre = values.astype(jnp.float32) * slope + offset
+    bend, _ = bent(half_pre)
+    return jnp.where(inside, half_pre + half_pre * bend, 0.0).astype(jnp.bfloat16)
+
+
+def edge_body(slots, windows, facts_ref, arrived_ref, moments_ref, params_ref, border_ref):
+    _, rows, width = arrived_ref.shape
     facts = Facts(facts_ref, windows, slots)
     per_half = HALF_WINDOW_ROWS // rows
     slope, offset = half_terms(moments_ref, params_ref, facts.row_count())
-
-    def work(block, carry):
-        source, slot = block // slots, block % slots
-        half, start = source // per_half, (source % per_half) * rows
-        inside = lax.broadcasted_iota(jnp.int32, (rows, 1), 0) < (
-            facts.half_limit(slot, half) - start
-        )
-        for lanes in column_slices(width):
-            values = arrived_ref[block, :, lanes].astype(jnp.float32)
-            half_pre = values * slope[:, lanes] + offset[:, lanes]
-            bend, _ = bent(half_pre)
-            act = jnp.where(inside, half_pre + half_pre * bend, 0.0)
-            act_ref[slot * 2 + half, pl.ds(pl.multiple_of(start, rows), rows), lanes] = act.astype(
-                jnp.bfloat16
-            )
-        return carry
-
-    lax.fori_loop(0, blocks, work, 0)
-    for piece in range(act_ref.shape[0]):
-        start = 0 if piece % 2 else HALF_WINDOW_ROWS - BORDER
-        border_ref[piece] = act_ref[piece, start : start + BORDER]
-
-
-def activate(facts, arrived, moments, params, slots, windows):
+    for piece in range(2 * slots):
+        slot, half = piece // 2, piece % 2
+        limit = facts.half_limit(slot, half)
+        first = 0 if half else HALF_WINDOW_ROWS - BORDER
+        row = first
+        while row < first + BORDER:
+            inner_row = row % rows
+            size = min(rows - inner_row, first + BORDER - row)
+            block = (half * per_half + row // rows) * slots + slot
+            inside = lax.broadcasted_iota(jnp.int32, (size, 1), 0) < limit - row
+            for lanes in column_slices(width):
+                border_ref[piece, row - first : row - first + size, lanes] = activated(
+                    arrived_ref[block, inner_row : inner_row + size, lanes],
+                    inside,
+                    slope[:, lanes],
+                    offset[:, lanes],
+                )
+            row += size
+
+
+def edge_rows(facts, arrived, moments, params, slots, windows):
     width = arrived.shape[2]
     return kernel_call(
-        functools.partial(activate_body, slots, windows),
-        "activate",
+        functools.partial(edge_body, slots, windows),
+        "edge_rows",
         (facts, arrived, moments, params),
         [SMEM, VMEM, VMEM, VMEM],
-        [
-            shape((2 * slots, HALF_WINDOW_ROWS, width), jnp.bfloat16),
-            shape((2 * slots, BORDER, width), jnp.bfloat16),
-        ],
-        [VMEM, VMEM],
-        flops=20 * arrived.size,
-        bytes_moved=4 * arrived.size,
+        shape((2 * slots, BORDER, width), jnp.bfloat16),
+        VMEM,
+        flops=40 * slots * BORDER * width,
+        bytes_moved=8 * slots * BORDER * width,
     )
 
 
@@ -619,21 +617,45 @@
     return block_sum, jnp.sum(deviation * deviation, axis=0, keepdims=True), count
 
 
-def convolve_body(slots, windows, facts_ref, act_ref, weight_ref, out_ref, moments_ref, wide):
+def convolve_body(
+    slots, windows, facts_ref, arrived_ref, entry_ref, params_ref, weight_ref,
+    act_ref, out_ref, moments_ref, wide,
+):
     facts = Facts(facts_ref, windows, slots)
     pieces, rows, inner = out_ref.shape
+    _, block_rows, width = arrived_ref.shape
+    per_half = rows // block_rows
+    slope, offset = half_terms(entry_ref, params_ref, facts.row_count())
     tiles = inner // LANES
-    for tile in range(3 * tiles):
-        wide[tile, 0:PAD] = jnp.zeros((PAD, LANES), jnp.float32)
-        wide[tile, PAD + rows : PADDED_ROWS] = jnp.zeros((PAD, LANES), jnp.float32)
+    for turn in range(2):
+        for tile in range(3 * tiles):
+            wide[turn, tile, 0:PAD] = jnp.zeros((PAD, LANES), jnp.float32)
+            wide[turn, tile, PAD + rows : PADDED_ROWS] = jnp.zeros((PAD, LANES), jnp.float32)
     moments_ref[...] = jnp.zeros_like(moments_ref)
     below, above = PAD - DILATION_STEP, PAD + DILATION_STEP
 
-    def work(piece, carry):
+    def lay_act(piece):
+        slot, half = piece // 2, piece % 2
+        limit = facts.half_limit(slot, half)
+        for part in range(per_half):
+            start = part * block_rows
+            inside = lax.broadcasted_iota(jnp.int32, (block_rows, 1), 0) < limit - start
+            for lanes in column_slices(width):
+                act_ref[piece, start : start + block_rows, lanes] = activated(
+                    arrived_ref[(half * per_half + part) * slots + slot, :, lanes],
+                    inside,
+                    slope[:, lanes],
+                    offset[:, lanes],
+                )
+
+    lay_act(0)
+    for piece in range(pieces):
+        turn, half = piece % 2, piece % 2
+        if piece + 1 < pieces:
+            lay_act(piece + 1)
         product = jnp.dot(act_ref[piece], weight_ref[...], preferred_element_type=jnp.float32)
         for tile, lanes in enumerate(column_slices(3 * inner)):
-            wide[tile, PAD : PAD + rows] = product[:, lanes]
-        half = piece % 2
+            wide[turn, tile, PAD : PAD + rows] = product[:, lanes]
         limit = facts.half_limit(piece // 2, half)
         start = half * STRIP
         row = lax.broadcasted_iota(jnp.int32, (rows, 1), 0)
@@ -642,33 +664,35 @@
         count = jnp.maximum(end - start, 0).astype(jnp.float32)
         for tile, lanes in enumerate(column_slices(inner)):
             out = (
-                wide[tiles + tile, PAD : PAD + rows]
-                + wide[tile, below : below + rows]
-                + wide[2 * tiles + tile, above : above + rows]
+                wide[turn, tiles + tile, PAD : PAD + rows]
+                + wide[turn, tile, below : below + rows]
+                + wide[turn, 2 * tiles + tile, above : above + rows]
             )
             out_ref[piece, :, lanes] = out
             held = (moments_ref[0:1, lanes], moments_ref[1:2, lanes], moments_ref[2:3, lanes])
             moments_ref[0:1, lanes], moments_ref[1:2, lanes], moments_ref[2:3, lanes] = merged(
                 held, block_moments(out, inside, count)
             )
-        return carry
-
-    lax.fori_loop(0, pieces, work, 0)
-
-
-def convolve(facts, act, weight, slots, windows):
-    pieces, rows, width = act.shape
-    inner = weight.shape[1] // 3
+
+
+def convolve(facts, arrived, entry_moments, params, weight, slots, windows):
+    width, inner = weight.shape[0], weight.shape[1] // 3
+    pieces, rows = 2 * slots, HALF_WINDOW_ROWS
     return kernel_call(
         functools.partial(convolve_body, slots, windows),
         "convolve",
-        (facts, act, weight),
-        [SMEM, VMEM, VMEM],
-        [shape((pieces, rows, inner), jnp.float32), shape((3, inner), jnp.float32)],
-        [VMEM, VMEM],
-        [pltpu.VMEM((3 * inner // LANES, PADDED_ROWS, LANES), jnp.float32)],
+        (facts, arrived, entry_moments, params, weight),
+        [SMEM] + [VMEM] * 4,
+        [
+            shape((pieces, rows, width), jnp.bfloat16),
+            shape((pieces, rows, inner), jnp.float32),
+            shape((3, inner), jnp.float32),
+        ],
+        [VMEM, VMEM, VMEM],
+        [pltpu.VMEM((2, 3 * inner // LANES, PADDED_ROWS, LANES), jnp.float32)],
         flops=6 * pieces * rows * width * inner,
         bytes_moved=pieces * rows * (width * 2 + inner * 4),
+        grant=16 << 20,
     )
 
 
@@ -964,9 +988,12 @@
                     packed[slot, source, :, lanes] = (pre * slope[:, lanes] + block).astype(
                         jnp.bfloat16
                     )
+        if piece == 0:
+            keeping(piece).start()
         for part in range(per_half):
             departure(slot, half * per_half + part).start()
-        keeping(piece).start()
+        if piece + 1 < pieces:
+            keeping(piece + 1).start()
     sums_ref[0:1] = (sums_ref[0:1] - centre * sums_ref[1:2]) * scale
     sums_ref[2:3] = bias_ref[...]
     for piece in range(pieces):
@@ -1395,9 +1422,12 @@
         )
     )
 
-    act, act_border = activate(facts, arrived, entry_moments, entry_params, slots, windows)
+    act_border = edge_rows(facts, arrived, entry_moments, entry_params, slots, windows)
+    tied, act_border = lax.optimization_barrier((arrived, act_border))
     act_border = from_partner(act_border, "seq", 1)
-    dilated, held_moments = convolve(facts, act, wide_kernel, slots, windows)
+    act, dilated, held_moments = convolve(
+        facts, tied, entry_moments, entry_params, wide_kernel, slots, windows
+    )
     strip, middle_moments = join(
         facts, dilated, act_border, wide_kernel, held_moments, slots, windows
     )
@@ -1435,7 +1465,7 @@
     flat_act = middle_act.reshape(-1, inner)
     for number, (axis, mask) in enumerate(exchange_steps()):
         other = from_partner(middle_sums, axis, mask)
-        if number == 1:
+        if number == len(exchange_steps()) - 1:
             tied, middle_sums = lax.optimization_barrier((flat_act, middle_sums))
             pointwise_part = jnp.einsum(
                 "rd,rf->df", grad_block, tied, preferred_element_type=jnp.float32

time: 253 us -> 251 us (level)
  transfers between devices with their start and end apart: 34 -> 34, of which waited for: 22 -> 23; matrix products, arithmetic and copies ran while one was open for 6% -> 6% of each run, Pallas kernels for 20% -> 20%
where the time goes in v6:
time: 251 us; the launch traced here: 247 us
  waiting for transfers between devices  84 us (33%)
  Pallas kernels  78.5 us (31%)
  starting transfers between devices  56.6 us (23%)
  local copies, waits for them, and re-layouts  14 us (6%)
  matrix products  11.5 us (5%)
    pallas_call x17, Pallas kernels, kernel_call(): pl.pallas_call(body, in_specs=specs, out_specs=out_specs, out_shape=outpu...  50.8 us
    ppermute x19, waiting for transfers between devices, from_partner(): lax.ppermute(block, axis, [(place, place ^ mask) for place in range(count)])  48.1 us
    ppermute x12, waiting for transfers between devices, from_flat_partner(): lax.ppermute(block, ('grp', 'seq'), [(place, place ^ mask) for place in r...  35.9 us
    ppermute x19, starting transfers between devices, from_partner(): lax.ppermute(block, axis, [(place, place ^ mask) for place in range(count)])  30.3 us
    unnamed x50, local copies, waits for them, and re-layouts  12.7 us
    ppermute x12, starting transfers between devices, from_flat_partner(): lax.ppermute(block, ('grp', 'seq'), [(place, place ^ mask) for place in r...  10.8 us
    pallas_call x2, Pallas kernels, unpool(): pl.pallas_call(functools.partial(unpool_body, slots, slot, windows), in_s...  10.4 us
    all_to_all x2, starting transfers between devices, send_back(): return lax.all_to_all(block, 'seq', split_axis=0, concat_axis=0, tiled=True)  9.83 us
  transfers between devices with their start and end apart: 34, of which 23 were waited for; matrix products, arithmetic and copies ran while one was open for 6% of the time, Pallas kernels for 20%

profile of v6, /device:TPU:17, one launch (start us, length us, event | category | flops | bytes accessed | tf_op | source)
XLA Modules:
  0.0 247.3 jit_solution(7993339883040862117)
XLA Ops:
  0.6 7.5 %pool.1 = (bf16[16,128,768]{2,1,0:T(8,128)(2,1)}, f32[3,768]{1,0:T(4,128)S(1)}) custom-call(s32[1,16]{1,0:T(1,128)} %order_ref.1, s32[64]{0:T(128)} %lengths_ref.1, f32[16,256,768]{2,1,0:T(8,128)} %signal_ref.3), custom_call_target="tpu_custom_call" | custom-call | flops 15728640 | bytes 15728640 | tf_op jit(solution)/shard_map/pool/pallas_call | solution.py:108
  8.2 5.6 %all-to-all-start = ((bf16[16,128,768]{2,1,0:T(8,128)(2,1)}), bf16[16,128,768]{2,1,0:T(8,128)(2,1)S(1)}, u32[]{:S(2)}, u32[]{:S(2)}) async-start(bf16[16,128,768]{2,1,0:T(8,128)(2,1)} %get-tuple-element.121.pooled_ref), calls=%async_computation | async-start | bytes 6291456 | tf_op jit(solution)/shard_map/all_to_all | solution.py:1378
  26.5 12.5 %collective-permute-done.2 = f32[3,768]{1,0:T(4,128)S(1)} collective-permute-done((f32[3,768]{1,0:T(4,128)S(1)}, f32[3,768]{1,0:T(4,128)S(1)}, u32[]{:S(2)}, u32[]{:S(2)}) %collective-permute-start.2) | collective-permute-done | bytes 9248 | tf_op jit(solution)/shard_map/ppermute | solution.py:34
  41.0 2.8 %copy-done.4 = f32[2048,768]{1,0:T(8,128)S(1)} copy-done((f32[2048,768]{1,0:T(8,128)S(1)}, f32[2048,768]{1,0:T(8,128)}, u32[]{:S(2)}) %copy-start.4) | copy-done | bytes 6291480
  43.8 4.1 %prepare_cotangent.1 = (bf16[2048,768]{1,0:T(8,128)(2,1)S(1)}, f32[2048,384]{1,0:T(8,128)S(1)}, f32[1,768]{1,0:T(1,128)S(1)}) custom-call(s32[83]{0:T(128)S(1)} %concatenate.61.facts_ref, f32[2048,768]{1,0:T(8,128)S(1)} %copy-done.4, bf16[384,768]{1,0:T(8,128)(2,1)S(1)} %get-tuple-element.205.weight_ref), custom_call_target="tpu_custom_call" | custom-call | flops 1207959552 | bytes 12582912 | tf_op jit(solution)/shard_map/prepare_cotangent/pallas_call | solution.py:457
  49.6 8.5 %first_marks.1.first_ref = bf16[16,128,768]{2,1,0:T(8,128)(2,1)} custom-call(s32[83]{0:T(128)S(1)} %concatenate.61.facts_ref, f32[16,256,768]{2,1,0:T(8,128)} %signal_ref.3), custom_call_target="tpu_custom_call" | custom-call | flops 4718592 | bytes 15728640 | tf_op jit(solution)/shard_map/first_marks/pallas_call | solution.py:108
  58.2 7.8 %collective-permute-done.3 = f32[3,768]{1,0:T(4,128)S(1)} collective-permute-done((f32[3,768]{1,0:T(4,128)S(1)}, f32[3,768]{1,0:T(4,128)S(1)}, u32[]{:S(2)}, u32[]{:S(2)}) %collective-permute-start.3) | collective-permute-done | bytes 9248 | tf_op jit(solution)/shard_map/ppermute | solution.py:34
  66.3 14.8 %collective-permute-done.4 = f32[3,768]{1,0:T(4,128)S(1)} collective-permute-done((f32[3,768]{1,0:T(4,128)S(1)}, f32[3,768]{1,0:T(4,128)S(1)}, u32[]{:S(2)}, u32[]{:S(2)}) %collective-permute-start.4) | collective-permute-done | bytes 9248 | tf_op jit(solution)/shard_map/ppermute | solution.py:34
  84.0 7.2 %convolve.1 = (bf16[4,512,768]{2,1,0:T(8,128)(2,1)S(1)}, f32[4,512,384]{2,1,0:T(8,128)S(1)}, f32[3,384]{1,0:T(4,128)S(1)}) custom-call(s32[83]{0:T(128)S(1)} %concatenate.61.facts_ref, bf16[16,128,768]{2,1,0:T(8,128)(2,1)S(1)} %all-to-all-done.arrived_ref.refs_4_, f32[3,768]{1,0:T(4,128)S(1)} %get-tuple-element.268.moments_ref.entry_ref.refs_6_, ...), custom_call_target="tpu_custom_call" | custom-call | flops 3623878656 | bytes 6291456 | tf_op jit(solution)/shard_map/convolve/pallas_call | solution.py:108
  100.7 3.3 %collective-permute-start.9 = (f32[3,384]{1,0:T(4,128)S(1)}, f32[3,384]{1,0:T(4,128)S(1)}, u32[]{:S(2)}, u32[]{:S(2)}) collective-permute-start(f32[3,384]{1,0:T(4,128)S(1)} %pad_maximum_fusion.8), channel_id=1, source_target_pairs={{0,2},{1,3},{2,0},{3,1},{4,6},{5,7},{6,4},{7,5},{8,10},{9,11},{10,... | collective-permute-start | bytes 13832 | tf_op jit(solution)/shard_map/ppermute | solution.py:34
  109.5 4.4 %middle_norm.1 = (bf16[4,512,384]{2,1,0:T(8,128)(2,1)S(1)}, f32[4,512,384]{2,1,0:T(8,128)S(1)}, f32[4,512,384]{2,1,0:T(8,128)S(1)}, f32[2,384]{1,0:T(2,128)S(1)}) custom-call(s32[83]{0:T(128)S(1)} %concatenate.61.facts_ref, f32[4,512,384]{2,1,0:T(8,128)S(1)} %get-tuple-element.140.out_ref, f32[4,64,384]{2,1,0:T(8,128)S(1)} %get-tuple-element.143.strip_ref, ...), custom_call_target="tpu_custom_call" | custom-call | flops 31457280 | bytes 14155776 | tf_op jit(solution)/shard_map/middle_norm/pallas_call | solution.py:108
  113.9 3.5 %collective-permute-start.11 = (f32[2,384]{1,0:T(2,128)S(1)}, f32[2,384]{1,0:T(2,128)S(1)}, u32[]{:S(2)}, u32[]{:S(2)}) collective-permute-start(f32[2,384]{1,0:T(2,128)S(1)} %get-tuple-element.162), channel_id=1, source_target_pairs={{0,8},{8,0},{16,24},{24,16},{1,9},{9,1},{17,25},{25,17},{2,10},{10... | collective-permute-start | bytes 9224 | tf_op jit(solution)/shard_map/ppermute | solution.py:34
  121.0 2.1 collective-permute-done.13
  126.8 2.9 %fusion.6.pointwise_ref = f32[768,384]{1,0:T(8,128)} fusion(bf16[2048,768]{1,0:T(8,128)(2,1)S(1)} %copy-done.1, bf16[2048,384]{1,0:T(8,128)(2,1)S(1)} %bitcast.18), kind=kOutput, calls=%fused_computation.61 | convolution fusion | flops 1207959552 | bytes 5898240 | tf_op jit(solution)/shard_map/rd,rf->df/dot_general | solution.py:1470
  129.8 2.1 middle_grad.1
  132.4 2.8 %convolution_bitcast_fusion.1.centre_ref = f32[768,384]{1,0:T(8,128)} fusion(bf16[4,512,768]{2,1,0:T(8,128)(2,1)S(1)} %get-tuple-element.169, bf16[4,512,384]{2,1,0:T(8,128)(2,1)S(1)} %get-tuple-element.170), kind=kOutput, calls=%fused_computation.1 | convolution fusion | flops 1207959552 | bytes 5898240 | tf_op jit(solution)/shard_map/hrc,hrf->cf/dot_general | solution.py:1478
  135.9 7.7 %entry_grad.1 = (bf16[8,128,768]{2,1,0:T(8,128)(2,1)}, bf16[8,128,768]{2,1,0:T(8,128)(2,1)}, bf16[4,512,768]{2,1,0:T(8,128)(2,1)}, f32[3,768]{1,0:T(4,128)S(1)}) custom-call(s32[83]{0:T(128)S(1)} %concatenate.61.facts_ref, f32[4,3,592,128]{3,2,1,0:T(8,128)S(1)} %get-tuple-element.167.padded_ref, bf16[4,48,384]{2,1,0:T(8,128)(2,1)S(1)} %collective-permute-done.16.border_ref, ...), custom_call_target="tpu_custom_call" | custom-call | flops 3623878656 | bytes 23592960 | tf_op jit(solution)/shard_map/entry_grad/pallas_call | solution.py:108
  143.6 5.3 %all-to-all-start.1 = ((bf16[8,128,768]{2,1,0:T(8,128)(2,1)}), bf16[8,128,768]{2,1,0:T(8,128)(2,1)}, u32[]{:S(2)}, u32[]{:S(2)}) async-start(bf16[8,128,768]{2,1,0:T(8,128)(2,1)} %get-tuple-element.181), calls=%async_computation.1 | async-start | bytes 3145728 | tf_op jit(solution)/shard_map/all_to_all | solution.py:1483
  148.9 5.7 %convolution_bitcast_fusion.sides_ref = f32[768,768]{1,0:T(8,128)S(1)} fusion(bf16[4,512,768]{2,1,0:T(8,128)(2,1)} %copy-done.8, bf16[4,512,768]{2,1,0:T(8,128)(2,1)} %get-tuple-element.183), kind=kOutput, calls=%fused_computation | convolution fusion | flops 2415919104 | bytes 8650752 | tf_op jit(solution)/shard_map/hrc,hrf->cf/dot_general | solution.py:1492
  155.3 5.8 %collective-permute-start.17 = (bf16[776,768]{1,0:T(8,128)(2,1)S(1)}, bf16[776,768]{1,0:T(8,128)(2,1)S(1)}, u32[]{:S(2)}, u32[]{:S(2)}) collective-permute-start(bf16[776,768]{1,0:T(8,128)(2,1)S(1)} %get-tuple-element.188), channel_id=1, source_target_pairs={{0,8},{8,0},{16,24},{24,16},{1,9},{9,1},{17,25},{25,17},{2,10},{10... | collective-permute-start | bytes 3575816 | tf_op jit(solution)/shard_map/ppermute | solution.py:34
  161.1 2.5 %collective-permute-done.17.other_ref = bf16[776,768]{1,0:T(8,128)(2,1)S(1)} collective-permute-done((bf16[776,768]{1,0:T(8,128)(2,1)S(1)}, bf16[776,768]{1,0:T(8,128)(2,1)S(1)}, u32[]{:S(2)}, u32[]{:S(2)}) %collective-permute-start.17) | collective-permute-done | bytes 1191968 | tf_op jit(solution)/shard_map/ppermute | solution.py:34
  167.3 5.9 %collective-permute-done.18.refs_0_ = bf16[200,768]{1,0:T(8,128)(2,1)S(1)} collective-permute-done((bf16[200,768]{1,0:T(8,128)(2,1)S(1)}, bf16[200,768]{1,0:T(8,128)(2,1)S(1)}, u32[]{:S(2)}, u32[]{:S(2)}) %collective-permute-start.18) | collective-permute-done | bytes 307232 | tf_op jit(solution)/shard_map/ppermute | solution.py:1044
  173.2 13.7 %collective-permute-done.19.refs_1_ = bf16[200,768]{1,0:T(8,128)(2,1)S(1)} collective-permute-done((bf16[200,768]{1,0:T(8,128)(2,1)S(1)}, bf16[200,768]{1,0:T(8,128)(2,1)S(1)}, u32[]{:S(2)}, u32[]{:S(2)}) %collective-permute-start.19) | collective-permute-done | bytes 307232 | tf_op jit(solution)/shard_map/ppermute | solution.py:1044
  188.1 2.3 collective-permute-start.23
  193.0 4.7 %collective-permute-done.23.refs_2_ = bf16[56,768]{1,0:T(8,128)(2,1)S(1)} collective-permute-done((bf16[56,768]{1,0:T(8,128)(2,1)S(1)}, bf16[56,768]{1,0:T(8,128)(2,1)S(1)}, u32[]{:S(2)}, u32[]{:S(2)}) %collective-permute-start.23) | collective-permute-done | bytes 86048 | tf_op jit(solution)/shard_map/ppermute | solution.py:1044
  201.6 4.5 %all-to-all-start.2 = ((bf16[8,128,768]{2,1,0:T(8,128)(2,1)}), bf16[8,128,768]{2,1,0:T(8,128)(2,1)}, u32[]{:S(2)}, u32[]{:S(2)}) async-start(bf16[8,128,768]{2,1,0:T(8,128)(2,1)} %get-tuple-element.212), calls=%async_computation.2 | async-start | bytes 3145728 | tf_op jit(solution)/shard_map/all_to_all | solution.py:1483
  212.4 9.0 %output_rows.1 = f32[2048,768]{1,0:T(8,128)} custom-call(s32[83]{0:T(128)S(1)} %concatenate.61.facts_ref, bf16[2048,384]{1,0:T(8,128)(2,1)S(1)} %bitcast.19, bf16[384,768]{1,0:T(8,128)(2,1)S(1)} %copy-done.17, bf16[16,128,768]{2,1,0:T(8,128)(2,1)S(1)} %all-to-all-done.arrived_ref.refs_4_, f32[3,768]{1,0:T(4,128)S(1)} %get-tuple-element.269.params_ref.refs_7_), custom_call_target="tpu_custom_call" | custom-call | flops 8455716864 | bytes 88080384 | tf_op jit(solution)/shard_map/output_rows/pallas_call | solution.py:899
  222.0 5.2 %unpool.2.refs_0_ = f32[16,256,768]{2,1,0:T(8,128)} custom-call(s32[83]{0:T(128)S(1)} %concatenate.61.facts_ref, bf16[8,128,768]{2,1,0:T(8,128)(2,1)} %all-to-all-done.1.returned_ref, bf16[16,128,768]{2,1,0:T(8,128)(2,1)} %get-tuple-element.121.pooled_ref, bf16[16,128,768]{2,1,0:T(8,128)(2,1)} %first_marks.1.first_ref, ...), custom_call_target="tpu_custom_call" | custom-call | flops 7864320 | bytes 11010048 | tf_op jit(solution)/shard_map/unpool/pallas_call | solution.py:407
  227.8 7.5 %collective-permute-done.28 = bf16[192,768]{1,0:T(8,128)(2,1)S(1)} collective-permute-done((bf16[192,768]{1,0:T(8,128)(2,1)S(1)}, bf16[192,768]{1,0:T(8,128)(2,1)S(1)}, u32[]{:S(2)}, u32[]{:S(2)}) %collective-permute-start.28) | collective-permute-done | bytes 294944 | tf_op jit(solution)/shard_map/ppermute | solution.py:1044
  237.4 2.2 finish_weights.2
  239.9 2.0 finish_weights.3
  242.0 5.2 %unpool.3 = f32[16,256,768]{2,1,0:T(8,128)} custom-call(s32[83]{0:T(128)S(1)} %concatenate.61.facts_ref, bf16[8,128,768]{2,1,0:T(8,128)(2,1)} %all-to-all-done.2.returned_ref, bf16[16,128,768]{2,1,0:T(8,128)(2,1)} %get-tuple-element.121.pooled_ref, bf16[16,128,768]{2,1,0:T(8,128)(2,1)} %first_marks.1.first_ref, ...), custom_call_target="tpu_custom_call", output_to_operand_aliasing={{}: (7, {})} | custom-call | flops 7864320 | bytes 11010048 | tf_op jit(solution)/shard_map/unpool/pallas_call | solution.py:407
  (148 shorter events, 64.9 us)
Async XLA Ops:
  8.2 73.0 %all-to-all-start = ((bf16[16,128,768]{2,1,0:T(8,128)(2,1)}), bf16[16,128,768]{2,1,0:T(8,128)(2,1)S(1)}, u32[]{:S(2)}, u32[]{:S(2)}) async-start(bf16[16,128,768]{2,1,0:T(8,128)(2,1)} %get-tuple-element.121.pooled_ref), calls=%async_computation | async-start | bytes 6291456 | tf_op jit(solution)/shard_map/all_to_all | solution.py:1378
  15.9 2.9 %collective-permute-start.1 = (f32[3,768]{1,0:T(4,128)S(1)}, f32[3,768]{1,0:T(4,128)S(1)}, u32[]{:S(2)}, u32[]{:S(2)}) collective-permute-start(f32[3,768]{1,0:T(4,128)S(1)} %pad_maximum_fusion), channel_id=1, source_target_pairs={{0,16},{8,24},{16,0},{24,8},{1,17},{9,25},{17,1},{25,9},{2,18},{10... | collective-permute-start | bytes 27656 | tf_op jit(solution)/shard_map/ppermute | solution.py:34
  18.9 20.2 %collective-permute-start.2 = (f32[3,768]{1,0:T(4,128)S(1)}, f32[3,768]{1,0:T(4,128)S(1)}, u32[]{:S(2)}, u32[]{:S(2)}) collective-permute-start(f32[3,768]{1,0:T(4,128)S(1)} %pad_maximum_fusion.1), channel_id=1, source_target_pairs={{0,1},{1,0},{2,3},{3,2},{4,5},{5,4},{6,7},{7,6},{8,9},{9,8},{10,11... | collective-permute-start | bytes 27656 | tf_op jit(solution)/shard_map/ppermute | solution.py:34
  39.1 26.9 %collective-permute-start.3 = (f32[3,768]{1,0:T(4,128)S(1)}, f32[3,768]{1,0:T(4,128)S(1)}, u32[]{:S(2)}, u32[]{:S(2)}) collective-permute-start(f32[3,768]{1,0:T(4,128)S(1)} %pad_maximum_fusion.2), channel_id=1, source_target_pairs={{0,2},{1,3},{2,0},{3,1},{4,6},{5,7},{6,4},{7,5},{8,10},{9,11},{10,... | collective-permute-start | bytes 27656 | tf_op jit(solution)/shard_map/ppermute | solution.py:34
  66.0 15.0 %collective-permute-start.4 = (f32[3,768]{1,0:T(4,128)S(1)}, f32[3,768]{1,0:T(4,128)S(1)}, u32[]{:S(2)}, u32[]{:S(2)}) collective-permute-start(f32[3,768]{1,0:T(4,128)S(1)} %pad_maximum_fusion.3), channel_id=1, source_target_pairs={{0,4},{1,5},{2,6},{3,7},{4,0},{5,1},{6,2},{7,3},{8,12},{9,13},{10,... | collective-permute-start | bytes 27656 | tf_op jit(solution)/shard_map/ppermute | solution.py:34
  82.3 8.8 %collective-permute-start.5 = (bf16[4,48,768]{2,1,0:T(8,128)(2,1)S(1)}, bf16[4,48,768]{2,1,0:T(8,128)(2,1)S(1)}, u32[]{:S(2)}, u32[]{:S(2)}) collective-permute-start(bf16[4,48,768]{2,1,0:T(8,128)(2,1)S(1)} %edge_rows.1), channel_id=1, source_target_pairs={{0,1},{1,0},{2,3},{3,2},{4,5},{5,4},{6,7},{7,6},{8,9},{9,8},{10,11... | collective-permute-start | bytes 884744 | tf_op jit(solution)/shard_map/ppermute | solution.py:34
  92.2 2.6 %collective-permute-start.6 = (f32[3,384]{1,0:T(4,128)S(1)}, f32[3,384]{1,0:T(4,128)S(1)}, u32[]{:S(2)}, u32[]{:S(2)}) collective-permute-start(f32[3,384]{1,0:T(4,128)S(1)} %get-tuple-element.144), channel_id=1, source_target_pairs={{0,8},{8,0},{16,24},{24,16},{1,9},{9,1},{17,25},{25,17},{2,10},{10... | collective-permute-start | bytes 13832 | tf_op jit(solution)/shard_map/ppermute | solution.py:34
  94.9 3.2 %collective-permute-start.7 = (f32[3,384]{1,0:T(4,128)S(1)}, f32[3,384]{1,0:T(4,128)S(1)}, u32[]{:S(2)}, u32[]{:S(2)}) collective-permute-start(f32[3,384]{1,0:T(4,128)S(1)} %pad_maximum_fusion.6), channel_id=1, source_target_pairs={{0,16},{8,24},{16,0},{24,8},{1,17},{9,25},{17,1},{25,9},{2,18},{10... | collective-permute-start | bytes 13832 | tf_op jit(solution)/shard_map/ppermute | solution.py:34
  98.1 2.5 %collective-permute-start.8 = (f32[3,384]{1,0:T(4,128)S(1)}, f32[3,384]{1,0:T(4,128)S(1)}, u32[]{:S(2)}, u32[]{:S(2)}) collective-permute-start(f32[3,384]{1,0:T(4,128)S(1)} %pad_maximum_fusion.7), channel_id=1, source_target_pairs={{0,1},{1,0},{2,3},{3,2},{4,5},{5,4},{6,7},{7,6},{8,9},{9,8},{10,11... | collective-permute-start | bytes 13832 | tf_op jit(solution)/shard_map/ppermute | solution.py:34
  100.7 5.2 %collective-permute-start.9 = (f32[3,384]{1,0:T(4,128)S(1)}, f32[3,384]{1,0:T(4,128)S(1)}, u32[]{:S(2)}, u32[]{:S(2)}) collective-permute-start(f32[3,384]{1,0:T(4,128)S(1)} %pad_maximum_fusion.8), channel_id=1, source_target_pairs={{0,2},{1,3},{2,0},{3,1},{4,6},{5,7},{6,4},{7,5},{8,10},{9,11},{10,... | collective-permute-start | bytes 13832 | tf_op jit(solution)/shard_map/ppermute | solution.py:34
  106.0 3.4 %collective-permute-start.10 = (f32[3,384]{1,0:T(4,128)S(1)}, f32[3,384]{1,0:T(4,128)S(1)}, u32[]{:S(2)}, u32[]{:S(2)}) collective-permute-start(f32[3,384]{1,0:T(4,128)S(1)} %pad_maximum_fusion.9), channel_id=1, source_target_pairs={{0,4},{1,5},{2,6},{3,7},{4,0},{5,1},{6,2},{7,3},{8,12},{9,13},{10,... | collective-permute-start | bytes 13832 | tf_op jit(solution)/shard_map/ppermute | solution.py:34
  113.9 4.3 %collective-permute-start.11 = (f32[2,384]{1,0:T(2,128)S(1)}, f32[2,384]{1,0:T(2,128)S(1)}, u32[]{:S(2)}, u32[]{:S(2)}) collective-permute-start(f32[2,384]{1,0:T(2,128)S(1)} %get-tuple-element.162), channel_id=1, source_target_pairs={{0,8},{8,0},{16,24},{24,16},{1,9},{9,1},{17,25},{25,17},{2,10},{10... | collective-permute-start | bytes 9224 | tf_op jit(solution)/shard_map/ppermute | solution.py:34
  118.2 2.4 collective-permute-start.12
  120.7 2.4 collective-permute-start.13
  125.6 4.2 %collective-permute-start.15 = (f32[2,384]{1,0:T(2,128)S(1)}, f32[2,384]{1,0:T(2,128)S(1)}, u32[]{:S(2)}, u32[]{:S(2)}) collective-permute-start(f32[2,384]{1,0:T(2,128)S(1)} %add.237), channel_id=1, source_target_pairs={{0,4},{1,5},{2,6},{3,7},{4,0},{5,1},{6,2},{7,3},{8,12},{9,13},{10,... | collective-permute-start | bytes 9224 | tf_op jit(solution)/shard_map/ppermute | solution.py:34
  131.9 4.1 %collective-permute-start.16 = (bf16[4,48,384]{2,1,0:T(8,128)(2,1)S(1)}, bf16[4,48,384]{2,1,0:T(8,128)(2,1)S(1)}, u32[]{:S(2)}, u32[]{:S(2)}) collective-permute-start(bf16[4,48,384]{2,1,0:T(8,128)(2,1)S(1)} %get-tuple-element.168), channel_id=1, source_target_pairs={{0,1},{1,0},{2,3},{3,2},{4,5},{5,4},{6,7},{7,6},{8,9},{9,8},{10,11... | collective-permute-start | bytes 442376 | tf_op jit(solution)/shard_map/ppermute | solution.py:34
  143.6 58.0 %all-to-all-start.1 = ((bf16[8,128,768]{2,1,0:T(8,128)(2,1)}), bf16[8,128,768]{2,1,0:T(8,128)(2,1)}, u32[]{:S(2)}, u32[]{:S(2)}) async-start(bf16[8,128,768]{2,1,0:T(8,128)(2,1)} %get-tuple-element.181), calls=%async_computation.1 | async-start | bytes 3145728 | tf_op jit(solution)/shard_map/all_to_all | solution.py:1483
  155.3 8.3 %collective-permute-start.17 = (bf16[776,768]{1,0:T(8,128)(2,1)S(1)}, bf16[776,768]{1,0:T(8,128)(2,1)S(1)}, u32[]{:S(2)}, u32[]{:S(2)}) collective-permute-start(bf16[776,768]{1,0:T(8,128)(2,1)S(1)} %get-tuple-element.188), channel_id=1, source_target_pairs={{0,8},{8,0},{16,24},{24,16},{1,9},{9,1},{17,25},{25,17},{2,10},{10... | collective-permute-start | bytes 3575816 | tf_op jit(solution)/shard_map/ppermute | solution.py:34
  164.6 8.6 %collective-permute-start.18 = (bf16[200,768]{1,0:T(8,128)(2,1)S(1)}, bf16[200,768]{1,0:T(8,128)(2,1)S(1)}, u32[]{:S(2)}, u32[]{:S(2)}) collective-permute-start(bf16[200,768]{1,0:T(8,128)(2,1)S(1)} %get-tuple-element.191), channel_id=1, source_target_pairs={{0,16},{1,17},{2,18},{3,19},{4,20},{5,21},{6,22},{7,23},{8,24},{9,... | collective-permute-start | bytes 921608 | tf_op jit(solution)/shard_map/ppermute | solution.py:1044
  165.9 21.0 %collective-permute-start.19 = (bf16[200,768]{1,0:T(8,128)(2,1)S(1)}, bf16[200,768]{1,0:T(8,128)(2,1)S(1)}, u32[]{:S(2)}, u32[]{:S(2)}) collective-permute-start(bf16[200,768]{1,0:T(8,128)(2,1)S(1)} %get-tuple-element.192), channel_id=1, source_target_pairs={{0,1},{1,0},{2,3},{3,2},{4,5},{5,4},{6,7},{7,6},{8,9},{9,8},{10,11... | collective-permute-start | bytes 921608 | tf_op jit(solution)/shard_map/ppermute | solution.py:1044
  167.1 19.8 %collective-permute-start.20 = (bf16[200,768]{1,0:T(8,128)(2,1)S(1)}, bf16[200,768]{1,0:T(8,128)(2,1)S(1)}, u32[]{:S(2)}, u32[]{:S(2)}) collective-permute-start(bf16[200,768]{1,0:T(8,128)(2,1)S(1)} %get-tuple-element.193), channel_id=1, source_target_pairs={{0,17},{1,16},{2,19},{3,18},{4,21},{5,20},{6,23},{7,22},{8,25},{9,... | collective-permute-start | bytes 921608 | tf_op jit(solution)/shard_map/ppermute | solution.py:1044
  187.7 3.4 %collective-permute-start.21 = (bf16[56,768]{1,0:T(8,128)(2,1)S(1)}, bf16[56,768]{1,0:T(8,128)(2,1)S(1)}, u32[]{:S(2)}, u32[]{:S(2)}) collective-permute-start(bf16[56,768]{1,0:T(8,128)(2,1)S(1)} %get-tuple-element.196), channel_id=1, source_target_pairs={{0,2},{1,3},{2,0},{3,1},{4,6},{5,7},{6,4},{7,5},{8,10},{9,11},{10,... | collective-permute-start | bytes 258056 | tf_op jit(solution)/shard_map/ppermute | solution.py:1044
  187.8 5.3 %collective-permute-start.22 = (bf16[56,768]{1,0:T(8,128)(2,1)S(1)}, bf16[56,768]{1,0:T(8,128)(2,1)S(1)}, u32[]{:S(2)}, u32[]{:S(2)}) collective-permute-start(bf16[56,768]{1,0:T(8,128)(2,1)S(1)} %get-tuple-element.197), channel_id=1, source_target_pairs={{0,4},{1,5},{2,6},{3,7},{4,0},{5,1},{6,2},{7,3},{8,12},{9,13},{10,... | collective-permute-start | bytes 258056 | tf_op jit(solution)/shard_map/ppermute | solution.py:1044
  188.1 9.6 %collective-permute-start.23 = (bf16[56,768]{1,0:T(8,128)(2,1)S(1)}, bf16[56,768]{1,0:T(8,128)(2,1)S(1)}, u32[]{:S(2)}, u32[]{:S(2)}) collective-permute-start(bf16[56,768]{1,0:T(8,128)(2,1)S(1)} %get-tuple-element.198), channel_id=1, source_target_pairs={{0,6},{1,7},{2,4},{3,5},{4,2},{5,3},{6,0},{7,1},{8,14},{9,15},{10,... | collective-permute-start | bytes 258056 | tf_op jit(solution)/shard_map/ppermute | solution.py:1044
  198.3 3.3 %collective-permute-start.24 = (bf16[48,768]{1,0:T(8,128)(2,1)S(1)}, bf16[48,768]{1,0:T(8,128)(2,1)S(1)}, u32[]{:S(2)}, u32[]{:S(2)}) collective-permute-start(bf16[48,768]{1,0:T(8,128)(2,1)S(1)} %get-tuple-element.199), channel_id=1, source_target_pairs={{0,2},{1,3},{2,0},{3,1},{4,6},{5,7},{6,4},{7,5},{8,10},{9,11},{10,... | collective-permute-start | bytes 221192 | tf_op jit(solution)/shard_map/ppermute | solution.py:1044
  198.4 7.7 %collective-permute-start.26 = (bf16[48,768]{1,0:T(8,128)(2,1)S(1)}, bf16[48,768]{1,0:T(8,128)(2,1)S(1)}, u32[]{:S(2)}, u32[]{:S(2)}) collective-permute-start(bf16[48,768]{1,0:T(8,128)(2,1)S(1)} %get-tuple-element.199), channel_id=1, source_target_pairs={{0,4},{1,5},{2,6},{3,7},{4,0},{5,1},{6,2},{7,3},{8,12},{9,13},{10,... | collective-permute-start | bytes 221192 | tf_op jit(solution)/shard_map/ppermute | solution.py:1044
  199.7 7.5 %collective-permute-start.25 = (bf16[48,768]{1,0:T(8,128)(2,1)S(1)}, bf16[48,768]{1,0:T(8,128)(2,1)S(1)}, u32[]{:S(2)}, u32[]{:S(2)}) collective-permute-start(bf16[48,768]{1,0:T(8,128)(2,1)S(1)} %get-tuple-element.199), channel_id=1, source_target_pairs={{0,6},{1,7},{2,4},{3,5},{4,2},{5,3},{6,0},{7,1},{8,14},{9,15},{10,... | collective-permute-start | bytes 221192 | tf_op jit(solution)/shard_map/ppermute | solution.py:1044
  201.6 40.4 %all-to-all-start.2 = ((bf16[8,128,768]{2,1,0:T(8,128)(2,1)}), bf16[8,128,768]{2,1,0:T(8,128)(2,1)}, u32[]{:S(2)}, u32[]{:S(2)}) async-start(bf16[8,128,768]{2,1,0:T(8,128)(2,1)} %get-tuple-element.212), calls=%async_computation.2 | async-start | bytes 3145728 | tf_op jit(solution)/shard_map/all_to_all | solution.py:1483
  207.2 20.6 %collective-permute-start.27 = (bf16[192,768]{1,0:T(8,128)(2,1)S(1)}, bf16[192,768]{1,0:T(8,128)(2,1)S(1)}, u32[]{:S(2)}, u32[]{:S(2)}) collective-permute-start(bf16[192,768]{1,0:T(8,128)(2,1)S(1)} %maximum_select_fusion.3), channel_id=1, source_target_pairs={{0,16},{1,17},{2,18},{3,19},{4,20},{5,21},{6,22},{7,23},{8,24},{9,... | collective-permute-start | bytes 884744 | tf_op jit(solution)/shard_map/ppermute | solution.py:1044
  208.0 27.2 %collective-permute-start.28 = (bf16[192,768]{1,0:T(8,128)(2,1)S(1)}, bf16[192,768]{1,0:T(8,128)(2,1)S(1)}, u32[]{:S(2)}, u32[]{:S(2)}) collective-permute-start(bf16[192,768]{1,0:T(8,128)(2,1)S(1)} %maximum_select_fusion.3), channel_id=1, source_target_pairs={{0,1},{1,0},{2,3},{3,2},{4,5},{5,4},{6,7},{7,6},{8,9},{9,8},{10,11... | collective-permute-start | bytes 884744 | tf_op jit(solution)/shard_map/ppermute | solution.py:1044
  208.2 27.1 %collective-permute-start.29 = (bf16[192,768]{1,0:T(8,128)(2,1)S(1)}, bf16[192,768]{1,0:T(8,128)(2,1)S(1)}, u32[]{:S(2)}, u32[]{:S(2)}) collective-permute-start(bf16[192,768]{1,0:T(8,128)(2,1)S(1)} %maximum_select_fusion.3), channel_id=1, source_target_pairs={{0,17},{1,16},{2,19},{3,18},{4,21},{5,20},{6,23},{7,22},{8,25},{9,... | collective-permute-start | bytes 884744 | tf_op jit(solution)/shard_map/ppermute | solution.py:1044
  235.9 4.0 %collective-permute-start.30 = (bf16[768,768]{1,0:T(8,128)(2,1)S(1)}, bf16[768,768]{1,0:T(8,128)(2,1)S(1)}, u32[]{:S(2)}, u32[]{:S(2)}) collective-permute-start(bf16[768,768]{1,0:T(8,128)(2,1)S(1)} %maximum_select_fusion.half_ref), channel_id=1, source_target_pairs={{0,8},{8,0},{16,24},{24,16},{1,9},{9,1},{17,25},{25,17},{2,10},{10... | collective-permute-start | bytes 3538952 | tf_op jit(solution)/shard_map/ppermute | solution.py:34
  (27 other events, 228.4 us)

commit v7 on v6

--- a/solution.py
+++ b/solution.py
@@ -84,24 +84,21 @@
     def slot_window(self, slot):
         upper = (2 * self.ref[1]) // self.ref[2]
         target = jnp.bitwise_xor(slot // self.slots, upper)
-        return self.ref[3 + target * self.slots + slot % self.slots]
+        return self.ref[4 + target * self.slots + slot % self.slots]
 
     def length(self, window):
-        return self.ref[3 + self.windows + self.ref[0] * self.windows + window]
+        return self.ref[4 + self.windows + self.ref[0] * self.windows + window]
 
     def slot_count(self, slot, rows):
         return jnp.clip(self.length(self.slot_window(slot)) - self.ref[1] * rows, 0, rows)
 
     def half_limit(self, slot, half):
         place = jnp.bitwise_xor(self.ref[1], half)
-        window = self.ref[3 + place * self.slots + slot]
+        window = self.ref[4 + place * self.slots + slot]
         return jnp.clip(self.length(window) - half * HALF_WINDOW_ROWS, 0, HALF_WINDOW_ROWS)
 
     def row_count(self):
-        start = 3 + self.windows
-        count = self.ref.shape[0] - start
-        added = lax.fori_loop(0, count, lambda i, held: held + self.ref[start + i], jnp.int32(0))
-        return added.astype(jnp.float32)
+        return self.ref[3].astype(jnp.float32)
 
 
 def kernel_call(body, name, inputs, specs, outputs, out_specs, scratch=(), flops=0, bytes_moved=0, grant=8 << 20):
@@ -527,8 +524,9 @@
 
 
 def gelu_slope(half, bend, square):
+    rise = 1.0 + bend
     inner = GELU_SLOPE + (12.0 * GELU_SLOPE * GELU_CUBE) * square
-    return (0.5 + 0.5 * bend) + (half - half * bend * bend) * inner
+    return rise * (0.5 + (half * inner) * (2.0 - rise))
 
 
 def activated(values, inside, slope, offset):
@@ -762,7 +760,7 @@
             norm = (values[:, lanes] - centre[:, lanes]) * scale[:, lanes]
             half_pre = norm * gain[:, lanes] + offset[:, lanes]
             bend, square = bent(half_pre)
-            act = jnp.where(inside, half_pre + half_pre * bend, 0.0)
+            act = jnp.where(inside, half_pre * (1.0 + bend), 0.0)
             act_ref[piece, here, lanes] = act.astype(jnp.bfloat16)
             grad = grad_ref[piece, here, lanes] * gelu_slope(half_pre, bend, square)
             grad = jnp.where(inside, grad, 0.0)
@@ -1370,7 +1368,8 @@
     rows = segment // 2
     pieces = 2 * slots
     places = jnp.stack([lax.axis_index("grp"), lax.axis_index("seq"), jnp.int32(seq_count)])
-    facts = jnp.concatenate([places.astype(jnp.int32), assignment[0], lengths])
+    row_count = jnp.sum(lengths, keepdims=True)
+    facts = jnp.concatenate([places.astype(jnp.int32), row_count, assignment[0], lengths])
     entry_params = jnp.stack([entry_gain, entry_shift, pointwise_bias])
     middle_params = jnp.stack([middle_gain, middle_shift])
 

time: 251 us -> 250 us (level)
  Pallas kernels: 78.5 us -> 75.6 us
    pallas_call x17, Pallas kernels: 50.8 us -> 47.9 us  [kernel_call(): pl.pallas_call(body, in_specs=specs, out_specs=out_specs, out_shape=outpu...]
  transfers between devices with their start and end apart: 34 -> 34, of which waited for: 23 -> 23; matrix products, arithmetic and copies ran while one was open for 6% -> 6% of each run, Pallas kernels for 20% -> 19%
where the time goes in v7:
time: 250 us; the launch traced here: 246 us
  waiting for transfers between devices  83 us (33%)
  Pallas kernels  75.6 us (30%)
  starting transfers between devices  58 us (23%)
  local copies, waits for them, and re-layouts  14.7 us (6%)
  matrix products  11.5 us (5%)
    pallas_call x17, Pallas kernels, kernel_call(): pl.pallas_call(body, in_specs=specs, out_specs=out_specs, out_shape=outpu...  47.9 us
    ppermute x19, waiting for transfers between devices, from_partner(): lax.ppermute(block, axis, [(place, place ^ mask) for place in range(count)])  47 us
    ppermute x12, waiting for transfers between devices, from_flat_partner(): lax.ppermute(block, ('grp', 'seq'), [(place, place ^ mask) for place in r...  35.9 us
    ppermute x19, starting transfers between devices, from_partner(): lax.ppermute(block, axis, [(place, place ^ mask) for place in range(count)])  31.7 us
    unnamed x50, local copies, waits for them, and re-layouts  12.7 us
    ppermute x12, starting transfers between devices, from_flat_partner(): lax.ppermute(block, ('grp', 'seq'), [(place, place ^ mask) for place in r...  10.8 us
    pallas_call x2, Pallas kernels, unpool(): pl.pallas_call(functools.partial(unpool_body, slots, slot, windows), in_s...  10.4 us
    all_to_all x2, starting transfers between devices, send_back(): return lax.all_to_all(block, 'seq', split_axis=0, concat_axis=0, tiled=True)  9.89 us
  transfers between devices with their start and end apart: 34, of which 23 were waited for; matrix products, arithmetic and copies ran while one was open for 6% of the time, Pallas kernels for 19%

profile of v7, /device:TPU:17, one launch (start us, length us, event | category | flops | bytes accessed | tf_op | source)
XLA Modules:
  0.0 246.0 jit_solution(15645108167222599369)
XLA Ops:
  0.6 7.5 %pool.1 = (bf16[16,128,768]{2,1,0:T(8,128)(2,1)}, f32[3,768]{1,0:T(4,128)S(1)}) custom-call(s32[1,16]{1,0:T(1,128)} %order_ref.1, s32[64]{0:T(128)} %lengths_ref.1, f32[16,256,768]{2,1,0:T(8,128)} %signal_ref.3), custom_call_target="tpu_custom_call" | custom-call | flops 15728640 | bytes 15728640 | tf_op jit(solution)/shard_map/pool/pallas_call | solution.py:105
  8.2 5.6 %all-to-all-start = ((bf16[16,128,768]{2,1,0:T(8,128)(2,1)}), bf16[16,128,768]{2,1,0:T(8,128)(2,1)S(1)}, u32[]{:S(2)}, u32[]{:S(2)}) async-start(bf16[16,128,768]{2,1,0:T(8,128)(2,1)} %get-tuple-element.121.pooled_ref), calls=%async_computation | async-start | bytes 6291456 | tf_op jit(solution)/shard_map/all_to_all | solution.py:1377
  21.5 2.0 copy-done.5
  27.8 11.2 %collective-permute-done.2 = f32[3,768]{1,0:T(4,128)S(1)} collective-permute-done((f32[3,768]{1,0:T(4,128)S(1)}, f32[3,768]{1,0:T(4,128)S(1)}, u32[]{:S(2)}, u32[]{:S(2)}) %collective-permute-start.2) | collective-permute-done | bytes 9248 | tf_op jit(solution)/shard_map/ppermute | solution.py:34
  41.0 2.8 %copy-done.4 = f32[2048,768]{1,0:T(8,128)S(1)} copy-done((f32[2048,768]{1,0:T(8,128)S(1)}, f32[2048,768]{1,0:T(8,128)}, u32[]{:S(2)}) %copy-start.4) | copy-done | bytes 6291480
  43.7 4.1 %prepare_cotangent.1 = (bf16[2048,768]{1,0:T(8,128)(2,1)S(1)}, f32[2048,384]{1,0:T(8,128)S(1)}, f32[1,768]{1,0:T(1,128)S(1)}) custom-call(s32[84]{0:T(128)S(1)} %concatenate.61.facts_ref, f32[2048,768]{1,0:T(8,128)S(1)} %copy-done.4, bf16[384,768]{1,0:T(8,128)(2,1)S(1)} %get-tuple-element.205.weight_ref), custom_call_target="tpu_custom_call" | custom-call | flops 1207959552 | bytes 12582912 | tf_op jit(solution)/shard_map/prepare_cotangent/pallas_call | solution.py:454
  49.6 8.5 %first_marks.1.first_ref = bf16[16,128,768]{2,1,0:T(8,128)(2,1)} custom-call(s32[84]{0:T(128)S(1)} %concatenate.61.facts_ref, f32[16,256,768]{2,1,0:T(8,128)} %signal_ref.3), custom_call_target="tpu_custom_call" | custom-call | flops 4718592 | bytes 15728640 | tf_op jit(solution)/shard_map/first_marks/pallas_call | solution.py:105
  58.1 7.8 %collective-permute-done.3 = f32[3,768]{1,0:T(4,128)S(1)} collective-permute-done((f32[3,768]{1,0:T(4,128)S(1)}, f32[3,768]{1,0:T(4,128)S(1)}, u32[]{:S(2)}, u32[]{:S(2)}) %collective-permute-start.3) | collective-permute-done | bytes 9248 | tf_op jit(solution)/shard_map/ppermute | solution.py:34
  66.3 14.8 %collective-permute-done.4 = f32[3,768]{1,0:T(4,128)S(1)} collective-permute-done((f32[3,768]{1,0:T(4,128)S(1)}, f32[3,768]{1,0:T(4,128)S(1)}, u32[]{:S(2)}, u32[]{:S(2)}) %collective-permute-start.4) | collective-permute-done | bytes 9248 | tf_op jit(solution)/shard_map/ppermute | solution.py:34
  83.6 7.1 %convolve.1 = (bf16[4,512,768]{2,1,0:T(8,128)(2,1)S(1)}, f32[4,512,384]{2,1,0:T(8,128)S(1)}, f32[3,384]{1,0:T(4,128)S(1)}) custom-call(s32[84]{0:T(128)S(1)} %concatenate.61.facts_ref, bf16[16,128,768]{2,1,0:T(8,128)(2,1)S(1)} %all-to-all-done.arrived_ref.refs_4_, f32[3,768]{1,0:T(4,128)S(1)} %get-tuple-element.268.moments_ref.entry_ref.refs_6_, ...), custom_call_target="tpu_custom_call" | custom-call | flops 3623878656 | bytes 6291456 | tf_op jit(solution)/shard_map/convolve/pallas_call | solution.py:105
  99.8 3.4 %collective-permute-start.9 = (f32[3,384]{1,0:T(4,128)S(1)}, f32[3,384]{1,0:T(4,128)S(1)}, u32[]{:S(2)}, u32[]{:S(2)}) collective-permute-start(f32[3,384]{1,0:T(4,128)S(1)} %pad_maximum_fusion.8), channel_id=1, source_target_pairs={{0,2},{1,3},{2,0},{3,1},{4,6},{5,7},{6,4},{7,5},{8,10},{9,11},{10,... | collective-permute-start | bytes 13832 | tf_op jit(solution)/shard_map/ppermute | solution.py:34
  108.3 4.0 %middle_norm.1 = (bf16[4,512,384]{2,1,0:T(8,128)(2,1)S(1)}, f32[4,512,384]{2,1,0:T(8,128)S(1)}, f32[4,512,384]{2,1,0:T(8,128)S(1)}, f32[2,384]{1,0:T(2,128)S(1)}) custom-call(s32[84]{0:T(128)S(1)} %concatenate.61.facts_ref, f32[4,512,384]{2,1,0:T(8,128)S(1)} %get-tuple-element.140.out_ref, f32[4,64,384]{2,1,0:T(8,128)S(1)} %get-tuple-element.143.strip_ref, ...), custom_call_target="tpu_custom_call" | custom-call | flops 31457280 | bytes 14155776 | tf_op jit(solution)/shard_map/middle_norm/pallas_call | solution.py:105
  112.3 4.0 %collective-permute-start.11 = (f32[2,384]{1,0:T(2,128)S(1)}, f32[2,384]{1,0:T(2,128)S(1)}, u32[]{:S(2)}, u32[]{:S(2)}) collective-permute-start(f32[2,384]{1,0:T(2,128)S(1)} %get-tuple-element.162), channel_id=1, source_target_pairs={{0,8},{8,0},{16,24},{24,16},{1,9},{9,1},{17,25},{25,17},{2,10},{10... | collective-permute-start | bytes 9224 | tf_op jit(solution)/shard_map/ppermute | solution.py:34
  120.0 2.1 collective-permute-done.13
  126.0 2.9 %fusion.6.pointwise_ref = f32[768,384]{1,0:T(8,128)} fusion(bf16[2048,768]{1,0:T(8,128)(2,1)S(1)} %copy-done.1, bf16[2048,384]{1,0:T(8,128)(2,1)S(1)} %bitcast.19), kind=kOutput, calls=%fused_computation.61 | convolution fusion | flops 1207959552 | bytes 5898240 | tf_op jit(solution)/shard_map/rd,rf->df/dot_general | solution.py:1469
  131.3 2.8 %convolution_bitcast_fusion.1.centre_ref = f32[768,384]{1,0:T(8,128)} fusion(bf16[4,512,768]{2,1,0:T(8,128)(2,1)S(1)} %get-tuple-element.169, bf16[4,512,384]{2,1,0:T(8,128)(2,1)S(1)} %get-tuple-element.170), kind=kOutput, calls=%fused_computation.1 | convolution fusion | flops 1207959552 | bytes 5898240 | tf_op jit(solution)/shard_map/hrc,hrf->cf/dot_general | solution.py:1477
  134.7 7.6 %entry_grad.1 = (bf16[8,128,768]{2,1,0:T(8,128)(2,1)}, bf16[8,128,768]{2,1,0:T(8,128)(2,1)}, bf16[4,512,768]{2,1,0:T(8,128)(2,1)}, f32[3,768]{1,0:T(4,128)S(1)}) custom-call(s32[84]{0:T(128)S(1)} %concatenate.61.facts_ref, f32[4,3,592,128]{3,2,1,0:T(8,128)S(1)} %get-tuple-element.167.padded_ref, bf16[4,48,384]{2,1,0:T(8,128)(2,1)S(1)} %collective-permute-done.16.border_ref, ...), custom_call_target="tpu_custom_call" | custom-call | flops 3623878656 | bytes 23592960 | tf_op jit(solution)/shard_map/entry_grad/pallas_call | solution.py:105
  142.3 5.4 %all-to-all-start.1 = ((bf16[8,128,768]{2,1,0:T(8,128)(2,1)}), bf16[8,128,768]{2,1,0:T(8,128)(2,1)}, u32[]{:S(2)}, u32[]{:S(2)}) async-start(bf16[8,128,768]{2,1,0:T(8,128)(2,1)} %get-tuple-element.181), calls=%async_computation.1 | async-start | bytes 3145728 | tf_op jit(solution)/shard_map/all_to_all | solution.py:1482
  147.7 5.7 %convolution_bitcast_fusion.sides_ref = f32[768,768]{1,0:T(8,128)S(1)} fusion(bf16[4,512,768]{2,1,0:T(8,128)(2,1)} %copy-done.8, bf16[4,512,768]{2,1,0:T(8,128)(2,1)} %get-tuple-element.183), kind=kOutput, calls=%fused_computation | convolution fusion | flops 2415919104 | bytes 8650752 | tf_op jit(solution)/shard_map/hrc,hrf->cf/dot_general | solution.py:1491
  154.1 5.7 %collective-permute-start.17 = (bf16[776,768]{1,0:T(8,128)(2,1)S(1)}, bf16[776,768]{1,0:T(8,128)(2,1)S(1)}, u32[]{:S(2)}, u32[]{:S(2)}) collective-permute-start(bf16[776,768]{1,0:T(8,128)(2,1)S(1)} %get-tuple-element.188), channel_id=1, source_target_pairs={{0,8},{8,0},{16,24},{24,16},{1,9},{9,1},{17,25},{25,17},{2,10},{10... | collective-permute-start | bytes 3575816 | tf_op jit(solution)/shard_map/ppermute | solution.py:34
  159.8 2.5 %collective-permute-done.17.other_ref = bf16[776,768]{1,0:T(8,128)(2,1)S(1)} collective-permute-done((bf16[776,768]{1,0:T(8,128)(2,1)S(1)}, bf16[776,768]{1,0:T(8,128)(2,1)S(1)}, u32[]{:S(2)}, u32[]{:S(2)}) %collective-permute-start.17) | collective-permute-done | bytes 1191968 | tf_op jit(solution)/shard_map/ppermute | solution.py:34
  166.0 5.9 %collective-permute-done.18.refs_0_ = bf16[200,768]{1,0:T(8,128)(2,1)S(1)} collective-permute-done((bf16[200,768]{1,0:T(8,128)(2,1)S(1)}, bf16[200,768]{1,0:T(8,128)(2,1)S(1)}, u32[]{:S(2)}, u32[]{:S(2)}) %collective-permute-start.18) | collective-permute-done | bytes 307232 | tf_op jit(solution)/shard_map/ppermute | solution.py:1042
  171.9 13.7 %collective-permute-done.19.refs_1_ = bf16[200,768]{1,0:T(8,128)(2,1)S(1)} collective-permute-done((bf16[200,768]{1,0:T(8,128)(2,1)S(1)}, bf16[200,768]{1,0:T(8,128)(2,1)S(1)}, u32[]{:S(2)}, u32[]{:S(2)}) %collective-permute-start.19) | collective-permute-done | bytes 307232 | tf_op jit(solution)/shard_map/ppermute | solution.py:1042
  186.8 2.3 collective-permute-start.23
  191.7 4.7 %collective-permute-done.23.refs_2_ = bf16[56,768]{1,0:T(8,128)(2,1)S(1)} collective-permute-done((bf16[56,768]{1,0:T(8,128)(2,1)S(1)}, bf16[56,768]{1,0:T(8,128)(2,1)S(1)}, u32[]{:S(2)}, u32[]{:S(2)}) %collective-permute-start.23) | collective-permute-done | bytes 86048 | tf_op jit(solution)/shard_map/ppermute | solution.py:1042
  200.3 4.5 %all-to-all-start.2 = ((bf16[8,128,768]{2,1,0:T(8,128)(2,1)}), bf16[8,128,768]{2,1,0:T(8,128)(2,1)}, u32[]{:S(2)}, u32[]{:S(2)}) async-start(bf16[8,128,768]{2,1,0:T(8,128)(2,1)} %get-tuple-element.212), calls=%async_computation.2 | async-start | bytes 3145728 | tf_op jit(solution)/shard_map/all_to_all | solution.py:1482
  211.1 9.0 %output_rows.1 = f32[2048,768]{1,0:T(8,128)} custom-call(s32[84]{0:T(128)S(1)} %concatenate.61.facts_ref, bf16[2048,384]{1,0:T(8,128)(2,1)S(1)} %bitcast.20, bf16[384,768]{1,0:T(8,128)(2,1)S(1)} %copy-done.17, bf16[16,128,768]{2,1,0:T(8,128)(2,1)S(1)} %all-to-all-done.arrived_ref.refs_4_, f32[3,768]{1,0:T(4,128)S(1)} %get-tuple-element.269.params_ref.refs_7_), custom_call_target="tpu_custom_call" | custom-call | flops 8455716864 | bytes 88080384 | tf_op jit(solution)/shard_map/output_rows/pallas_call | solution.py:897
  220.7 5.2 %unpool.2.refs_0_ = f32[16,256,768]{2,1,0:T(8,128)} custom-call(s32[84]{0:T(128)S(1)} %concatenate.61.facts_ref, bf16[8,128,768]{2,1,0:T(8,128)(2,1)} %all-to-all-done.1.returned_ref, bf16[16,128,768]{2,1,0:T(8,128)(2,1)} %get-tuple-element.121.pooled_ref, bf16[16,128,768]{2,1,0:T(8,128)(2,1)} %first_marks.1.first_ref, ...), custom_call_target="tpu_custom_call" | custom-call | flops 7864320 | bytes 11010048 | tf_op jit(solution)/shard_map/unpool/pallas_call | solution.py:404
  226.5 7.5 %collective-permute-done.28 = bf16[192,768]{1,0:T(8,128)(2,1)S(1)} collective-permute-done((bf16[192,768]{1,0:T(8,128)(2,1)S(1)}, bf16[192,768]{1,0:T(8,128)(2,1)S(1)}, u32[]{:S(2)}, u32[]{:S(2)}) %collective-permute-start.28) | collective-permute-done | bytes 294944 | tf_op jit(solution)/shard_map/ppermute | solution.py:1042
  236.1 2.2 finish_weights.2
  238.6 2.0 finish_weights.3
  240.6 5.2 %unpool.3 = f32[16,256,768]{2,1,0:T(8,128)} custom-call(s32[84]{0:T(128)S(1)} %concatenate.61.facts_ref, bf16[8,128,768]{2,1,0:T(8,128)(2,1)} %all-to-all-done.2.returned_ref, bf16[16,128,768]{2,1,0:T(8,128)(2,1)} %get-tuple-element.121.pooled_ref, bf16[16,128,768]{2,1,0:T(8,128)(2,1)} %first_marks.1.first_ref, ...), custom_call_target="tpu_custom_call", output_to_operand_aliasing={{}: (7, {})} | custom-call | flops 7864320 | bytes 11010048 | tf_op jit(solution)/shard_map/unpool/pallas_call | solution.py:404
  (149 shorter events, 64.9 us)
Async XLA Ops:
  8.2 73.0 %all-to-all-start = ((bf16[16,128,768]{2,1,0:T(8,128)(2,1)}), bf16[16,128,768]{2,1,0:T(8,128)(2,1)S(1)}, u32[]{:S(2)}, u32[]{:S(2)}) async-start(bf16[16,128,768]{2,1,0:T(8,128)(2,1)} %get-tuple-element.121.pooled_ref), calls=%async_computation | async-start | bytes 6291456 | tf_op jit(solution)/shard_map/all_to_all | solution.py:1377
  15.9 2.9 %collective-permute-start.1 = (f32[3,768]{1,0:T(4,128)S(1)}, f32[3,768]{1,0:T(4,128)S(1)}, u32[]{:S(2)}, u32[]{:S(2)}) collective-permute-start(f32[3,768]{1,0:T(4,128)S(1)} %pad_maximum_fusion), channel_id=1, source_target_pairs={{0,16},{8,24},{16,0},{24,8},{1,17},{9,25},{17,1},{25,9},{2,18},{10... | collective-permute-start | bytes 27656 | tf_op jit(solution)/shard_map/ppermute | solution.py:34
  18.9 20.2 %collective-permute-start.2 = (f32[3,768]{1,0:T(4,128)S(1)}, f32[3,768]{1,0:T(4,128)S(1)}, u32[]{:S(2)}, u32[]{:S(2)}) collective-permute-start(f32[3,768]{1,0:T(4,128)S(1)} %pad_maximum_fusion.1), channel_id=1, source_target_pairs={{0,1},{1,0},{2,3},{3,2},{4,5},{5,4},{6,7},{7,6},{8,9},{9,8},{10,11... | collective-permute-start | bytes 27656 | tf_op jit(solution)/shard_map/ppermute | solution.py:34
  39.1 26.9 %collective-permute-start.3 = (f32[3,768]{1,0:T(4,128)S(1)}, f32[3,768]{1,0:T(4,128)S(1)}, u32[]{:S(2)}, u32[]{:S(2)}) collective-permute-start(f32[3,768]{1,0:T(4,128)S(1)} %pad_maximum_fusion.2), channel_id=1, source_target_pairs={{0,2},{1,3},{2,0},{3,1},{4,6},{5,7},{6,4},{7,5},{8,10},{9,11},{10,... | collective-permute-start | bytes 27656 | tf_op jit(solution)/shard_map/ppermute | solution.py:34
  66.0 15.0 %collective-permute-start.4 = (f32[3,768]{1,0:T(4,128)S(1)}, f32[3,768]{1,0:T(4,128)S(1)}, u32[]{:S(2)}, u32[]{:S(2)}) collective-permute-start(f32[3,768]{1,0:T(4,128)S(1)} %pad_maximum_fusion.3), channel_id=1, source_target_pairs={{0,4},{1,5},{2,6},{3,7},{4,0},{5,1},{6,2},{7,3},{8,12},{9,13},{10,... | collective-permute-start | bytes 27656 | tf_op jit(solution)/shard_map/ppermute | solution.py:34
  81.9 8.8 %collective-permute-start.5 = (bf16[4,48,768]{2,1,0:T(8,128)(2,1)S(1)}, bf16[4,48,768]{2,1,0:T(8,128)(2,1)S(1)}, u32[]{:S(2)}, u32[]{:S(2)}) collective-permute-start(bf16[4,48,768]{2,1,0:T(8,128)(2,1)S(1)} %edge_rows.1), channel_id=1, source_target_pairs={{0,1},{1,0},{2,3},{3,2},{4,5},{5,4},{6,7},{7,6},{8,9},{9,8},{10,11... | collective-permute-start | bytes 884744 | tf_op jit(solution)/shard_map/ppermute | solution.py:34
  91.8 2.6 %collective-permute-start.6 = (f32[3,384]{1,0:T(4,128)S(1)}, f32[3,384]{1,0:T(4,128)S(1)}, u32[]{:S(2)}, u32[]{:S(2)}) collective-permute-start(f32[3,384]{1,0:T(4,128)S(1)} %get-tuple-element.144), channel_id=1, source_target_pairs={{0,8},{8,0},{16,24},{24,16},{1,9},{9,1},{17,25},{25,17},{2,10},{10... | collective-permute-start | bytes 13832 | tf_op jit(solution)/shard_map/ppermute | solution.py:34
  94.4 2.8 %collective-permute-start.7 = (f32[3,384]{1,0:T(4,128)S(1)}, f32[3,384]{1,0:T(4,128)S(1)}, u32[]{:S(2)}, u32[]{:S(2)}) collective-permute-start(f32[3,384]{1,0:T(4,128)S(1)} %pad_maximum_fusion.6), channel_id=1, source_target_pairs={{0,16},{8,24},{16,0},{24,8},{1,17},{9,25},{17,1},{25,9},{2,18},{10... | collective-permute-start | bytes 13832 | tf_op jit(solution)/shard_map/ppermute | solution.py:34
  97.3 2.5 %collective-permute-start.8 = (f32[3,384]{1,0:T(4,128)S(1)}, f32[3,384]{1,0:T(4,128)S(1)}, u32[]{:S(2)}, u32[]{:S(2)}) collective-permute-start(f32[3,384]{1,0:T(4,128)S(1)} %pad_maximum_fusion.7), channel_id=1, source_target_pairs={{0,1},{1,0},{2,3},{3,2},{4,5},{5,4},{6,7},{7,6},{8,9},{9,8},{10,11... | collective-permute-start | bytes 13832 | tf_op jit(solution)/shard_map/ppermute | solution.py:34
  99.8 4.9 %collective-permute-start.9 = (f32[3,384]{1,0:T(4,128)S(1)}, f32[3,384]{1,0:T(4,128)S(1)}, u32[]{:S(2)}, u32[]{:S(2)}) collective-permute-start(f32[3,384]{1,0:T(4,128)S(1)} %pad_maximum_fusion.8), channel_id=1, source_target_pairs={{0,2},{1,3},{2,0},{3,1},{4,6},{5,7},{6,4},{7,5},{8,10},{9,11},{10,... | collective-permute-start | bytes 13832 | tf_op jit(solution)/shard_map/ppermute | solution.py:34
  104.8 3.4 %collective-permute-start.10 = (f32[3,384]{1,0:T(4,128)S(1)}, f32[3,384]{1,0:T(4,128)S(1)}, u32[]{:S(2)}, u32[]{:S(2)}) collective-permute-start(f32[3,384]{1,0:T(4,128)S(1)} %pad_maximum_fusion.9), channel_id=1, source_target_pairs={{0,4},{1,5},{2,6},{3,7},{4,0},{5,1},{6,2},{7,3},{8,12},{9,13},{10,... | collective-permute-start | bytes 13832 | tf_op jit(solution)/shard_map/ppermute | solution.py:34
  112.3 4.8 %collective-permute-start.11 = (f32[2,384]{1,0:T(2,128)S(1)}, f32[2,384]{1,0:T(2,128)S(1)}, u32[]{:S(2)}, u32[]{:S(2)}) collective-permute-start(f32[2,384]{1,0:T(2,128)S(1)} %get-tuple-element.162), channel_id=1, source_target_pairs={{0,8},{8,0},{16,24},{24,16},{1,9},{9,1},{17,25},{25,17},{2,10},{10... | collective-permute-start | bytes 9224 | tf_op jit(solution)/shard_map/ppermute | solution.py:34
  117.2 2.4 collective-permute-start.12
  122.1 2.7 %collective-permute-start.14 = (f32[2,384]{1,0:T(2,128)S(1)}, f32[2,384]{1,0:T(2,128)S(1)}, u32[]{:S(2)}, u32[]{:S(2)}) collective-permute-start(f32[2,384]{1,0:T(2,128)S(1)} %add.236), channel_id=1, source_target_pairs={{0,2},{1,3},{2,0},{3,1},{4,6},{5,7},{6,4},{7,5},{8,10},{9,11},{10,... | collective-permute-start | bytes 9224 | tf_op jit(solution)/shard_map/ppermute | solution.py:34
  124.8 4.1 %collective-permute-start.15 = (f32[2,384]{1,0:T(2,128)S(1)}, f32[2,384]{1,0:T(2,128)S(1)}, u32[]{:S(2)}, u32[]{:S(2)}) collective-permute-start(f32[2,384]{1,0:T(2,128)S(1)} %add.237), channel_id=1, source_target_pairs={{0,4},{1,5},{2,6},{3,7},{4,0},{5,1},{6,2},{7,3},{8,12},{9,13},{10,... | collective-permute-start | bytes 9224 | tf_op jit(solution)/shard_map/ppermute | solution.py:34
  130.7 4.1 %collective-permute-start.16 = (bf16[4,48,384]{2,1,0:T(8,128)(2,1)S(1)}, bf16[4,48,384]{2,1,0:T(8,128)(2,1)S(1)}, u32[]{:S(2)}, u32[]{:S(2)}) collective-permute-start(bf16[4,48,384]{2,1,0:T(8,128)(2,1)S(1)} %get-tuple-element.168), channel_id=1, source_target_pairs={{0,1},{1,0},{2,3},{3,2},{4,5},{5,4},{6,7},{7,6},{8,9},{9,8},{10,11... | collective-permute-start | bytes 442376 | tf_op jit(solution)/shard_map/ppermute | solution.py:34
  142.3 58.0 %all-to-all-start.1 = ((bf16[8,128,768]{2,1,0:T(8,128)(2,1)}), bf16[8,128,768]{2,1,0:T(8,128)(2,1)}, u32[]{:S(2)}, u32[]{:S(2)}) async-start(bf16[8,128,768]{2,1,0:T(8,128)(2,1)} %get-tuple-element.181), calls=%async_computation.1 | async-start | bytes 3145728 | tf_op jit(solution)/shard_map/all_to_all | solution.py:1482
  154.1 8.2 %collective-permute-start.17 = (bf16[776,768]{1,0:T(8,128)(2,1)S(1)}, bf16[776,768]{1,0:T(8,128)(2,1)S(1)}, u32[]{:S(2)}, u32[]{:S(2)}) collective-permute-start(bf16[776,768]{1,0:T(8,128)(2,1)S(1)} %get-tuple-element.188), channel_id=1, source_target_pairs={{0,8},{8,0},{16,24},{24,16},{1,9},{9,1},{17,25},{25,17},{2,10},{10... | collective-permute-start | bytes 3575816 | tf_op jit(solution)/shard_map/ppermute | solution.py:34
  163.3 8.6 %collective-permute-start.18 = (bf16[200,768]{1,0:T(8,128)(2,1)S(1)}, bf16[200,768]{1,0:T(8,128)(2,1)S(1)}, u32[]{:S(2)}, u32[]{:S(2)}) collective-permute-start(bf16[200,768]{1,0:T(8,128)(2,1)S(1)} %get-tuple-element.191), channel_id=1, source_target_pairs={{0,16},{1,17},{2,18},{3,19},{4,20},{5,21},{6,22},{7,23},{8,24},{9,... | collective-permute-start | bytes 921608 | tf_op jit(solution)/shard_map/ppermute | solution.py:1042
  164.6 21.0 %collective-permute-start.19 = (bf16[200,768]{1,0:T(8,128)(2,1)S(1)}, bf16[200,768]{1,0:T(8,128)(2,1)S(1)}, u32[]{:S(2)}, u32[]{:S(2)}) collective-permute-start(bf16[200,768]{1,0:T(8,128)(2,1)S(1)} %get-tuple-element.192), channel_id=1, source_target_pairs={{0,1},{1,0},{2,3},{3,2},{4,5},{5,4},{6,7},{7,6},{8,9},{9,8},{10,11... | collective-permute-start | bytes 921608 | tf_op jit(solution)/shard_map/ppermute | solution.py:1042
  165.8 19.9 %collective-permute-start.20 = (bf16[200,768]{1,0:T(8,128)(2,1)S(1)}, bf16[200,768]{1,0:T(8,128)(2,1)S(1)}, u32[]{:S(2)}, u32[]{:S(2)}) collective-permute-start(bf16[200,768]{1,0:T(8,128)(2,1)S(1)} %get-tuple-element.193), channel_id=1, source_target_pairs={{0,17},{1,16},{2,19},{3,18},{4,21},{5,20},{6,23},{7,22},{8,25},{9,... | collective-permute-start | bytes 921608 | tf_op jit(solution)/shard_map/ppermute | solution.py:1042
  186.4 3.4 %collective-permute-start.21 = (bf16[56,768]{1,0:T(8,128)(2,1)S(1)}, bf16[56,768]{1,0:T(8,128)(2,1)S(1)}, u32[]{:S(2)}, u32[]{:S(2)}) collective-permute-start(bf16[56,768]{1,0:T(8,128)(2,1)S(1)} %get-tuple-element.196), channel_id=1, source_target_pairs={{0,2},{1,3},{2,0},{3,1},{4,6},{5,7},{6,4},{7,5},{8,10},{9,11},{10,... | collective-permute-start | bytes 258056 | tf_op jit(solution)/shard_map/ppermute | solution.py:1042
  186.5 5.3 %collective-permute-start.22 = (bf16[56,768]{1,0:T(8,128)(2,1)S(1)}, bf16[56,768]{1,0:T(8,128)(2,1)S(1)}, u32[]{:S(2)}, u32[]{:S(2)}) collective-permute-start(bf16[56,768]{1,0:T(8,128)(2,1)S(1)} %get-tuple-element.197), channel_id=1, source_target_pairs={{0,4},{1,5},{2,6},{3,7},{4,0},{5,1},{6,2},{7,3},{8,12},{9,13},{10,... | collective-permute-start | bytes 258056 | tf_op jit(solution)/shard_map/ppermute | solution.py:1042
  186.8 9.6 %collective-permute-start.23 = (bf16[56,768]{1,0:T(8,128)(2,1)S(1)}, bf16[56,768]{1,0:T(8,128)(2,1)S(1)}, u32[]{:S(2)}, u32[]{:S(2)}) collective-permute-start(bf16[56,768]{1,0:T(8,128)(2,1)S(1)} %get-tuple-element.198), channel_id=1, source_target_pairs={{0,6},{1,7},{2,4},{3,5},{4,2},{5,3},{6,0},{7,1},{8,14},{9,15},{10,... | collective-permute-start | bytes 258056 | tf_op jit(solution)/shard_map/ppermute | solution.py:1042
  197.0 3.3 %collective-permute-start.24 = (bf16[48,768]{1,0:T(8,128)(2,1)S(1)}, bf16[48,768]{1,0:T(8,128)(2,1)S(1)}, u32[]{:S(2)}, u32[]{:S(2)}) collective-permute-start(bf16[48,768]{1,0:T(8,128)(2,1)S(1)} %get-tuple-element.199), channel_id=1, source_target_pairs={{0,2},{1,3},{2,0},{3,1},{4,6},{5,7},{6,4},{7,5},{8,10},{9,11},{10,... | collective-permute-start | bytes 221192 | tf_op jit(solution)/shard_map/ppermute | solution.py:1042
  197.1 7.7 %collective-permute-start.26 = (bf16[48,768]{1,0:T(8,128)(2,1)S(1)}, bf16[48,768]{1,0:T(8,128)(2,1)S(1)}, u32[]{:S(2)}, u32[]{:S(2)}) collective-permute-start(bf16[48,768]{1,0:T(8,128)(2,1)S(1)} %get-tuple-element.199), channel_id=1, source_target_pairs={{0,4},{1,5},{2,6},{3,7},{4,0},{5,1},{6,2},{7,3},{8,12},{9,13},{10,... | collective-permute-start | bytes 221192 | tf_op jit(solution)/shard_map/ppermute | solution.py:1042
  198.3 7.5 %collective-permute-start.25 = (bf16[48,768]{1,0:T(8,128)(2,1)S(1)}, bf16[48,768]{1,0:T(8,128)(2,1)S(1)}, u32[]{:S(2)}, u32[]{:S(2)}) collective-permute-start(bf16[48,768]{1,0:T(8,128)(2,1)S(1)} %get-tuple-element.199), channel_id=1, source_target_pairs={{0,6},{1,7},{2,4},{3,5},{4,2},{5,3},{6,0},{7,1},{8,14},{9,15},{10,... | collective-permute-start | bytes 221192 | tf_op jit(solution)/shard_map/ppermute | solution.py:1042
  200.3 40.4 %all-to-all-start.2 = ((bf16[8,128,768]{2,1,0:T(8,128)(2,1)}), bf16[8,128,768]{2,1,0:T(8,128)(2,1)}, u32[]{:S(2)}, u32[]{:S(2)}) async-start(bf16[8,128,768]{2,1,0:T(8,128)(2,1)} %get-tuple-element.212), calls=%async_computation.2 | async-start | bytes 3145728 | tf_op jit(solution)/shard_map/all_to_all | solution.py:1482
  205.9 20.6 %collective-permute-start.27 = (bf16[192,768]{1,0:T(8,128)(2,1)S(1)}, bf16[192,768]{1,0:T(8,128)(2,1)S(1)}, u32[]{:S(2)}, u32[]{:S(2)}) collective-permute-start(bf16[192,768]{1,0:T(8,128)(2,1)S(1)} %maximum_select_fusion.3), channel_id=1, source_target_pairs={{0,16},{1,17},{2,18},{3,19},{4,20},{5,21},{6,22},{7,23},{8,24},{9,... | collective-permute-start | bytes 884744 | tf_op jit(solution)/shard_map/ppermute | solution.py:1042
  206.8 27.1 %collective-permute-start.28 = (bf16[192,768]{1,0:T(8,128)(2,1)S(1)}, bf16[192,768]{1,0:T(8,128)(2,1)S(1)}, u32[]{:S(2)}, u32[]{:S(2)}) collective-permute-start(bf16[192,768]{1,0:T(8,128)(2,1)S(1)} %maximum_select_fusion.3), channel_id=1, source_target_pairs={{0,1},{1,0},{2,3},{3,2},{4,5},{5,4},{6,7},{7,6},{8,9},{9,8},{10,11... | collective-permute-start | bytes 884744 | tf_op jit(solution)/shard_map/ppermute | solution.py:1042
  206.9 27.0 %collective-permute-start.29 = (bf16[192,768]{1,0:T(8,128)(2,1)S(1)}, bf16[192,768]{1,0:T(8,128)(2,1)S(1)}, u32[]{:S(2)}, u32[]{:S(2)}) collective-permute-start(bf16[192,768]{1,0:T(8,128)(2,1)S(1)} %maximum_select_fusion.3), channel_id=1, source_target_pairs={{0,17},{1,16},{2,19},{3,18},{4,21},{5,20},{6,23},{7,22},{8,25},{9,... | collective-permute-start | bytes 884744 | tf_op jit(solution)/shard_map/ppermute | solution.py:1042
  234.6 4.0 %collective-permute-start.30 = (bf16[768,768]{1,0:T(8,128)(2,1)S(1)}, bf16[768,768]{1,0:T(8,128)(2,1)S(1)}, u32[]{:S(2)}, u32[]{:S(2)}) collective-permute-start(bf16[768,768]{1,0:T(8,128)(2,1)S(1)} %maximum_select_fusion.half_ref), channel_id=1, source_target_pairs={{0,8},{8,0},{16,24},{24,16},{1,9},{9,1},{17,25},{25,17},{2,10},{10... | collective-permute-start | bytes 3538952 | tf_op jit(solution)/shard_map/ppermute | solution.py:34
  (27 other events, 227.7 us)

commit v8 on v7

--- a/solution.py
+++ b/solution.py
@@ -21,6 +21,7 @@
 PAD = 40
 PADDED_ROWS = HALF_WINDOW_ROWS + 2 * PAD
 EXTRA = 8
+EARLY_SHARE = 8
 GELU_SLOPE = math.sqrt(2.0 / math.pi)
 GELU_CUBE = 0.044715
 
@@ -324,9 +325,10 @@
 
 
 def unpool_body(
-    slots, slot, windows, facts_ref, returned_ref, pooled_ref, first_ref, moments_ref, sums_ref,
-    params_ref, *refs,
+    slots, slot, windows, span, segment_rows, facts_ref, returned_ref, pooled_ref, first_ref,
+    moments_ref, sums_ref, params_ref, *refs,
 ):
+    start, row, size = span
     out_ref, back, low, mark, held, arrivals, departures = refs[-7:]
     targets, rows, width = back.shape
     columns = held.shape[1]
@@ -335,16 +337,22 @@
     def arrival(target):
         place = target * slots + slot
         return [
-            pltpu.make_async_copy(returned_ref.at[target], back.at[target], arrivals.at[target, 0]),
-            pltpu.make_async_copy(pooled_ref.at[place], low.at[target], arrivals.at[target, 1]),
-            pltpu.make_async_copy(first_ref.at[place], mark.at[target], arrivals.at[target, 2]),
+            pltpu.make_async_copy(
+                returned_ref.at[target, pl.ds(start, size)], back.at[target], arrivals.at[target, 0]
+            ),
+            pltpu.make_async_copy(
+                pooled_ref.at[place, pl.ds(row, size)], low.at[target], arrivals.at[target, 1]
+            ),
+            pltpu.make_async_copy(
+                first_ref.at[place, pl.ds(row, size)], mark.at[target], arrivals.at[target, 2]
+            ),
         ]
 
     def departure(target, column):
         window = facts.slot_window(target * slots + slot)
         return pltpu.make_async_copy(
             held.at[target, column],
-            out_ref.at[window, :, pl.ds(column * LANES, LANES)],
+            out_ref.at[window, pl.ds(2 * row, 2 * size), pl.ds(column * LANES, LANES)],
             departures.at[target, column],
         )
 
@@ -364,8 +372,8 @@
     def work(target, carry):
         for copy in arrival(target):
             copy.wait()
-        inside = lax.broadcasted_iota(jnp.int32, (rows, LANES), 0) < facts.slot_count(
-            target * slots + slot, rows
+        inside = lax.broadcasted_iota(jnp.int32, (rows, LANES), 0) < (
+            facts.slot_count(target * slots + slot, segment_rows) - row
         )
         for column, lanes in enumerate(column_slices(width)):
             centred = low[target, :, lanes].astype(jnp.float32) - centre[:, lanes]
@@ -390,9 +398,12 @@
     lax.fori_loop(0, targets, finish, 0)
 
 
-def unpool(facts, returned, pooled, first, moments, sums, params, slots, slot, held_output):
-    targets, rows, width = returned.shape
-    windows, columns = targets * slots, width // LANES
+def unpool(
+    facts, returned, pooled, first, moments, sums, params, slots, slot, span, held_output
+):
+    windows, all_rows, width = pooled.shape
+    targets, rows = windows // slots, span[2]
+    columns = width // LANES
     inputs = [facts, in_hbm(returned), in_hbm(pooled), in_hbm(first), moments, sums, params]
     specs = [SMEM, HBM, HBM, HBM, VMEM, VMEM, VMEM]
     aliases = {}
@@ -402,10 +413,10 @@
         specs.append(HBM)
     block = (targets, rows, width)
     return pl.pallas_call(
-        functools.partial(unpool_body, slots, slot, windows),
+        functools.partial(unpool_body, slots, slot, windows, span, all_rows),
         in_specs=specs,
         out_specs=HBM,
-        out_shape=pltpu.HBM((windows, 2 * rows, width), jnp.float32),
+        out_shape=pltpu.HBM((windows, 2 * all_rows, width), jnp.float32),
         input_output_aliases=aliases,
         scratch_shapes=[
             pltpu.VMEM(block, jnp.bfloat16),
@@ -908,10 +919,15 @@
         out_shape=shape((blocks * rows, width), jnp.float32),
         compiler_params=pltpu.CompilerParams(vmem_limit_bytes=16 << 20),
         cost_estimate=pl.CostEstimate(
-            flops=2 * act.size * width * 7, bytes_accessed=8 * arrived.size * 7, transcendentals=0
+            flops=2 * act.size * width * 40 // 10, bytes_accessed=8 * arrived.size * 40 // 10, transcendentals=0
         ),
         name="output_rows",
     )(facts, act, weight, arrived, params)
+
+
+def transfer_rows(rows, slots):
+    early = -(-rows // EARLY_SHARE // 8) * 8
+    return [rows + early, rows - early] + [rows] * (slots - 2)
 
 
 def entry_grad_body(slots, windows, facts_ref, padded_ref, border_ref, weight_ref, *refs):
@@ -930,10 +946,26 @@
     skip = BORDER - DILATION_STEP
     sums_ref[...] = jnp.zeros_like(sums_ref)
 
+    early = sent_refs[0].shape[1] - rows
+
     def departure(slot, source):
-        return pltpu.make_async_copy(
-            packed.at[slot, source], sent_refs[slot].at[source], departures.at[slot, source]
-        )
+        if slot != 1:
+            target = sent_refs[slot].at[source, pl.ds(0, rows)]
+            return [
+                pltpu.make_async_copy(packed.at[slot, source], target, departures.at[slot, source])
+            ]
+        return [
+            pltpu.make_async_copy(
+                packed.at[1, source, pl.ds(0, early)],
+                sent_refs[0].at[source, pl.ds(rows, early)],
+                departures.at[1, source],
+            ),
+            pltpu.make_async_copy(
+                packed.at[1, source, pl.ds(early, rows - early)],
+                sent_refs[1].at[source],
+                departures.at[slots, source],
+            ),
+        ]
 
     def keeping(piece):
         return pltpu.make_async_copy(
@@ -989,7 +1021,8 @@
         if piece == 0:
             keeping(piece).start()
         for part in range(per_half):
-            departure(slot, half * per_half + part).start()
+            for copy in departure(slot, half * per_half + part):
+                copy.start()
         if piece + 1 < pieces:
             keeping(piece + 1).start()
     sums_ref[0:1] = (sums_ref[0:1] - centre * sums_ref[1:2]) * scale
@@ -998,7 +1031,8 @@
         keeping(piece).wait()
     for slot in range(slots):
         for source in range(sources):
-            departure(slot, source).wait()
+            for copy in departure(slot, source):
+                copy.wait()
 
 
 def entry_grad(
@@ -1015,7 +1049,10 @@
         inputs,
         [SMEM] + [VMEM] * (len(inputs) - 1),
         [
-            *[pltpu.HBM((sources, rows, width), jnp.bfloat16)] * slots,
+            *[
+                pltpu.HBM((sources, size, width), jnp.bfloat16)
+                for size in transfer_rows(rows, slots)
+            ],
             pltpu.HBM((pieces, HALF_WINDOW_ROWS, 2 * inner), jnp.bfloat16),
             shape((3, width), jnp.float32),
         ],
@@ -1024,7 +1061,7 @@
             pltpu.VMEM((2, inner // LANES, PADDED_ROWS, LANES), jnp.float32),
             pltpu.VMEM((slots, sources, rows, width), jnp.bfloat16),
             pltpu.VMEM((pieces, *taps_shape), jnp.bfloat16),
-            pltpu.SemaphoreType.DMA((slots, sources)),
+            pltpu.SemaphoreType.DMA((slots + 1, sources)),
             pltpu.SemaphoreType.DMA((pieces,)),
         ],
         flops=2 * pieces * HALF_WINDOW_ROWS * 3 * inner * width,
@@ -1506,10 +1543,12 @@
             )
             returned += [send_back(block) for block in later]
         if number == 0:
-            signal_gradient = unpool(
-                facts, returned[0], outgoing, first_chosen, entry_moments, entry_sums,
-                entry_params, slots, 0, None,
-            )
+            early = returned[0].shape[1] - rows
+            for slot, span in ((0, (0, 0, rows)), (1, (rows, 0, early))):
+                signal_gradient = unpool(
+                    facts, returned[0], outgoing, first_chosen, entry_moments, entry_sums,
+                    entry_params, slots, slot, span, signal_gradient,
+                )
             activations = output_rows(
                 facts, flat_act, pointwise_low, arrived, entry_params, slots, windows
             )
@@ -1522,10 +1561,16 @@
     begun = finish_weights(facts, buffer, 1, None)
     other, *begun = lax.optimization_barrier((other, *begun))
     dilated_kernel_gradient, pointwise_kernel_gradient = finish_weights(facts, other, 0, begun)
+    signal_gradient, dilated_kernel_gradient, pointwise_kernel_gradient = (
+        lax.optimization_barrier(
+            (signal_gradient, dilated_kernel_gradient, pointwise_kernel_gradient)
+        )
+    )
     for slot in range(1, slots):
+        span = (0, early, rows - early) if slot == 1 else (0, 0, rows)
         signal_gradient = unpool(
             facts, returned[slot], outgoing, first_chosen, entry_moments, entry_sums,
-            entry_params, slots, slot, signal_gradient,
+            entry_params, slots, slot, span, signal_gradient,
         )
     return (
         activations,

time: 250 us -> 249 us (level)
  Pallas kernels: 75.6 us -> 78.2 us
    pallas_call x2 -> x3, Pallas kernels: 10.4 us -> 12.9 us  [unpool(): pl.pallas_call(functools.partial(unpool_body, slots, slot, windows, span,...]
  transfers between devices with their start and end apart: 34 -> 34, of which waited for: 23 -> 23; matrix products, arithmetic and copies ran while one was open for 6% -> 6% of each run, Pallas kernels for 19% -> 21%
where the time goes in v8:
time: 249 us; the launch traced here: 247 us
  waiting for transfers between devices  82 us (33%)
  Pallas kernels  78.2 us (31%)
  starting transfers between devices  57.5 us (23%)
  local copies, waits for them, and re-layouts  14.7 us (6%)
  matrix products  11.4 us (5%)
    pallas_call x17, Pallas kernels, kernel_call(): pl.pallas_call(body, in_specs=specs, out_specs=out_specs, out_shape=outpu...  47.9 us
    ppermute x19, waiting for transfers between devices, from_partner(): lax.ppermute(block, axis, [(place, place ^ mask) for place in range(count)])  47 us
    ppermute x12, waiting for transfers between devices, from_flat_partner(): lax.ppermute(block, ('grp', 'seq'), [(place, place ^ mask) for place in r...  34.9 us
    ppermute x19, starting transfers between devices, from_partner(): lax.ppermute(block, axis, [(place, place ^ mask) for place in range(count)])  31.1 us
    pallas_call x3, Pallas kernels, unpool(): pl.pallas_call(functools.partial(unpool_body, slots, slot, windows, span,...  12.9 us
    unnamed x50, local copies, waits for them, and re-layouts  12.8 us
    ppermute x12, starting transfers between devices, from_flat_partner(): lax.ppermute(block, ('grp', 'seq'), [(place, place ^ mask) for place in r...  10.8 us
    all_to_all x2, starting transfers between devices, send_back(): return lax.all_to_all(block, 'seq', split_axis=0, concat_axis=0, tiled=True)  9.91 us
  transfers between devices with their start and end apart: 34, of which 23 were waited for; matrix products, arithmetic and copies ran while one was open for 6% of the time, Pallas kernels for 21%

profile of v8, /device:TPU:17, one launch (start us, length us, event | category | flops | bytes accessed | tf_op | source)
XLA Modules:
  0.0 247.0 jit_solution(18105344861788488463)
XLA Ops:
  0.6 7.5 %pool.1 = (bf16[16,128,768]{2,1,0:T(8,128)(2,1)}, f32[3,768]{1,0:T(4,128)S(1)}) custom-call(s32[1,16]{1,0:T(1,128)} %order_ref.1, s32[64]{0:T(128)} %lengths_ref.1, f32[16,256,768]{2,1,0:T(8,128)} %signal_ref.3), custom_call_target="tpu_custom_call" | custom-call | flops 15728640 | bytes 15728640 | tf_op jit(solution)/shard_map/pool/pallas_call | solution.py:106
  8.2 5.6 %all-to-all-start = ((bf16[16,128,768]{2,1,0:T(8,128)(2,1)}), bf16[16,128,768]{2,1,0:T(8,128)(2,1)S(1)}, u32[]{:S(2)}, u32[]{:S(2)}) async-start(bf16[16,128,768]{2,1,0:T(8,128)(2,1)} %get-tuple-element.124.pooled_ref), calls=%async_computation | async-start | bytes 6291456 | tf_op jit(solution)/shard_map/all_to_all | solution.py:1414
  27.9 11.2 %collective-permute-done.2 = f32[3,768]{1,0:T(4,128)S(1)} collective-permute-done((f32[3,768]{1,0:T(4,128)S(1)}, f32[3,768]{1,0:T(4,128)S(1)}, u32[]{:S(2)}, u32[]{:S(2)}) %collective-permute-start.2) | collective-permute-done | bytes 9248 | tf_op jit(solution)/shard_map/ppermute | solution.py:35
  41.0 2.8 %copy-done.4 = f32[2048,768]{1,0:T(8,128)S(1)} copy-done((f32[2048,768]{1,0:T(8,128)S(1)}, f32[2048,768]{1,0:T(8,128)}, u32[]{:S(2)}) %copy-start.4) | copy-done | bytes 6291480
  43.8 4.1 %prepare_cotangent.1 = (bf16[2048,768]{1,0:T(8,128)(2,1)S(1)}, f32[2048,384]{1,0:T(8,128)S(1)}, f32[1,768]{1,0:T(1,128)S(1)}) custom-call(s32[84]{0:T(128)S(1)} %concatenate.61.facts_ref, f32[2048,768]{1,0:T(8,128)S(1)} %copy-done.4, bf16[384,768]{1,0:T(8,128)(2,1)S(1)} %get-tuple-element.208.weight_ref), custom_call_target="tpu_custom_call" | custom-call | flops 1207959552 | bytes 12582912 | tf_op jit(solution)/shard_map/prepare_cotangent/pallas_call | solution.py:465
  49.6 8.5 %first_marks.1.first_ref = bf16[16,128,768]{2,1,0:T(8,128)(2,1)} custom-call(s32[84]{0:T(128)S(1)} %concatenate.61.facts_ref, f32[16,256,768]{2,1,0:T(8,128)} %signal_ref.3), custom_call_target="tpu_custom_call" | custom-call | flops 4718592 | bytes 15728640 | tf_op jit(solution)/shard_map/first_marks/pallas_call | solution.py:106
  58.2 7.8 %collective-permute-done.3 = f32[3,768]{1,0:T(4,128)S(1)} collective-permute-done((f32[3,768]{1,0:T(4,128)S(1)}, f32[3,768]{1,0:T(4,128)S(1)}, u32[]{:S(2)}, u32[]{:S(2)}) %collective-permute-start.3) | collective-permute-done | bytes 9248 | tf_op jit(solution)/shard_map/ppermute | solution.py:35
  66.3 14.8 %collective-permute-done.4 = f32[3,768]{1,0:T(4,128)S(1)} collective-permute-done((f32[3,768]{1,0:T(4,128)S(1)}, f32[3,768]{1,0:T(4,128)S(1)}, u32[]{:S(2)}, u32[]{:S(2)}) %collective-permute-start.4) | collective-permute-done | bytes 9248 | tf_op jit(solution)/shard_map/ppermute | solution.py:35
  83.6 7.1 %convolve.1 = (bf16[4,512,768]{2,1,0:T(8,128)(2,1)S(1)}, f32[4,512,384]{2,1,0:T(8,128)S(1)}, f32[3,384]{1,0:T(4,128)S(1)}) custom-call(s32[84]{0:T(128)S(1)} %concatenate.61.facts_ref, bf16[16,128,768]{2,1,0:T(8,128)(2,1)S(1)} %all-to-all-done.arrived_ref.refs_4_, f32[3,768]{1,0:T(4,128)S(1)} %get-tuple-element.274.moments_ref.entry_ref.refs_6_, ...), custom_call_target="tpu_custom_call" | custom-call | flops 3623878656 | bytes 6291456 | tf_op jit(solution)/shard_map/convolve/pallas_call | solution.py:106
  99.8 3.4 %collective-permute-start.9 = (f32[3,384]{1,0:T(4,128)S(1)}, f32[3,384]{1,0:T(4,128)S(1)}, u32[]{:S(2)}, u32[]{:S(2)}) collective-permute-start(f32[3,384]{1,0:T(4,128)S(1)} %pad_maximum_fusion.8), channel_id=1, source_target_pairs={{0,2},{1,3},{2,0},{3,1},{4,6},{5,7},{6,4},{7,5},{8,10},{9,11},{10,... | collective-permute-start | bytes 13832 | tf_op jit(solution)/shard_map/ppermute | solution.py:35
  108.3 4.0 %middle_norm.1 = (bf16[4,512,384]{2,1,0:T(8,128)(2,1)S(1)}, f32[4,512,384]{2,1,0:T(8,128)S(1)}, f32[4,512,384]{2,1,0:T(8,128)S(1)}, f32[2,384]{1,0:T(2,128)S(1)}) custom-call(s32[84]{0:T(128)S(1)} %concatenate.61.facts_ref, f32[4,512,384]{2,1,0:T(8,128)S(1)} %get-tuple-element.143.out_ref, f32[4,64,384]{2,1,0:T(8,128)S(1)} %get-tuple-element.146.strip_ref, ...), custom_call_target="tpu_custom_call" | custom-call | flops 31457280 | bytes 14155776 | tf_op jit(solution)/shard_map/middle_norm/pallas_call | solution.py:106
  112.3 4.0 %collective-permute-start.11 = (f32[2,384]{1,0:T(2,128)S(1)}, f32[2,384]{1,0:T(2,128)S(1)}, u32[]{:S(2)}, u32[]{:S(2)}) collective-permute-start(f32[2,384]{1,0:T(2,128)S(1)} %get-tuple-element.165), channel_id=1, source_target_pairs={{0,8},{8,0},{16,24},{24,16},{1,9},{9,1},{17,25},{25,17},{2,10},{10... | collective-permute-start | bytes 9224 | tf_op jit(solution)/shard_map/ppermute | solution.py:35
  120.0 2.1 collective-permute-done.13
  126.0 2.8 %fusion.6.pointwise_ref = f32[768,384]{1,0:T(8,128)} fusion(bf16[2048,768]{1,0:T(8,128)(2,1)S(1)} %copy-done.1, bf16[2048,384]{1,0:T(8,128)(2,1)S(1)} %bitcast.19), kind=kOutput, calls=%fused_computation.61 | convolution fusion | flops 1207959552 | bytes 5898240 | tf_op jit(solution)/shard_map/rd,rf->df/dot_general | solution.py:1506
  131.2 2.8 %convolution_bitcast_fusion.1.centre_ref = f32[768,384]{1,0:T(8,128)} fusion(bf16[4,512,768]{2,1,0:T(8,128)(2,1)S(1)} %get-tuple-element.172, bf16[4,512,384]{2,1,0:T(8,128)(2,1)S(1)} %get-tuple-element.173), kind=kOutput, calls=%fused_computation.1 | convolution fusion | flops 1207959552 | bytes 5898240 | tf_op jit(solution)/shard_map/hrc,hrf->cf/dot_general | solution.py:1514
  134.7 7.6 %entry_grad.1 = (bf16[8,144,768]{2,1,0:T(8,128)(2,1)}, bf16[8,112,768]{2,1,0:T(8,128)(2,1)}, bf16[4,512,768]{2,1,0:T(8,128)(2,1)}, f32[3,768]{1,0:T(4,128)S(1)}) custom-call(s32[84]{0:T(128)S(1)} %concatenate.61.facts_ref, f32[4,3,592,128]{3,2,1,0:T(8,128)S(1)} %get-tuple-element.170.padded_ref, bf16[4,48,384]{2,1,0:T(8,128)(2,1)S(1)} %collective-permute-done.16.border_ref, ...), custom_call_target="tpu_custom_call" | custom-call | flops 3623878656 | bytes 23592960 | tf_op jit(solution)/shard_map/entry_grad/pallas_call | solution.py:106
  142.3 5.4 %all-to-all-start.1 = ((bf16[8,144,768]{2,1,0:T(8,128)(2,1)}), bf16[8,144,768]{2,1,0:T(8,128)(2,1)}, u32[]{:S(2)}, u32[]{:S(2)}) async-start(bf16[8,144,768]{2,1,0:T(8,128)(2,1)} %get-tuple-element.184), calls=%async_computation.1 | async-start | bytes 3538944 | tf_op jit(solution)/shard_map/all_to_all | solution.py:1519
  147.7 5.7 %convolution_bitcast_fusion.sides_ref = f32[768,768]{1,0:T(8,128)S(1)} fusion(bf16[4,512,768]{2,1,0:T(8,128)(2,1)} %copy-done.8, bf16[4,512,768]{2,1,0:T(8,128)(2,1)} %get-tuple-element.186), kind=kOutput, calls=%fused_computation | convolution fusion | flops 2415919104 | bytes 8650752 | tf_op jit(solution)/shard_map/hrc,hrf->cf/dot_general | solution.py:1528
  154.1 5.8 %collective-permute-start.17 = (bf16[776,768]{1,0:T(8,128)(2,1)S(1)}, bf16[776,768]{1,0:T(8,128)(2,1)S(1)}, u32[]{:S(2)}, u32[]{:S(2)}) collective-permute-start(bf16[776,768]{1,0:T(8,128)(2,1)S(1)} %get-tuple-element.191), channel_id=1, source_target_pairs={{0,8},{8,0},{16,24},{24,16},{1,9},{9,1},{17,25},{25,17},{2,10},{10... | collective-permute-start | bytes 3575816 | tf_op jit(solution)/shard_map/ppermute | solution.py:35
  159.9 2.5 %collective-permute-done.17.other_ref = bf16[776,768]{1,0:T(8,128)(2,1)S(1)} collective-permute-done((bf16[776,768]{1,0:T(8,128)(2,1)S(1)}, bf16[776,768]{1,0:T(8,128)(2,1)S(1)}, u32[]{:S(2)}, u32[]{:S(2)}) %collective-permute-start.17) | collective-permute-done | bytes 1191968 | tf_op jit(solution)/shard_map/ppermute | solution.py:35
  166.1 5.9 %collective-permute-done.18.refs_0_ = bf16[200,768]{1,0:T(8,128)(2,1)S(1)} collective-permute-done((bf16[200,768]{1,0:T(8,128)(2,1)S(1)}, bf16[200,768]{1,0:T(8,128)(2,1)S(1)}, u32[]{:S(2)}, u32[]{:S(2)}) %collective-permute-start.18) | collective-permute-done | bytes 307232 | tf_op jit(solution)/shard_map/ppermute | solution.py:1079
  172.1 14.5 %collective-permute-done.19.refs_1_ = bf16[200,768]{1,0:T(8,128)(2,1)S(1)} collective-permute-done((bf16[200,768]{1,0:T(8,128)(2,1)S(1)}, bf16[200,768]{1,0:T(8,128)(2,1)S(1)}, u32[]{:S(2)}, u32[]{:S(2)}) %collective-permute-start.19) | collective-permute-done | bytes 307232 | tf_op jit(solution)/shard_map/ppermute | solution.py:1079
  192.4 5.6 %collective-permute-done.23.refs_2_ = bf16[56,768]{1,0:T(8,128)(2,1)S(1)} collective-permute-done((bf16[56,768]{1,0:T(8,128)(2,1)S(1)}, bf16[56,768]{1,0:T(8,128)(2,1)S(1)}, u32[]{:S(2)}, u32[]{:S(2)}) %collective-permute-start.23) | collective-permute-done | bytes 86048 | tf_op jit(solution)/shard_map/ppermute | solution.py:1079
  201.9 4.5 %all-to-all-start.2 = ((bf16[8,112,768]{2,1,0:T(8,128)(2,1)}), bf16[8,112,768]{2,1,0:T(8,128)(2,1)}, u32[]{:S(2)}, u32[]{:S(2)}) async-start(bf16[8,112,768]{2,1,0:T(8,128)(2,1)} %get-tuple-element.215), calls=%async_computation.2 | async-start | bytes 2752512 | tf_op jit(solution)/shard_map/all_to_all | solution.py:1519
  208.1 2.2 collective-permute-start.27
  212.8 9.0 %output_rows.1 = f32[2048,768]{1,0:T(8,128)} custom-call(s32[84]{0:T(128)S(1)} %concatenate.61.facts_ref, bf16[2048,384]{1,0:T(8,128)(2,1)S(1)} %bitcast.20, bf16[384,768]{1,0:T(8,128)(2,1)S(1)} %copy-done.17, bf16[16,128,768]{2,1,0:T(8,128)(2,1)S(1)} %all-to-all-done.arrived_ref.refs_4_, f32[3,768]{1,0:T(4,128)S(1)} %get-tuple-element.275.params_ref.refs_7_), custom_call_target="tpu_custom_call" | custom-call | flops 4831838208 | bytes 50331648 | tf_op jit(solution)/shard_map/output_rows/pallas_call | solution.py:908
  222.3 5.2 %unpool.3.refs_0_ = f32[16,256,768]{2,1,0:T(8,128)} custom-call(s32[84]{0:T(128)S(1)} %concatenate.61.facts_ref, bf16[8,144,768]{2,1,0:T(8,128)(2,1)} %all-to-all-done.1.returned_ref, bf16[16,128,768]{2,1,0:T(8,128)(2,1)} %get-tuple-element.124.pooled_ref, bf16[16,128,768]{2,1,0:T(8,128)(2,1)} %first_marks.1.first_ref, ...), custom_call_target="tpu_custom_call" | custom-call | flops 7864320 | bytes 11010048 | tf_op jit(solution)/shard_map/unpool/pallas_call | solution.py:415
  227.5 3.0 %unpool.4.refs_0_ = f32[16,256,768]{2,1,0:T(8,128)} custom-call(s32[84]{0:T(128)S(1)} %concatenate.61.facts_ref, bf16[8,144,768]{2,1,0:T(8,128)(2,1)} %all-to-all-done.1.returned_ref, bf16[16,128,768]{2,1,0:T(8,128)(2,1)} %get-tuple-element.124.pooled_ref, bf16[16,128,768]{2,1,0:T(8,128)(2,1)} %first_marks.1.first_ref, ...), custom_call_target="tpu_custom_call", output_to_operand_aliasing={{}: (7, {})} | custom-call | flops 983040 | bytes 1376256 | tf_op jit(solution)/shard_map/unpool/pallas_call | solution.py:415
  231.1 4.9 %collective-permute-done.28 = bf16[192,768]{1,0:T(8,128)(2,1)S(1)} collective-permute-done((bf16[192,768]{1,0:T(8,128)(2,1)S(1)}, bf16[192,768]{1,0:T(8,128)(2,1)S(1)}, u32[]{:S(2)}, u32[]{:S(2)}) %collective-permute-start.28) | collective-permute-done | bytes 294944 | tf_op jit(solution)/shard_map/ppermute | solution.py:1079
  237.5 2.2 finish_weights.2
  240.0 2.0 finish_weights.3
  242.1 4.8 %unpool.5 = f32[16,256,768]{2,1,0:T(8,128)} custom-call(s32[84]{0:T(128)S(1)} %concatenate.61.facts_ref, bf16[8,112,768]{2,1,0:T(8,128)(2,1)} %all-to-all-done.2.returned_ref, bf16[16,128,768]{2,1,0:T(8,128)(2,1)} %get-tuple-element.124.pooled_ref, bf16[16,128,768]{2,1,0:T(8,128)(2,1)} %first_marks.1.first_ref, ...), custom_call_target="tpu_custom_call", output_to_operand_aliasing={{}: (7, {})} | custom-call | flops 6881280 | bytes 9633792 | tf_op jit(solution)/shard_map/unpool/pallas_call | solution.py:415
  (150 shorter events, 66.2 us)
Async XLA Ops:
  8.2 73.0 %all-to-all-start = ((bf16[16,128,768]{2,1,0:T(8,128)(2,1)}), bf16[16,128,768]{2,1,0:T(8,128)(2,1)S(1)}, u32[]{:S(2)}, u32[]{:S(2)}) async-start(bf16[16,128,768]{2,1,0:T(8,128)(2,1)} %get-tuple-element.124.pooled_ref), calls=%async_computation | async-start | bytes 6291456 | tf_op jit(solution)/shard_map/all_to_all | solution.py:1414
  15.9 2.9 %collective-permute-start.1 = (f32[3,768]{1,0:T(4,128)S(1)}, f32[3,768]{1,0:T(4,128)S(1)}, u32[]{:S(2)}, u32[]{:S(2)}) collective-permute-start(f32[3,768]{1,0:T(4,128)S(1)} %pad_maximum_fusion), channel_id=1, source_target_pairs={{0,16},{8,24},{16,0},{24,8},{1,17},{9,25},{17,1},{25,9},{2,18},{10... | collective-permute-start | bytes 27656 | tf_op jit(solution)/shard_map/ppermute | solution.py:35
  18.9 20.2 %collective-permute-start.2 = (f32[3,768]{1,0:T(4,128)S(1)}, f32[3,768]{1,0:T(4,128)S(1)}, u32[]{:S(2)}, u32[]{:S(2)}) collective-permute-start(f32[3,768]{1,0:T(4,128)S(1)} %pad_maximum_fusion.1), channel_id=1, source_target_pairs={{0,1},{1,0},{2,3},{3,2},{4,5},{5,4},{6,7},{7,6},{8,9},{9,8},{10,11... | collective-permute-start | bytes 27656 | tf_op jit(solution)/shard_map/ppermute | solution.py:35
  39.1 26.9 %collective-permute-start.3 = (f32[3,768]{1,0:T(4,128)S(1)}, f32[3,768]{1,0:T(4,128)S(1)}, u32[]{:S(2)}, u32[]{:S(2)}) collective-permute-start(f32[3,768]{1,0:T(4,128)S(1)} %pad_maximum_fusion.2), channel_id=1, source_target_pairs={{0,2},{1,3},{2,0},{3,1},{4,6},{5,7},{6,4},{7,5},{8,10},{9,11},{10,... | collective-permute-start | bytes 27656 | tf_op jit(solution)/shard_map/ppermute | solution.py:35
  66.0 15.0 %collective-permute-start.4 = (f32[3,768]{1,0:T(4,128)S(1)}, f32[3,768]{1,0:T(4,128)S(1)}, u32[]{:S(2)}, u32[]{:S(2)}) collective-permute-start(f32[3,768]{1,0:T(4,128)S(1)} %pad_maximum_fusion.3), channel_id=1, source_target_pairs={{0,4},{1,5},{2,6},{3,7},{4,0},{5,1},{6,2},{7,3},{8,12},{9,13},{10,... | collective-permute-start | bytes 27656 | tf_op jit(solution)/shard_map/ppermute | solution.py:35
  82.0 8.7 %collective-permute-start.5 = (bf16[4,48,768]{2,1,0:T(8,128)(2,1)S(1)}, bf16[4,48,768]{2,1,0:T(8,128)(2,1)S(1)}, u32[]{:S(2)}, u32[]{:S(2)}) collective-permute-start(bf16[4,48,768]{2,1,0:T(8,128)(2,1)S(1)} %edge_rows.1), channel_id=1, source_target_pairs={{0,1},{1,0},{2,3},{3,2},{4,5},{5,4},{6,7},{7,6},{8,9},{9,8},{10,11... | collective-permute-start | bytes 884744 | tf_op jit(solution)/shard_map/ppermute | solution.py:35
  91.8 2.6 %collective-permute-start.6 = (f32[3,384]{1,0:T(4,128)S(1)}, f32[3,384]{1,0:T(4,128)S(1)}, u32[]{:S(2)}, u32[]{:S(2)}) collective-permute-start(f32[3,384]{1,0:T(4,128)S(1)} %get-tuple-element.147), channel_id=1, source_target_pairs={{0,8},{8,0},{16,24},{24,16},{1,9},{9,1},{17,25},{25,17},{2,10},{10... | collective-permute-start | bytes 13832 | tf_op jit(solution)/shard_map/ppermute | solution.py:35
  94.4 2.8 %collective-permute-start.7 = (f32[3,384]{1,0:T(4,128)S(1)}, f32[3,384]{1,0:T(4,128)S(1)}, u32[]{:S(2)}, u32[]{:S(2)}) collective-permute-start(f32[3,384]{1,0:T(4,128)S(1)} %pad_maximum_fusion.6), channel_id=1, source_target_pairs={{0,16},{8,24},{16,0},{24,8},{1,17},{9,25},{17,1},{25,9},{2,18},{10... | collective-permute-start | bytes 13832 | tf_op jit(solution)/shard_map/ppermute | solution.py:35
  97.2 2.5 %collective-permute-start.8 = (f32[3,384]{1,0:T(4,128)S(1)}, f32[3,384]{1,0:T(4,128)S(1)}, u32[]{:S(2)}, u32[]{:S(2)}) collective-permute-start(f32[3,384]{1,0:T(4,128)S(1)} %pad_maximum_fusion.7), channel_id=1, source_target_pairs={{0,1},{1,0},{2,3},{3,2},{4,5},{5,4},{6,7},{7,6},{8,9},{9,8},{10,11... | collective-permute-start | bytes 13832 | tf_op jit(solution)/shard_map/ppermute | solution.py:35
  99.8 4.9 %collective-permute-start.9 = (f32[3,384]{1,0:T(4,128)S(1)}, f32[3,384]{1,0:T(4,128)S(1)}, u32[]{:S(2)}, u32[]{:S(2)}) collective-permute-start(f32[3,384]{1,0:T(4,128)S(1)} %pad_maximum_fusion.8), channel_id=1, source_target_pairs={{0,2},{1,3},{2,0},{3,1},{4,6},{5,7},{6,4},{7,5},{8,10},{9,11},{10,... | collective-permute-start | bytes 13832 | tf_op jit(solution)/shard_map/ppermute | solution.py:35
  104.8 3.4 %collective-permute-start.10 = (f32[3,384]{1,0:T(4,128)S(1)}, f32[3,384]{1,0:T(4,128)S(1)}, u32[]{:S(2)}, u32[]{:S(2)}) collective-permute-start(f32[3,384]{1,0:T(4,128)S(1)} %pad_maximum_fusion.9), channel_id=1, source_target_pairs={{0,4},{1,5},{2,6},{3,7},{4,0},{5,1},{6,2},{7,3},{8,12},{9,13},{10,... | collective-permute-start | bytes 13832 | tf_op jit(solution)/shard_map/ppermute | solution.py:35
  112.3 4.8 %collective-permute-start.11 = (f32[2,384]{1,0:T(2,128)S(1)}, f32[2,384]{1,0:T(2,128)S(1)}, u32[]{:S(2)}, u32[]{:S(2)}) collective-permute-start(f32[2,384]{1,0:T(2,128)S(1)} %get-tuple-element.165), channel_id=1, source_target_pairs={{0,8},{8,0},{16,24},{24,16},{1,9},{9,1},{17,25},{25,17},{2,10},{10... | collective-permute-start | bytes 9224 | tf_op jit(solution)/shard_map/ppermute | solution.py:35
  117.2 2.4 collective-permute-start.12
  122.1 2.7 %collective-permute-start.14 = (f32[2,384]{1,0:T(2,128)S(1)}, f32[2,384]{1,0:T(2,128)S(1)}, u32[]{:S(2)}, u32[]{:S(2)}) collective-permute-start(f32[2,384]{1,0:T(2,128)S(1)} %add.236), channel_id=1, source_target_pairs={{0,2},{1,3},{2,0},{3,1},{4,6},{5,7},{6,4},{7,5},{8,10},{9,11},{10,... | collective-permute-start | bytes 9224 | tf_op jit(solution)/shard_map/ppermute | solution.py:35
  124.8 4.1 %collective-permute-start.15 = (f32[2,384]{1,0:T(2,128)S(1)}, f32[2,384]{1,0:T(2,128)S(1)}, u32[]{:S(2)}, u32[]{:S(2)}) collective-permute-start(f32[2,384]{1,0:T(2,128)S(1)} %add.237), channel_id=1, source_target_pairs={{0,4},{1,5},{2,6},{3,7},{4,0},{5,1},{6,2},{7,3},{8,12},{9,13},{10,... | collective-permute-start | bytes 9224 | tf_op jit(solution)/shard_map/ppermute | solution.py:35
  130.6 4.1 %collective-permute-start.16 = (bf16[4,48,384]{2,1,0:T(8,128)(2,1)S(1)}, bf16[4,48,384]{2,1,0:T(8,128)(2,1)S(1)}, u32[]{:S(2)}, u32[]{:S(2)}) collective-permute-start(bf16[4,48,384]{2,1,0:T(8,128)(2,1)S(1)} %get-tuple-element.171), channel_id=1, source_target_pairs={{0,1},{1,0},{2,3},{3,2},{4,5},{5,4},{6,7},{7,6},{8,9},{9,8},{10,11... | collective-permute-start | bytes 442376 | tf_op jit(solution)/shard_map/ppermute | solution.py:35
  142.3 59.6 %all-to-all-start.1 = ((bf16[8,144,768]{2,1,0:T(8,128)(2,1)}), bf16[8,144,768]{2,1,0:T(8,128)(2,1)}, u32[]{:S(2)}, u32[]{:S(2)}) async-start(bf16[8,144,768]{2,1,0:T(8,128)(2,1)} %get-tuple-element.184), calls=%async_computation.1 | async-start | bytes 3538944 | tf_op jit(solution)/shard_map/all_to_all | solution.py:1519
  154.1 8.3 %collective-permute-start.17 = (bf16[776,768]{1,0:T(8,128)(2,1)S(1)}, bf16[776,768]{1,0:T(8,128)(2,1)S(1)}, u32[]{:S(2)}, u32[]{:S(2)}) collective-permute-start(bf16[776,768]{1,0:T(8,128)(2,1)S(1)} %get-tuple-element.191), channel_id=1, source_target_pairs={{0,8},{8,0},{16,24},{24,16},{1,9},{9,1},{17,25},{25,17},{2,10},{10... | collective-permute-start | bytes 3575816 | tf_op jit(solution)/shard_map/ppermute | solution.py:35
  163.4 8.6 %collective-permute-start.18 = (bf16[200,768]{1,0:T(8,128)(2,1)S(1)}, bf16[200,768]{1,0:T(8,128)(2,1)S(1)}, u32[]{:S(2)}, u32[]{:S(2)}) collective-permute-start(bf16[200,768]{1,0:T(8,128)(2,1)S(1)} %get-tuple-element.194), channel_id=1, source_target_pairs={{0,16},{1,17},{2,18},{3,19},{4,20},{5,21},{6,22},{7,23},{8,24},{9,... | collective-permute-start | bytes 921608 | tf_op jit(solution)/shard_map/ppermute | solution.py:1079
  164.7 21.8 %collective-permute-start.19 = (bf16[200,768]{1,0:T(8,128)(2,1)S(1)}, bf16[200,768]{1,0:T(8,128)(2,1)S(1)}, u32[]{:S(2)}, u32[]{:S(2)}) collective-permute-start(bf16[200,768]{1,0:T(8,128)(2,1)S(1)} %get-tuple-element.195), channel_id=1, source_target_pairs={{0,1},{1,0},{2,3},{3,2},{4,5},{5,4},{6,7},{7,6},{8,9},{9,8},{10,11... | collective-permute-start | bytes 921608 | tf_op jit(solution)/shard_map/ppermute | solution.py:1079
  165.9 20.6 %collective-permute-start.20 = (bf16[200,768]{1,0:T(8,128)(2,1)S(1)}, bf16[200,768]{1,0:T(8,128)(2,1)S(1)}, u32[]{:S(2)}, u32[]{:S(2)}) collective-permute-start(bf16[200,768]{1,0:T(8,128)(2,1)S(1)} %get-tuple-element.196), channel_id=1, source_target_pairs={{0,17},{1,16},{2,19},{3,18},{4,21},{5,20},{6,23},{7,22},{8,25},{9,... | collective-permute-start | bytes 921608 | tf_op jit(solution)/shard_map/ppermute | solution.py:1079
  187.3 3.4 %collective-permute-start.21 = (bf16[56,768]{1,0:T(8,128)(2,1)S(1)}, bf16[56,768]{1,0:T(8,128)(2,1)S(1)}, u32[]{:S(2)}, u32[]{:S(2)}) collective-permute-start(bf16[56,768]{1,0:T(8,128)(2,1)S(1)} %get-tuple-element.199), channel_id=1, source_target_pairs={{0,2},{1,3},{2,0},{3,1},{4,6},{5,7},{6,4},{7,5},{8,10},{9,11},{10,... | collective-permute-start | bytes 258056 | tf_op jit(solution)/shard_map/ppermute | solution.py:1079
  188.0 4.3 %collective-permute-start.22 = (bf16[56,768]{1,0:T(8,128)(2,1)S(1)}, bf16[56,768]{1,0:T(8,128)(2,1)S(1)}, u32[]{:S(2)}, u32[]{:S(2)}) collective-permute-start(bf16[56,768]{1,0:T(8,128)(2,1)S(1)} %get-tuple-element.200), channel_id=1, source_target_pairs={{0,4},{1,5},{2,6},{3,7},{4,0},{5,1},{6,2},{7,3},{8,12},{9,13},{10,... | collective-permute-start | bytes 258056 | tf_op jit(solution)/shard_map/ppermute | solution.py:1079
  188.0 10.0 %collective-permute-start.23 = (bf16[56,768]{1,0:T(8,128)(2,1)S(1)}, bf16[56,768]{1,0:T(8,128)(2,1)S(1)}, u32[]{:S(2)}, u32[]{:S(2)}) collective-permute-start(bf16[56,768]{1,0:T(8,128)(2,1)S(1)} %get-tuple-element.201), channel_id=1, source_target_pairs={{0,6},{1,7},{2,4},{3,5},{4,2},{5,3},{6,0},{7,1},{8,14},{9,15},{10,... | collective-permute-start | bytes 258056 | tf_op jit(solution)/shard_map/ppermute | solution.py:1079
  198.6 3.3 %collective-permute-start.24 = (bf16[48,768]{1,0:T(8,128)(2,1)S(1)}, bf16[48,768]{1,0:T(8,128)(2,1)S(1)}, u32[]{:S(2)}, u32[]{:S(2)}) collective-permute-start(bf16[48,768]{1,0:T(8,128)(2,1)S(1)} %get-tuple-element.202), channel_id=1, source_target_pairs={{0,2},{1,3},{2,0},{3,1},{4,6},{5,7},{6,4},{7,5},{8,10},{9,11},{10,... | collective-permute-start | bytes 221192 | tf_op jit(solution)/shard_map/ppermute | solution.py:1079
  198.7 7.7 %collective-permute-start.26 = (bf16[48,768]{1,0:T(8,128)(2,1)S(1)}, bf16[48,768]{1,0:T(8,128)(2,1)S(1)}, u32[]{:S(2)}, u32[]{:S(2)}) collective-permute-start(bf16[48,768]{1,0:T(8,128)(2,1)S(1)} %get-tuple-element.202), channel_id=1, source_target_pairs={{0,4},{1,5},{2,6},{3,7},{4,0},{5,1},{6,2},{7,3},{8,12},{9,13},{10,... | collective-permute-start | bytes 221192 | tf_op jit(solution)/shard_map/ppermute | solution.py:1079
  199.5 7.9 %collective-permute-start.25 = (bf16[48,768]{1,0:T(8,128)(2,1)S(1)}, bf16[48,768]{1,0:T(8,128)(2,1)S(1)}, u32[]{:S(2)}, u32[]{:S(2)}) collective-permute-start(bf16[48,768]{1,0:T(8,128)(2,1)S(1)} %get-tuple-element.202), channel_id=1, source_target_pairs={{0,6},{1,7},{2,4},{3,5},{4,2},{5,3},{6,0},{7,1},{8,14},{9,15},{10,... | collective-permute-start | bytes 221192 | tf_op jit(solution)/shard_map/ppermute | solution.py:1079
  201.9 40.2 %all-to-all-start.2 = ((bf16[8,112,768]{2,1,0:T(8,128)(2,1)}), bf16[8,112,768]{2,1,0:T(8,128)(2,1)}, u32[]{:S(2)}, u32[]{:S(2)}) async-start(bf16[8,112,768]{2,1,0:T(8,128)(2,1)} %get-tuple-element.215), calls=%async_computation.2 | async-start | bytes 2752512 | tf_op jit(solution)/shard_map/all_to_all | solution.py:1519
  207.6 23.5 %collective-permute-start.29 = (bf16[192,768]{1,0:T(8,128)(2,1)S(1)}, bf16[192,768]{1,0:T(8,128)(2,1)S(1)}, u32[]{:S(2)}, u32[]{:S(2)}) collective-permute-start(bf16[192,768]{1,0:T(8,128)(2,1)S(1)} %maximum_select_fusion.3), channel_id=1, source_target_pairs={{0,17},{1,16},{2,19},{3,18},{4,21},{5,20},{6,23},{7,22},{8,25},{9,... | collective-permute-start | bytes 884744 | tf_op jit(solution)/shard_map/ppermute | solution.py:1079
  207.8 28.2 %collective-permute-start.28 = (bf16[192,768]{1,0:T(8,128)(2,1)S(1)}, bf16[192,768]{1,0:T(8,128)(2,1)S(1)}, u32[]{:S(2)}, u32[]{:S(2)}) collective-permute-start(bf16[192,768]{1,0:T(8,128)(2,1)S(1)} %maximum_select_fusion.3), channel_id=1, source_target_pairs={{0,1},{1,0},{2,3},{3,2},{4,5},{5,4},{6,7},{7,6},{8,9},{9,8},{10,11... | collective-permute-start | bytes 884744 | tf_op jit(solution)/shard_map/ppermute | solution.py:1079
  208.1 27.9 %collective-permute-start.27 = (bf16[192,768]{1,0:T(8,128)(2,1)S(1)}, bf16[192,768]{1,0:T(8,128)(2,1)S(1)}, u32[]{:S(2)}, u32[]{:S(2)}) collective-permute-start(bf16[192,768]{1,0:T(8,128)(2,1)S(1)} %maximum_select_fusion.3), channel_id=1, source_target_pairs={{0,16},{1,17},{2,18},{3,19},{4,20},{5,21},{6,22},{7,23},{8,24},{9,... | collective-permute-start | bytes 884744 | tf_op jit(solution)/shard_map/ppermute | solution.py:1079
  236.6 3.4 %collective-permute-start.30 = (bf16[768,768]{1,0:T(8,128)(2,1)S(1)}, bf16[768,768]{1,0:T(8,128)(2,1)S(1)}, u32[]{:S(2)}, u32[]{:S(2)}) collective-permute-start(bf16[768,768]{1,0:T(8,128)(2,1)S(1)} %maximum_select_fusion.half_ref), channel_id=1, source_target_pairs={{0,8},{8,0},{16,24},{24,16},{1,9},{9,1},{17,25},{25,17},{2,10},{10... | collective-permute-start | bytes 3538952 | tf_op jit(solution)/shard_map/ppermute | solution.py:35
  (27 other events, 227.6 us)
